TPU v7x, 512 devices: a whole 4x4x16 slice. The times are simulated.
512 devices in a mesh: member: 16 (over z), tile: 32 (over x, y, core).
Axes of the slice: x: 4, y: 4, z: 16, core: 2. Of those that a mesh axis runs over, the one named last changes fastest.
Arguments:
- adjoint_final: bfloat16 [16, 32, 1024, 192], P('member', None, 'tile'), may hold values from -6 to 6
- states: bfloat16 [2, 16, 32, 1024, 192], P(None, 'member', None, 'tile'), may hold values from -12 to 12
- kernel: float32 [7, 7, 192], replicated, may hold values from -0.875 to 0.875
- norm_gain: float32 [192], replicated, may hold values from 0.1 to 1.9
- up_weight: bfloat16 [192, 768], replicated, may hold values from -0.4375 to 0.4375
- up_bias: float32 [768], replicated, may hold values from -4 to 4
- down_weight: bfloat16 [768, 192], replicated, may hold values from -0.21875 to 0.21875
- obs_cell: int32 [2, 32, 32, 16], P(None, 'tile'), may hold values from 0 to 31
- obs_count: int32 [2, 32, 32], P(None, 'tile'), may hold values from 1 to 16, 256 in all within a row
- obs_value: bfloat16 [2, 32, 32, 16, 192], P(None, 'tile'), may hold values from -6 to 6
- obs_error: bfloat16 [2, 32, 32, 16], P(None, 'tile'), may hold values from 0.099609375 to 1
Outputs:
- adjoint_initial: bfloat16 [16, 32, 1024, 192], P('member', None, 'tile')
Inputs may be any that keep to these rules, and one draw needn't show every extreme that they name: `obs_cell`: a cell number is latitude offset within the band times 32 plus longitude offset within the tile. `obs_count`: the counts of one band and time add up to 256, and the largest of them is 16.
All inputs are finite; a program needn't handle non-finite values.
Results may differ from a plain program's by a relative error of at most 0.006.
Values may be sent and summed in bfloat16 or wider, within the bound.
No kernel may reach another device: no remote copies, remote signals or barrier semaphores. Data moves between devices by JAX's collectives and lax.ppermute only.
A program may use at most 64 MiB of HBM per device.

v0:
```python
import math

import jax
import jax.numpy as jnp
from jax import lax
from jax.sharding import PartitionSpec as P

slope_coef = math.sqrt(2.0 / math.pi)
cubic_coef = 0.044715
norm_eps = 1e-06


def extended(array, sides, width):
    for axis, dim in sides:
        peers, length = (lax.axis_size(axis), array.shape[dim])
        up = [(i, (i + 1) % peers) for i in range(peers)]
        down = [(j, i) for i, j in up]
        last = lax.slice_in_dim(array, length - width, length, axis=dim)
        initial = lax.slice_in_dim(array, 0, width, axis=dim)
        before = lax.ppermute(last, axis, up)
        after = lax.ppermute(initial, axis, down)
        array = jnp.concatenate([before, array, after], axis=dim)
    return array


def gelu_slope(preact):
    inner_arg = slope_coef * (preact + cubic_coef * preact * preact * preact)
    tanh_val = jnp.tanh(inner_arg)
    return 0.5 * (1.0 + tanh_val) + 0.5 * preact * (1.0 - tanh_val * tanh_val) * slope_coef * (
        1.0 + 3.0 * cubic_coef * preact * preact
    )


def wrap_edges(field_in):
    return extended(field_in, (("tile", 1),), 3)


def pad_rows(field_in):
    return jnp.pad(field_in, ((3, 3), (0, 0), (0, 0)))


def depthwise(padded, kernel, lat_count, lon_width):
    summed = jnp.zeros((lat_count, lon_width, padded.shape[2]), jnp.float32)
    for row_tap in range(7):
        for col_tap in range(7):
            summed = (
                summed
                + kernel[row_tap, col_tap]
                * padded[row_tap : row_tap + lat_count, col_tap : col_tap + lon_width]
            )
    return summed


def depthwise_adjoint(padded, kernel, lat_count, lon_width):
    summed = jnp.zeros((lat_count, lon_width, padded.shape[2]), jnp.float32)
    for row_tap in range(7):
        for col_tap in range(7):
            summed = (
                summed
                + kernel[row_tap, col_tap]
                * padded[
                    6 - row_tap : 6 - row_tap + lat_count, 6 - col_tap : 6 - col_tap + lon_width
                ]
            )
    return summed


def departures(sampled_raw, values, errors, live_mask):
    members = lax.axis_size("member")
    sampled = sampled_raw.astype(jnp.float32)
    summed, squares = lax.psum((sampled, sampled * sampled), "member")
    ens_mean = summed / members
    ens_var = squares / members - ens_mean * ens_mean
    ratio = (sampled - values.astype(jnp.float32)) / (
        errors.astype(jnp.float32)[..., None] + ens_var
    )
    return jnp.where(live_mask[..., None], ratio, 0.0).astype(jnp.bfloat16)


def local_index(band_cells, lon_width, band_rows):
    band_ids = jnp.arange(band_cells.shape[0], dtype=jnp.int32)[:, None]
    return (band_ids * band_rows + band_cells // lon_width) * lon_width + band_cells % lon_width


def scatter_rows(row_vals, flat_index, cell_total, channels):
    target = jnp.zeros((cell_total, channels), jnp.float32)
    return target.at[flat_index.reshape(-1)].add(row_vals.reshape(-1, channels).astype(jnp.float32))


def obs_forcing(state_now, cell_ids, counts, values, errors):
    lat_count, lon_width, channels = state_now.shape
    tile_count = lax.axis_size("tile")
    band_rows = lat_count // tile_count
    slot_count = cell_ids.shape[1]
    banded = lax.all_to_all(state_now, "tile", split_axis=0, concat_axis=1, tiled=True)
    tile_ids = jnp.arange(tile_count, dtype=jnp.int32)[:, None]
    band_index = (
        cell_ids // lon_width * (tile_count * lon_width)
        + tile_ids * lon_width
        + cell_ids % lon_width
    )
    sampled = banded.reshape(-1, channels)[band_index]
    live_mask = jnp.arange(slot_count, dtype=jnp.int32)[None, :] < counts[:, None]
    dep_rows = departures(sampled, values, errors, live_mask)
    got_rows, got_cells = (
        lax.all_to_all(dep_rows, "tile", split_axis=0, concat_axis=0, tiled=True),
        lax.all_to_all(cell_ids, "tile", split_axis=0, concat_axis=0, tiled=True),
    )
    forcing = scatter_rows(
        got_rows, local_index(got_cells, lon_width, band_rows), lat_count * lon_width, channels
    )
    return forcing.reshape(lat_count, lon_width, channels)


def member_step(adjoint, state, forcing, kernel, norm_gain, up_weight, up_bias, down_weight):
    lat_count, lon_width, channels = state.shape
    hidden = depthwise(
        pad_rows(wrap_edges(state).astype(jnp.float32)), kernel, lat_count, lon_width
    )
    centred = hidden - jnp.mean(hidden, axis=-1, keepdims=True)
    inv_std = lax.rsqrt(jnp.mean(centred * centred, axis=-1, keepdims=True) + norm_eps)
    unit_norm = centred * inv_std
    normed = (unit_norm * norm_gain).astype(jnp.bfloat16)
    preact = (
        jnp.dot(normed.reshape(-1, channels), up_weight, preferred_element_type=jnp.float32)
        + up_bias
    )
    adj_act = lax.dot_general(
        adjoint.reshape(-1, channels),
        down_weight,
        (((1,), (1,)), ((), ())),
        preferred_element_type=jnp.float32,
    )
    adj_pre = (adj_act * gelu_slope(preact)).astype(jnp.bfloat16)
    adj_norm = lax.dot_general(
        adj_pre, up_weight, (((1,), (1,)), ((), ())), preferred_element_type=jnp.float32
    ).reshape(state.shape)
    scaled = adj_norm * norm_gain
    adj_hidden = (
        inv_std
        * (
            scaled
            - jnp.mean(scaled, axis=-1, keepdims=True)
            - unit_norm * jnp.mean(scaled * unit_norm, axis=-1, keepdims=True)
        )
    ).astype(jnp.bfloat16)
    spread_back = depthwise_adjoint(
        pad_rows(wrap_edges(adj_hidden).astype(jnp.float32)), kernel, lat_count, lon_width
    )
    return (adjoint.astype(jnp.float32) + spread_back + forcing).astype(jnp.bfloat16)


def per_device(
    adjoint_final,
    states,
    kernel,
    norm_gain,
    up_weight,
    up_bias,
    down_weight,
    obs_cell,
    obs_count,
    obs_value,
    obs_error,
):
    adjoint = adjoint_final[0]
    for section_idx in range(states.shape[0]):
        state_now = states[section_idx, 0]
        forcing = obs_forcing(
            state_now,
            obs_cell[section_idx, 0],
            obs_count[section_idx, 0],
            obs_value[section_idx, 0],
            obs_error[section_idx, 0],
        )
        adjoint = member_step(
            adjoint, state_now, forcing, kernel, norm_gain, up_weight, up_bias, down_weight
        )
    return adjoint[None]


def solution(mesh):
    placed = (
        P("member", None, "tile", None),
        P(None, "member", None, "tile", None),
        P(),
        P(),
        P(),
        P(),
        P(),
        P(None, "tile", None, None),
        P(None, "tile", None),
        P(None, "tile", None, None, None),
        P(None, "tile", None, None),
    )
    return jax.shard_map(
        per_device,
        mesh=mesh,
        in_specs=placed,
        out_specs=P("member", None, "tile", None),
        check_vma=False,
    )
```

profile of v0, /device:TPU:32, one launch (start us, length us, event | category | flops | bytes accessed | tf_op | source)
XLA Modules:
  0.0 338.2 jit_solution(7707354068628930029)
XLA Ops:
  6.5 2.3 slice_bitcast_fusion.1
  8.9 1.0 fusion.425
  9.9 1.9 collective-permute-start
  11.8 7.0 %collective-permute-start.1 = (bf16[32,3,192]{2,1,0:T(4,128)(2,1)S(1)}, bf16[32,3,192]{2,1,0:T(4,128)(2,1)S(1)}, u32[]{:S(2)}, u32[]{:S(2)}) collective-permute-start(bf16[32,3,192]{2,1,0:T(4,128)(2,1)S(1)} %get-tuple-element.20), channel_id=1, source_target_pairs={{1,0},{2,1},{3,2},{4,3},{5,4},{6,5},{7,6},{8,7},{9,8},{10,9},{11,1... | collective-permute-start | bytes 110600 | tf_op jit(solution)/shard_map/ppermute | solution.py:21
  18.8 1.0 fusion.426
  19.8 1.9 collective-permute-start.4
  21.7 7.0 %collective-permute-start.5 = (bf16[32,3,192]{2,1,0:T(4,128)(2,1)S(1)}, bf16[32,3,192]{2,1,0:T(4,128)(2,1)S(1)}, u32[]{:S(2)}, u32[]{:S(2)}) collective-permute-start(bf16[32,3,192]{2,1,0:T(4,128)(2,1)S(1)} %get-tuple-element.24), channel_id=1, source_target_pairs={{1,0},{2,1},{3,2},{4,3},{5,4},{6,5},{7,6},{8,7},{9,8},{10,9},{11,1... | collective-permute-start | bytes 110600 | tf_op jit(solution)/shard_map/ppermute | solution.py:21
  28.7 0.7 fusion.430
  29.4 0.7 copy.31
  30.1 3.8 %all-to-all-start = ((s32[32,1,16]{2,1,0:T(1,128)}), s32[32,1,16]{2,1,0:T(1,128)S(1)}, u32[]{:S(2)}, u32[]{:S(2)}) async-start(s32[32,1,16]{2,1,0:T(1,128)} %bitcast.54), calls=%async_computation | async-start | bytes 32768 | tf_op jit(solution)/shard_map/all_to_all | solution.py:107
  33.9 1.0 fusion.427
  35.0 1.0 fusion.428
  36.2 0.9 fusion.429
  37.3 0.7 copy.32
  38.0 0.8 compare_select_fusion.1
  38.9 0.7 slice_bitcast_fusion.3
  39.5 0.7 bitcast_convert_fusion.1
  40.2 2.2 fusion.431
  42.4 0.7 iota_compare_fusion
  43.2 7.4 %all-to-all-start.3 = ((s32[32,1,16]{2,1,0:T(1,128)}), s32[32,1,16]{2,1,0:T(1,128)S(1)}, u32[]{:S(2)}, u32[]{:S(2)}) async-start(s32[32,1,16]{2,1,0:T(1,128)} %bitcast.70), calls=%async_computation.3 | async-start | bytes 32768 | tf_op jit(solution)/shard_map/all_to_all | solution.py:107
  50.8 0.7 add.1013
  51.4 0.6 broadcast.684
  52.0 0.7 reduce.9
  52.7 0.7 all_to_all.38
  53.4 4.5 %all-to-all-done.3 = s32[32,1,16]{2,1,0:T(1,128)S(1)} async-done(((s32[32,1,16]{2,1,0:T(1,128)}), s32[32,1,16]{2,1,0:T(1,128)S(1)}, u32[]{:S(2)}, u32[]{:S(2)}) %all-to-all-start.3) | async-done | bytes 2080 | tf_op jit(solution)/shard_map/all_to_all | solution.py:107
  58.0 3.9 %all-to-all-start.1 = ((bf16[32,32,192]{2,1,0:T(8,128)(2,1)}), bf16[32,32,192]{2,1,0:T(8,128)(2,1)S(1)}, u32[]{:S(2)}, u32[]{:S(2)}) async-start(bf16[32,32,192]{2,1,0:T(8,128)(2,1)} %get-tuple-element.13), calls=%async_computation.1 | async-start | bytes 1048576 | tf_op jit(solution)/shard_map/all_to_all | solution.py:95
  61.9 0.7 reduce.8
  62.6 0.7 all_to_all.43
  63.2 1.3 maximum_convert_fusion
  64.6 8.5 %fusion.421 = (f32[32,32]{1,0:T(8,128)S(1)}, f32[32,32,192]{2,1,0:T(8,128)}) fusion(f32[192]{0:T(256)S(1)} %bitcast.358, f32[192]{0:T(256)S(1)} %bitcast.362, f32[192]{0:T(256)S(1)} %bitcast.174, f32[192]{0:T(256)S(1)} %bitcast.178, f32[192]{0:T(256)S(1)} %bitcast.182, f32[192]{0:T(256)S(1)} %bitcast.186, f32[192]{0:T(256)S(1)} %bitcast.190, ...), kind=kLoop, calls=%fused_computation.693 | loop fusion | flops 19266560 | bytes 9491456 | tf_op jit(solution)/shard_map/reduce_sum | solution.py:120
  73.1 1.3 maximum_convert_fusion.2
  74.5 8.7 %fusion.419 = (f32[32,32]{1,0:T(8,128)S(1)}, f32[32,32,192]{2,1,0:T(8,128)S(1)}) fusion(f32[192]{0:T(256)} %bitcast.359, f32[192]{0:T(256)} %bitcast.363, f32[192]{0:T(256)S(1)} %bitcast.175, f32[192]{0:T(256)S(1)} %bitcast.179, f32[192]{0:T(256)S(1)} %bitcast.183, f32[192]{0:T(256)S(1)} %bitcast.187, f32[192]{0:T(256)S(1)} %bitcast.191, ...), kind=kLoop, calls=%fused_computation.692 | loop fusion | flops 19266560 | bytes 9488896 | tf_op jit(solution)/shard_map/reduce_sum | solution.py:120
  83.3 1.6 multiply_reduce_fusion.3
  85.3 1.6 multiply_convert_fusion.3
  86.9 5.4 %multiply_reduce_fusion.5 = (f32[1024]{0:T(1024)S(1)}, f32[1024,192]{0,1:T(8,128)}) fusion(f32[192]{0:T(256)S(1)} %copy-done.5, bf16[192,768]{1,0:T(8,128)(2,1)S(1)} %copy-done.67, f32[1024,768]{1,0:T(8,128)} %fusion.431, bf16[1024,192]{1,0:T(8,128)(2,1)S(1)} %bitcast.169, f32[768]{0:T(1024)S(1)} %copy-done.69), kind=kOutput, calls=%fused_computation.595 | convolution fusion | flops 620100608 | bytes 4628224 | tf_op jit(solution)/shard_map/dot_general | solution.py:135
  92.3 2.6 copy.24
  94.9 7.7 %all-to-all-start.4 = ((bf16[32,32,192]{2,1,0:T(8,128)(2,1)}), bf16[32,32,192]{2,1,0:T(8,128)(2,1)}, u32[]{:S(2)}, u32[]{:S(2)}) async-start(bf16[32,32,192]{2,1,0:T(8,128)(2,1)} %get-tuple-element.14), calls=%async_computation.4 | async-start | bytes 1048576 | tf_op jit(solution)/shard_map/all_to_all | solution.py:95
  102.6 1.7 multiply_reduce_fusion.2
  104.4 2.0 gather_fusion
  106.4 7.4 %all-to-all-done.4 = bf16[32,32,192]{2,1,0:T(8,128)(2,1)} async-done(((bf16[32,32,192]{2,1,0:T(8,128)(2,1)}), bf16[32,32,192]{2,1,0:T(8,128)(2,1)}, u32[]{:S(2)}, u32[]{:S(2)}) %all-to-all-start.4) | async-done | bytes 393248 | tf_op jit(solution)/shard_map/all_to_all | solution.py:95
  113.8 2.7 gather_fusion.1
  116.4 1.1 convert_multiply_fusion
  117.7 2.7 multiply_convert_fusion.1
  120.4 0.8 copy-done.2
  121.3 2.6 collective-permute-start.2
  123.9 6.3 %collective-permute-start.3 = (bf16[32,3,192]{2,1,0:T(4,128)(2,1)S(1)}, bf16[32,3,192]{2,1,0:T(4,128)(2,1)S(1)}, u32[]{:S(2)}, u32[]{:S(2)}) collective-permute-start(bf16[32,3,192]{2,1,0:T(4,128)(2,1)S(1)} %get-tuple-element.18), channel_id=1, source_target_pairs={{1,0},{2,1},{3,2},{4,3},{5,4},{6,5},{7,6},{8,7},{9,8},{10,9},{11,1... | collective-permute-start | bytes 110600 | tf_op jit(solution)/shard_map/ppermute | solution.py:21
  130.2 74.7 %all-reduce.10 = (f32[32,16,192]{2,1,0:T(8,128)S(1)}, f32[32,16,192]{2,1,0:T(8,128)S(1)}) all-reduce(bf16[32,16,192]{2,1,0:T(8,128)(2,1)S(1)} %bitcast.162, bf16[32,16,192]{2,1,0:T(8,128)(2,1)S(1)} %bitcast.159), channel_id=1, replica_groups=mesh['member'=16,'tile'=32] {'member'}, use_global_device_ids=true, to_apply=%region_12.13 | all-reduce | flops 196608 | bytes 1179648 | tf_op jit(solution)/shard_map/psum | solution.py:71
  204.9 53.8 %all-reduce.9.cloned.1.call-done = (f32[32,16,192]{2,1,0:T(8,128)}, f32[32,16,192]{2,1,0:T(8,128)}) async-done(((f32[32,16,192]{2,1,0:T(8,128)}, f32[32,16,192]{2,1,0:T(8,128)}), (f32[32,16,192]{2,1,0:T(8,128)}, f32[32,16,192]{2,1,0:T(8,128)})) %all-reduce.9.cloned.1.call-update) | async-done | bytes 786448 | tf_op jit(solution)/shard_map/psum | solution.py:71
  258.8 2.6 fusion.387
  261.4 7.1 %all-to-all-start.2 = ((bf16[32,16,192]{2,1,0:T(8,128)(2,1)}), bf16[32,16,192]{2,1,0:T(8,128)(2,1)S(1)}, u32[]{:S(2)}, u32[]{:S(2)}) async-start(bf16[32,16,192]{2,1,0:T(8,128)(2,1)} %get-tuple-element.21), calls=%async_computation.2 | async-start | bytes 524288 | tf_op jit(solution)/shard_map/all_to_all | solution.py:106
  268.6 0.6 compare_select_fusion.3
  269.2 1.3 maximum_convert_fusion.1
  270.5 7.0 %all-to-all-done.2 = bf16[32,16,192]{2,1,0:T(8,128)(2,1)S(1)} async-done(((bf16[32,16,192]{2,1,0:T(8,128)(2,1)}), bf16[32,16,192]{2,1,0:T(8,128)(2,1)S(1)}, u32[]{:S(2)}, u32[]{:S(2)}) %all-to-all-start.2) | async-done | bytes 196640 | tf_op jit(solution)/shard_map/all_to_all | solution.py:106
  277.5 4.6 %all-to-all-start.5 = ((bf16[32,16,192]{2,1,0:T(8,128)(2,1)}), bf16[32,16,192]{2,1,0:T(8,128)(2,1)}, u32[]{:S(2)}, u32[]{:S(2)}) async-start(bf16[32,16,192]{2,1,0:T(8,128)(2,1)} %get-tuple-element.22), calls=%async_computation.5 | async-start | bytes 524288 | tf_op jit(solution)/shard_map/all_to_all | solution.py:106
  282.1 4.4 %scatter_custom_fusion = f32[1024,192]{1,0:T(8,128)} fusion(s32[512]{0:T(512)S(1)} %bitcast.367, bf16[512,192]{1,0:T(8,128)(2,1)S(1)} %bitcast.167, f32[]{:T(128)} %constant.88.clone.1), kind=kCustom, calls=%fused_computation.606 | custom fusion | flops 196608 | bytes 1048580 | tf_op jit(solution)/shard_map/scatter-add | solution.py:87
  286.8 9.8 %add_convert_fusion.1 = bf16[32,32,192]{2,1,0:T(8,128)(2,1)S(1)} fusion(f32[32,32,192]{2,1,0:T(8,128)} %bitcast.165, f32[32,38,192]{2,1,0:T(8,128)S(1)} %maximum_convert_fusion.1, bf16[1,32,32,192]{3,2,1,0:T(8,128)(2,1)} %param.11, f32[192]{0:T(256)S(1)} %bitcast.361, f32[192]{0:T(256)S(1)} %bitcast.365, f32[192]{0:T(256)S(1)} %bitcast.176, ...), kind=kLoop, calls=%fused_computation.587 | loop fusion | flops 19857408 | bytes 10273792 | tf_op jit(solution)/shard_map/convert_element_type | solution.py:150
  296.7 2.2 fusion.432
  298.9 5.4 %multiply_reduce_fusion.4 = (f32[1024]{0:T(1024)S(1)}, f32[1024,192]{0,1:T(8,128)}) fusion(f32[192]{0:T(256)S(1)} %copy-done.5, bf16[192,768]{1,0:T(8,128)(2,1)S(1)} %copy-done.68, f32[1024,768]{1,0:T(8,128)} %fusion.432, bf16[1024,192]{1,0:T(8,128)(2,1)S(1)} %bitcast.168, f32[768]{0:T(1024)S(1)} %copy-done.70), kind=kOutput, calls=%fused_computation.594 | convolution fusion | flops 620100608 | bytes 4628224 | tf_op jit(solution)/shard_map/dot_general | solution.py:135
  304.2 1.5 copy.27
  306.3 0.7 multiply_convert_fusion
  307.1 2.0 collective-permute-start.6
  309.1 6.9 %collective-permute-start.7 = (bf16[32,3,192]{2,1,0:T(4,128)(2,1)S(1)}, bf16[32,3,192]{2,1,0:T(4,128)(2,1)S(1)}, u32[]{:S(2)}, u32[]{:S(2)}) collective-permute-start(bf16[32,3,192]{2,1,0:T(4,128)(2,1)S(1)} %get-tuple-element.16), channel_id=1, source_target_pairs={{1,0},{2,1},{3,2},{4,3},{5,4},{6,5},{7,6},{8,7},{9,8},{10,9},{11,1... | collective-permute-start | bytes 110600 | tf_op jit(solution)/shard_map/ppermute | solution.py:21
  316.0 4.3 %scatter_custom_fusion.1 = f32[1024,192]{1,0:T(8,128)S(1)} fusion(s32[512]{0:T(512)} %bitcast.366, bf16[512,192]{1,0:T(8,128)(2,1)} %bitcast.89, f32[]{:T(128)} %constant.88.clone.1), kind=kCustom, calls=%fused_computation.600 | custom fusion | flops 196608 | bytes 1049088 | tf_op jit(solution)/shard_map/scatter-add | solution.py:87
  320.5 10.8 %fusion.390 = bf16[1,32,32,192]{3,2,1,0:T(8,128)(2,1)} fusion(f32[32,32,192]{2,1,0:T(8,128)S(1)} %bitcast.164, f32[32,38,192]{2,1,0:T(8,128)S(1)} %maximum_convert_fusion.3, f32[192]{0:T(256)} %bitcast.360, f32[192]{0:T(256)} %bitcast.364, f32[192]{0:T(256)S(1)} %bitcast.177, f32[192]{0:T(256)S(1)} %bitcast.181, f32[192]{0:T(256)S(1)} %bitcast.185, ...), kind=kLoop, calls=%fused_computation.616 | loop fusion | flops 19857408 | bytes 10657280 | tf_op jit(solution)/shard_map/broadcast_in_dim | solution.py:179
  (176 shorter events, 2.1 us)
Async XLA Ops:
  6.5 33.7 %copy-start = (bf16[768,192]{0,1:T(8,128)(2,1)S(1)}, bf16[768,192]{0,1:T(8,128)(2,1)}, u32[]{:S(2)}) copy-start(bf16[768,192]{0,1:T(8,128)(2,1)} %param.17) | copy-start | bytes 884740
  6.5 33.7 %copy-start.3 = (bf16[1,32,32,192]{3,2,1,0:T(8,128)(2,1)S(1)}, bf16[1,32,32,192]{3,2,1,0:T(8,128)(2,1)}, u32[]{:S(2)}) copy-start(bf16[1,32,32,192]{3,2,1,0:T(8,128)(2,1)} %param.11) | copy-start | bytes 1179652
  9.9 53.4 %collective-permute-start = (bf16[32,3,192]{2,1,0:T(4,128)(2,1)S(1)}, bf16[32,3,192]{2,1,0:T(4,128)(2,1)S(1)}, u32[]{:S(2)}, u32[]{:S(2)}) collective-permute-start(bf16[32,3,192]{2,1,0:T(4,128)(2,1)S(1)} %get-tuple-element.19), channel_id=1, source_target_pairs={{0,1},{1,2},{2,3},{3,4},{4,5},{5,6},{6,7},{7,8},{8,9},{9,10},{10,1... | collective-permute-start | bytes 110600 | tf_op jit(solution)/shard_map/ppermute | solution.py:20
  11.8 51.4 %collective-permute-start.1 = (bf16[32,3,192]{2,1,0:T(4,128)(2,1)S(1)}, bf16[32,3,192]{2,1,0:T(4,128)(2,1)S(1)}, u32[]{:S(2)}, u32[]{:S(2)}) collective-permute-start(bf16[32,3,192]{2,1,0:T(4,128)(2,1)S(1)} %get-tuple-element.20), channel_id=1, source_target_pairs={{1,0},{2,1},{3,2},{4,3},{5,4},{6,5},{7,6},{8,7},{9,8},{10,9},{11,1... | collective-permute-start | bytes 110600 | tf_op jit(solution)/shard_map/ppermute | solution.py:21
  19.8 53.3 %collective-permute-start.4 = (bf16[32,3,192]{2,1,0:T(4,128)(2,1)S(1)}, bf16[32,3,192]{2,1,0:T(4,128)(2,1)S(1)}, u32[]{:S(2)}, u32[]{:S(2)}) collective-permute-start(bf16[32,3,192]{2,1,0:T(4,128)(2,1)S(1)} %get-tuple-element.23), channel_id=1, source_target_pairs={{0,1},{1,2},{2,3},{3,4},{4,5},{5,6},{6,7},{7,8},{8,9},{9,10},{10,1... | collective-permute-start | bytes 110600 | tf_op jit(solution)/shard_map/ppermute | solution.py:20
  21.7 51.4 %collective-permute-start.5 = (bf16[32,3,192]{2,1,0:T(4,128)(2,1)S(1)}, bf16[32,3,192]{2,1,0:T(4,128)(2,1)S(1)}, u32[]{:S(2)}, u32[]{:S(2)}) collective-permute-start(bf16[32,3,192]{2,1,0:T(4,128)(2,1)S(1)} %get-tuple-element.24), channel_id=1, source_target_pairs={{1,0},{2,1},{3,2},{4,3},{5,4},{6,5},{7,6},{8,7},{9,8},{10,9},{11,1... | collective-permute-start | bytes 110600 | tf_op jit(solution)/shard_map/ppermute | solution.py:21
  30.1 13.1 %all-to-all-start = ((s32[32,1,16]{2,1,0:T(1,128)}), s32[32,1,16]{2,1,0:T(1,128)S(1)}, u32[]{:S(2)}, u32[]{:S(2)}) async-start(s32[32,1,16]{2,1,0:T(1,128)} %bitcast.54), calls=%async_computation | async-start | bytes 32768 | tf_op jit(solution)/shard_map/all_to_all | solution.py:107
  34.9 251.5 %copy-start.6 = (f32[1,1,192]{2,1,0:T(1,128)}, f32[1,1,192]{2,1,0:T(1,128)S(1)}, u32[]{:S(2)}) copy-start(f32[1,1,192]{2,1,0:T(1,128)S(1)} %get-tuple-element.36) | copy-start | bytes 2308
  35.0 251.5 %copy-start.7 = (f32[1,1,192]{2,1,0:T(1,128)}, f32[1,1,192]{2,1,0:T(1,128)S(1)}, u32[]{:S(2)}) copy-start(f32[1,1,192]{2,1,0:T(1,128)S(1)} %get-tuple-element.37) | copy-start | bytes 2308
  35.0 251.5 %copy-start.8 = (f32[1,1,192]{2,1,0:T(1,128)}, f32[1,1,192]{2,1,0:T(1,128)S(1)}, u32[]{:S(2)}) copy-start(f32[1,1,192]{2,1,0:T(1,128)S(1)} %get-tuple-element.38) | copy-start | bytes 2308
  35.0 251.5 %copy-start.9 = (f32[1,1,192]{2,1,0:T(1,128)}, f32[1,1,192]{2,1,0:T(1,128)S(1)}, u32[]{:S(2)}) copy-start(f32[1,1,192]{2,1,0:T(1,128)S(1)} %get-tuple-element.39) | copy-start | bytes 2308
  35.0 251.5 %copy-start.10 = (f32[1,1,192]{2,1,0:T(1,128)}, f32[1,1,192]{2,1,0:T(1,128)S(1)}, u32[]{:S(2)}) copy-start(f32[1,1,192]{2,1,0:T(1,128)S(1)} %get-tuple-element.40) | copy-start | bytes 2308
  35.0 251.5 %copy-start.11 = (f32[1,1,192]{2,1,0:T(1,128)}, f32[1,1,192]{2,1,0:T(1,128)S(1)}, u32[]{:S(2)}) copy-start(f32[1,1,192]{2,1,0:T(1,128)S(1)} %get-tuple-element.41) | copy-start | bytes 2308
  35.0 251.5 %copy-start.12 = (f32[1,1,192]{2,1,0:T(1,128)}, f32[1,1,192]{2,1,0:T(1,128)S(1)}, u32[]{:S(2)}) copy-start(f32[1,1,192]{2,1,0:T(1,128)S(1)} %get-tuple-element.42) | copy-start | bytes 2308
  35.0 251.5 %copy-start.13 = (f32[1,1,192]{2,1,0:T(1,128)}, f32[1,1,192]{2,1,0:T(1,128)S(1)}, u32[]{:S(2)}) copy-start(f32[1,1,192]{2,1,0:T(1,128)S(1)} %get-tuple-element.43) | copy-start | bytes 2308
  36.1 38.4 %copy-start.26 = (f32[1,1,192]{2,1,0:T(1,128)}, f32[1,1,192]{2,1,0:T(1,128)S(1)}, u32[]{:S(2)}) copy-start(f32[1,1,192]{2,1,0:T(1,128)S(1)} %get-tuple-element.56) | copy-start | bytes 2308
  36.1 38.4 %copy-start.28 = (f32[1,1,192]{2,1,0:T(1,128)}, f32[1,1,192]{2,1,0:T(1,128)S(1)}, u32[]{:S(2)}) copy-start(f32[1,1,192]{2,1,0:T(1,128)S(1)} %get-tuple-element.57) | copy-start | bytes 2308
  36.1 38.4 %copy-start.30 = (f32[1,1,192]{2,1,0:T(1,128)}, f32[1,1,192]{2,1,0:T(1,128)S(1)}, u32[]{:S(2)}) copy-start(f32[1,1,192]{2,1,0:T(1,128)S(1)} %get-tuple-element.58) | copy-start | bytes 2308
  36.1 38.4 %copy-start.32 = (f32[1,1,192]{2,1,0:T(1,128)}, f32[1,1,192]{2,1,0:T(1,128)S(1)}, u32[]{:S(2)}) copy-start(f32[1,1,192]{2,1,0:T(1,128)S(1)} %get-tuple-element.59) | copy-start | bytes 2308
  36.1 38.4 %copy-start.34 = (f32[1,1,192]{2,1,0:T(1,128)}, f32[1,1,192]{2,1,0:T(1,128)S(1)}, u32[]{:S(2)}) copy-start(f32[1,1,192]{2,1,0:T(1,128)S(1)} %get-tuple-element.60) | copy-start | bytes 2308
  36.1 38.4 %copy-start.36 = (f32[1,1,192]{2,1,0:T(1,128)}, f32[1,1,192]{2,1,0:T(1,128)S(1)}, u32[]{:S(2)}) copy-start(f32[1,1,192]{2,1,0:T(1,128)S(1)} %get-tuple-element.61) | copy-start | bytes 2308
  36.1 38.4 %copy-start.38 = (f32[1,1,192]{2,1,0:T(1,128)}, f32[1,1,192]{2,1,0:T(1,128)S(1)}, u32[]{:S(2)}) copy-start(f32[1,1,192]{2,1,0:T(1,128)S(1)} %get-tuple-element.62) | copy-start | bytes 2308
  36.1 250.4 %copy-start.14 = (f32[1,1,192]{2,1,0:T(1,128)}, f32[1,1,192]{2,1,0:T(1,128)S(1)}, u32[]{:S(2)}) copy-start(f32[1,1,192]{2,1,0:T(1,128)S(1)} %get-tuple-element.44) | copy-start | bytes 2308
  36.1 250.4 %copy-start.15 = (f32[1,1,192]{2,1,0:T(1,128)}, f32[1,1,192]{2,1,0:T(1,128)S(1)}, u32[]{:S(2)}) copy-start(f32[1,1,192]{2,1,0:T(1,128)S(1)} %get-tuple-element.45) | copy-start | bytes 2308
  36.1 250.4 %copy-start.16 = (f32[1,1,192]{2,1,0:T(1,128)}, f32[1,1,192]{2,1,0:T(1,128)S(1)}, u32[]{:S(2)}) copy-start(f32[1,1,192]{2,1,0:T(1,128)S(1)} %get-tuple-element.46) | copy-start | bytes 2308
  36.2 250.4 %copy-start.17 = (f32[1,1,192]{2,1,0:T(1,128)}, f32[1,1,192]{2,1,0:T(1,128)S(1)}, u32[]{:S(2)}) copy-start(f32[1,1,192]{2,1,0:T(1,128)S(1)} %get-tuple-element.47) | copy-start | bytes 2308
  36.2 250.4 %copy-start.18 = (f32[1,1,192]{2,1,0:T(1,128)}, f32[1,1,192]{2,1,0:T(1,128)S(1)}, u32[]{:S(2)}) copy-start(f32[1,1,192]{2,1,0:T(1,128)S(1)} %get-tuple-element.48) | copy-start | bytes 2308
  36.2 250.4 %copy-start.19 = (f32[1,1,192]{2,1,0:T(1,128)}, f32[1,1,192]{2,1,0:T(1,128)S(1)}, u32[]{:S(2)}) copy-start(f32[1,1,192]{2,1,0:T(1,128)S(1)} %get-tuple-element.49) | copy-start | bytes 2308
  36.2 250.4 %copy-start.20 = (f32[1,1,192]{2,1,0:T(1,128)}, f32[1,1,192]{2,1,0:T(1,128)S(1)}, u32[]{:S(2)}) copy-start(f32[1,1,192]{2,1,0:T(1,128)S(1)} %get-tuple-element.50) | copy-start | bytes 2308
  36.2 250.4 %copy-start.21 = (f32[1,1,192]{2,1,0:T(1,128)}, f32[1,1,192]{2,1,0:T(1,128)S(1)}, u32[]{:S(2)}) copy-start(f32[1,1,192]{2,1,0:T(1,128)S(1)} %get-tuple-element.51) | copy-start | bytes 2308
  36.2 250.4 %copy-start.22 = (f32[1,1,192]{2,1,0:T(1,128)}, f32[1,1,192]{2,1,0:T(1,128)S(1)}, u32[]{:S(2)}) copy-start(f32[1,1,192]{2,1,0:T(1,128)S(1)} %get-tuple-element.52) | copy-start | bytes 2308
  36.2 250.4 %copy-start.23 = (f32[1,1,192]{2,1,0:T(1,128)}, f32[1,1,192]{2,1,0:T(1,128)S(1)}, u32[]{:S(2)}) copy-start(f32[1,1,192]{2,1,0:T(1,128)S(1)} %get-tuple-element.53) | copy-start | bytes 2308
  36.2 250.4 %copy-start.24 = (f32[1,1,192]{2,1,0:T(1,128)}, f32[1,1,192]{2,1,0:T(1,128)S(1)}, u32[]{:S(2)}) copy-start(f32[1,1,192]{2,1,0:T(1,128)S(1)} %get-tuple-element.54) | copy-start | bytes 2308
  36.2 250.4 %copy-start.25 = (f32[1,1,192]{2,1,0:T(1,128)}, f32[1,1,192]{2,1,0:T(1,128)S(1)}, u32[]{:S(2)}) copy-start(f32[1,1,192]{2,1,0:T(1,128)S(1)} %get-tuple-element.55) | copy-start | bytes 2308
  37.2 27.4 %copy-start.42 = (f32[1,1,192]{2,1,0:T(1,128)}, f32[1,1,192]{2,1,0:T(1,128)S(1)}, u32[]{:S(2)}) copy-start(f32[1,1,192]{2,1,0:T(1,128)S(1)} %get-tuple-element.64) | copy-start | bytes 2308
  37.2 27.4 %copy-start.44 = (f32[1,1,192]{2,1,0:T(1,128)}, f32[1,1,192]{2,1,0:T(1,128)S(1)}, u32[]{:S(2)}) copy-start(f32[1,1,192]{2,1,0:T(1,128)S(1)} %get-tuple-element.65) | copy-start | bytes 2308
  37.3 37.3 %copy-start.40 = (f32[1,1,192]{2,1,0:T(1,128)}, f32[1,1,192]{2,1,0:T(1,128)S(1)}, u32[]{:S(2)}) copy-start(f32[1,1,192]{2,1,0:T(1,128)S(1)} %get-tuple-element.63) | copy-start | bytes 2308
  43.2 14.8 %all-to-all-start.3 = ((s32[32,1,16]{2,1,0:T(1,128)}), s32[32,1,16]{2,1,0:T(1,128)S(1)}, u32[]{:S(2)}, u32[]{:S(2)}) async-start(s32[32,1,16]{2,1,0:T(1,128)} %bitcast.70), calls=%async_computation.3 | async-start | bytes 32768 | tf_op jit(solution)/shard_map/all_to_all | solution.py:107
  58.0 36.9 %all-to-all-start.1 = ((bf16[32,32,192]{2,1,0:T(8,128)(2,1)}), bf16[32,32,192]{2,1,0:T(8,128)(2,1)S(1)}, u32[]{:S(2)}, u32[]{:S(2)}) async-start(bf16[32,32,192]{2,1,0:T(8,128)(2,1)} %get-tuple-element.13), calls=%async_computation.1 | async-start | bytes 1048576 | tf_op jit(solution)/shard_map/all_to_all | solution.py:95
  94.9 18.9 %all-to-all-start.4 = ((bf16[32,32,192]{2,1,0:T(8,128)(2,1)}), bf16[32,32,192]{2,1,0:T(8,128)(2,1)}, u32[]{:S(2)}, u32[]{:S(2)}) async-start(bf16[32,32,192]{2,1,0:T(8,128)(2,1)} %get-tuple-element.14), calls=%async_computation.4 | async-start | bytes 1048576 | tf_op jit(solution)/shard_map/all_to_all | solution.py:95
  102.6 156.1 %all-reduce.9.cloned.1.call-start = ((), (), s32[]{:S(2)}) async-start(), calls=%async_computation.6 | async-start | bytes 2097152 | tf_op jit(solution)/shard_map/psum | solution.py:71
  117.6 141.1 %copy-start.62 = (pred[32,16]{1,0:T(8,128)(4,1)S(1)}, pred[32,16]{1,0:T(8,128)(4,1)}, u32[]{:S(2)}) copy-start(pred[32,16]{1,0:T(8,128)(4,1)} %get-tuple-element.94) | copy-start | bytes 1540
  117.6 141.1 %copy-start.63 = (pred[32,16]{1,0:T(8,128)(4,1)S(1)}, pred[32,16]{1,0:T(8,128)(4,1)}, u32[]{:S(2)}) copy-start(pred[32,16]{1,0:T(8,128)(4,1)} %get-tuple-element.95) | copy-start | bytes 1540
  120.4 148.1 %copy-start.64 = (s32[512,1]{0,1:T(1,128)S(1)}, s32[512,1]{0,1:T(1,128)}, u32[]{:S(2)}) copy-start(s32[512,1]{0,1:T(1,128)} %add.1013) | copy-start | bytes 6148
  120.4 148.1 %copy-start.65 = (s32[512,1]{0,1:T(1,128)S(1)}, s32[512,1]{0,1:T(1,128)}, u32[]{:S(2)}) copy-start(s32[512,1]{0,1:T(1,128)} %all_to_all.38) | copy-start | bytes 6148
  120.4 148.2 %copy-start.66 = (s32[512,1]{0,1:T(1,128)S(1)}, s32[512,1]{0,1:T(1,128)}, u32[]{:S(2)}) copy-start(s32[512,1]{0,1:T(1,128)} %all_to_all.43) | copy-start | bytes 6148
  121.3 147.9 %collective-permute-start.2 = (bf16[32,3,192]{2,1,0:T(4,128)(2,1)S(1)}, bf16[32,3,192]{2,1,0:T(4,128)(2,1)S(1)}, u32[]{:S(2)}, u32[]{:S(2)}) collective-permute-start(bf16[32,3,192]{2,1,0:T(4,128)(2,1)S(1)} %get-tuple-element.17), channel_id=1, source_target_pairs={{0,1},{1,2},{2,3},{3,4},{4,5},{5,6},{6,7},{7,8},{8,9},{9,10},{10,1... | collective-permute-start | bytes 110600 | tf_op jit(solution)/shard_map/ppermute | solution.py:20
  123.9 145.3 %collective-permute-start.3 = (bf16[32,3,192]{2,1,0:T(4,128)(2,1)S(1)}, bf16[32,3,192]{2,1,0:T(4,128)(2,1)S(1)}, u32[]{:S(2)}, u32[]{:S(2)}) collective-permute-start(bf16[32,3,192]{2,1,0:T(4,128)(2,1)S(1)} %get-tuple-element.18), channel_id=1, source_target_pairs={{1,0},{2,1},{3,2},{4,3},{5,4},{6,5},{7,6},{8,7},{9,8},{10,9},{11,1... | collective-permute-start | bytes 110600 | tf_op jit(solution)/shard_map/ppermute | solution.py:21
  258.7 27.9 %copy-start.27 = (f32[1,1,192]{2,1,0:T(1,128)S(1)}, f32[1,1,192]{2,1,0:T(1,128)}, u32[]{:S(2)}) copy-start(f32[1,1,192]{2,1,0:T(1,128)} %copy-done.26) | copy-start | bytes 2308
  258.7 28.0 %copy-start.29 = (f32[1,1,192]{2,1,0:T(1,128)S(1)}, f32[1,1,192]{2,1,0:T(1,128)}, u32[]{:S(2)}) copy-start(f32[1,1,192]{2,1,0:T(1,128)} %copy-done.28) | copy-start | bytes 2308
  258.7 28.0 %copy-start.31 = (f32[1,1,192]{2,1,0:T(1,128)S(1)}, f32[1,1,192]{2,1,0:T(1,128)}, u32[]{:S(2)}) copy-start(f32[1,1,192]{2,1,0:T(1,128)} %copy-done.30) | copy-start | bytes 2308
  258.7 28.0 %copy-start.33 = (f32[1,1,192]{2,1,0:T(1,128)S(1)}, f32[1,1,192]{2,1,0:T(1,128)}, u32[]{:S(2)}) copy-start(f32[1,1,192]{2,1,0:T(1,128)} %copy-done.32) | copy-start | bytes 2308
  258.7 28.0 %copy-start.35 = (f32[1,1,192]{2,1,0:T(1,128)S(1)}, f32[1,1,192]{2,1,0:T(1,128)}, u32[]{:S(2)}) copy-start(f32[1,1,192]{2,1,0:T(1,128)} %copy-done.34) | copy-start | bytes 2308
  258.7 28.0 %copy-start.37 = (f32[1,1,192]{2,1,0:T(1,128)S(1)}, f32[1,1,192]{2,1,0:T(1,128)}, u32[]{:S(2)}) copy-start(f32[1,1,192]{2,1,0:T(1,128)} %copy-done.36) | copy-start | bytes 2308
  258.7 28.0 %copy-start.39 = (f32[1,1,192]{2,1,0:T(1,128)S(1)}, f32[1,1,192]{2,1,0:T(1,128)}, u32[]{:S(2)}) copy-start(f32[1,1,192]{2,1,0:T(1,128)} %copy-done.38) | copy-start | bytes 2308
  258.7 28.0 %copy-start.41 = (f32[1,1,192]{2,1,0:T(1,128)S(1)}, f32[1,1,192]{2,1,0:T(1,128)}, u32[]{:S(2)}) copy-start(f32[1,1,192]{2,1,0:T(1,128)} %copy-done.40) | copy-start | bytes 2308
  258.7 28.0 %copy-start.43 = (f32[1,1,192]{2,1,0:T(1,128)S(1)}, f32[1,1,192]{2,1,0:T(1,128)}, u32[]{:S(2)}) copy-start(f32[1,1,192]{2,1,0:T(1,128)} %copy-done.42) | copy-start | bytes 2308
  258.7 28.0 %copy-start.45 = (f32[1,1,192]{2,1,0:T(1,128)S(1)}, f32[1,1,192]{2,1,0:T(1,128)}, u32[]{:S(2)}) copy-start(f32[1,1,192]{2,1,0:T(1,128)} %copy-done.44) | copy-start | bytes 2308
  258.8 28.0 %copy-start.47 = (f32[1,1,192]{2,1,0:T(1,128)S(1)}, f32[1,1,192]{2,1,0:T(1,128)}, u32[]{:S(2)}) copy-start(f32[1,1,192]{2,1,0:T(1,128)} %copy-done.46) | copy-start | bytes 2308
  258.8 28.0 %copy-start.49 = (f32[1,1,192]{2,1,0:T(1,128)S(1)}, f32[1,1,192]{2,1,0:T(1,128)}, u32[]{:S(2)}) copy-start(f32[1,1,192]{2,1,0:T(1,128)} %copy-done.48) | copy-start | bytes 2308
  261.4 16.1 %all-to-all-start.2 = ((bf16[32,16,192]{2,1,0:T(8,128)(2,1)}), bf16[32,16,192]{2,1,0:T(8,128)(2,1)S(1)}, u32[]{:S(2)}, u32[]{:S(2)}) async-start(bf16[32,16,192]{2,1,0:T(8,128)(2,1)} %get-tuple-element.21), calls=%async_computation.2 | async-start | bytes 524288 | tf_op jit(solution)/shard_map/all_to_all | solution.py:106
  277.5 38.5 %all-to-all-start.5 = ((bf16[32,16,192]{2,1,0:T(8,128)(2,1)}), bf16[32,16,192]{2,1,0:T(8,128)(2,1)}, u32[]{:S(2)}, u32[]{:S(2)}) async-start(bf16[32,16,192]{2,1,0:T(8,128)(2,1)} %get-tuple-element.22), calls=%async_computation.5 | async-start | bytes 524288 | tf_op jit(solution)/shard_map/all_to_all | solution.py:106
  307.1 13.2 %collective-permute-start.6 = (bf16[32,3,192]{2,1,0:T(4,128)(2,1)S(1)}, bf16[32,3,192]{2,1,0:T(4,128)(2,1)S(1)}, u32[]{:S(2)}, u32[]{:S(2)}) collective-permute-start(bf16[32,3,192]{2,1,0:T(4,128)(2,1)S(1)} %get-tuple-element.15), channel_id=1, source_target_pairs={{0,1},{1,2},{2,3},{3,4},{4,5},{5,6},{6,7},{7,8},{8,9},{9,10},{10,1... | collective-permute-start | bytes 110600 | tf_op jit(solution)/shard_map/ppermute | solution.py:20
  309.1 11.1 %collective-permute-start.7 = (bf16[32,3,192]{2,1,0:T(4,128)(2,1)S(1)}, bf16[32,3,192]{2,1,0:T(4,128)(2,1)S(1)}, u32[]{:S(2)}, u32[]{:S(2)}) collective-permute-start(bf16[32,3,192]{2,1,0:T(4,128)(2,1)S(1)} %get-tuple-element.16), channel_id=1, source_target_pairs={{1,0},{2,1},{3,2},{4,3},{5,4},{6,5},{7,6},{8,7},{9,8},{10,9},{11,1... | collective-permute-start | bytes 110600 | tf_op jit(solution)/shard_map/ppermute | solution.py:21
  (22 other events, 407.3 us)
Sparse Core Ops, SparseCore 0:
  117.7 140.9 all-reduce.8
where the time goes:
time: 340 us; the launch traced here: 338 us
  blocking collectives  74.7 us (22%)
  waiting for transfers between devices  72.7 us (21%)
  starting transfers between devices  70.1 us (21%)
  other arithmetic  67.8 us (20%)
  local copies, waits for them, and re-layouts  22.9 us (7%)
  matrix products  15.1 us (4%)
  between operations  14.7 us (4%)
    psum x1, blocking collectives, departures(): summed, squares = lax.psum((sampled, sampled * sampled), 'member')  74.7 us
    psum x1, waiting for transfers between devices, departures(): summed, squares = lax.psum((sampled, sampled * sampled), 'member')  53.8 us
    ppermute x4, starting transfers between devices, extended(): after = lax.ppermute(initial, axis, down)  27 us
    reduce_sum x2, other arithmetic, member_step(): centred = hidden - jnp.mean(hidden, axis=-1, keepdims=True)  17.2 us
    all_to_all x2, starting transfers between devices, obs_forcing(): lax.all_to_all(dep_rows, 'tile', split_axis=0, concat_axis=0, tiled=True)  11.7 us
    all_to_all x2, starting transfers between devices, obs_forcing(): lax.all_to_all(state_now, 'tile', split_axis=0, concat_axis=1, tiled=True)  11.6 us
    all_to_all x2, starting transfers between devices, obs_forcing(): lax.all_to_all(cell_ids, 'tile', split_axis=0, concat_axis=0, tiled=True)  11.2 us
    broadcast_in_dim x1, other arithmetic, per_device(): return adjoint[None]  10.8 us
  transfers between devices with their start and end apart: 15, of which 4 were waited for; matrix products, arithmetic and copies ran while one was open for 25% of the time, Pallas kernels for 0%

commit v1 on v0

v1 whole, which is shorter than its diff:
```python
import functools
import math

import jax
import jax.numpy as jnp
from jax import lax
from jax.experimental import pallas as pl
from jax.experimental.pallas import tpu as pltpu
from jax.sharding import PartitionSpec as P

slope_coef = math.sqrt(2.0 / math.pi)
cubic_coef = 0.044715
norm_eps = 1e-06

LAT = 32
WID = 32
CH = 192
HID = 768
CAP = 16
CELLS = LAT * WID
SLOTS = LAT * CAP
BLK = 8
ROWS = BLK * WID
f32 = jnp.float32
bf16 = jnp.bfloat16
NT = (((1,), (1,)), ((), ()))
TN = (((0,), (0,)), ((), ()))


def gelu_slope(preact):
    square = preact * preact
    tanh_val = jnp.tanh(preact * (slope_coef + (slope_coef * cubic_coef) * square))
    tail = preact * (0.5 * slope_coef + (1.5 * slope_coef * cubic_coef) * square)
    return (0.5 + 0.5 * tanh_val) + tail * (1.0 - tanh_val * tanh_val)


def mean_lanes(value):
    return jnp.sum(value, axis=-1, keepdims=True) * (1.0 / CH)


def build_shifts(shifts, padded, centre, left, right):
    for edge in range(3):
        zeros = jnp.zeros((WID, CH), f32)
        for col in range(7):
            shifts[col, edge] = zeros
            shifts[col, LAT + 3 + edge] = zeros

    def one_row(row, carry):
        padded[0:3] = left(row).astype(f32)
        padded[3 : WID + 3] = centre(row).astype(f32)
        padded[WID + 3 : WID + 6] = right(row).astype(f32)
        for col in range(7):
            shifts[col, row + 3] = padded[col : col + WID]
        return carry

    lax.fori_loop(0, LAT, one_row, 0)


def convolve(shifts, kernel_ref, first, flip, emit):
    for low, high in ((0, 128), (128, CH)):
        sums = [None] * BLK
        for col in range(7):
            taps = []
            for row in range(7):
                index = (6 - row) * 7 + 6 - col if flip else row * 7 + col
                taps.append(jnp.broadcast_to(kernel_ref[index : index + 1, low:high], (WID, high - low)))
            for source in range(BLK + 6):
                field = shifts[col, first + source, :, low:high]
                for row in range(7):
                    target = source - row
                    if 0 <= target < BLK:
                        term = taps[row] * field
                        sums[target] = term if sums[target] is None else sums[target] + term
        for target in range(BLK):
            emit(target, low, high, sums[target])


def gather_kernel(got_ref, state_ref, out_ref, hot_ref):
    for step in range(2):
        cells = got_ref[:, step, CH : CH + CAP].astype(f32)
        lane = lax.broadcasted_iota(jnp.int32, (LAT, CELLS), 1)
        band = lax.broadcasted_iota(jnp.int32, (LAT, CELLS), 0)
        offset = (lane - band * WID).astype(f32)
        for slot in range(CAP):
            hot = jnp.where(offset == cells[:, slot : slot + 1], 1.0, 0.0)
            hot_ref[slot * LAT : (slot + 1) * LAT] = hot.astype(bf16)
        rows = jnp.dot(hot_ref[...], state_ref[step], preferred_element_type=f32)
        out_ref[:, :, step * CH : (step + 1) * CH] = rows.astype(bf16).reshape(CAP, LAT, CH)


def gather_rows(got, states):
    return pl.pallas_call(
        gather_kernel,
        out_shape=jax.ShapeDtypeStruct((CAP, LAT, 2 * CH), bf16),
        scratch_shapes=[pltpu.VMEM((SLOTS, CELLS), bf16)],
        cost_estimate=pl.CostEstimate(flops=2 * 2 * SLOTS * CELLS * CH, bytes_accessed=2000000, transcendentals=0),
    )(got, states)


def departure_kernel(step, rows_ref, got_ref, out_ref):
    sampled = rows_ref[:, :, step * CH : (step + 1) * CH].astype(f32)
    members = sampled.shape[0]
    own = got_ref[:, step, :].astype(f32)
    ens_mean = jnp.sum(sampled, axis=0) * (1.0 / members)
    ens_var = jnp.sum(sampled * sampled, axis=0) * (1.0 / members) - ens_mean * ens_mean
    weight = 1.0 / (own[:, CH + CAP : CH + CAP + 1] + ens_var)
    ratio = (sampled - own[None, :, :CH]) * weight[None]
    live = own[:, CH + CAP + 1 : CH + CAP + 2] >= 0.0
    out_ref[...] = jnp.where(live[None], ratio, 0.0).astype(bf16)


def departures(step, rows, got):
    return pl.pallas_call(
        functools.partial(departure_kernel, step),
        out_shape=jax.ShapeDtypeStruct((CAP, LAT, CH), bf16),
        cost_estimate=pl.CostEstimate(flops=600000, bytes_accessed=600000, transcendentals=0),
    )(rows, got)


def forcing_of(step, rows_ref, got_ref, hot_ref, first, count):
    cells = got_ref[:, step, CH : CH + CAP].astype(f32)
    lane = lax.broadcasted_iota(jnp.int32, (LAT, count), 1) + first
    band = lax.broadcasted_iota(jnp.int32, (LAT, count), 0)
    offset = (lane - band * WID).astype(f32)
    for slot in range(CAP):
        hot = jnp.where(offset == cells[:, slot : slot + 1], 1.0, 0.0)
        hot_ref[slot * LAT : (slot + 1) * LAT] = hot.astype(bf16)
    rows = rows_ref[...].reshape(SLOTS, CH)
    return lax.dot_general(hot_ref[...], rows, TN, preferred_element_type=f32)


def normalise(hidden):
    centred = hidden - mean_lanes(hidden)
    inv_std = lax.rsqrt(mean_lanes(centred * centred) + norm_eps)
    return centred * inv_std, inv_std


def backward(adjoint, slope_at, down_ref, up_ref, gain, unit, inv_std):
    adj_norm = jnp.zeros((ROWS, CH), f32)
    for part in range(3):
        cols = slice(part * 256, (part + 1) * 256)
        act = lax.dot_general(adjoint, down_ref[cols, :], NT, preferred_element_type=f32)
        pre = (act * slope_at(cols)).astype(bf16)
        adj_norm = adj_norm + lax.dot_general(pre, up_ref[:, cols], NT, preferred_element_type=f32)
    scaled = adj_norm * gain
    return inv_std * (scaled - mean_lanes(scaled) - unit * mean_lanes(scaled * unit))


def put_hidden(adj_hidden, first, out_ref, head_ref, tail_ref):
    block = adj_hidden.astype(bf16).reshape(BLK, WID, CH)
    out_ref[pl.ds(first, BLK)] = block
    head_ref[pl.ds(first, BLK)] = block[:, 0:3]
    tail_ref[pl.ds(first, BLK)] = block[:, WID - 3 : WID]


def forward_kernel(
    state_ref, left_ref, right_ref, adjoint_ref, kernel_ref, gain_ref, up_ref, bias_ref, down_ref,
    hidden_out, head_out, tail_out, slope_out, unit_out,
    shifts, padded, hidden,
):
    gain = gain_ref[...]
    for step in range(2):
        build_shifts(
            shifts, padded,
            lambda row: state_ref[step, row],
            lambda row: left_ref[step, row],
            lambda row: right_ref[step, row],
        )

        def block(index, carry):
            first = index * BLK

            def emit(target, low, high, value):
                hidden[target, :, low:high] = value

            convolve(shifts, kernel_ref, first, False, emit)
            unit, inv_std = normalise(hidden[...].reshape(ROWS, CH))
            normed = (unit * gain).astype(bf16)

            def slope_at(cols):
                preact = jnp.dot(normed, up_ref[:, cols], preferred_element_type=f32)
                return gelu_slope(preact + bias_ref[:, cols])

            if step == 0:
                adjoint = adjoint_ref[pl.ds(first, BLK)].reshape(ROWS, CH)
                result = backward(adjoint, slope_at, down_ref, up_ref, gain, unit, inv_std)
                put_hidden(result, first, hidden_out, head_out, tail_out)
            else:
                rows = pl.ds(pl.multiple_of(index * ROWS, ROWS), ROWS)
                for part in range(3):
                    cols = slice(part * 256, (part + 1) * 256)
                    slope_out[rows, cols] = slope_at(cols).astype(bf16)
                unit_out[rows, 0:CH] = unit
                unit_out[rows, CH:256] = jnp.broadcast_to(inv_std, (ROWS, 256 - CH))
            return carry

        lax.fori_loop(0, LAT // BLK, block, 0)


EDGE = jax.ShapeDtypeStruct((LAT, 3, CH), bf16)
FIELD = jax.ShapeDtypeStruct((LAT, WID, CH), bf16)
SHIFT_SCRATCH = [pltpu.VMEM((7, LAT + 6, WID, CH), f32), pltpu.VMEM((WID + 8, CH), f32)]
BIG = pltpu.CompilerParams(vmem_limit_bytes=40 * 1024 * 1024)


def forward_both(states, left, right, adjoint, kernel, gain, up, bias, down):
    return pl.pallas_call(
        forward_kernel,
        out_shape=(
            FIELD, EDGE, EDGE,
            jax.ShapeDtypeStruct((CELLS, HID), bf16),
            jax.ShapeDtypeStruct((CELLS, 256), f32),
        ),
        scratch_shapes=SHIFT_SCRATCH + [pltpu.VMEM((BLK, WID, CH), f32)],
        compiler_params=BIG,
        cost_estimate=pl.CostEstimate(flops=8 * CELLS * CH * HID, bytes_accessed=8000000, transcendentals=2 * CELLS * HID),
    )(states, left, right, adjoint, kernel, gain, up, bias, down)


def spread_kernel(hidden_ref, left_ref, right_ref, base_ref, kernel_ref, out_ref, shifts, padded):
    build_shifts(
        shifts, padded,
        lambda row: hidden_ref[row],
        lambda row: left_ref[row],
        lambda row: right_ref[row],
    )

    def block(index, carry):
        first = index * BLK

        def emit(target, low, high, value):
            base = base_ref[first + target, :, low:high].astype(f32)
            out_ref[first + target, :, low:high] = (base + value).astype(out_ref.dtype)

        convolve(shifts, kernel_ref, first, True, emit)
        return carry

    lax.fori_loop(0, LAT // BLK, block, 0)


def spread_back(hidden, left, right, base, kernel, dtype):
    return pl.pallas_call(
        spread_kernel,
        out_shape=jax.ShapeDtypeStruct((LAT, WID, CH), dtype),
        scratch_shapes=SHIFT_SCRATCH,
        compiler_params=BIG,
        cost_estimate=pl.CostEstimate(flops=98 * CELLS * CH, bytes_accessed=3000000, transcendentals=0),
    )(hidden, left, right, base, kernel)


def second_kernel(
    partial_ref, rows_ref, got_ref, slope_ref, unit_ref, gain_ref, up_ref, down_ref,
    hidden_out, head_out, tail_out, adjoint_out, hot,
):
    gain = gain_ref[...]
    forcing = forcing_of(0, rows_ref, got_ref, hot, 0, CELLS)
    adjoint_all = (partial_ref[...].reshape(CELLS, CH) + forcing).astype(bf16)
    adjoint_out[...] = adjoint_all.reshape(LAT, WID, CH)

    def block(index, carry):
        first = index * BLK
        rows = pl.ds(pl.multiple_of(index * ROWS, ROWS), ROWS)
        adjoint = adjoint_out[pl.ds(first, BLK)].reshape(ROWS, CH)
        result = backward(
            adjoint,
            lambda cols: slope_ref[rows, cols].astype(f32),
            down_ref, up_ref, gain,
            unit_ref[rows, 0:CH], unit_ref[rows, CH : CH + 1],
        )
        put_hidden(result, first, hidden_out, head_out, tail_out)
        return carry

    lax.fori_loop(0, LAT // BLK, block, 0)


def second_step(partial, rows, got, slope, unit, gain, up, down):
    return pl.pallas_call(
        second_kernel,
        out_shape=(FIELD, EDGE, EDGE, FIELD),
        scratch_shapes=[pltpu.VMEM((SLOTS, CELLS), bf16)],
        compiler_params=BIG,
        cost_estimate=pl.CostEstimate(flops=4 * CELLS * CH * HID, bytes_accessed=5000000, transcendentals=0),
    )(partial, rows, got, slope, unit, gain, up, down)


def base_kernel(adjoint_ref, rows_ref, got_ref, out_ref, hot):
    forcing = forcing_of(1, rows_ref, got_ref, hot, 0, CELLS)
    out_ref[...] = adjoint_ref[...].astype(f32) + forcing.reshape(LAT, WID, CH)


def last_base(adjoint, rows, got):
    return pl.pallas_call(
        base_kernel,
        out_shape=jax.ShapeDtypeStruct((LAT, WID, CH), f32),
        scratch_shapes=[pltpu.VMEM((SLOTS, CELLS), bf16)],
        compiler_params=BIG,
        cost_estimate=pl.CostEstimate(flops=2 * SLOTS * CELLS * CH, bytes_accessed=1500000, transcendentals=0),
    )(adjoint, rows, got)


def swap_edges(head, tail):
    peers = lax.axis_size("tile")
    up = [(i, (i + 1) % peers) for i in range(peers)]
    down = [(j, i) for i, j in up]
    return lax.ppermute(tail, "tile", up), lax.ppermute(head, "tile", down)


def pack_observations(cells, counts, values, errors):
    member = lax.axis_index("member")
    live = lax.broadcasted_iota(jnp.int32, cells.shape, 2) < counts[:, :, None]
    masked = jnp.where(live, cells, -1).astype(bf16)
    pick = lambda array: lax.dynamic_slice_in_dim(array, member, 1, axis=2)
    packed = jnp.concatenate(
        [pick(values)[:, :, 0], masked, pick(errors), pick(masked), jnp.zeros(cells.shape[:2] + (256 - CH - CAP - 2,), bf16)],
        axis=2,
    )
    return packed.transpose(1, 0, 2)


def exchange(array, axis):
    return lax.all_to_all(array, axis, split_axis=0, concat_axis=0, tiled=True)


def per_device(
    adjoint_final, states, kernel, norm_gain, up_weight, up_bias, down_weight,
    obs_cell, obs_count, obs_value, obs_error,
):
    adjoint = adjoint_final[0]
    states = states[:, 0]
    taps = kernel.reshape(49, CH)
    gain = norm_gain[None]
    bias = up_bias[None]

    packed = pack_observations(obs_cell[:, 0], obs_count[:, 0], obs_value[:, 0], obs_error[:, 0])
    got = exchange(packed, "tile")
    left, right = swap_edges(states[:, :, 0:3], states[:, :, WID - 3 : WID])

    rows = gather_rows(got, states.reshape(2, CELLS, CH))
    owned = exchange(rows, "member")

    hidden, head, tail, slope, unit = forward_both(
        states, left, right, adjoint, taps, gain, up_weight, bias, down_weight
    )
    partial = spread_back(hidden, *swap_edges(head, tail), adjoint, taps, f32)

    back0 = exchange(departures(0, owned, got), "member")
    back1 = exchange(departures(1, owned, got), "member")

    hidden, head, tail, adjoint = second_step(partial, back0, got, slope, unit, gain, up_weight, down_weight)
    base = last_base(adjoint, back1, got)
    return spread_back(hidden, *swap_edges(head, tail), base, taps, bf16)[None]


def solution(mesh):
    placed = (
        P("member", None, "tile", None),
        P(None, "member", None, "tile", None),
        P(),
        P(),
        P(),
        P(),
        P(),
        P(None, "tile", None, None),
        P(None, "tile", None),
        P(None, "tile", None, None, None),
        P(None, "tile", None, None),
    )
    return jax.shard_map(
        per_device,
        mesh=mesh,
        in_specs=placed,
        out_specs=P("member", None, "tile", None),
        check_vma=False,
    )
```

time: 340 us -> 163 us (0.48)
  the two profiles are of different devices: /device:TPU:32 before, /device:TPU:31 now
where the time goes in v1:
time: 163 us; the launch traced here: 162 us
  starting transfers between devices  46.1 us (28%)
  blocking collectives  43.8 us (27%)
  Pallas kernels  42.2 us (26%)
  waiting for transfers between devices  25.1 us (15%)
  local copies, waits for them, and re-layouts  4.92 us (3%)
    all_to_all x2, blocking collectives, exchange(): return lax.all_to_all(array, axis, split_axis=0, concat_axis=0, tiled=True)  43.8 us
    all_to_all x2, starting transfers between devices, exchange(): return lax.all_to_all(array, axis, split_axis=0, concat_axis=0, tiled=True)  23.3 us
    ppermute x6, starting transfers between devices, swap_edges(): return (lax.ppermute(tail, 'tile', up), lax.ppermute(head, 'tile', down))  22.8 us
    pallas_call x1, Pallas kernels, forward_both(): pl.pallas_call(forward_kernel, out_shape=(FIELD, EDGE, EDGE, jax.ShapeDty...  18.8 us
    ppermute x6, waiting for transfers between devices, swap_edges(): return (lax.ppermute(tail, 'tile', up), lax.ppermute(head, 'tile', down))  13.5 us
    all_to_all x2, waiting for transfers between devices, exchange(): return lax.all_to_all(array, axis, split_axis=0, concat_axis=0, tiled=True)  11.6 us
    pallas_call x2, Pallas kernels, spread_back(): pl.pallas_call(spread_kernel, out_shape=jax.ShapeDtypeStruct((LAT, WID, C...  11.1 us
    pallas_call x2, Pallas kernels, departures(): pl.pallas_call(functools.partial(departure_kernel, step), out_shape=jax.S...  4.16 us
  transfers between devices with their start and end apart: 8, of which 4 were waited for; matrix products, arithmetic and copies ran while one was open for 1% of the time, Pallas kernels for 19%

profile of v1, /device:TPU:31, one launch (start us, length us, event | category | flops | bytes accessed | tf_op | source)
XLA Modules:
  0.0 162.4 jit_solution(2921345963551527889)
XLA Ops:
  0.0 0.0 copy-start
  0.0 0.8 constant_dynamic-slice_fusion.1
  0.8 0.1 copy.22
  0.9 0.8 copy.20
  1.6 0.8 copy.21
  2.4 0.1 fusion
  2.5 0.1 constant_dynamic-slice_fusion
  2.6 0.0 copy-done
  2.6 0.1 constant_dynamic-slice_fusion.2
  2.7 0.1 copy.27
  2.8 0.3 concatenate.3
  3.1 13.2 %all_to_all.20.got_ref = bf16[32,2,256]{2,1,0:T(2,128)(2,1)} all-to-all(bf16[32,2,256]{2,1,0:T(2,128)(2,1)S(1)} %bitcast.23), channel_id=1, replica_groups=mesh['member'=16,'tile'=32] {'tile'}, dimensions={0} | all-to-all | bytes 65536 | tf_op jit(solution)/shard_map/all_to_all | solution.py:321
  16.4 3.5 %shard_map.111 = bf16[16,32,384]{2,1,0:T(8,128)(2,1)} custom-call(bf16[32,2,256]{2,1,0:T(2,128)(2,1)} %all_to_all.20.got_ref, bf16[2,1024,192]{2,1,0:T(8,128)(2,1)} %bitcast.17), custom_call_target="tpu_custom_call" | custom-call | flops 402653184 | bytes 2000000 | tf_op jit(solution)/shard_map/pallas_call | solution.py:92
  19.8 0.0 copy-start.4
  19.8 30.5 %all_to_all.21.rows_ref = bf16[16,32,384]{2,1,0:T(8,128)(2,1)} all-to-all(bf16[16,32,384]{2,1,0:T(8,128)(2,1)} %shard_map.111), channel_id=1, replica_groups=mesh['member'=16,'tile'=32] {'member'}, dimensions={0} | all-to-all | bytes 786432 | tf_op jit(solution)/shard_map/all_to_all | solution.py:321
  50.4 0.0 copy-start.7
  50.4 0.0 copy-start.6
  50.4 2.0 %shard_map.112 = bf16[16,32,192]{2,1,0:T(8,128)(2,1)} custom-call(bf16[16,32,384]{2,1,0:T(8,128)(2,1)} %all_to_all.21.rows_ref, bf16[32,2,256]{2,1,0:T(2,128)(2,1)} %all_to_all.20.got_ref), custom_call_target="tpu_custom_call" | custom-call | flops 600000 | bytes 600000 | tf_op jit(solution)/shard_map/pallas_call | solution.py:113
  52.4 0.0 copy-start.2
  52.4 0.0 copy-start.3
  52.4 0.0 copy-start.5
  52.4 13.0 %all-to-all-start.2 = ((bf16[16,32,192]{2,1,0:T(8,128)(2,1)}), bf16[16,32,192]{2,1,0:T(8,128)(2,1)S(1)}, u32[]{:S(2)}, u32[]{:S(2)}) async-start(bf16[16,32,192]{2,1,0:T(8,128)(2,1)} %shard_map.112), calls=%async_computation.2 | async-start | bytes 524288 | tf_op jit(solution)/shard_map/all_to_all | solution.py:321
  65.4 2.1 %shard_map.114 = bf16[16,32,192]{2,1,0:T(8,128)(2,1)} custom-call(bf16[16,32,384]{2,1,0:T(8,128)(2,1)} %all_to_all.21.rows_ref, bf16[32,2,256]{2,1,0:T(2,128)(2,1)} %all_to_all.20.got_ref), custom_call_target="tpu_custom_call" | custom-call | flops 600000 | bytes 600000 | tf_op jit(solution)/shard_map/pallas_call | solution.py:113
  67.5 11.6 %all-to-all-done.2.rows_ref = bf16[16,32,192]{2,1,0:T(8,128)(2,1)S(1)} async-done(((bf16[16,32,192]{2,1,0:T(8,128)(2,1)}), bf16[16,32,192]{2,1,0:T(8,128)(2,1)S(1)}, u32[]{:S(2)}, u32[]{:S(2)}) %all-to-all-start.2) | async-done | bytes 196640 | tf_op jit(solution)/shard_map/all_to_all | solution.py:321
  79.1 10.4 %all-to-all-start.3 = ((bf16[16,32,192]{2,1,0:T(8,128)(2,1)}), bf16[16,32,192]{2,1,0:T(8,128)(2,1)S(1)}, u32[]{:S(2)}, u32[]{:S(2)}) async-start(bf16[16,32,192]{2,1,0:T(8,128)(2,1)} %shard_map.114), calls=%async_computation.3 | async-start | bytes 524288 | tf_op jit(solution)/shard_map/all_to_all | solution.py:321
  89.5 0.0 copy-done.4
  89.5 0.8 fusion.1
  90.3 2.9 %collective-permute-start.1 = (bf16[2,32,3,192]{3,2,1,0:T(4,128)(2,1)}, bf16[2,32,3,192]{3,2,1,0:T(4,128)(2,1)S(1)}, u32[]{:S(2)}, u32[]{:S(2)}) collective-permute-start(bf16[2,32,3,192]{3,2,1,0:T(4,128)(2,1)} %get-tuple-element.23), channel_id=1, source_target_pairs={{1,0},{2,1},{3,2},{4,3},{5,4},{6,5},{7,6},{8,7},{9,8},{10,9},{11,1... | collective-permute-start | bytes 221192 | tf_op jit(solution)/shard_map/ppermute | solution.py:305
  93.2 6.0 %collective-permute-start = (bf16[2,32,3,192]{3,2,1,0:T(4,128)(2,1)}, bf16[2,32,3,192]{3,2,1,0:T(4,128)(2,1)}, u32[]{:S(2)}, u32[]{:S(2)}) collective-permute-start(bf16[2,32,3,192]{3,2,1,0:T(4,128)(2,1)} %get-tuple-element.24), channel_id=1, source_target_pairs={{0,1},{1,2},{2,3},{3,4},{4,5},{5,6},{6,7},{7,8},{8,9},{9,10},{10,1... | collective-permute-start | bytes 221192 | tf_op jit(solution)/shard_map/ppermute | solution.py:305
  99.2 0.0 copy-done.7
  99.2 0.0 copy-done.6
  99.2 1.1 copy.18.down_ref
  100.4 0.0 collective-permute-done.1.right_ref
  100.4 1.0 collective-permute-done.left_ref
  101.4 0.0 copy-done.2
  101.4 0.0 copy-done.3
  101.4 0.0 copy-done.5
  101.4 18.8 %shard_map.109 = (bf16[32,32,192]{2,1,0:T(8,128)(2,1)S(1)}, bf16[32,3,192]{2,1,0:T(4,128)(2,1)S(1)}, bf16[32,3,192]{2,1,0:T(4,128)(2,1)S(1)}, bf16[1024,768]{1,0:T(8,128)(2,1)S(1)}, f32[1024,256]{1,0:T(8,128)S(1)}) custom-call(bf16[2,32,32,192]{3,2,1,0:T(8,128)(2,1)S(1)} %bitcast.19, bf16[2,32,3,192]{3,2,1,0:T(4,128)(2,1)} %collective-permute-done.left_ref, ...), custom_call_target="tpu_custom_call" | custom-call | flops 1207959552 | bytes 8000000 | tf_op jit(solution)/shard_map/pallas_call | solution.py:207
  120.3 0.0 copy-start.1
  120.3 7.7 %collective-permute-start.2 = (bf16[32,3,192]{2,1,0:T(4,128)(2,1)S(1)}, bf16[32,3,192]{2,1,0:T(4,128)(2,1)S(1)}, u32[]{:S(2)}, u32[]{:S(2)}) collective-permute-start(bf16[32,3,192]{2,1,0:T(4,128)(2,1)S(1)} %get-tuple-element.15), channel_id=1, source_target_pairs={{0,1},{1,2},{2,3},{3,4},{4,5},{5,6},{6,7},{7,8},{8,9},{9,10},{10,1... | collective-permute-start | bytes 110600 | tf_op jit(solution)/shard_map/ppermute | solution.py:305
  128.0 1.9 %collective-permute-start.3 = (bf16[32,3,192]{2,1,0:T(4,128)(2,1)S(1)}, bf16[32,3,192]{2,1,0:T(4,128)(2,1)S(1)}, u32[]{:S(2)}, u32[]{:S(2)}) collective-permute-start(bf16[32,3,192]{2,1,0:T(4,128)(2,1)S(1)} %get-tuple-element.16), channel_id=1, source_target_pairs={{1,0},{2,1},{3,2},{4,3},{5,4},{6,5},{7,6},{8,7},{9,8},{10,9},{11,1... | collective-permute-start | bytes 110600 | tf_op jit(solution)/shard_map/ppermute | solution.py:305
  129.9 0.0 collective-permute-done.2.left_ref
  129.9 7.0 %collective-permute-done.3.right_ref = bf16[32,3,192]{2,1,0:T(4,128)(2,1)S(1)} collective-permute-done((bf16[32,3,192]{2,1,0:T(4,128)(2,1)S(1)}, bf16[32,3,192]{2,1,0:T(4,128)(2,1)S(1)}, u32[]{:S(2)}, u32[]{:S(2)}) %collective-permute-start.3) | collective-permute-done | bytes 36896 | tf_op jit(solution)/shard_map/ppermute | solution.py:305
  136.9 5.1 %shard_map.110.partial_ref = f32[32,32,192]{2,1,0:T(8,128)S(1)} custom-call(bf16[32,32,192]{2,1,0:T(8,128)(2,1)S(1)} %get-tuple-element.14.hidden_ref, bf16[32,3,192]{2,1,0:T(4,128)(2,1)S(1)} %collective-permute-done.2.left_ref, bf16[32,3,192]{2,1,0:T(4,128)(2,1)S(1)} %collective-permute-done.3.right_ref, bf16[32,32,192]{2,1,0:T(8,128)(2,1)S(1)} %bitcast.16, ...), custom_call_target="tpu_custom_call" | custom-call | flops 19267584 | bytes 3000000 | tf_op jit(solution)/shard_map/pallas_call | solution.py:242
  141.9 0.0 copy-done.1
  141.9 3.6 %shard_map.113 = (bf16[32,32,192]{2,1,0:T(8,128)(2,1)S(1)}, bf16[32,3,192]{2,1,0:T(4,128)(2,1)S(1)}, bf16[32,3,192]{2,1,0:T(4,128)(2,1)S(1)}, bf16[32,32,192]{2,1,0:T(8,128)(2,1)S(1)}) custom-call(f32[32,32,192]{2,1,0:T(8,128)S(1)} %shard_map.110.partial_ref, bf16[16,32,192]{2,1,0:T(8,128)(2,1)S(1)} %all-to-all-done.2.rows_ref, ...), custom_call_target="tpu_custom_call" | custom-call | flops 603979776 | bytes 5000000 | tf_op jit(solution)/shard_map/pallas_call | solution.py:277
  145.6 1.9 %collective-permute-start.4 = (bf16[32,3,192]{2,1,0:T(4,128)(2,1)S(1)}, bf16[32,3,192]{2,1,0:T(4,128)(2,1)S(1)}, u32[]{:S(2)}, u32[]{:S(2)}) collective-permute-start(bf16[32,3,192]{2,1,0:T(4,128)(2,1)S(1)} %get-tuple-element.20), channel_id=1, source_target_pairs={{0,1},{1,2},{2,3},{3,4},{4,5},{5,6},{6,7},{7,8},{8,9},{9,10},{10,1... | collective-permute-start | bytes 110600 | tf_op jit(solution)/shard_map/ppermute | solution.py:305
  147.5 2.4 %collective-permute-start.5 = (bf16[32,3,192]{2,1,0:T(4,128)(2,1)S(1)}, bf16[32,3,192]{2,1,0:T(4,128)(2,1)S(1)}, u32[]{:S(2)}, u32[]{:S(2)}) collective-permute-start(bf16[32,3,192]{2,1,0:T(4,128)(2,1)S(1)} %get-tuple-element.21), channel_id=1, source_target_pairs={{1,0},{2,1},{3,2},{4,3},{5,4},{6,5},{7,6},{8,7},{9,8},{10,9},{11,1... | collective-permute-start | bytes 110600 | tf_op jit(solution)/shard_map/ppermute | solution.py:305
  149.9 0.0 all-to-all-done.3.rows_ref
  149.9 1.0 shard_map.115.base_ref
  150.9 0.0 collective-permute-done.4.left_ref
  150.9 5.5 %collective-permute-done.5.right_ref = bf16[32,3,192]{2,1,0:T(4,128)(2,1)S(1)} collective-permute-done((bf16[32,3,192]{2,1,0:T(4,128)(2,1)S(1)}, bf16[32,3,192]{2,1,0:T(4,128)(2,1)S(1)}, u32[]{:S(2)}, u32[]{:S(2)}) %collective-permute-start.5) | collective-permute-done | bytes 36896 | tf_op jit(solution)/shard_map/ppermute | solution.py:305
  156.4 6.0 %shard_map.116 = bf16[32,32,192]{2,1,0:T(8,128)(2,1)} custom-call(bf16[32,32,192]{2,1,0:T(8,128)(2,1)S(1)} %get-tuple-element.19.hidden_ref, bf16[32,3,192]{2,1,0:T(4,128)(2,1)S(1)} %collective-permute-done.4.left_ref, bf16[32,3,192]{2,1,0:T(4,128)(2,1)S(1)} %collective-permute-done.5.right_ref, f32[32,32,192]{2,1,0:T(8,128)S(1)} %shard_map.115.base_ref, ...), custom_call_target="tpu_custom_call" | custom-call | flops 19267584 | bytes 3000000 | tf_op jit(solution)/shard_map/pallas_call | solution.py:242
  (4 shorter events, 0.0 us)
Async XLA Ops:
  0.0 2.6 %copy-start = (bf16[2,1,32,16,192]{4,3,2,1,0:T(8,128)(2,1)S(1)}, bf16[2,1,32,16,192]{4,3,2,1,0:T(8,128)(2,1)}, u32[]{:S(2)}) copy-start(bf16[2,1,32,16,192]{4,3,2,1,0:T(8,128)(2,1)} %param.20) | copy-start | bytes 1179652
  19.8 69.6 %copy-start.4 = (bf16[2,1,32,32,192]{4,3,2,1,0:T(8,128)(2,1)S(1)}, bf16[2,1,32,32,192]{4,3,2,1,0:T(8,128)(2,1)}, u32[]{:S(2)}) copy-start(bf16[2,1,32,32,192]{4,3,2,1,0:T(8,128)(2,1)} %param.12) | copy-start | bytes 2359300
  50.4 48.8 %copy-start.7 = (f32[768]{0:T(1024)S(1)}, f32[768]{0:T(1024)}, u32[]{:S(2)}) copy-start(f32[768]{0:T(1024)} %param.16) | copy-start | bytes 9220
  50.4 48.8 %copy-start.6 = (f32[7,7,192]{2,1,0:T(8,128)S(1)}, f32[7,7,192]{2,1,0:T(8,128)}, u32[]{:S(2)}) copy-start(f32[7,7,192]{2,1,0:T(8,128)} %param.13) | copy-start | bytes 112900
  52.4 49.0 %copy-start.2 = (bf16[1,32,32,192]{3,2,1,0:T(8,128)(2,1)S(1)}, bf16[1,32,32,192]{3,2,1,0:T(8,128)(2,1)}, u32[]{:S(2)}) copy-start(bf16[1,32,32,192]{3,2,1,0:T(8,128)(2,1)} %param.11) | copy-start | bytes 1179652
  52.4 49.0 %copy-start.3 = (bf16[192,768]{1,0:T(8,128)(2,1)S(1)}, bf16[192,768]{1,0:T(8,128)(2,1)}, u32[]{:S(2)}) copy-start(bf16[192,768]{1,0:T(8,128)(2,1)} %up_ref.3) | copy-start | bytes 884740
  52.4 49.0 %copy-start.5 = (f32[192]{0:T(256)S(1)}, f32[192]{0:T(256)}, u32[]{:S(2)}) copy-start(f32[192]{0:T(256)} %param.14) | copy-start | bytes 2308
  52.4 26.7 %all-to-all-start.2 = ((bf16[16,32,192]{2,1,0:T(8,128)(2,1)}), bf16[16,32,192]{2,1,0:T(8,128)(2,1)S(1)}, u32[]{:S(2)}, u32[]{:S(2)}) async-start(bf16[16,32,192]{2,1,0:T(8,128)(2,1)} %shard_map.112), calls=%async_computation.2 | async-start | bytes 524288 | tf_op jit(solution)/shard_map/all_to_all | solution.py:321
  79.1 70.8 %all-to-all-start.3 = ((bf16[16,32,192]{2,1,0:T(8,128)(2,1)}), bf16[16,32,192]{2,1,0:T(8,128)(2,1)S(1)}, u32[]{:S(2)}, u32[]{:S(2)}) async-start(bf16[16,32,192]{2,1,0:T(8,128)(2,1)} %shard_map.114), calls=%async_computation.3 | async-start | bytes 524288 | tf_op jit(solution)/shard_map/all_to_all | solution.py:321
  90.3 10.1 %collective-permute-start.1 = (bf16[2,32,3,192]{3,2,1,0:T(4,128)(2,1)}, bf16[2,32,3,192]{3,2,1,0:T(4,128)(2,1)S(1)}, u32[]{:S(2)}, u32[]{:S(2)}) collective-permute-start(bf16[2,32,3,192]{3,2,1,0:T(4,128)(2,1)} %get-tuple-element.23), channel_id=1, source_target_pairs={{1,0},{2,1},{3,2},{4,3},{5,4},{6,5},{7,6},{8,7},{9,8},{10,9},{11,1... | collective-permute-start | bytes 221192 | tf_op jit(solution)/shard_map/ppermute | solution.py:305
  93.2 8.2 %collective-permute-start = (bf16[2,32,3,192]{3,2,1,0:T(4,128)(2,1)}, bf16[2,32,3,192]{3,2,1,0:T(4,128)(2,1)}, u32[]{:S(2)}, u32[]{:S(2)}) collective-permute-start(bf16[2,32,3,192]{3,2,1,0:T(4,128)(2,1)} %get-tuple-element.24), channel_id=1, source_target_pairs={{0,1},{1,2},{2,3},{3,4},{4,5},{5,6},{6,7},{7,8},{8,9},{9,10},{10,1... | collective-permute-start | bytes 221192 | tf_op jit(solution)/shard_map/ppermute | solution.py:305
  120.3 21.7 %copy-start.1 = (bf16[32,2,256]{2,1,0:T(2,128)(2,1)S(1)}, bf16[32,2,256]{2,1,0:T(2,128)(2,1)}, u32[]{:S(2)}) copy-start(bf16[32,2,256]{2,1,0:T(2,128)(2,1)} %all_to_all.20.got_ref) | copy-start | bytes 98308
  120.3 9.6 %collective-permute-start.2 = (bf16[32,3,192]{2,1,0:T(4,128)(2,1)S(1)}, bf16[32,3,192]{2,1,0:T(4,128)(2,1)S(1)}, u32[]{:S(2)}, u32[]{:S(2)}) collective-permute-start(bf16[32,3,192]{2,1,0:T(4,128)(2,1)S(1)} %get-tuple-element.15), channel_id=1, source_target_pairs={{0,1},{1,2},{2,3},{3,4},{4,5},{5,6},{6,7},{7,8},{8,9},{9,10},{10,1... | collective-permute-start | bytes 110600 | tf_op jit(solution)/shard_map/ppermute | solution.py:305
  128.0 8.9 %collective-permute-start.3 = (bf16[32,3,192]{2,1,0:T(4,128)(2,1)S(1)}, bf16[32,3,192]{2,1,0:T(4,128)(2,1)S(1)}, u32[]{:S(2)}, u32[]{:S(2)}) collective-permute-start(bf16[32,3,192]{2,1,0:T(4,128)(2,1)S(1)} %get-tuple-element.16), channel_id=1, source_target_pairs={{1,0},{2,1},{3,2},{4,3},{5,4},{6,5},{7,6},{8,7},{9,8},{10,9},{11,1... | collective-permute-start | bytes 110600 | tf_op jit(solution)/shard_map/ppermute | solution.py:305
  145.6 5.3 %collective-permute-start.4 = (bf16[32,3,192]{2,1,0:T(4,128)(2,1)S(1)}, bf16[32,3,192]{2,1,0:T(4,128)(2,1)S(1)}, u32[]{:S(2)}, u32[]{:S(2)}) collective-permute-start(bf16[32,3,192]{2,1,0:T(4,128)(2,1)S(1)} %get-tuple-element.20), channel_id=1, source_target_pairs={{0,1},{1,2},{2,3},{3,4},{4,5},{5,6},{6,7},{7,8},{8,9},{9,10},{10,1... | collective-permute-start | bytes 110600 | tf_op jit(solution)/shard_map/ppermute | solution.py:305
  147.5 8.9 %collective-permute-start.5 = (bf16[32,3,192]{2,1,0:T(4,128)(2,1)S(1)}, bf16[32,3,192]{2,1,0:T(4,128)(2,1)S(1)}, u32[]{:S(2)}, u32[]{:S(2)}) collective-permute-start(bf16[32,3,192]{2,1,0:T(4,128)(2,1)S(1)} %get-tuple-element.21), channel_id=1, source_target_pairs={{1,0},{2,1},{3,2},{4,3},{5,4},{6,5},{7,6},{8,7},{9,8},{10,9},{11,1... | collective-permute-start | bytes 110600 | tf_op jit(solution)/shard_map/ppermute | solution.py:305

commit v2 on v1

v2 whole, which is shorter than its diff:
```python
import functools
import math

import jax
import jax.numpy as jnp
from jax import lax
from jax.experimental import pallas as pl
from jax.experimental.pallas import tpu as pltpu
from jax.sharding import PartitionSpec as P

slope_coef = math.sqrt(2.0 / math.pi)
cubic_coef = 0.044715
norm_eps = 1e-06

LAT = 32
WID = 32
CH = 192
HID = 768
CAP = 16
CELLS = LAT * WID
SLOTS = LAT * CAP
BLK = 8
ROWS = BLK * WID
f32 = jnp.float32
bf16 = jnp.bfloat16
NT = (((1,), (1,)), ((), ()))
TN = (((0,), (0,)), ((), ()))


def gelu_slope(preact):
    square = preact * preact
    tanh_val = jnp.tanh(preact * (slope_coef + (slope_coef * cubic_coef) * square))
    tail = preact * (0.5 * slope_coef + (1.5 * slope_coef * cubic_coef) * square)
    return (0.5 + 0.5 * tanh_val) + tail * (1.0 - tanh_val * tanh_val)


def mean_lanes(value):
    return jnp.sum(value, axis=-1, keepdims=True) * (1.0 / CH)


def build_shifts(shifts, padded, centre, left, right):
    for edge in range(3):
        zeros = jnp.zeros((WID, CH), f32)
        for col in range(7):
            shifts[col, edge] = zeros
            shifts[col, LAT + 3 + edge] = zeros

    def one_row(row, carry):
        padded[0:3] = left(row).astype(f32)
        padded[3 : WID + 3] = centre(row).astype(f32)
        padded[WID + 3 : WID + 6] = right(row).astype(f32)
        for col in range(7):
            shifts[col, row + 3] = padded[col : col + WID]
        return carry

    lax.fori_loop(0, LAT, one_row, 0)


def convolve(shifts, kernel_ref, first, flip, emit):
    for low, high in ((0, 128), (128, CH)):
        sums = [None] * BLK
        for col in range(7):
            taps = []
            for row in range(7):
                index = (6 - row) * 7 + 6 - col if flip else row * 7 + col
                taps.append(jnp.broadcast_to(kernel_ref[index : index + 1, low:high], (WID, high - low)))
            for source in range(BLK + 6):
                field = shifts[col, first + source, :, low:high]
                for row in range(7):
                    target = source - row
                    if 0 <= target < BLK:
                        term = taps[row] * field
                        sums[target] = term if sums[target] is None else sums[target] + term
        for target in range(BLK):
            emit(target, low, high, sums[target])


def cut_kernel(state_ref, head_ref, tail_ref):
    head_ref[...] = state_ref[:, :, 0:3]
    tail_ref[...] = state_ref[:, :, WID - 3 : WID]


def cut_edges(states):
    edge = jax.ShapeDtypeStruct((2, LAT, 3, CH), bf16)
    return pl.pallas_call(cut_kernel, out_shape=(edge, edge))(states)


def pack_kernel(cell_ref, count_ref, value_ref, error_ref, out_ref):
    member = lax.axis_index("member")
    tiles = cell_ref.shape[1]
    slot = lax.broadcasted_iota(jnp.int32, (tiles, CAP), 1)
    same = lax.broadcasted_iota(jnp.int32, (tiles, tiles), 0) == lax.broadcasted_iota(jnp.int32, (tiles, tiles), 1)
    deep = lax.broadcasted_iota(jnp.int32, (tiles, CAP, CH), 1)
    for step in range(2):
        counts = count_ref[step : step + 1, :].astype(f32)
        count = jnp.sum(jnp.where(same, jnp.broadcast_to(counts, (tiles, tiles)), 0.0), axis=1, keepdims=True)
        cells = jnp.where(slot.astype(f32) < count, cell_ref[step].astype(f32), -1.0)
        pick = lambda array: jnp.sum(jnp.where(slot == member, array, 0.0), axis=1, keepdims=True)
        values = jnp.sum(jnp.where(deep == member, value_ref[step].astype(f32), 0.0), axis=1)
        out_ref[:, 2 * step, :] = values[:, 0:128]
        out_ref[:, 2 * step + 1, :] = jnp.concatenate(
            [values[:, 128:CH], cells, jnp.broadcast_to(pick(error_ref[step].astype(f32)), (tiles, CAP)),
             jnp.broadcast_to(pick(cells), (tiles, 2 * CAP))], axis=1)


def pack_observations(cells, counts, values, errors):
    return pl.pallas_call(
        pack_kernel,
        out_shape=jax.ShapeDtypeStruct((cells.shape[1], 4, 128), f32),
    )(cells, counts, values, errors)


def one_hot(step, got_ref, hot_ref):
    cells = got_ref[:, 2 * step + 1, 64 : 64 + CAP]
    lane = lax.broadcasted_iota(jnp.int32, (LAT, CELLS), 1)
    band = lax.broadcasted_iota(jnp.int32, (LAT, CELLS), 0)
    offset = (lane - band * WID).astype(f32)
    for slot in range(CAP):
        hot = jnp.where(offset == cells[:, slot : slot + 1], 1.0, 0.0)
        hot_ref[slot * LAT : (slot + 1) * LAT] = hot.astype(bf16)


def gather_kernel(got_ref, state_ref, out_ref, *hots):
    for step in range(2):
        one_hot(step, got_ref, hots[step])
        rows = jnp.dot(hots[step][...], state_ref[step].reshape(CELLS, CH), preferred_element_type=f32)
        out_ref[:, :, step * CH : (step + 1) * CH] = rows.astype(bf16).reshape(CAP, LAT, CH)


def gather_rows(got, states):
    hot = jax.ShapeDtypeStruct((SLOTS, CELLS), bf16)
    return pl.pallas_call(
        gather_kernel,
        out_shape=(jax.ShapeDtypeStruct((CAP, LAT, 2 * CH), bf16), hot, hot),
        cost_estimate=pl.CostEstimate(flops=4 * SLOTS * CELLS * CH, bytes_accessed=4000000, transcendentals=0),
    )(got, states)


def departure_kernel(rows_ref, got_ref, out_ref):
    for step in range(2):
        lanes = slice(step * CH, (step + 1) * CH)
        sampled = rows_ref[:, :, lanes].astype(f32)
        members = sampled.shape[0]
        other = got_ref[:, 2 * step + 1, :]
        values = jnp.concatenate([got_ref[:, 2 * step, :], other[:, 0:64]], axis=1)
        ens_mean = jnp.sum(sampled, axis=0) * (1.0 / members)
        ens_var = jnp.sum(sampled * sampled, axis=0) * (1.0 / members) - ens_mean * ens_mean
        weight = 1.0 / (other[:, 64 + CAP : 65 + CAP] + ens_var)
        ratio = (sampled - values[None]) * weight[None]
        live = other[:, 64 + 2 * CAP : 65 + 2 * CAP] >= 0.0
        out_ref[:, :, lanes] = jnp.where(live[None], ratio, 0.0).astype(bf16)


def departures(rows, got):
    return pl.pallas_call(
        departure_kernel,
        out_shape=jax.ShapeDtypeStruct((CAP, LAT, 2 * CH), bf16),
        cost_estimate=pl.CostEstimate(flops=1200000, bytes_accessed=1200000, transcendentals=0),
    )(rows, got)


def forcing_of(step, rows_ref, hot_ref):
    rows = rows_ref[:, :, step * CH : (step + 1) * CH].reshape(SLOTS, CH)
    return lax.dot_general(hot_ref[...], rows, TN, preferred_element_type=f32)


def normalise(hidden):
    centred = hidden - mean_lanes(hidden)
    inv_std = lax.rsqrt(mean_lanes(centred * centred) + norm_eps)
    return centred * inv_std, inv_std


def backward(adjoint, slope_at, down_ref, up_ref, gain, unit, inv_std):
    adj_norm = jnp.zeros((ROWS, CH), f32)
    for part in range(3):
        cols = slice(part * 256, (part + 1) * 256)
        act = lax.dot_general(adjoint, down_ref[cols, :], NT, preferred_element_type=f32)
        pre = (act * slope_at(cols)).astype(bf16)
        adj_norm = adj_norm + lax.dot_general(pre, up_ref[:, cols], NT, preferred_element_type=f32)
    scaled = adj_norm * gain
    return inv_std * (scaled - mean_lanes(scaled) - unit * mean_lanes(scaled * unit))


def put_hidden(adj_hidden, first, out_ref, head_ref, tail_ref):
    block = adj_hidden.astype(bf16).reshape(BLK, WID, CH)
    out_ref[pl.ds(first, BLK)] = block
    head_ref[pl.ds(first, BLK)] = block[:, 0:3]
    tail_ref[pl.ds(first, BLK)] = block[:, WID - 3 : WID]


def forward_kernel(step, state_ref, left_ref, right_ref, kernel_ref, gain_ref, up_ref, bias_ref, *rest):
    shifts, padded, hidden = rest[-3:]
    gain = gain_ref[...]
    build_shifts(
        shifts, padded,
        lambda row: state_ref[step, row],
        lambda row: left_ref[step, row],
        lambda row: right_ref[step, row],
    )

    def block(index, carry):
        first = index * BLK

        def emit(target, low, high, value):
            hidden[target, :, low:high] = value

        convolve(shifts, kernel_ref, first, False, emit)
        unit, inv_std = normalise(hidden[...].reshape(ROWS, CH))
        normed = (unit * gain).astype(bf16)

        def slope_at(cols):
            preact = jnp.dot(normed, up_ref[:, cols], preferred_element_type=f32)
            return gelu_slope(preact + bias_ref[:, cols])

        if step == 0:
            down_ref, adjoint_ref, hidden_out, head_out, tail_out = rest[:5]
            adjoint = adjoint_ref[pl.ds(first, BLK)].reshape(ROWS, CH)
            result = backward(adjoint, slope_at, down_ref, up_ref, gain, unit, inv_std)
            put_hidden(result, first, hidden_out, head_out, tail_out)
        else:
            slope_out, unit_out = rest[:2]
            rows = pl.ds(pl.multiple_of(index * ROWS, ROWS), ROWS)
            for part in range(3):
                cols = slice(part * 256, (part + 1) * 256)
                slope_out[rows, cols] = slope_at(cols).astype(bf16)
            unit_out[rows, 0:CH] = unit
            unit_out[rows, CH:256] = jnp.broadcast_to(inv_std, (ROWS, 256 - CH))
        return carry

    lax.fori_loop(0, LAT // BLK, block, 0)


EDGE = jax.ShapeDtypeStruct((LAT, 3, CH), bf16)
FIELD = jax.ShapeDtypeStruct((LAT, WID, CH), bf16)
SHIFT_SCRATCH = [pltpu.VMEM((7, LAT + 6, WID, CH), f32), pltpu.VMEM((WID + 8, CH), f32)]
BIG = pltpu.CompilerParams(vmem_limit_bytes=24 * 1024 * 1024)


def forward(step, *operands):
    shapes = (FIELD, EDGE, EDGE) if step == 0 else (
        jax.ShapeDtypeStruct((CELLS, HID), bf16),
        jax.ShapeDtypeStruct((CELLS, 256), f32),
    )
    return pl.pallas_call(
        functools.partial(forward_kernel, step),
        out_shape=shapes,
        scratch_shapes=SHIFT_SCRATCH + [pltpu.VMEM((BLK, WID, CH), f32)],
        compiler_params=BIG,
        cost_estimate=pl.CostEstimate(flops=6 * CELLS * CH * HID, bytes_accessed=8000000, transcendentals=CELLS * HID),
    )(*operands)


def spread_kernel(hidden_ref, left_ref, right_ref, base_ref, kernel_ref, out_ref, shifts, padded):
    build_shifts(
        shifts, padded,
        lambda row: hidden_ref[row],
        lambda row: left_ref[row],
        lambda row: right_ref[row],
    )

    def block(index, carry):
        first = index * BLK

        def emit(target, low, high, value):
            base = base_ref[first + target, :, low:high].astype(f32)
            out_ref[first + target, :, low:high] = (base + value).astype(out_ref.dtype)

        convolve(shifts, kernel_ref, first, True, emit)
        return carry

    lax.fori_loop(0, LAT // BLK, block, 0)


def spread_back(hidden, left, right, base, kernel, dtype):
    return pl.pallas_call(
        spread_kernel,
        out_shape=jax.ShapeDtypeStruct((LAT, WID, CH), dtype),
        scratch_shapes=SHIFT_SCRATCH,
        compiler_params=BIG,
        cost_estimate=pl.CostEstimate(flops=98 * CELLS * CH, bytes_accessed=3000000, transcendentals=0),
    )(hidden, left, right, base, kernel)


def second_kernel(
    partial_ref, rows_ref, hot_ref, slope_ref, unit_ref, gain_ref, up_ref, down_ref,
    hidden_out, head_out, tail_out, adjoint_out,
):
    gain = gain_ref[...]
    forcing = forcing_of(0, rows_ref, hot_ref)
    adjoint_all = (partial_ref[...].reshape(CELLS, CH) + forcing).astype(bf16)
    adjoint_out[...] = adjoint_all.reshape(LAT, WID, CH)

    def block(index, carry):
        first = index * BLK
        rows = pl.ds(pl.multiple_of(index * ROWS, ROWS), ROWS)
        adjoint = adjoint_out[pl.ds(first, BLK)].reshape(ROWS, CH)
        result = backward(
            adjoint,
            lambda cols: slope_ref[rows, cols].astype(f32),
            down_ref, up_ref, gain,
            unit_ref[rows, 0:CH], unit_ref[rows, CH : CH + 1],
        )
        put_hidden(result, first, hidden_out, head_out, tail_out)
        return carry

    lax.fori_loop(0, LAT // BLK, block, 0)


def second_step(partial, rows, hot, slope, unit, gain, up, down):
    return pl.pallas_call(
        second_kernel,
        out_shape=(FIELD, EDGE, EDGE, FIELD),
        compiler_params=BIG,
        cost_estimate=pl.CostEstimate(flops=4 * CELLS * CH * HID, bytes_accessed=5000000, transcendentals=0),
    )(partial, rows, hot, slope, unit, gain, up, down)


def base_kernel(adjoint_ref, rows_ref, hot_ref, out_ref):
    forcing = forcing_of(1, rows_ref, hot_ref)
    out_ref[...] = adjoint_ref[...].astype(f32) + forcing.reshape(LAT, WID, CH)


def last_base(adjoint, rows, hot):
    return pl.pallas_call(
        base_kernel,
        out_shape=jax.ShapeDtypeStruct((LAT, WID, CH), f32),
        compiler_params=BIG,
        cost_estimate=pl.CostEstimate(flops=2 * SLOTS * CELLS * CH, bytes_accessed=1500000, transcendentals=0),
    )(adjoint, rows, hot)


def swap_edges(head, tail):
    peers = lax.axis_size("tile")
    up = [(i, (i + 1) % peers) for i in range(peers)]
    down = [(j, i) for i, j in up]
    return lax.ppermute(tail, "tile", up), lax.ppermute(head, "tile", down)


def after(array, other):
    return lax.optimization_barrier((array, other))[0]


def exchange(array, axis):
    return lax.all_to_all(array, axis, split_axis=0, concat_axis=0, tiled=True)


def per_device(
    adjoint_final, states, kernel, norm_gain, up_weight, up_bias, down_weight,
    obs_cell, obs_count, obs_value, obs_error,
):
    adjoint = adjoint_final[0]
    states = states[:, 0]
    taps = kernel.reshape(49, CH)
    gain = norm_gain[None]
    bias = up_bias[None]

    packed = pack_observations(obs_cell[:, 0], obs_count[:, 0], obs_value[:, 0], obs_error[:, 0])
    got = exchange(packed, "tile")
    left, right = swap_edges(*cut_edges(after(states, packed)))

    rows, hot0, hot1 = gather_rows(got, states)
    owned = exchange(rows, "member")

    hidden, head, tail = forward(
        0, states, left, after(right, rows), taps, gain, up_weight, bias, down_weight, adjoint
    )
    before, behind = swap_edges(head, tail)

    deps = departures(after(owned, hidden), got)
    back = exchange(deps, "member")

    slope, unit = forward(1, states, left, after(right, deps), taps, gain, up_weight, bias)
    partial = spread_back(hidden, before, after(behind, deps), adjoint, taps, f32)

    hidden, head, tail, adjoint = second_step(
        partial, after(back, (slope, partial)), hot0, slope, unit, gain, up_weight, down_weight
    )
    base = last_base(adjoint, back, hot1)
    return spread_back(hidden, *swap_edges(head, tail), base, taps, bf16)[None]


def solution(mesh):
    placed = (
        P("member", None, "tile", None),
        P(None, "member", None, "tile", None),
        P(),
        P(),
        P(),
        P(),
        P(),
        P(None, "tile", None, None),
        P(None, "tile", None),
        P(None, "tile", None, None, None),
        P(None, "tile", None, None),
    )
    return jax.shard_map(
        per_device,
        mesh=mesh,
        in_specs=placed,
        out_specs=P("member", None, "tile", None),
        check_vma=False,
    )
```

time: 163 us -> 126 us (0.77)
  blocking collectives: 43.8 us -> 14.2 us
  waiting for transfers between devices: 25.1 us -> 9.69 us
  starting transfers between devices: 46.1 us -> 52.4 us
  local copies, waits for them, and re-layouts: 4.92 us -> 7.41 us
    all_to_all x2 -> x1, blocking collectives: 43.8 us -> 14.2 us  [exchange(): return lax.all_to_all(array, axis, split_axis=0, concat_axis=0, tiled=True)]
    all_to_all x2, waiting for transfers between devices: 11.6 us -> 0.01 us  [exchange(): return lax.all_to_all(array, axis, split_axis=0, concat_axis=0, tiled=True)]
    ppermute x6, starting transfers between devices: 22.8 us -> 28.3 us  [swap_edges(): return (lax.ppermute(tail, 'tile', up), lax.ppermute(head, 'tile', down))]
    unnamed x19 -> x39, local copies, waits for them, and re-layouts: 1.97 us -> 7.4 us
    ppermute x6, waiting for transfers between devices: 13.5 us -> 9.68 us  [swap_edges(): return (lax.ppermute(tail, 'tile', up), lax.ppermute(head, 'tile', down))]
    pallas_call x5 -> x7, Pallas kernels: 30.1 us -> 29.5 us  [the longest x2 16.2 us: forward(): pl.pallas_call(functools.partial(forward_kernel, step), out_shape=shapes,...]
  transfers between devices with their start and end apart: 8 -> 8, of which waited for: 4 -> 5; matrix products, arithmetic and copies ran while one was open for 1% -> 0% of each run, Pallas kernels for 19% -> 19%
where the time goes in v2:
time: 126 us; the launch traced here: 125 us
  starting transfers between devices  52.4 us (42%)
  Pallas kernels  40.9 us (32%)
  blocking collectives  14.2 us (11%)
  waiting for transfers between devices  9.69 us (8%)
  local copies, waits for them, and re-layouts  7.41 us (6%)
    ppermute x6, starting transfers between devices, swap_edges(): return (lax.ppermute(tail, 'tile', up), lax.ppermute(head, 'tile', down))  28.3 us
    all_to_all x2, starting transfers between devices, exchange(): return lax.all_to_all(array, axis, split_axis=0, concat_axis=0, tiled=True)  24.1 us
    pallas_call x2, Pallas kernels, forward(): pl.pallas_call(functools.partial(forward_kernel, step), out_shape=shapes,...  16.2 us
    all_to_all x1, blocking collectives, exchange(): return lax.all_to_all(array, axis, split_axis=0, concat_axis=0, tiled=True)  14.2 us
    pallas_call x2, Pallas kernels, spread_back(): pl.pallas_call(spread_kernel, out_shape=jax.ShapeDtypeStruct((LAT, WID, C...  10.8 us
    ppermute x6, waiting for transfers between devices, swap_edges(): return (lax.ppermute(tail, 'tile', up), lax.ppermute(head, 'tile', down))  9.68 us
    unnamed x39, local copies, waits for them, and re-layouts  7.4 us
    pallas_call x1, Pallas kernels, gather_rows(): pl.pallas_call(gather_kernel, out_shape=(jax.ShapeDtypeStruct((CAP, LAT,...  3.86 us
  transfers between devices with their start and end apart: 8, of which 5 were waited for; matrix products, arithmetic and copies ran while one was open for 0% of the time, Pallas kernels for 19%

profile of v2, /device:TPU:31, one launch (start us, length us, event | category | flops | bytes accessed | tf_op | source)
XLA Modules:
  0.0 124.9 jit_solution(7919094298426486350)
XLA Ops:
  0.0 1.4 %copy.13 = bf16[2,1,32,16]{3,2,0,1:T(8,128)(2,1)} copy(bf16[2,1,32,16]{2,3,1,0:T(8,128)(2,1)} %param.21) | data formatting | bytes 4096 | tf_op args[10]
  1.4 1.4 %copy.12 = s32[2,1,32,16]{3,2,0,1:T(8,128)} copy(s32[2,1,32,16]{2,3,1,0:T(8,128)} %param.18) | data formatting | bytes 8192 | tf_op args[7]
  2.8 2.0 %shard_map.109 = f32[32,4,128]{2,1,0:T(4,128)} custom-call(s32[2,32,16]{2,1,0:T(8,128)} %bitcast.18, s32[2,32]{1,0:T(2,128)} %bitcast.20, bf16[2,32,16,192]{3,2,1,0:T(8,128)(2,1)} %bitcast.17, bf16[2,32,16]{2,1,0:T(8,128)(2,1)} %bitcast.19), custom_call_target="tpu_custom_call" | custom-call | tf_op jit(solution)/shard_map/pallas_call | solution.py:107
  4.8 14.2 %all_to_all.15.got_ref = f32[32,4,128]{2,1,0:T(4,128)} all-to-all(f32[32,4,128]{2,1,0:T(4,128)} %shard_map.109), channel_id=1, replica_groups=mesh['member'=16,'tile'=32] {'tile'}, dimensions={0} | all-to-all | bytes 131072 | tf_op jit(solution)/shard_map/all_to_all | solution.py:344
  19.0 0.0 copy-start.17
  19.0 0.0 copy-start.15
  19.0 3.9 %shard_map.111 = (bf16[16,32,384]{2,1,0:T(8,128)(2,1)}, bf16[512,1024]{1,0:T(8,128)(2,1)}, bf16[512,1024]{1,0:T(8,128)(2,1)}) custom-call(f32[32,4,128]{2,1,0:T(4,128)} %all_to_all.15.got_ref, bf16[2,32,32,192]{3,2,1,0:T(8,128)(2,1)} %bitcast.8), custom_call_target="tpu_custom_call" | custom-call | flops 402653184 | bytes 4000000 | tf_op jit(solution)/shard_map/pallas_call | solution.py:132
  22.8 0.0 copy-start.4
  22.8 0.0 copy-start.6
  22.9 0.0 copy-start.7
  22.9 0.0 copy-start.10
  22.9 12.7 %all-to-all-start.1 = ((bf16[16,32,384]{2,1,0:T(8,128)(2,1)}), bf16[16,32,384]{2,1,0:T(8,128)(2,1)}, u32[]{:S(2)}, u32[]{:S(2)}) async-start(bf16[16,32,384]{2,1,0:T(8,128)(2,1)} %get-tuple-element.28), calls=%async_computation.1 | async-start | bytes 786432 | tf_op jit(solution)/shard_map/all_to_all | solution.py:344
  35.6 2.0 %shard_map.110 = (bf16[2,32,3,192]{3,2,1,0:T(4,128)(2,1)}, bf16[2,32,3,192]{3,2,1,0:T(4,128)(2,1)}) custom-call(bf16[2,32,32,192]{3,2,1,0:T(8,128)(2,1)} %bitcast.9), custom_call_target="tpu_custom_call" | custom-call | tf_op jit(solution)/shard_map/pallas_call | solution.py:85
  37.6 2.6 %collective-permute-start.1 = (bf16[2,32,3,192]{3,2,1,0:T(4,128)(2,1)}, bf16[2,32,3,192]{3,2,1,0:T(4,128)(2,1)S(1)}, u32[]{:S(2)}, u32[]{:S(2)}) collective-permute-start(bf16[2,32,3,192]{3,2,1,0:T(4,128)(2,1)} %get-tuple-element.27), channel_id=1, source_target_pairs={{1,0},{2,1},{3,2},{4,3},{5,4},{6,5},{7,6},{8,7},{9,8},{10,9},{11,1... | collective-permute-start | bytes 221192 | tf_op jit(solution)/shard_map/ppermute | solution.py:336
  40.2 6.3 %collective-permute-start = (bf16[2,32,3,192]{3,2,1,0:T(4,128)(2,1)}, bf16[2,32,3,192]{3,2,1,0:T(4,128)(2,1)S(1)}, u32[]{:S(2)}, u32[]{:S(2)}) collective-permute-start(bf16[2,32,3,192]{3,2,1,0:T(4,128)(2,1)} %get-tuple-element.26), channel_id=1, source_target_pairs={{0,1},{1,2},{2,3},{3,4},{4,5},{5,6},{6,7},{7,8},{8,9},{9,10},{10,1... | collective-permute-start | bytes 221192 | tf_op jit(solution)/shard_map/ppermute | solution.py:336
  46.5 0.0 copy-done.17
  46.5 0.0 copy-done.16
  46.6 0.0 copy-done.15
  46.6 0.2 copy.14.rest_0_.down_ref
  46.8 1.1 collective-permute-done.1.right_ref
  47.8 0.0 copy-start.11
  47.8 0.9 collective-permute-done.left_ref
  48.8 0.0 copy-start.13
  48.8 0.0 copy-done.4
  48.8 0.0 copy-done.6
  48.8 0.0 copy-done.7
  48.8 0.0 copy-done.10
  48.8 8.6 %shard_map.112 = (bf16[32,32,192]{2,1,0:T(8,128)(2,1)S(1)}, bf16[32,3,192]{2,1,0:T(4,128)(2,1)S(1)}, bf16[32,3,192]{2,1,0:T(4,128)(2,1)S(1)}) custom-call(bf16[2,32,32,192]{3,2,1,0:T(8,128)(2,1)S(1)} %bitcast.10, bf16[2,32,3,192]{3,2,1,0:T(4,128)(2,1)S(1)} %collective-permute-done.left_ref, bf16[2,32,3,192]{3,2,1,0:T(4,128)(2,1)S(1)} %collective-permute-done.1.right_ref, ...), custom_call_target="tpu_custom_call" | custom-call | flops 905969664 | bytes 8000000 | tf_op jit(solution)/shard_map/pallas_call | solution.py:244
  57.4 0.0 copy-done.11
  57.4 0.0 copy-done.13
  57.4 0.0 all-to-all-done.1.rows_ref
  57.4 2.2 %shard_map.113 = bf16[16,32,384]{2,1,0:T(8,128)(2,1)} custom-call(bf16[16,32,384]{2,1,0:T(8,128)(2,1)} %all-to-all-done.1.rows_ref, f32[32,4,128]{2,1,0:T(4,128)} %all_to_all.15.got_ref), custom_call_target="tpu_custom_call" | custom-call | flops 1200000 | bytes 1200000 | tf_op jit(solution)/shard_map/pallas_call | solution.py:155
  59.6 11.4 %all-to-all-start.2 = ((bf16[16,32,384]{2,1,0:T(8,128)(2,1)}), bf16[16,32,384]{2,1,0:T(8,128)(2,1)S(1)}, u32[]{:S(2)}, u32[]{:S(2)}) async-start(bf16[16,32,384]{2,1,0:T(8,128)(2,1)} %shard_map.113), calls=%async_computation.2 | async-start | bytes 786432 | tf_op jit(solution)/shard_map/all_to_all | solution.py:344
  71.0 0.0 copy-start.5
  71.0 0.0 copy-start.8
  71.1 0.0 copy-start.12
  71.1 0.0 copy-start.14
  71.1 2.1 %collective-permute-start.3 = (bf16[32,3,192]{2,1,0:T(4,128)(2,1)S(1)}, bf16[32,3,192]{2,1,0:T(4,128)(2,1)S(1)}, u32[]{:S(2)}, u32[]{:S(2)}) collective-permute-start(bf16[32,3,192]{2,1,0:T(4,128)(2,1)S(1)} %get-tuple-element.32), channel_id=1, source_target_pairs={{1,0},{2,1},{3,2},{4,3},{5,4},{6,5},{7,6},{8,7},{9,8},{10,9},{11,1... | collective-permute-start | bytes 110600 | tf_op jit(solution)/shard_map/ppermute | solution.py:336
  73.1 7.8 %collective-permute-start.2 = (bf16[32,3,192]{2,1,0:T(4,128)(2,1)S(1)}, bf16[32,3,192]{2,1,0:T(4,128)(2,1)S(1)}, u32[]{:S(2)}, u32[]{:S(2)}) collective-permute-start(bf16[32,3,192]{2,1,0:T(4,128)(2,1)S(1)} %get-tuple-element.31), channel_id=1, source_target_pairs={{0,1},{1,2},{2,3},{3,4},{4,5},{5,6},{6,7},{7,8},{8,9},{9,10},{10,1... | collective-permute-start | bytes 110600 | tf_op jit(solution)/shard_map/ppermute | solution.py:336
  81.0 0.3 collective-permute-done.3.right_ref
  81.3 1.0 collective-permute-done.2.left_ref
  82.3 4.8 %shard_map.114.partial_ref = f32[32,32,192]{2,1,0:T(8,128)S(1)} custom-call(bf16[32,32,192]{2,1,0:T(8,128)(2,1)S(1)} %get-tuple-element.30.hidden_ref, bf16[32,3,192]{2,1,0:T(4,128)(2,1)S(1)} %collective-permute-done.2.left_ref, bf16[32,3,192]{2,1,0:T(4,128)(2,1)S(1)} %collective-permute-done.3.right_ref, bf16[32,32,192]{2,1,0:T(8,128)(2,1)S(1)} %bitcast.13, ...), custom_call_target="tpu_custom_call" | custom-call | flops 19267584 | bytes 3000000 | tf_op jit(solution)/shard_map/pallas_call | solution.py:275
  87.1 0.0 copy-done.5
  87.1 0.0 copy-done.8
  87.1 0.0 copy-done.12
  87.1 0.0 copy-done.14
  87.1 7.6 %shard_map.115 = (bf16[1024,768]{1,0:T(8,128)(2,1)S(1)}, f32[1024,256]{1,0:T(8,128)S(1)}) custom-call(bf16[2,32,32,192]{3,2,1,0:T(8,128)(2,1)S(1)} %bitcast.11, bf16[2,32,3,192]{3,2,1,0:T(4,128)(2,1)S(1)} %copy-done.14, bf16[2,32,3,192]{3,2,1,0:T(4,128)(2,1)S(1)} %copy-done.12, f32[49,192]{1,0:T(8,128)S(1)} %reshape.3.kernel_ref, f32[1,192]{1,0:T(1,128)S(1)} %bitcast.15, ...), custom_call_target="tpu_custom_call" | custom-call | flops 905969664 | bytes 8000000 | tf_op jit(solution)/shard_map/pallas_call | solution.py:244
  94.7 0.0 copy-start.2
  94.7 1.0 copy-done.2
  95.7 0.0 all-to-all-done.2.rows_ref
  95.7 0.0 copy-start.1
  95.7 1.2 copy-done.1
  96.9 0.0 copy-start.3
  96.9 1.2 copy-done.3
  98.2 0.0 copy-start.9
  98.2 1.0 copy-done.9
  99.1 3.3 %shard_map.116 = (bf16[32,32,192]{2,1,0:T(8,128)(2,1)S(1)}, bf16[32,3,192]{2,1,0:T(4,128)(2,1)S(1)}, bf16[32,3,192]{2,1,0:T(4,128)(2,1)S(1)}, bf16[32,32,192]{2,1,0:T(8,128)(2,1)S(1)}) custom-call(f32[32,32,192]{2,1,0:T(8,128)S(1)} %shard_map.114.partial_ref, bf16[16,32,384]{2,1,0:T(8,128)(2,1)S(1)} %all-to-all-done.2.rows_ref, ...), custom_call_target="tpu_custom_call" | custom-call | flops 603979776 | bytes 5000000 | tf_op jit(solution)/shard_map/pallas_call | solution.py:310
  102.4 7.6 %collective-permute-start.4 = (bf16[32,3,192]{2,1,0:T(4,128)(2,1)S(1)}, bf16[32,3,192]{2,1,0:T(4,128)(2,1)S(1)}, u32[]{:S(2)}, u32[]{:S(2)}) collective-permute-start(bf16[32,3,192]{2,1,0:T(4,128)(2,1)S(1)} %get-tuple-element.41), channel_id=1, source_target_pairs={{0,1},{1,2},{2,3},{3,4},{4,5},{5,6},{6,7},{7,8},{8,9},{9,10},{10,1... | collective-permute-start | bytes 110600 | tf_op jit(solution)/shard_map/ppermute | solution.py:336
  110.0 1.9 %collective-permute-start.5 = (bf16[32,3,192]{2,1,0:T(4,128)(2,1)S(1)}, bf16[32,3,192]{2,1,0:T(4,128)(2,1)S(1)}, u32[]{:S(2)}, u32[]{:S(2)}) collective-permute-start(bf16[32,3,192]{2,1,0:T(4,128)(2,1)S(1)} %get-tuple-element.42), channel_id=1, source_target_pairs={{1,0},{2,1},{3,2},{4,3},{5,4},{6,5},{7,6},{8,7},{9,8},{10,9},{11,1... | collective-permute-start | bytes 110600 | tf_op jit(solution)/shard_map/ppermute | solution.py:336
  111.9 0.0 copy-done
  111.9 0.6 shard_map.117.base_ref
  112.5 0.0 collective-permute-done.4.left_ref
  112.5 6.4 %collective-permute-done.5.right_ref = bf16[32,3,192]{2,1,0:T(4,128)(2,1)S(1)} collective-permute-done((bf16[32,3,192]{2,1,0:T(4,128)(2,1)S(1)}, bf16[32,3,192]{2,1,0:T(4,128)(2,1)S(1)}, u32[]{:S(2)}, u32[]{:S(2)}) %collective-permute-start.5) | collective-permute-done | bytes 36896 | tf_op jit(solution)/shard_map/ppermute | solution.py:336
  118.9 6.0 %shard_map.118 = bf16[32,32,192]{2,1,0:T(8,128)(2,1)} custom-call(bf16[32,32,192]{2,1,0:T(8,128)(2,1)S(1)} %get-tuple-element.40.hidden_ref, bf16[32,3,192]{2,1,0:T(4,128)(2,1)S(1)} %collective-permute-done.4.left_ref, bf16[32,3,192]{2,1,0:T(4,128)(2,1)S(1)} %collective-permute-done.5.right_ref, f32[32,32,192]{2,1,0:T(8,128)S(1)} %shard_map.117.base_ref, ...), custom_call_target="tpu_custom_call" | custom-call | flops 19267584 | bytes 3000000 | tf_op jit(solution)/shard_map/pallas_call | solution.py:275
  (4 shorter events, 0.0 us)
Async XLA Ops:
  19.0 27.5 %copy-start.17 = (f32[768]{0:T(1024)S(1)}, f32[768]{0:T(1024)}, u32[]{:S(2)}) copy-start(f32[768]{0:T(1024)} %param.16) | copy-start | bytes 9220
  19.0 27.6 %copy-start.16 = (f32[7,7,192]{2,1,0:T(8,128)S(1)}, f32[7,7,192]{2,1,0:T(8,128)}, u32[]{:S(2)}) copy-start(f32[7,7,192]{2,1,0:T(8,128)} %param.13) | copy-start | bytes 112900
  19.0 27.6 %copy-start.15 = (bf16[768,192]{0,1:T(8,128)(2,1)S(1)}, bf16[768,192]{0,1:T(8,128)(2,1)}, u32[]{:S(2)}) copy-start(bf16[768,192]{0,1:T(8,128)(2,1)} %param.17) | copy-start | bytes 884740
  22.8 25.9 %copy-start.4 = (bf16[2,1,32,32,192]{4,3,2,1,0:T(8,128)(2,1)S(1)}, bf16[2,1,32,32,192]{4,3,2,1,0:T(8,128)(2,1)}, u32[]{:S(2)}) copy-start(bf16[2,1,32,32,192]{4,3,2,1,0:T(8,128)(2,1)} %param.12) | copy-start | bytes 2359300
  22.8 25.9 %copy-start.6 = (bf16[1,32,32,192]{3,2,1,0:T(8,128)(2,1)S(1)}, bf16[1,32,32,192]{3,2,1,0:T(8,128)(2,1)}, u32[]{:S(2)}) copy-start(bf16[1,32,32,192]{3,2,1,0:T(8,128)(2,1)} %param.11) | copy-start | bytes 1179652
  22.9 25.9 %copy-start.7 = (bf16[192,768]{1,0:T(8,128)(2,1)S(1)}, bf16[192,768]{1,0:T(8,128)(2,1)}, u32[]{:S(2)}) copy-start(bf16[192,768]{1,0:T(8,128)(2,1)} %up_ref.5) | copy-start | bytes 884740
  22.9 25.9 %copy-start.10 = (f32[192]{0:T(256)S(1)}, f32[192]{0:T(256)}, u32[]{:S(2)}) copy-start(f32[192]{0:T(256)} %param.14) | copy-start | bytes 2308
  22.9 34.5 %all-to-all-start.1 = ((bf16[16,32,384]{2,1,0:T(8,128)(2,1)}), bf16[16,32,384]{2,1,0:T(8,128)(2,1)}, u32[]{:S(2)}, u32[]{:S(2)}) async-start(bf16[16,32,384]{2,1,0:T(8,128)(2,1)} %get-tuple-element.28), calls=%async_computation.1 | async-start | bytes 786432 | tf_op jit(solution)/shard_map/all_to_all | solution.py:344
  37.6 10.2 %collective-permute-start.1 = (bf16[2,32,3,192]{3,2,1,0:T(4,128)(2,1)}, bf16[2,32,3,192]{3,2,1,0:T(4,128)(2,1)S(1)}, u32[]{:S(2)}, u32[]{:S(2)}) collective-permute-start(bf16[2,32,3,192]{3,2,1,0:T(4,128)(2,1)} %get-tuple-element.27), channel_id=1, source_target_pairs={{1,0},{2,1},{3,2},{4,3},{5,4},{6,5},{7,6},{8,7},{9,8},{10,9},{11,1... | collective-permute-start | bytes 221192 | tf_op jit(solution)/shard_map/ppermute | solution.py:336
  40.2 8.5 %collective-permute-start = (bf16[2,32,3,192]{3,2,1,0:T(4,128)(2,1)}, bf16[2,32,3,192]{3,2,1,0:T(4,128)(2,1)S(1)}, u32[]{:S(2)}, u32[]{:S(2)}) collective-permute-start(bf16[2,32,3,192]{3,2,1,0:T(4,128)(2,1)} %get-tuple-element.26), channel_id=1, source_target_pairs={{0,1},{1,2},{2,3},{3,4},{4,5},{5,6},{6,7},{7,8},{8,9},{9,10},{10,1... | collective-permute-start | bytes 221192 | tf_op jit(solution)/shard_map/ppermute | solution.py:336
  47.8 9.5 %copy-start.11 = (bf16[2,32,3,192]{3,2,1,0:T(4,128)(2,1)}, bf16[2,32,3,192]{3,2,1,0:T(4,128)(2,1)S(1)}, u32[]{:S(2)}) copy-start(bf16[2,32,3,192]{3,2,1,0:T(4,128)(2,1)S(1)} %collective-permute-done.1.right_ref) | copy-start | bytes 221188
  48.8 8.6 %copy-start.13 = (bf16[2,32,3,192]{3,2,1,0:T(4,128)(2,1)}, bf16[2,32,3,192]{3,2,1,0:T(4,128)(2,1)S(1)}, u32[]{:S(2)}) copy-start(bf16[2,32,3,192]{3,2,1,0:T(4,128)(2,1)S(1)} %collective-permute-done.left_ref) | copy-start | bytes 221188
  59.6 36.1 %all-to-all-start.2 = ((bf16[16,32,384]{2,1,0:T(8,128)(2,1)}), bf16[16,32,384]{2,1,0:T(8,128)(2,1)S(1)}, u32[]{:S(2)}, u32[]{:S(2)}) async-start(bf16[16,32,384]{2,1,0:T(8,128)(2,1)} %shard_map.113), calls=%async_computation.2 | async-start | bytes 786432 | tf_op jit(solution)/shard_map/all_to_all | solution.py:344
  71.0 16.1 %copy-start.5 = (bf16[2,1,32,32,192]{4,3,2,1,0:T(8,128)(2,1)S(1)}, bf16[2,1,32,32,192]{4,3,2,1,0:T(8,128)(2,1)}, u32[]{:S(2)}) copy-start(bf16[2,1,32,32,192]{4,3,2,1,0:T(8,128)(2,1)} %param.12) | copy-start | bytes 2359300
  71.0 16.1 %copy-start.8 = (bf16[192,768]{1,0:T(8,128)(2,1)S(1)}, bf16[192,768]{1,0:T(8,128)(2,1)}, u32[]{:S(2)}) copy-start(bf16[192,768]{1,0:T(8,128)(2,1)} %up_ref.5) | copy-start | bytes 884740
  71.1 16.1 %copy-start.12 = (bf16[2,32,3,192]{3,2,1,0:T(4,128)(2,1)S(1)}, bf16[2,32,3,192]{3,2,1,0:T(4,128)(2,1)}, u32[]{:S(2)}) copy-start(bf16[2,32,3,192]{3,2,1,0:T(4,128)(2,1)} %copy-done.11) | copy-start | bytes 221188
  71.1 16.1 %copy-start.14 = (bf16[2,32,3,192]{3,2,1,0:T(4,128)(2,1)S(1)}, bf16[2,32,3,192]{3,2,1,0:T(4,128)(2,1)}, u32[]{:S(2)}) copy-start(bf16[2,32,3,192]{3,2,1,0:T(4,128)(2,1)} %copy-done.13) | copy-start | bytes 221188
  71.1 10.2 %collective-permute-start.3 = (bf16[32,3,192]{2,1,0:T(4,128)(2,1)S(1)}, bf16[32,3,192]{2,1,0:T(4,128)(2,1)S(1)}, u32[]{:S(2)}, u32[]{:S(2)}) collective-permute-start(bf16[32,3,192]{2,1,0:T(4,128)(2,1)S(1)} %get-tuple-element.32), channel_id=1, source_target_pairs={{1,0},{2,1},{3,2},{4,3},{5,4},{6,5},{7,6},{8,7},{9,8},{10,9},{11,1... | collective-permute-start | bytes 110600 | tf_op jit(solution)/shard_map/ppermute | solution.py:336
  73.1 9.2 %collective-permute-start.2 = (bf16[32,3,192]{2,1,0:T(4,128)(2,1)S(1)}, bf16[32,3,192]{2,1,0:T(4,128)(2,1)S(1)}, u32[]{:S(2)}, u32[]{:S(2)}) collective-permute-start(bf16[32,3,192]{2,1,0:T(4,128)(2,1)S(1)} %get-tuple-element.31), channel_id=1, source_target_pairs={{0,1},{1,2},{2,3},{3,4},{4,5},{5,6},{6,7},{7,8},{8,9},{9,10},{10,1... | collective-permute-start | bytes 110600 | tf_op jit(solution)/shard_map/ppermute | solution.py:336
  94.7 1.0 copy-start.2
  95.7 1.2 copy-start.1
  96.9 1.2 copy-start.3
  98.2 1.0 copy-start.9
  99.1 12.8 %copy-start = (bf16[512,1024]{1,0:T(8,128)(2,1)S(1)}, bf16[512,1024]{1,0:T(8,128)(2,1)}, u32[]{:S(2)}) copy-start(bf16[512,1024]{1,0:T(8,128)(2,1)} %get-tuple-element.44.hot_ref) | copy-start | bytes 3145732
  102.4 10.1 %collective-permute-start.4 = (bf16[32,3,192]{2,1,0:T(4,128)(2,1)S(1)}, bf16[32,3,192]{2,1,0:T(4,128)(2,1)S(1)}, u32[]{:S(2)}, u32[]{:S(2)}) collective-permute-start(bf16[32,3,192]{2,1,0:T(4,128)(2,1)S(1)} %get-tuple-element.41), channel_id=1, source_target_pairs={{0,1},{1,2},{2,3},{3,4},{4,5},{5,6},{6,7},{7,8},{8,9},{9,10},{10,1... | collective-permute-start | bytes 110600 | tf_op jit(solution)/shard_map/ppermute | solution.py:336
  110.0 8.9 %collective-permute-start.5 = (bf16[32,3,192]{2,1,0:T(4,128)(2,1)S(1)}, bf16[32,3,192]{2,1,0:T(4,128)(2,1)S(1)}, u32[]{:S(2)}, u32[]{:S(2)}) collective-permute-start(bf16[32,3,192]{2,1,0:T(4,128)(2,1)S(1)} %get-tuple-element.42), channel_id=1, source_target_pairs={{1,0},{2,1},{3,2},{4,3},{5,4},{6,5},{7,6},{8,7},{9,8},{10,9},{11,1... | collective-permute-start | bytes 110600 | tf_op jit(solution)/shard_map/ppermute | solution.py:336

commit v3 on v2

v3 whole, which is shorter than its diff:
```python
import functools
import math

import jax
import jax.numpy as jnp
from jax import lax
from jax.experimental import pallas as pl
from jax.experimental.pallas import tpu as pltpu
from jax.sharding import PartitionSpec as P

slope_coef = math.sqrt(2.0 / math.pi)
cubic_coef = 0.044715
norm_eps = 1e-06

LAT = 32
WID = 32
CH = 192
HID = 768
CAP = 16
CELLS = LAT * WID
SLOTS = LAT * CAP
BLK = 8
ROWS = BLK * WID
f32 = jnp.float32
bf16 = jnp.bfloat16
NT = (((1,), (1,)), ((), ()))
TN = (((0,), (0,)), ((), ()))


def gelu_slope(preact):
    square = preact * preact
    tanh_val = jnp.tanh(preact * (slope_coef + (slope_coef * cubic_coef) * square))
    tail = preact * (0.5 * slope_coef + (1.5 * slope_coef * cubic_coef) * square)
    return (0.5 + 0.5 * tanh_val) + tail * (1.0 - tanh_val * tanh_val)


def mean_lanes(value):
    return jnp.sum(value, axis=-1, keepdims=True) * (1.0 / CH)


def clear_rims(shifts, count, width):
    for edge in range(3):
        zeros = jnp.zeros((width, CH), f32)
        for col in range(count):
            shifts[col, edge] = zeros
            shifts[col, LAT + 3 + edge] = zeros


def build_shifts(shifts, padded, centre, left=None, right=None):
    clear_rims(shifts, 7, WID)
    if left is None:
        padded[...] = jnp.zeros(padded.shape, f32)

    def one_row(row, carry):
        if left is not None:
            padded[0:3] = left(row).astype(f32)
            padded[WID + 3 : WID + 6] = right(row).astype(f32)
        padded[3 : WID + 3] = centre(row).astype(f32)
        for col in range(7):
            shifts[col, row + 3] = padded[col : col + WID]
        return carry

    lax.fori_loop(0, LAT, one_row, 0)


def convolve(shifts, kernel_ref, first, flip, emit, cols=range(7), width=WID):
    for low, high in ((0, 128), (128, CH)):
        sums = [None] * BLK
        for place, col in enumerate(cols):
            taps = []
            for row in range(7):
                down, across = (6 - row, 6 - col) if flip else (row, col)
                taps.append(jnp.broadcast_to(kernel_ref[down, across : across + 1, low:high], (width, high - low)))
            for source in range(BLK + 6):
                field = shifts[place, first + source, :, low:high]
                for row in range(7):
                    target = source - row
                    if 0 <= target < BLK:
                        term = taps[row] * field
                        sums[target] = term if sums[target] is None else sums[target] + term
        for target in range(BLK):
            emit(target, low, high, sums[target])


def cut_kernel(first_ref, last_ref, head_ref, tail_ref):
    head_ref[...] = first_ref[:, 0, :, 0:3]
    tail_ref[...] = last_ref[:, 0, :, 5:8]


def cut_edges(states):
    edge = jax.ShapeDtypeStruct((2, LAT, 3, CH), bf16)
    whole = pl.BlockSpec((2, LAT, 3, CH), lambda i: (0, 0, 0, 0))
    part = lambda block: pl.BlockSpec((2, 1, LAT, 8, CH), lambda i: (0, 0, 0, block, 0))
    return pl.pallas_call(
        cut_kernel, grid=(1,), in_specs=[part(0), part(3)], out_specs=[whole, whole], out_shape=(edge, edge)
    )(states, states)


def pack_kernel(cell_ref, count_ref, value_ref, error_ref, out_ref):
    member = lax.axis_index("member")
    tiles = cell_ref.shape[2]
    slot = lax.broadcasted_iota(jnp.int32, (CAP, tiles), 0)
    across = lax.broadcasted_iota(jnp.int32, (CAP, CAP), 1)
    same = jnp.where(lax.broadcasted_iota(jnp.int32, (CAP, CAP), 0) == across, 1.0, 0.0).astype(bf16)
    own = jnp.where(lax.broadcasted_iota(jnp.int32, (CAP, CAP), 0) == member, 1.0, 0.0).astype(bf16)
    deep = lax.broadcasted_iota(jnp.int32, (tiles, CAP, CH), 1)
    for step in range(2):
        live = slot < count_ref[step]
        cells = jnp.where(live, cell_ref[step], -1).astype(f32).astype(bf16)
        values = jnp.sum(jnp.where(deep == member, value_ref[step, 0].astype(f32), 0.0), axis=1)
        turn = lambda array, pick: lax.dot_general(array, pick, TN, preferred_element_type=f32)
        out_ref[:, 2 * step, :] = values[:, 0:128]
        out_ref[:, 2 * step + 1, :] = jnp.concatenate(
            [values[:, 128:CH], turn(cells, same), turn(error_ref[step], own), turn(cells, own), jnp.zeros((tiles, CAP), f32)],
            axis=1)


def pack_observations(cells, counts, values, errors):
    return pl.pallas_call(
        pack_kernel,
        out_shape=jax.ShapeDtypeStruct((cells.shape[2], 4, 128), f32),
    )(cells, counts, values, errors)


def one_hot(step, got_ref, group):
    cells = got_ref[group * BLK : (group + 1) * BLK, 2 * step + 1, 64 : 64 + CAP]
    lane = lax.broadcasted_iota(jnp.int32, (BLK, ROWS), 1)
    band = lax.broadcasted_iota(jnp.int32, (BLK, ROWS), 0)
    offset = (lane - band * WID).astype(f32)
    rows = [jnp.where(offset == cells[:, slot : slot + 1], 1.0, 0.0) for slot in range(CAP)]
    return jnp.concatenate(rows, axis=0).astype(bf16)


def gather_kernel(got_ref, state_ref, out_ref):
    for step in range(2):
        for pair in range(2):
            found = []
            for group in (2 * pair, 2 * pair + 1):
                field = state_ref[step, 0, group * BLK : (group + 1) * BLK].reshape(ROWS, CH)
                rows = jnp.dot(one_hot(step, got_ref, group), field, preferred_element_type=f32)
                found.append(rows.reshape(CAP, BLK, CH))
            both = jnp.concatenate(found, axis=1).astype(bf16)
            out_ref[:, 2 * BLK * pair : 2 * BLK * (pair + 1), step * CH : (step + 1) * CH] = both


def gather_rows(got, states):
    return pl.pallas_call(
        gather_kernel,
        out_shape=jax.ShapeDtypeStruct((CAP, LAT, 2 * CH), bf16),
        cost_estimate=pl.CostEstimate(flops=1000000, bytes_accessed=2000000, transcendentals=0),
    )(got, states)


def departure_kernel(rows_ref, got_ref, out_ref):
    for step in range(2):
        lanes = slice(step * CH, (step + 1) * CH)
        sampled = rows_ref[:, :, lanes].astype(f32)
        members = sampled.shape[0]
        other = got_ref[:, 2 * step + 1, :]
        values = jnp.concatenate([got_ref[:, 2 * step, :], other[:, 0:64]], axis=1)
        ens_mean = jnp.sum(sampled, axis=0) * (1.0 / members)
        ens_var = jnp.sum(sampled * sampled, axis=0) * (1.0 / members) - ens_mean * ens_mean
        weight = 1.0 / (other[:, 64 + CAP : 65 + CAP] + ens_var)
        ratio = (sampled - values[None]) * weight[None]
        live = other[:, 64 + 2 * CAP : 65 + 2 * CAP] >= 0.0
        out_ref[:, :, lanes] = jnp.where(live[None], ratio, 0.0).astype(bf16)


def departures(rows, got):
    return pl.pallas_call(
        departure_kernel,
        out_shape=jax.ShapeDtypeStruct((CAP, LAT, 2 * CH), bf16),
        cost_estimate=pl.CostEstimate(flops=1200000, bytes_accessed=1200000, transcendentals=0),
    )(rows, got)


def forcing_of(step, rows_ref, got_ref, group):
    rows = rows_ref[:, :, step * CH : (step + 1) * CH].astype(f32)[:, group * BLK : (group + 1) * BLK]
    rows = rows.reshape(CAP * BLK, CH).astype(bf16)
    return lax.dot_general(one_hot(step, got_ref, group), rows, TN, preferred_element_type=f32)


def normalise(hidden):
    centred = hidden - mean_lanes(hidden)
    inv_std = lax.rsqrt(mean_lanes(centred * centred) + norm_eps)
    return centred * inv_std, inv_std


def backward(adjoint, slope_at, down_ref, up_ref, gain, unit):
    adj_norm = jnp.zeros((ROWS, CH), f32)
    for part in range(3):
        cols = slice(part * 256, (part + 1) * 256)
        act = jnp.dot(adjoint, down_ref[:, cols], preferred_element_type=f32)
        pre = (act * slope_at(cols)).astype(bf16)
        adj_norm = adj_norm + lax.dot_general(pre, up_ref[:, cols], NT, preferred_element_type=f32)
    scaled = adj_norm * gain
    return scaled - mean_lanes(scaled) - unit * mean_lanes(scaled * unit)


def put_hidden(adj_hidden, first, out_ref, head_ref, tail_ref):
    block = adj_hidden.astype(bf16).reshape(BLK, WID, CH)
    out_ref[pl.ds(first, BLK)] = block
    head_ref[pl.ds(first, BLK)] = block[:, 0:3]
    tail_ref[pl.ds(first, BLK)] = block[:, WID - 3 : WID]


def forward_kernel(step, state_ref, left_ref, right_ref, kernel_ref, gain_ref, up_ref, bias_ref, *rest):
    shifts, padded, hidden = rest[-3:]
    gain = gain_ref[...]
    build_shifts(
        shifts, padded,
        lambda row: state_ref[step, 0, row],
        lambda row: left_ref[step, row],
        lambda row: right_ref[step, row],
    )

    def block(index, carry):
        first = index * BLK

        def emit(target, low, high, value):
            hidden[target, :, low:high] = value

        convolve(shifts, kernel_ref, first, False, emit)
        unit, inv_std = normalise(hidden[...].reshape(ROWS, CH))
        normed = (unit * gain).astype(bf16)

        def slope_at(cols):
            preact = jnp.dot(normed, up_ref[:, cols], preferred_element_type=f32)
            return gelu_slope(preact + bias_ref[:, cols]) * inv_std

        if step == 0:
            down_ref, adjoint_ref, hidden_out, head_out, tail_out = rest[:5]
            adjoint = adjoint_ref[0, pl.ds(first, BLK)].reshape(ROWS, CH)
            result = backward(adjoint, slope_at, down_ref, up_ref, gain, unit)
            put_hidden(result, first, hidden_out, head_out, tail_out)
        else:
            slope_out, unit_out = rest[:2]
            rows = pl.ds(pl.multiple_of(index * ROWS, ROWS), ROWS)
            for part in range(3):
                cols = slice(part * 256, (part + 1) * 256)
                slope_out[rows, cols] = slope_at(cols).astype(bf16)
            unit_out[rows, :] = unit.astype(bf16)
        return carry

    lax.fori_loop(0, LAT // BLK, block, 0)


EDGE = jax.ShapeDtypeStruct((LAT, 3, CH), bf16)
FIELD = jax.ShapeDtypeStruct((LAT, WID, CH), bf16)
SHIFT_SCRATCH = [pltpu.VMEM((7, LAT + 6, WID, CH), f32), pltpu.VMEM((WID + 8, CH), f32)]
BIG = pltpu.CompilerParams(vmem_limit_bytes=16 * 1024 * 1024)


def forward(step, *operands):
    shapes = (FIELD, EDGE, EDGE) if step == 0 else (
        jax.ShapeDtypeStruct((CELLS, HID), bf16),
        jax.ShapeDtypeStruct((CELLS, CH), bf16),
    )
    return pl.pallas_call(
        functools.partial(forward_kernel, step),
        out_shape=shapes,
        scratch_shapes=SHIFT_SCRATCH + [pltpu.VMEM((BLK, WID, CH), f32)],
        compiler_params=BIG,
        cost_estimate=pl.CostEstimate(flops=6 * CELLS * CH * HID, bytes_accessed=8000000, transcendentals=CELLS * HID),
    )(*operands)


def spread_kernel(hidden_ref, left_ref, right_ref, base_ref, kernel_ref, out_ref, shifts, padded):
    build_shifts(
        shifts, padded,
        lambda row: hidden_ref[row],
        lambda row: left_ref[row],
        lambda row: right_ref[row],
    )

    def block(index, carry):
        first = index * BLK

        def emit(target, low, high, value):
            base = base_ref[0, first + target, :, low:high].astype(f32)
            out_ref[first + target, :, low:high] = base + value

        convolve(shifts, kernel_ref, first, True, emit)
        return carry

    lax.fori_loop(0, LAT // BLK, block, 0)


def spread_back(hidden, left, right, base, kernel):
    return pl.pallas_call(
        spread_kernel,
        out_shape=jax.ShapeDtypeStruct((LAT, WID, CH), f32),
        scratch_shapes=SHIFT_SCRATCH,
        compiler_params=BIG,
        cost_estimate=pl.CostEstimate(flops=98 * CELLS * CH, bytes_accessed=3000000, transcendentals=0),
    )(hidden, left, right, base, kernel)


def second_kernel(
    partial_ref, rows_ref, got_ref, slope_ref, unit_ref, gain_ref, up_ref, down_ref,
    hidden_out, head_out, tail_out, adjoint_out,
):
    gain = gain_ref[...]
    for group in range(LAT // BLK):
        first = group * BLK
        rows = slice(group * ROWS, (group + 1) * ROWS)
        forcing = forcing_of(0, rows_ref, got_ref, group)
        adjoint = (partial_ref[first : first + BLK].reshape(ROWS, CH) + forcing).astype(bf16)
        adjoint_out[first : first + BLK] = adjoint.reshape(BLK, WID, CH)
        result = backward(
            adjoint,
            lambda cols: slope_ref[rows, cols].astype(f32),
            down_ref, up_ref, gain,
            unit_ref[rows, :].astype(f32),
        )
        put_hidden(result, first, hidden_out, head_out, tail_out)


def second_step(partial, rows, got, slope, unit, gain, up, down):
    return pl.pallas_call(
        second_kernel,
        out_shape=(FIELD, EDGE, EDGE, FIELD),
        compiler_params=pltpu.CompilerParams(vmem_limit_bytes=12 * 1024 * 1024),
        cost_estimate=pl.CostEstimate(flops=4 * CELLS * CH * HID, bytes_accessed=5000000, transcendentals=0),
    )(partial, rows, got, slope, unit, gain, up, down)


def interior_kernel(hidden_ref, adjoint_ref, rows_ref, got_ref, kernel_ref, out_ref, west_ref, east_ref, shifts, padded, total):
    build_shifts(shifts, padded, lambda row: hidden_ref[row])
    for group in range(LAT // BLK):
        first = group * BLK
        forcing = forcing_of(1, rows_ref, got_ref, group).reshape(BLK, WID, CH)
        total[first : first + BLK] = adjoint_ref[first : first + BLK].astype(f32) + forcing

    def block(index, carry):
        first = index * BLK

        def emit(target, low, high, value):
            value = total[first + target, :, low:high] + value
            out_ref[first + target, :, low:high] = value.astype(bf16)
            west_ref[first + target, :, low:high] = value[0:8]
            east_ref[first + target, :, low:high] = value[WID - 8 : WID]

        convolve(shifts, kernel_ref, first, True, emit)
        return carry

    lax.fori_loop(0, LAT // BLK, block, 0)


STRIP = jax.ShapeDtypeStruct((LAT, 8, CH), f32)


def interior(hidden, adjoint, rows, got, kernel):
    return pl.pallas_call(
        interior_kernel,
        out_shape=(FIELD, STRIP, STRIP),
        scratch_shapes=SHIFT_SCRATCH + [pltpu.VMEM((LAT, WID, CH), f32)],
        compiler_params=BIG,
        cost_estimate=pl.CostEstimate(flops=98 * CELLS * CH, bytes_accessed=3000000, transcendentals=0),
    )(hidden, adjoint, rows, got, kernel)


def edge_kernel(inner_ref, west_ref, east_ref, left_ref, right_ref, kernel_ref, out_ref, shifts, padded):
    def side(halo_ref, strip_ref, place, offset, cols):
        clear_rims(shifts, 3, 8)
        padded[...] = jnp.zeros(padded.shape, f32)

        def one_row(row, carry):
            padded[place : place + 3] = halo_ref[row].astype(f32)
            for col in range(3):
                shifts[col, row + 3] = padded[col + offset : col + offset + 8]
            return carry

        lax.fori_loop(0, LAT, one_row, 0)

        def block(index, carry):
            first = index * BLK

            def emit(target, low, high, value):
                out_ref[first + target, :, low:high] = (strip_ref[first + target, :, low:high] + value).astype(bf16)

            convolve(shifts, kernel_ref, first, True, emit, cols, 8)
            return carry

        lax.fori_loop(0, LAT // BLK, block, 0)

    @pl.when(pl.program_id(0) == 0)
    def _():
        side(left_ref, west_ref, 0, 0, range(0, 3))

    @pl.when(pl.program_id(0) == 1)
    def _():
        side(right_ref, east_ref, 8, 1, range(4, 7))


def finish_edges(inner, west, east, left, right, kernel):
    whole = lambda array: pl.BlockSpec(array.shape, lambda i: (0,) * array.ndim)
    return pl.pallas_call(
        edge_kernel,
        grid=(2,),
        in_specs=[pl.BlockSpec(memory_space=pl.ANY)] + [whole(x) for x in (west, east, left, right, kernel)],
        out_specs=pl.BlockSpec((LAT, 8, CH), lambda i: (0, 3 * i, 0)),
        out_shape=FIELD,
        input_output_aliases={0: 0},
        scratch_shapes=[pltpu.VMEM((3, LAT + 6, 8, CH), f32), pltpu.VMEM((16, CH), f32)],
        cost_estimate=pl.CostEstimate(flops=5000000, bytes_accessed=700000, transcendentals=0),
    )(inner, west, east, left, right, kernel)


def swap_edges(head, tail):
    peers = lax.axis_size("tile")
    up = [(i, (i + 1) % peers) for i in range(peers)]
    down = [(j, i) for i, j in up]
    return lax.ppermute(tail, "tile", up), lax.ppermute(head, "tile", down)


def after(array, other):
    return lax.optimization_barrier((array, other))[0]


def exchange(array, axis):
    return lax.all_to_all(array, axis, split_axis=0, concat_axis=0, tiled=True)


def per_device(
    adjoint_final, states, kernel, norm_gain, up_weight, up_bias, down_weight,
    obs_cell, obs_count, obs_value, obs_error,
):
    gain = norm_gain[None]
    bias = up_bias[None]
    down = down_weight.T

    packed = pack_observations(
        obs_cell[:, 0].transpose(0, 2, 1), obs_count, obs_value, obs_error[:, 0].transpose(0, 2, 1)
    )
    got = exchange(packed, "tile")
    head, tail = cut_edges(after(states, packed))
    left, right = swap_edges(head, tail)

    rows = gather_rows(after(got, head), states)
    owned = exchange(rows, "member")

    hidden, head, tail = forward(
        0, states, left, after(right, rows), kernel, gain, up_weight, bias, down, adjoint_final
    )
    before, behind = swap_edges(head, tail)

    deps = departures(after(owned, hidden), got)
    back = exchange(deps, "member")

    slope, unit = forward(1, states, left, after(right, deps), kernel, gain, up_weight, bias)
    partial = spread_back(hidden, before, after(behind, slope), adjoint_final, kernel)

    hidden, head, tail, adjoint = second_step(
        partial, after(back, partial), got, slope, unit, gain, up_weight, down
    )
    left, right = swap_edges(head, tail)
    inner, west, east = interior(hidden, adjoint, back, got, kernel)
    return finish_edges(inner, west, east, left, right, kernel)[None]


def solution(mesh):
    placed = (
        P("member", None, "tile", None),
        P(None, "member", None, "tile", None),
        P(),
        P(),
        P(),
        P(),
        P(),
        P(None, "tile", None, None),
        P(None, "tile", None),
        P(None, "tile", None, None, None),
        P(None, "tile", None, None),
    )
    return jax.shard_map(
        per_device,
        mesh=mesh,
        in_specs=placed,
        out_specs=P("member", None, "tile", None),
        check_vma=False,
    )
```

time: 126 us -> 126 us (level)
  the two profiles are of different devices: /device:TPU:31 before, /device:TPU:32 now
where the time goes in v3:
time: 126 us
  starting transfers between devices  57.4 us (46%)
  Pallas kernels  44.3 us (35%)
  waiting for transfers between devices  13.5 us (11%)
  local copies, waits for them, and re-layouts  10.2 us (8%)
    all_to_all x3, starting transfers between devices, exchange(): return lax.all_to_all(array, axis, split_axis=0, concat_axis=0, tiled=True)  34.6 us
    ppermute x6, starting transfers between devices, swap_edges(): return (lax.ppermute(tail, 'tile', up), lax.ppermute(head, 'tile', down))  22.8 us
    pallas_call x2, Pallas kernels, forward(): pl.pallas_call(functools.partial(forward_kernel, step), out_shape=shapes,...  17.1 us
    unnamed x48, local copies, waits for them, and re-layouts  10.2 us
    ppermute x6, waiting for transfers between devices, swap_edges(): return (lax.ppermute(tail, 'tile', up), lax.ppermute(head, 'tile', down))  7.88 us
    pallas_call x1, Pallas kernels, interior(): pl.pallas_call(interior_kernel, out_shape=(FIELD, STRIP, STRIP), scratch_...  6.99 us
    all_to_all x3, waiting for transfers between devices, exchange(): return lax.all_to_all(array, axis, split_axis=0, concat_axis=0, tiled=True)  5.66 us
    pallas_call x1, Pallas kernels, spread_back(): pl.pallas_call(spread_kernel, out_shape=jax.ShapeDtypeStruct((LAT, WID, C...  4.91 us
  transfers between devices with their start and end apart: 9, of which 3 were waited for; matrix products, arithmetic and copies ran while one was open for 0% of the time, Pallas kernels for 24%

profile of v3, /device:TPU:32, one launch (start us, length us, event | category | flops | bytes accessed | tf_op | source)
XLA Modules:
  0.0 125.6 jit_solution(3944836391842185492)
XLA Ops:
  0.0 2.1 %shard_map.109 = f32[32,4,128]{2,1,0:T(4,128)} custom-call(s32[2,16,32]{2,1,0:T(8,128)} %bitcast.14, s32[2,1,32]{2,1,0:T(1,128)} %count_ref.1, bf16[2,1,32,16,192]{4,3,2,1,0:T(8,128)(2,1)} %value_ref.1, bf16[2,16,32]{2,1,0:T(8,128)(2,1)} %bitcast.15), custom_call_target="tpu_custom_call" | custom-call | tf_op jit(solution)/shard_map/pallas_call | solution.py:119
  2.1 7.3 %all-to-all-start = ((f32[32,4,128]{2,1,0:T(4,128)}), f32[32,4,128]{2,1,0:T(4,128)S(1)}, u32[]{:S(2)}, u32[]{:S(2)}) async-start(f32[32,4,128]{2,1,0:T(4,128)} %shard_map.109), calls=%async_computation | async-start | bytes 131072 | tf_op jit(solution)/shard_map/all_to_all | solution.py:422
  9.4 1.8 %shard_map.110 = (bf16[2,32,3,192]{3,2,1,0:T(4,128)(2,1)}, bf16[2,32,3,192]{3,2,1,0:T(4,128)(2,1)}) custom-call(bf16[2,1,32,32,192]{4,3,2,1,0:T(8,128)(2,1)} %state_ref.5, bf16[2,1,32,32,192]{4,3,2,1,0:T(8,128)(2,1)} %state_ref.5), custom_call_target="tpu_custom_call" | custom-call | tf_op jit(solution)/shard_map/pallas_call | solution.py:94
  11.2 0.0 copy-start.23
  11.2 0.0 copy-start
  11.2 0.0 copy-start.5
  11.3 0.0 copy-start.10
  11.3 0.0 copy-start.11
  11.3 0.0 copy-start.15
  11.3 5.7 %all-to-all-done.got_ref = f32[32,4,128]{2,1,0:T(4,128)S(1)} async-done(((f32[32,4,128]{2,1,0:T(4,128)}), f32[32,4,128]{2,1,0:T(4,128)S(1)}, u32[]{:S(2)}, u32[]{:S(2)}) %all-to-all-start) | async-done | bytes 65568 | tf_op jit(solution)/shard_map/all_to_all | solution.py:422
  16.9 0.6 copy-done.1
  17.6 3.7 %shard_map.111 = bf16[16,32,384]{2,1,0:T(8,128)(2,1)} custom-call(f32[32,4,128]{2,1,0:T(4,128)} %copy-done.1, bf16[2,1,32,32,192]{4,3,2,1,0:T(8,128)(2,1)} %state_ref.5), custom_call_target="tpu_custom_call" | custom-call | flops 1000000 | bytes 2000000 | tf_op jit(solution)/shard_map/pallas_call | solution.py:147
  21.3 15.2 %all-to-all-start.1 = ((bf16[16,32,384]{2,1,0:T(8,128)(2,1)}), bf16[16,32,384]{2,1,0:T(8,128)(2,1)S(1)}, u32[]{:S(2)}, u32[]{:S(2)}) async-start(bf16[16,32,384]{2,1,0:T(8,128)(2,1)} %shard_map.111), calls=%async_computation.1 | async-start | bytes 786432 | tf_op jit(solution)/shard_map/all_to_all | solution.py:422
  36.5 2.8 %collective-permute-start.1 = (bf16[2,32,3,192]{3,2,1,0:T(4,128)(2,1)}, bf16[2,32,3,192]{3,2,1,0:T(4,128)(2,1)S(1)}, u32[]{:S(2)}, u32[]{:S(2)}) collective-permute-start(bf16[2,32,3,192]{3,2,1,0:T(4,128)(2,1)} %get-tuple-element.28), channel_id=1, source_target_pairs={{1,0},{2,1},{3,2},{4,3},{5,4},{6,5},{7,6},{8,7},{9,8},{10,9},{11,1... | collective-permute-start | bytes 221192 | tf_op jit(solution)/shard_map/ppermute | solution.py:414
  39.3 1.9 %collective-permute-start = (bf16[2,32,3,192]{3,2,1,0:T(4,128)(2,1)}, bf16[2,32,3,192]{3,2,1,0:T(4,128)(2,1)S(1)}, u32[]{:S(2)}, u32[]{:S(2)}) collective-permute-start(bf16[2,32,3,192]{3,2,1,0:T(4,128)(2,1)} %get-tuple-element.27), channel_id=1, source_target_pairs={{0,1},{1,2},{2,3},{3,4},{4,5},{5,6},{6,7},{7,8},{8,9},{9,10},{10,1... | collective-permute-start | bytes 221192 | tf_op jit(solution)/shard_map/ppermute | solution.py:414
  41.2 0.0 copy-done.23
  41.3 0.9 collective-permute-done.1.right_ref
  42.1 7.0 %collective-permute-done.left_ref = bf16[2,32,3,192]{3,2,1,0:T(4,128)(2,1)S(1)} collective-permute-done((bf16[2,32,3,192]{3,2,1,0:T(4,128)(2,1)}, bf16[2,32,3,192]{3,2,1,0:T(4,128)(2,1)S(1)}, u32[]{:S(2)}, u32[]{:S(2)}) %collective-permute-start) | collective-permute-done | bytes 73760 | tf_op jit(solution)/shard_map/ppermute | solution.py:414
  49.1 0.0 copy-done
  49.1 0.0 copy-done.5
  49.1 0.0 copy-done.9
  49.1 0.0 copy-done.10
  49.2 0.0 copy-done.11
  49.2 0.0 copy-done.15
  49.2 9.3 %shard_map.112 = (bf16[32,32,192]{2,1,0:T(8,128)(2,1)S(1)}, bf16[32,3,192]{2,1,0:T(4,128)(2,1)}, bf16[32,3,192]{2,1,0:T(4,128)(2,1)S(1)}) custom-call(bf16[2,1,32,32,192]{4,3,2,1,0:T(8,128)(2,1)S(1)} %copy-done, bf16[2,32,3,192]{3,2,1,0:T(4,128)(2,1)S(1)} %collective-permute-done.left_ref, bf16[2,32,3,192]{3,2,1,0:T(4,128)(2,1)S(1)} %collective-permute-done.1.right_ref, ...), custom_call_target="tpu_custom_call" | custom-call | flops 905969664 | bytes 8000000 | tf_op jit(solution)/shard_map/pallas_call | solution.py:259
  58.5 0.8 copy-done.7
  59.3 0.6 copy-done.16
  59.9 0.6 copy-done.18
  60.6 0.0 all-to-all-done.1.rows_ref
  60.6 0.8 copy-done.20
  61.3 2.2 %shard_map.113 = bf16[16,32,384]{2,1,0:T(8,128)(2,1)} custom-call(bf16[16,32,384]{2,1,0:T(8,128)(2,1)} %copy-done.20, f32[32,4,128]{2,1,0:T(4,128)} %copy-done.1), custom_call_target="tpu_custom_call" | custom-call | flops 1200000 | bytes 1200000 | tf_op jit(solution)/shard_map/pallas_call | solution.py:170
  63.5 12.0 %all-to-all-start.2 = ((bf16[16,32,384]{2,1,0:T(8,128)(2,1)}), bf16[16,32,384]{2,1,0:T(8,128)(2,1)S(1)}, u32[]{:S(2)}, u32[]{:S(2)}) async-start(bf16[16,32,384]{2,1,0:T(8,128)(2,1)} %shard_map.113), calls=%async_computation.2 | async-start | bytes 786432 | tf_op jit(solution)/shard_map/all_to_all | solution.py:422
  75.6 1.9 %collective-permute-start.2 = (bf16[32,3,192]{2,1,0:T(4,128)(2,1)S(1)}, bf16[32,3,192]{2,1,0:T(4,128)(2,1)S(1)}, u32[]{:S(2)}, u32[]{:S(2)}) collective-permute-start(bf16[32,3,192]{2,1,0:T(4,128)(2,1)S(1)} %get-tuple-element.32), channel_id=1, source_target_pairs={{0,1},{1,2},{2,3},{3,4},{4,5},{5,6},{6,7},{7,8},{8,9},{9,10},{10,1... | collective-permute-start | bytes 110600 | tf_op jit(solution)/shard_map/ppermute | solution.py:414
  77.5 0.0 copy-start.6
  77.5 0.0 copy-start.8
  77.5 7.1 %collective-permute-start.3 = (bf16[32,3,192]{2,1,0:T(4,128)(2,1)}, bf16[32,3,192]{2,1,0:T(4,128)(2,1)S(1)}, u32[]{:S(2)}, u32[]{:S(2)}) collective-permute-start(bf16[32,3,192]{2,1,0:T(4,128)(2,1)} %get-tuple-element.33), channel_id=1, source_target_pairs={{1,0},{2,1},{3,2},{4,3},{5,4},{6,5},{7,6},{8,7},{9,8},{10,9},{11,1... | collective-permute-start | bytes 110600 | tf_op jit(solution)/shard_map/ppermute | solution.py:414
  84.6 0.0 copy-start.17
  84.6 0.9 copy-done.17
  85.5 0.9 copy-done.19
  86.4 7.8 %shard_map.114 = (bf16[1024,768]{1,0:T(8,128)(2,1)S(1)}, bf16[1024,192]{1,0:T(8,128)(2,1)S(1)}) custom-call(bf16[2,1,32,32,192]{4,3,2,1,0:T(8,128)(2,1)S(1)} %copy-done, bf16[2,32,3,192]{3,2,1,0:T(4,128)(2,1)S(1)} %copy-done.19, bf16[2,32,3,192]{3,2,1,0:T(4,128)(2,1)S(1)} %copy-done.17, f32[7,7,192]{2,1,0:T(8,128)S(1)} %copy-done.9, f32[1,192]{1,0:T(1,128)S(1)} %bitcast.12, ...), custom_call_target="tpu_custom_call" | custom-call | flops 905969664 | bytes 8000000 | tf_op jit(solution)/shard_map/pallas_call | solution.py:259
  94.2 0.0 copy-start.3
  94.2 0.8 copy-done.3
  95.0 0.0 collective-permute-done.3.right_ref
  95.0 0.0 collective-permute-done.2.left_ref
  95.0 0.0 copy-done.6
  95.0 0.0 copy-done.8
  95.0 4.9 %shard_map.115.partial_ref = f32[32,32,192]{2,1,0:T(8,128)S(1)} custom-call(bf16[32,32,192]{2,1,0:T(8,128)(2,1)S(1)} %copy-done.8, bf16[32,3,192]{2,1,0:T(4,128)(2,1)S(1)} %collective-permute-done.2.left_ref, bf16[32,3,192]{2,1,0:T(4,128)(2,1)S(1)} %collective-permute-done.3.right_ref, bf16[1,32,32,192]{3,2,1,0:T(8,128)(2,1)S(1)} %copy-done.6, ...), custom_call_target="tpu_custom_call" | custom-call | flops 19267584 | bytes 3000000 | tf_op jit(solution)/shard_map/pallas_call | solution.py:290
  99.9 0.0 all-to-all-done.2.rows_ref
  99.9 0.0 copy-done.2
  100.0 0.0 copy-start.4
  100.0 1.0 copy-done.4
  101.0 1.0 copy-done.12
  102.0 2.1 %shard_map.116 = (bf16[32,32,192]{2,1,0:T(8,128)(2,1)S(1)}, bf16[32,3,192]{2,1,0:T(4,128)(2,1)S(1)}, bf16[32,3,192]{2,1,0:T(4,128)(2,1)S(1)}, bf16[32,32,192]{2,1,0:T(8,128)(2,1)S(1)}) custom-call(f32[32,32,192]{2,1,0:T(8,128)S(1)} %shard_map.115.partial_ref, bf16[16,32,384]{2,1,0:T(8,128)(2,1)S(1)} %all-to-all-done.2.rows_ref, f32[32,4,128]{2,1,0:T(4,128)S(1)} %copy-done.2, ...), custom_call_target="tpu_custom_call" | custom-call | flops 603979776 | bytes 5000000 | tf_op jit(solution)/shard_map/pallas_call | solution.py:320
  104.0 1.9 %collective-permute-start.4 = (bf16[32,3,192]{2,1,0:T(4,128)(2,1)S(1)}, bf16[32,3,192]{2,1,0:T(4,128)(2,1)S(1)}, u32[]{:S(2)}, u32[]{:S(2)}) collective-permute-start(bf16[32,3,192]{2,1,0:T(4,128)(2,1)S(1)} %get-tuple-element.45), channel_id=1, source_target_pairs={{0,1},{1,2},{2,3},{3,4},{4,5},{5,6},{6,7},{7,8},{8,9},{9,10},{10,1... | collective-permute-start | bytes 110600 | tf_op jit(solution)/shard_map/ppermute | solution.py:414
  106.0 7.1 %collective-permute-start.5 = (bf16[32,3,192]{2,1,0:T(4,128)(2,1)S(1)}, bf16[32,3,192]{2,1,0:T(4,128)(2,1)S(1)}, u32[]{:S(2)}, u32[]{:S(2)}) collective-permute-start(bf16[32,3,192]{2,1,0:T(4,128)(2,1)S(1)} %get-tuple-element.46), channel_id=1, source_target_pairs={{1,0},{2,1},{3,2},{4,3},{5,4},{6,5},{7,6},{8,7},{9,8},{10,9},{11,1... | collective-permute-start | bytes 110600 | tf_op jit(solution)/shard_map/ppermute | solution.py:414
  113.1 7.0 %shard_map.117 = (bf16[32,32,192]{2,1,0:T(8,128)(2,1)}, f32[32,8,192]{2,1,0:T(8,128)S(1)}, f32[32,8,192]{2,1,0:T(8,128)S(1)}) custom-call(bf16[32,32,192]{2,1,0:T(8,128)(2,1)S(1)} %get-tuple-element.40.hidden_ref, bf16[32,32,192]{2,1,0:T(8,128)(2,1)S(1)} %get-tuple-element.41.adjoint_ref, bf16[16,32,384]{2,1,0:T(8,128)(2,1)S(1)} %all-to-all-done.2.rows_ref, ...), custom_call_target="tpu_custom_call" | custom-call | flops 19267584 | bytes 3000000 | tf_op jit(solution)/shard_map/pallas_call | solution.py:354
  120.1 0.7 copy-done.13
  120.8 0.7 copy-done.14
  121.5 0.0 collective-permute-done.4.left_ref
  121.5 0.0 collective-permute-done.5.right_ref
  121.5 0.0 copy-start.22
  121.5 0.6 copy-done.21
  122.1 0.0 copy-done.22
  122.2 3.5 %shard_map.118 = bf16[32,32,192]{2,1,0:T(8,128)(2,1)} custom-call(bf16[32,32,192]{2,1,0:T(8,128)(2,1)} %get-tuple-element.42.inner_ref, f32[32,8,192]{2,1,0:T(8,128)} %copy-done.13, f32[32,8,192]{2,1,0:T(8,128)} %copy-done.14, bf16[32,3,192]{2,1,0:T(4,128)(2,1)} %copy-done.21, bf16[32,3,192]{2,1,0:T(4,128)(2,1)} %copy-done.22, ...), custom_call_target="tpu_custom_call", output_to_operand_aliasing={{}: (0, {})} | custom-call | flops 5000000 | bytes 700000 | tf_op jit(solution)/shard_map/pallas_call | solution.py:398
  (13 shorter events, 0.0 us)
Async XLA Ops:
  2.1 14.9 %all-to-all-start = ((f32[32,4,128]{2,1,0:T(4,128)}), f32[32,4,128]{2,1,0:T(4,128)S(1)}, u32[]{:S(2)}, u32[]{:S(2)}) async-start(f32[32,4,128]{2,1,0:T(4,128)} %shard_map.109), calls=%async_computation | async-start | bytes 131072 | tf_op jit(solution)/shard_map/all_to_all | solution.py:422
  11.2 30.0 %copy-start.23 = (f32[768]{0:T(1024)S(1)}, f32[768]{0:T(1024)}, u32[]{:S(2)}) copy-start(f32[768]{0:T(1024)} %param.16) | copy-start | bytes 9220
  11.2 37.9 %copy-start = (bf16[2,1,32,32,192]{4,3,2,1,0:T(8,128)(2,1)S(1)}, bf16[2,1,32,32,192]{4,3,2,1,0:T(8,128)(2,1)}, u32[]{:S(2)}) copy-start(bf16[2,1,32,32,192]{4,3,2,1,0:T(8,128)(2,1)} %state_ref.5) | copy-start | bytes 2359300
  11.2 37.9 %copy-start.5 = (bf16[1,32,32,192]{3,2,1,0:T(8,128)(2,1)S(1)}, bf16[1,32,32,192]{3,2,1,0:T(8,128)(2,1)}, u32[]{:S(2)}) copy-start(bf16[1,32,32,192]{3,2,1,0:T(8,128)(2,1)} %base_ref.1) | copy-start | bytes 1179652
  11.2 37.9 %copy-start.9 = (f32[7,7,192]{2,1,0:T(8,128)S(1)}, f32[7,7,192]{2,1,0:T(8,128)}, u32[]{:S(2)}) copy-start(f32[7,7,192]{2,1,0:T(8,128)} %kernel_ref.9) | copy-start | bytes 112900
  11.3 37.9 %copy-start.10 = (bf16[192,768]{1,0:T(8,128)(2,1)S(1)}, bf16[192,768]{1,0:T(8,128)(2,1)}, u32[]{:S(2)}) copy-start(bf16[192,768]{1,0:T(8,128)(2,1)} %up_ref.5) | copy-start | bytes 884740
  11.3 37.9 %copy-start.11 = (bf16[768,192]{0,1:T(8,128)(2,1)S(1)}, bf16[768,192]{0,1:T(8,128)(2,1)}, u32[]{:S(2)}) copy-start(bf16[768,192]{0,1:T(8,128)(2,1)} %param.17) | copy-start | bytes 884740
  11.3 37.9 %copy-start.15 = (f32[192]{0:T(256)S(1)}, f32[192]{0:T(256)}, u32[]{:S(2)}) copy-start(f32[192]{0:T(256)} %param.14) | copy-start | bytes 2308
  16.9 0.6 copy-start.1
  21.3 39.3 %all-to-all-start.1 = ((bf16[16,32,384]{2,1,0:T(8,128)(2,1)}), bf16[16,32,384]{2,1,0:T(8,128)(2,1)S(1)}, u32[]{:S(2)}, u32[]{:S(2)}) async-start(bf16[16,32,384]{2,1,0:T(8,128)(2,1)} %shard_map.111), calls=%async_computation.1 | async-start | bytes 786432 | tf_op jit(solution)/shard_map/all_to_all | solution.py:422
  36.5 5.7 %collective-permute-start.1 = (bf16[2,32,3,192]{3,2,1,0:T(4,128)(2,1)}, bf16[2,32,3,192]{3,2,1,0:T(4,128)(2,1)S(1)}, u32[]{:S(2)}, u32[]{:S(2)}) collective-permute-start(bf16[2,32,3,192]{3,2,1,0:T(4,128)(2,1)} %get-tuple-element.28), channel_id=1, source_target_pairs={{1,0},{2,1},{3,2},{4,3},{5,4},{6,5},{7,6},{8,7},{9,8},{10,9},{11,1... | collective-permute-start | bytes 221192 | tf_op jit(solution)/shard_map/ppermute | solution.py:414
  39.3 9.8 %collective-permute-start = (bf16[2,32,3,192]{3,2,1,0:T(4,128)(2,1)}, bf16[2,32,3,192]{3,2,1,0:T(4,128)(2,1)S(1)}, u32[]{:S(2)}, u32[]{:S(2)}) collective-permute-start(bf16[2,32,3,192]{3,2,1,0:T(4,128)(2,1)} %get-tuple-element.27), channel_id=1, source_target_pairs={{0,1},{1,2},{2,3},{3,4},{4,5},{5,6},{6,7},{7,8},{8,9},{9,10},{10,1... | collective-permute-start | bytes 221192 | tf_op jit(solution)/shard_map/ppermute | solution.py:414
  58.5 0.8 copy-start.7
  59.3 0.6 copy-start.16
  59.9 0.7 copy-start.18
  60.6 0.8 copy-start.20
  63.5 36.4 %all-to-all-start.2 = ((bf16[16,32,384]{2,1,0:T(8,128)(2,1)}), bf16[16,32,384]{2,1,0:T(8,128)(2,1)S(1)}, u32[]{:S(2)}, u32[]{:S(2)}) async-start(bf16[16,32,384]{2,1,0:T(8,128)(2,1)} %shard_map.113), calls=%async_computation.2 | async-start | bytes 786432 | tf_op jit(solution)/shard_map/all_to_all | solution.py:422
  75.6 19.4 %collective-permute-start.2 = (bf16[32,3,192]{2,1,0:T(4,128)(2,1)S(1)}, bf16[32,3,192]{2,1,0:T(4,128)(2,1)S(1)}, u32[]{:S(2)}, u32[]{:S(2)}) collective-permute-start(bf16[32,3,192]{2,1,0:T(4,128)(2,1)S(1)} %get-tuple-element.32), channel_id=1, source_target_pairs={{0,1},{1,2},{2,3},{3,4},{4,5},{5,6},{6,7},{7,8},{8,9},{9,10},{10,1... | collective-permute-start | bytes 110600 | tf_op jit(solution)/shard_map/ppermute | solution.py:414
  77.5 17.5 %copy-start.6 = (bf16[1,32,32,192]{3,2,1,0:T(8,128)(2,1)S(1)}, bf16[1,32,32,192]{3,2,1,0:T(8,128)(2,1)}, u32[]{:S(2)}) copy-start(bf16[1,32,32,192]{3,2,1,0:T(8,128)(2,1)} %base_ref.1) | copy-start | bytes 1179652
  77.5 17.5 %copy-start.8 = (bf16[32,32,192]{2,1,0:T(8,128)(2,1)S(1)}, bf16[32,32,192]{2,1,0:T(8,128)(2,1)}, u32[]{:S(2)}) copy-start(bf16[32,32,192]{2,1,0:T(8,128)(2,1)} %copy-done.7) | copy-start | bytes 1179652
  77.5 17.5 %collective-permute-start.3 = (bf16[32,3,192]{2,1,0:T(4,128)(2,1)}, bf16[32,3,192]{2,1,0:T(4,128)(2,1)S(1)}, u32[]{:S(2)}, u32[]{:S(2)}) collective-permute-start(bf16[32,3,192]{2,1,0:T(4,128)(2,1)} %get-tuple-element.33), channel_id=1, source_target_pairs={{1,0},{2,1},{3,2},{4,3},{5,4},{6,5},{7,6},{8,7},{9,8},{10,9},{11,1... | collective-permute-start | bytes 110600 | tf_op jit(solution)/shard_map/ppermute | solution.py:414
  84.6 0.9 copy-start.17
  85.5 0.9 copy-start.19
  94.2 0.8 copy-start.3
  95.0 5.0 %copy-start.2 = (f32[32,4,128]{2,1,0:T(4,128)S(1)}, f32[32,4,128]{2,1,0:T(4,128)}, u32[]{:S(2)}) copy-start(f32[32,4,128]{2,1,0:T(4,128)} %copy-done.1) | copy-start | bytes 196612
  100.0 1.0 copy-start.4
  101.0 1.0 copy-start.12
  104.0 17.5 %collective-permute-start.4 = (bf16[32,3,192]{2,1,0:T(4,128)(2,1)S(1)}, bf16[32,3,192]{2,1,0:T(4,128)(2,1)S(1)}, u32[]{:S(2)}, u32[]{:S(2)}) collective-permute-start(bf16[32,3,192]{2,1,0:T(4,128)(2,1)S(1)} %get-tuple-element.45), channel_id=1, source_target_pairs={{0,1},{1,2},{2,3},{3,4},{4,5},{5,6},{6,7},{7,8},{8,9},{9,10},{10,1... | collective-permute-start | bytes 110600 | tf_op jit(solution)/shard_map/ppermute | solution.py:414
  106.0 15.6 %collective-permute-start.5 = (bf16[32,3,192]{2,1,0:T(4,128)(2,1)S(1)}, bf16[32,3,192]{2,1,0:T(4,128)(2,1)S(1)}, u32[]{:S(2)}, u32[]{:S(2)}) collective-permute-start(bf16[32,3,192]{2,1,0:T(4,128)(2,1)S(1)} %get-tuple-element.46), channel_id=1, source_target_pairs={{1,0},{2,1},{3,2},{4,3},{5,4},{6,5},{7,6},{8,7},{9,8},{10,9},{11,1... | collective-permute-start | bytes 110600 | tf_op jit(solution)/shard_map/ppermute | solution.py:414
  120.1 0.7 copy-start.13
  120.8 0.7 copy-start.14
  121.5 0.6 copy-start.21
  121.5 0.7 copy-start.22

commit v4 on v3

--- a/solution.py
+++ b/solution.py
@@ -21,6 +21,7 @@
 SLOTS = LAT * CAP
 BLK = 8
 ROWS = BLK * WID
+UNROLL = 4
 f32 = jnp.float32
 bf16 = jnp.bfloat16
 NT = (((1,), (1,)), ((), ()))
@@ -34,8 +35,23 @@
     return (0.5 + 0.5 * tanh_val) + tail * (1.0 - tanh_val * tanh_val)
 
 
+def limit(mebibytes):
+    return pltpu.CompilerParams(vmem_limit_bytes=mebibytes * 1024 * 1024)
+
+
 def mean_lanes(value):
     return jnp.sum(value, axis=-1, keepdims=True) * (1.0 / CH)
+
+
+HBM = pl.BlockSpec(memory_space=pltpu.HBM)
+VM = pl.BlockSpec(memory_space=pltpu.VMEM)
+
+
+def fetch(pairs, sems):
+    copies = [pltpu.make_async_copy(src, dst, sems.at[i]) for i, (src, dst) in enumerate(pairs)]
+    for copy in copies:
+        copy.start()
+    return copies
 
 
 def clear_rims(shifts, count, width):
@@ -51,16 +67,20 @@
     if left is None:
         padded[...] = jnp.zeros(padded.shape, f32)
 
-    def one_row(row, carry):
-        if left is not None:
-            padded[0:3] = left(row).astype(f32)
-            padded[WID + 3 : WID + 6] = right(row).astype(f32)
-        padded[3 : WID + 3] = centre(row).astype(f32)
-        for col in range(7):
-            shifts[col, row + 3] = padded[col : col + WID]
+    def some_rows(index, carry):
+        for lane in range(UNROLL):
+            row = index * UNROLL + lane
+            if left is not None:
+                padded[lane, 0:3] = left(row).astype(f32)
+                padded[lane, WID + 3 : WID + 6] = right(row).astype(f32)
+            padded[lane, 3 : WID + 3] = centre(row).astype(f32)
+        for lane in range(UNROLL):
+            row = index * UNROLL + lane
+            for col in range(7):
+                shifts[col, row + 3] = padded[lane, col : col + WID]
         return carry
 
-    lax.fori_loop(0, LAT, one_row, 0)
+    lax.fori_loop(0, LAT // UNROLL, some_rows, 0)
 
 
 def convolve(shifts, kernel_ref, first, flip, emit, cols=range(7), width=WID):
@@ -82,20 +102,6 @@
             emit(target, low, high, sums[target])
 
 
-def cut_kernel(first_ref, last_ref, head_ref, tail_ref):
-    head_ref[...] = first_ref[:, 0, :, 0:3]
-    tail_ref[...] = last_ref[:, 0, :, 5:8]
-
-
-def cut_edges(states):
-    edge = jax.ShapeDtypeStruct((2, LAT, 3, CH), bf16)
-    whole = pl.BlockSpec((2, LAT, 3, CH), lambda i: (0, 0, 0, 0))
-    part = lambda block: pl.BlockSpec((2, 1, LAT, 8, CH), lambda i: (0, 0, 0, block, 0))
-    return pl.pallas_call(
-        cut_kernel, grid=(1,), in_specs=[part(0), part(3)], out_specs=[whole, whole], out_shape=(edge, edge)
-    )(states, states)
-
-
 def pack_kernel(cell_ref, count_ref, value_ref, error_ref, out_ref):
     member = lax.axis_index("member")
     tiles = cell_ref.shape[2]
@@ -119,6 +125,7 @@
     return pl.pallas_call(
         pack_kernel,
         out_shape=jax.ShapeDtypeStruct((cells.shape[2], 4, 128), f32),
+        compiler_params=limit(6),
     )(cells, counts, values, errors)
 
 
@@ -147,6 +154,7 @@
     return pl.pallas_call(
         gather_kernel,
         out_shape=jax.ShapeDtypeStruct((CAP, LAT, 2 * CH), bf16),
+        compiler_params=limit(6),
         cost_estimate=pl.CostEstimate(flops=1000000, bytes_accessed=2000000, transcendentals=0),
     )(got, states)
 
@@ -170,6 +178,7 @@
     return pl.pallas_call(
         departure_kernel,
         out_shape=jax.ShapeDtypeStruct((CAP, LAT, 2 * CH), bf16),
+        compiler_params=limit(6),
         cost_estimate=pl.CostEstimate(flops=1200000, bytes_accessed=1200000, transcendentals=0),
     )(rows, got)
 
@@ -197,75 +206,78 @@
     return scaled - mean_lanes(scaled) - unit * mean_lanes(scaled * unit)
 
 
-def put_hidden(adj_hidden, first, out_ref, head_ref, tail_ref):
+def put_hidden(adj_hidden, first, out_ref, tail_ref, head_ref):
     block = adj_hidden.astype(bf16).reshape(BLK, WID, CH)
     out_ref[pl.ds(first, BLK)] = block
     head_ref[pl.ds(first, BLK)] = block[:, 0:3]
     tail_ref[pl.ds(first, BLK)] = block[:, WID - 3 : WID]
 
 
-def forward_kernel(step, state_ref, left_ref, right_ref, kernel_ref, gain_ref, up_ref, bias_ref, *rest):
-    shifts, padded, hidden = rest[-3:]
+def forward_kernel(
+    state_ref, right_ref, left_ref, kernel_ref, gain_ref, up_ref, bias_ref, down_ref, adjoint_ref,
+    hidden_out, tail_out, head_out, slope_out, unit_out,
+    shifts, padded, hidden,
+):
     gain = gain_ref[...]
-    build_shifts(
-        shifts, padded,
-        lambda row: state_ref[step, 0, row],
-        lambda row: left_ref[step, row],
-        lambda row: right_ref[step, row],
-    )
-
-    def block(index, carry):
-        first = index * BLK
-
-        def emit(target, low, high, value):
-            hidden[target, :, low:high] = value
-
-        convolve(shifts, kernel_ref, first, False, emit)
-        unit, inv_std = normalise(hidden[...].reshape(ROWS, CH))
-        normed = (unit * gain).astype(bf16)
-
-        def slope_at(cols):
-            preact = jnp.dot(normed, up_ref[:, cols], preferred_element_type=f32)
-            return gelu_slope(preact + bias_ref[:, cols]) * inv_std
-
-        if step == 0:
-            down_ref, adjoint_ref, hidden_out, head_out, tail_out = rest[:5]
-            adjoint = adjoint_ref[0, pl.ds(first, BLK)].reshape(ROWS, CH)
-            result = backward(adjoint, slope_at, down_ref, up_ref, gain, unit)
-            put_hidden(result, first, hidden_out, head_out, tail_out)
-        else:
-            slope_out, unit_out = rest[:2]
-            rows = pl.ds(pl.multiple_of(index * ROWS, ROWS), ROWS)
-            for part in range(3):
-                cols = slice(part * 256, (part + 1) * 256)
-                slope_out[rows, cols] = slope_at(cols).astype(bf16)
-            unit_out[rows, :] = unit.astype(bf16)
-        return carry
-
-    lax.fori_loop(0, LAT // BLK, block, 0)
-
-
+    for step in range(2):
+        build_shifts(
+            shifts, padded,
+            lambda row: state_ref[step, 0, row],
+            lambda row: left_ref[step, row],
+            lambda row: right_ref[step, row],
+        )
+
+        def block(index, carry):
+            first = index * BLK
+
+            def emit(target, low, high, value):
+                hidden[target, :, low:high] = value
+
+            convolve(shifts, kernel_ref, first, False, emit)
+            unit, inv_std = normalise(hidden[...].reshape(ROWS, CH))
+            normed = (unit * gain).astype(bf16)
+
+            def slope_at(cols):
+                preact = jnp.dot(normed, up_ref[:, cols], preferred_element_type=f32)
+                return gelu_slope(preact + bias_ref[:, cols]) * inv_std
+
+            if step == 0:
+                adjoint = adjoint_ref[0, pl.ds(first, BLK)].reshape(ROWS, CH)
+                result = backward(adjoint, slope_at, down_ref, up_ref, gain, unit)
+                put_hidden(result, first, hidden_out, tail_out, head_out)
+            else:
+                rows = pl.ds(pl.multiple_of(index * ROWS, ROWS), ROWS)
+                for part in range(3):
+                    cols = slice(part * 256, (part + 1) * 256)
+                    slope_out[rows, cols] = slope_at(cols).astype(bf16)
+                unit_out[rows, :] = unit.astype(bf16)
+            return carry
+
+        lax.fori_loop(0, LAT // BLK, block, 0)
+
+
+FAR_EDGE = pltpu.HBM((LAT, 3, CH), bf16)
 EDGE = jax.ShapeDtypeStruct((LAT, 3, CH), bf16)
 FIELD = jax.ShapeDtypeStruct((LAT, WID, CH), bf16)
-SHIFT_SCRATCH = [pltpu.VMEM((7, LAT + 6, WID, CH), f32), pltpu.VMEM((WID + 8, CH), f32)]
-BIG = pltpu.CompilerParams(vmem_limit_bytes=16 * 1024 * 1024)
-
-
-def forward(step, *operands):
-    shapes = (FIELD, EDGE, EDGE) if step == 0 else (
-        jax.ShapeDtypeStruct((CELLS, HID), bf16),
-        jax.ShapeDtypeStruct((CELLS, CH), bf16),
-    )
-    return pl.pallas_call(
-        functools.partial(forward_kernel, step),
-        out_shape=shapes,
+SHIFT_SCRATCH = [pltpu.VMEM((7, LAT + 6, WID, CH), f32), pltpu.VMEM((UNROLL, WID + 8, CH), f32)]
+
+
+def forward(*operands):
+    return pl.pallas_call(
+        forward_kernel,
+        out_shape=(
+            pltpu.HBM((LAT, WID, CH), bf16), FAR_EDGE, FAR_EDGE,
+            pltpu.HBM((CELLS, HID), bf16),
+            pltpu.HBM((CELLS, CH), bf16),
+        ),
+        out_specs=(VM,) * 5,
         scratch_shapes=SHIFT_SCRATCH + [pltpu.VMEM((BLK, WID, CH), f32)],
-        compiler_params=BIG,
-        cost_estimate=pl.CostEstimate(flops=6 * CELLS * CH * HID, bytes_accessed=8000000, transcendentals=CELLS * HID),
+        compiler_params=limit(18),
+        cost_estimate=pl.CostEstimate(flops=12 * CELLS * CH * HID, bytes_accessed=16000000, transcendentals=2 * CELLS * HID),
     )(*operands)
 
 
-def spread_kernel(hidden_ref, left_ref, right_ref, base_ref, kernel_ref, out_ref, shifts, padded):
+def spread_kernel(hidden_ref, right_ref, left_ref, base_ref, kernel_ref, out_ref, shifts, padded):
     build_shifts(
         shifts, padded,
         lambda row: hidden_ref[row],
@@ -286,20 +298,23 @@
     lax.fori_loop(0, LAT // BLK, block, 0)
 
 
-def spread_back(hidden, left, right, base, kernel):
+def spread_back(hidden, right, left, base, kernel):
     return pl.pallas_call(
         spread_kernel,
         out_shape=jax.ShapeDtypeStruct((LAT, WID, CH), f32),
         scratch_shapes=SHIFT_SCRATCH,
-        compiler_params=BIG,
+        compiler_params=limit(16),
         cost_estimate=pl.CostEstimate(flops=98 * CELLS * CH, bytes_accessed=3000000, transcendentals=0),
-    )(hidden, left, right, base, kernel)
+    )(hidden, right, left, base, kernel)
 
 
 def second_kernel(
     partial_ref, rows_ref, got_ref, slope_ref, unit_ref, gain_ref, up_ref, down_ref,
-    hidden_out, head_out, tail_out, adjoint_out,
+    hidden_out, tail_out, head_out, adjoint_out, slope_buf, unit_buf, down_buf, sems,
 ):
+    parts = [slice(group * ROWS, (group + 1) * ROWS) for group in range(LAT // BLK)]
+    pairs = [(down_ref, down_buf), (unit_ref, unit_buf)]
+    copies = fetch(pairs + [(slope_ref.at[rows], slope_buf.at[rows]) for rows in parts], sems)
     gain = gain_ref[...]
     for group in range(LAT // BLK):
         first = group * BLK
@@ -307,22 +322,35 @@
         forcing = forcing_of(0, rows_ref, got_ref, group)
         adjoint = (partial_ref[first : first + BLK].reshape(ROWS, CH) + forcing).astype(bf16)
         adjoint_out[first : first + BLK] = adjoint.reshape(BLK, WID, CH)
+        if group == 0:
+            copies[0].wait()
+            copies[1].wait()
+        copies[2 + group].wait()
         result = backward(
             adjoint,
-            lambda cols: slope_ref[rows, cols].astype(f32),
-            down_ref, up_ref, gain,
-            unit_ref[rows, :].astype(f32),
+            lambda cols: slope_buf[rows, cols].astype(f32),
+            down_buf, up_ref, gain,
+            unit_buf[rows, :].astype(f32),
         )
-        put_hidden(result, first, hidden_out, head_out, tail_out)
+        put_hidden(result, first, hidden_out, tail_out, head_out)
+
+
+def far(array):
+    return pltpu.with_memory_space_constraint(array, pltpu.HBM)
 
 
 def second_step(partial, rows, got, slope, unit, gain, up, down):
     return pl.pallas_call(
         second_kernel,
         out_shape=(FIELD, EDGE, EDGE, FIELD),
-        compiler_params=pltpu.CompilerParams(vmem_limit_bytes=12 * 1024 * 1024),
+        in_specs=[VM, VM, VM, HBM, HBM, VM, VM, HBM],
+        scratch_shapes=[
+            pltpu.VMEM((CELLS, HID), bf16), pltpu.VMEM((CELLS, CH), bf16), pltpu.VMEM((CH, HID), bf16),
+            pltpu.SemaphoreType.DMA((6,)),
+        ],
+        compiler_params=limit(12),
         cost_estimate=pl.CostEstimate(flops=4 * CELLS * CH * HID, bytes_accessed=5000000, transcendentals=0),
-    )(partial, rows, got, slope, unit, gain, up, down)
+    )(partial, rows, got, far(slope), far(unit), gain, up, far(down))
 
 
 def interior_kernel(hidden_ref, adjoint_ref, rows_ref, got_ref, kernel_ref, out_ref, west_ref, east_ref, shifts, padded, total):
@@ -355,23 +383,25 @@
         interior_kernel,
         out_shape=(FIELD, STRIP, STRIP),
         scratch_shapes=SHIFT_SCRATCH + [pltpu.VMEM((LAT, WID, CH), f32)],
-        compiler_params=BIG,
+        compiler_params=limit(16),
         cost_estimate=pl.CostEstimate(flops=98 * CELLS * CH, bytes_accessed=3000000, transcendentals=0),
     )(hidden, adjoint, rows, got, kernel)
 
 
-def edge_kernel(inner_ref, west_ref, east_ref, left_ref, right_ref, kernel_ref, out_ref, shifts, padded):
+def edge_kernel(inner_ref, west_ref, east_ref, right_ref, left_ref, kernel_ref, out_ref, shifts, padded):
     def side(halo_ref, strip_ref, place, offset, cols):
         clear_rims(shifts, 3, 8)
         padded[...] = jnp.zeros(padded.shape, f32)
 
-        def one_row(row, carry):
-            padded[place : place + 3] = halo_ref[row].astype(f32)
-            for col in range(3):
-                shifts[col, row + 3] = padded[col + offset : col + offset + 8]
+        def some_rows(index, carry):
+            for lane in range(BLK):
+                padded[lane, place : place + 3] = halo_ref[index * BLK + lane].astype(f32)
+            for lane in range(BLK):
+                for col in range(3):
+                    shifts[col, index * BLK + lane + 3] = padded[lane, col + offset : col + offset + 8]
             return carry
 
-        lax.fori_loop(0, LAT, one_row, 0)
+        lax.fori_loop(0, LAT // BLK, some_rows, 0)
 
         def block(index, carry):
             first = index * BLK
@@ -398,20 +428,23 @@
     return pl.pallas_call(
         edge_kernel,
         grid=(2,),
-        in_specs=[pl.BlockSpec(memory_space=pl.ANY)] + [whole(x) for x in (west, east, left, right, kernel)],
+        in_specs=[pl.BlockSpec(memory_space=pl.ANY)] + [whole(x) for x in (west, east, right, left, kernel)],
         out_specs=pl.BlockSpec((LAT, 8, CH), lambda i: (0, 3 * i, 0)),
         out_shape=FIELD,
         input_output_aliases={0: 0},
-        scratch_shapes=[pltpu.VMEM((3, LAT + 6, 8, CH), f32), pltpu.VMEM((16, CH), f32)],
+        compiler_params=limit(4),
+        scratch_shapes=[pltpu.VMEM((3, LAT + 6, 8, CH), f32), pltpu.VMEM((BLK, 16, CH), f32)],
         cost_estimate=pl.CostEstimate(flops=5000000, bytes_accessed=700000, transcendentals=0),
-    )(inner, west, east, left, right, kernel)
+    )(inner, west, east, right, left, kernel)
 
 
 def swap_edges(head, tail):
     peers = lax.axis_size("tile")
     up = [(i, (i + 1) % peers) for i in range(peers)]
     down = [(j, i) for i, j in up]
-    return lax.ppermute(tail, "tile", up), lax.ppermute(head, "tile", down)
+    right = lax.ppermute(head, "tile", down)
+    left = lax.ppermute(tail, "tile", up)
+    return left, right
 
 
 def after(array, other):
@@ -434,24 +467,21 @@
         obs_cell[:, 0].transpose(0, 2, 1), obs_count, obs_value, obs_error[:, 0].transpose(0, 2, 1)
     )
     got = exchange(packed, "tile")
-    head, tail = cut_edges(after(states, packed))
-    left, right = swap_edges(head, tail)
-
-    rows = gather_rows(after(got, head), states)
-    owned = exchange(rows, "member")
-
-    hidden, head, tail = forward(
-        0, states, left, after(right, rows), kernel, gain, up_weight, bias, down, adjoint_final
+    left, right = swap_edges(states[:, 0, :, 0:3], states[:, 0, :, WID - 3 : WID])
+
+    rows = gather_rows(got, states)
+    owned = exchange(after(rows, (right, left)), "member")
+
+    hidden, tail, head, slope, unit = forward(
+        states, after(right, rows), left, kernel, gain, up_weight, bias, down, adjoint_final
     )
     before, behind = swap_edges(head, tail)
 
-    deps = departures(after(owned, hidden), got)
+    deps = departures(after(owned, slope), got)
     back = exchange(deps, "member")
-
-    slope, unit = forward(1, states, left, after(right, deps), kernel, gain, up_weight, bias)
-    partial = spread_back(hidden, before, after(behind, slope), adjoint_final, kernel)
-
-    hidden, head, tail, adjoint = second_step(
+    partial = spread_back(hidden, after(behind, deps), before, adjoint_final, kernel)
+
+    hidden, tail, head, adjoint = second_step(
         partial, after(back, partial), got, slope, unit, gain, up_weight, down
     )
     left, right = swap_edges(head, tail)

time: 126 us -> 117 us (0.929)
  the two profiles are of different devices: /device:TPU:32 before, /device:TPU:1 now
where the time goes in v4:
time: 117 us; the launch traced here: 116 us
  starting transfers between devices  50.7 us (43%)
  Pallas kernels  38.7 us (33%)
  blocking collectives  15.1 us (13%)
  waiting for transfers between devices  7.35 us (6%)
  local copies, waits for them, and re-layouts  4.4 us (4%)
    all_to_all x2, starting transfers between devices, exchange(): return lax.all_to_all(array, axis, split_axis=0, concat_axis=0, tiled=True)  22.9 us
    ppermute x3, starting transfers between devices, swap_edges(): right = lax.ppermute(head, 'tile', down)  18 us
    pallas_call x1, Pallas kernels, forward(): pl.pallas_call(forward_kernel, out_shape=(pltpu.HBM((LAT, WID, CH), bf16)...  17.3 us
    all_to_all x1, blocking collectives, exchange(): return lax.all_to_all(array, axis, split_axis=0, concat_axis=0, tiled=True)  15.1 us
    ppermute x3, starting transfers between devices, swap_edges(): left = lax.ppermute(tail, 'tile', up)  9.72 us
    pallas_call x1, Pallas kernels, interior(): pl.pallas_call(interior_kernel, out_shape=(FIELD, STRIP, STRIP), scratch_...  6.73 us
    all_to_all x2, waiting for transfers between devices, exchange(): return lax.all_to_all(array, axis, split_axis=0, concat_axis=0, tiled=True)  6.04 us
    pallas_call x1, Pallas kernels, spread_back(): pl.pallas_call(spread_kernel, out_shape=jax.ShapeDtypeStruct((LAT, WID, C...  4.67 us
  transfers between devices with their start and end apart: 8, of which 2 were waited for; matrix products, arithmetic and copies ran while one was open for 0% of the time, Pallas kernels for 27%

profile of v4, /device:TPU:1, one launch (start us, length us, event | category | flops | bytes accessed | tf_op | source)
XLA Modules:
  0.0 116.4 jit_solution(17009087091011203090)
XLA Ops:
  0.0 0.0 copy-start
  0.0 1.2 %slice_bitcast_fusion = (bf16[2,32,3,192]{3,2,1,0:T(4,128)(2,1)S(1)}, bf16[2,32,3,192]{3,2,1,0:T(4,128)(2,1)S(1)}) fusion(bf16[2,1,32,32,192]{4,3,2,0,1:T(8,128)(2,1)} %bitcast.14), kind=kLoop, calls=%fused_computation | loop fusion | bytes 294912 | tf_op jit(solution)/shard_map/squeeze | solution.py:470
  1.2 4.6 %collective-permute-start.1 = (bf16[2,32,3,192]{3,2,1,0:T(4,128)(2,1)S(1)}, bf16[2,32,3,192]{3,2,1,0:T(4,128)(2,1)S(1)}, u32[]{:S(2)}, u32[]{:S(2)}) collective-permute-start(bf16[2,32,3,192]{3,2,1,0:T(4,128)(2,1)S(1)} %get-tuple-element.39), channel_id=1, source_target_pairs={{0,1},{1,2},{2,3},{3,4},{4,5},{5,6},{6,7},{7,8},{8,9},{9,10},{10,1... | collective-permute-start | bytes 221192 | tf_op jit(solution)/shard_map/ppermute | solution.py:446
  5.8 6.1 %collective-permute-start = (bf16[2,32,3,192]{3,2,1,0:T(4,128)(2,1)S(1)}, bf16[2,32,3,192]{3,2,1,0:T(4,128)(2,1)S(1)}, u32[]{:S(2)}, u32[]{:S(2)}) collective-permute-start(bf16[2,32,3,192]{3,2,1,0:T(4,128)(2,1)S(1)} %get-tuple-element.40), channel_id=1, source_target_pairs={{1,0},{2,1},{3,2},{4,3},{5,4},{6,5},{7,6},{8,7},{9,8},{10,9},{11,1... | collective-permute-start | bytes 221192 | tf_op jit(solution)/shard_map/ppermute | solution.py:445
  12.0 0.0 copy-start.1
  12.0 1.0 copy-done.1
  13.0 0.0 copy-start.7
  13.0 0.7 copy-done.7
  13.7 0.0 copy-start.8
  13.7 0.7 copy-done.8
  14.4 0.0 copy-start.9
  14.4 0.7 copy-done.9
  15.1 0.0 copy-start.11
  15.1 0.0 copy-start.2
  15.1 0.0 copy-start.4
  15.1 0.0 copy-start.5
  15.1 0.0 copy-start.6
  15.1 0.0 copy-start.10
  15.1 0.4 shard_map.109
  15.5 15.1 %all_to_all.15.got_ref = f32[32,4,128]{2,1,0:T(4,128)S(1)} all-to-all(f32[32,4,128]{2,1,0:T(4,128)S(1)} %shard_map.109), channel_id=1, replica_groups=mesh['member'=16,'tile'=32] {'tile'}, dimensions={0} | all-to-all | bytes 131072 | tf_op jit(solution)/shard_map/all_to_all | solution.py:455
  30.7 0.0 copy-done
  30.7 2.4 %shard_map.110 = bf16[16,32,384]{2,1,0:T(8,128)(2,1)} custom-call(f32[32,4,128]{2,1,0:T(4,128)S(1)} %all_to_all.15.got_ref, bf16[2,1,32,32,192]{4,3,2,1,0:T(8,128)(2,1)S(1)} %copy-done), custom_call_target="tpu_custom_call" | custom-call | flops 1000000 | bytes 2000000 | tf_op jit(solution)/shard_map/pallas_call | solution.py:154
  33.1 0.0 collective-permute-done.1.left_ref
  33.1 0.0 collective-permute-done.right_ref
  33.1 10.4 %all-to-all-start.1 = ((bf16[16,32,384]{2,1,0:T(8,128)(2,1)}), bf16[16,32,384]{2,1,0:T(8,128)(2,1)S(1)}, u32[]{:S(2)}, u32[]{:S(2)}) async-start(bf16[16,32,384]{2,1,0:T(8,128)(2,1)} %shard_map.110), calls=%async_computation.1 | async-start | bytes 786432 | tf_op jit(solution)/shard_map/all_to_all | solution.py:455
  43.5 0.0 copy-done.11
  43.5 0.0 copy-done.2
  43.5 0.0 copy-done.4
  43.5 0.0 copy-done.5
  43.6 0.0 copy-done.6
  43.6 0.0 copy-done.10
  43.6 17.3 %shard_map.111 = (bf16[32,32,192]{2,1,0:T(8,128)(2,1)}, bf16[32,3,192]{2,1,0:T(4,128)(2,1)}, bf16[32,3,192]{2,1,0:T(4,128)(2,1)}, bf16[1024,768]{1,0:T(8,128)(2,1)}, bf16[1024,192]{1,0:T(8,128)(2,1)}) custom-call(bf16[2,1,32,32,192]{4,3,2,1,0:T(8,128)(2,1)S(1)} %copy-done, bf16[2,32,3,192]{3,2,1,0:T(4,128)(2,1)S(1)} %collective-permute-done.right_ref, ...), custom_call_target="tpu_custom_call" | custom-call | flops 1811939328 | bytes 16000000 | tf_op jit(solution)/shard_map/pallas_call | solution.py:266
  60.9 0.0 copy-start.13
  60.9 0.0 copy-start.12
  60.9 0.0 copy-start.3
  60.9 0.0 all-to-all-done.1.rows_ref
  60.9 1.2 %shard_map.112 = bf16[16,32,384]{2,1,0:T(8,128)(2,1)} custom-call(bf16[16,32,384]{2,1,0:T(8,128)(2,1)S(1)} %all-to-all-done.1.rows_ref, f32[32,4,128]{2,1,0:T(4,128)S(1)} %all_to_all.15.got_ref), custom_call_target="tpu_custom_call" | custom-call | flops 1200000 | bytes 1200000 | tf_op jit(solution)/shard_map/pallas_call | solution.py:178
  62.1 12.5 %all-to-all-start.2 = ((bf16[16,32,384]{2,1,0:T(8,128)(2,1)}), bf16[16,32,384]{2,1,0:T(8,128)(2,1)S(1)}, u32[]{:S(2)}, u32[]{:S(2)}) async-start(bf16[16,32,384]{2,1,0:T(8,128)(2,1)} %shard_map.112), calls=%async_computation.2 | async-start | bytes 786432 | tf_op jit(solution)/shard_map/all_to_all | solution.py:455
  74.6 0.0 copy-done.13
  74.6 2.7 %collective-permute-start.2 = (bf16[32,3,192]{2,1,0:T(4,128)(2,1)S(1)}, bf16[32,3,192]{2,1,0:T(4,128)(2,1)S(1)}, u32[]{:S(2)}, u32[]{:S(2)}) collective-permute-start(bf16[32,3,192]{2,1,0:T(4,128)(2,1)S(1)} %copy-done.13), channel_id=1, source_target_pairs={{1,0},{2,1},{3,2},{4,3},{5,4},{6,5},{7,6},{8,7},{9,8},{10,9},{11,1... | collective-permute-start | bytes 110600 | tf_op jit(solution)/shard_map/ppermute | solution.py:445
  77.3 0.0 copy-done.12
  77.4 2.9 %collective-permute-start.3 = (bf16[32,3,192]{2,1,0:T(4,128)(2,1)S(1)}, bf16[32,3,192]{2,1,0:T(4,128)(2,1)S(1)}, u32[]{:S(2)}, u32[]{:S(2)}) collective-permute-start(bf16[32,3,192]{2,1,0:T(4,128)(2,1)S(1)} %copy-done.12), channel_id=1, source_target_pairs={{0,1},{1,2},{2,3},{3,4},{4,5},{5,6},{6,7},{7,8},{8,9},{9,10},{10,1... | collective-permute-start | bytes 110600 | tf_op jit(solution)/shard_map/ppermute | solution.py:446
  80.2 0.0 collective-permute-done.2.right_ref
  80.2 1.3 %collective-permute-done.3.left_ref = bf16[32,3,192]{2,1,0:T(4,128)(2,1)S(1)} collective-permute-done((bf16[32,3,192]{2,1,0:T(4,128)(2,1)S(1)}, bf16[32,3,192]{2,1,0:T(4,128)(2,1)S(1)}, u32[]{:S(2)}, u32[]{:S(2)}) %collective-permute-start.3) | collective-permute-done | bytes 36896 | tf_op jit(solution)/shard_map/ppermute | solution.py:446
  81.5 0.0 copy-done.3
  81.5 4.7 %shard_map.113.partial_ref = f32[32,32,192]{2,1,0:T(8,128)S(1)} custom-call(bf16[32,32,192]{2,1,0:T(8,128)(2,1)S(1)} %copy-done.3, bf16[32,3,192]{2,1,0:T(4,128)(2,1)S(1)} %collective-permute-done.2.right_ref, bf16[32,3,192]{2,1,0:T(4,128)(2,1)S(1)} %collective-permute-done.3.left_ref, bf16[1,32,32,192]{3,2,1,0:T(8,128)(2,1)S(1)} %copy-done.2, ...), custom_call_target="tpu_custom_call" | custom-call | flops 19267584 | bytes 3000000 | tf_op jit(solution)/shard_map/pallas_call | solution.py:302
  86.2 6.0 %all-to-all-done.2.rows_ref = bf16[16,32,384]{2,1,0:T(8,128)(2,1)S(1)} async-done(((bf16[16,32,384]{2,1,0:T(8,128)(2,1)}), bf16[16,32,384]{2,1,0:T(8,128)(2,1)S(1)}, u32[]{:S(2)}, u32[]{:S(2)}) %all-to-all-start.2) | async-done | bytes 393248 | tf_op jit(solution)/shard_map/all_to_all | solution.py:455
  92.3 4.1 %shard_map.114 = (bf16[32,32,192]{2,1,0:T(8,128)(2,1)S(1)}, bf16[32,3,192]{2,1,0:T(4,128)(2,1)S(1)}, bf16[32,3,192]{2,1,0:T(4,128)(2,1)S(1)}, bf16[32,32,192]{2,1,0:T(8,128)(2,1)S(1)}) custom-call(f32[32,32,192]{2,1,0:T(8,128)S(1)} %shard_map.113.partial_ref, bf16[16,32,384]{2,1,0:T(8,128)(2,1)S(1)} %all-to-all-done.2.rows_ref, ...), custom_call_target="tpu_custom_call" | custom-call | flops 603979776 | bytes 5000000 | tf_op jit(solution)/shard_map/pallas_call | solution.py:343
  96.4 9.2 %collective-permute-start.4 = (bf16[32,3,192]{2,1,0:T(4,128)(2,1)S(1)}, bf16[32,3,192]{2,1,0:T(4,128)(2,1)S(1)}, u32[]{:S(2)}, u32[]{:S(2)}) collective-permute-start(bf16[32,3,192]{2,1,0:T(4,128)(2,1)S(1)} %get-tuple-element.37), channel_id=1, source_target_pairs={{1,0},{2,1},{3,2},{4,3},{5,4},{6,5},{7,6},{8,7},{9,8},{10,9},{11,1... | collective-permute-start | bytes 110600 | tf_op jit(solution)/shard_map/ppermute | solution.py:445
  105.6 2.3 %collective-permute-start.5 = (bf16[32,3,192]{2,1,0:T(4,128)(2,1)S(1)}, bf16[32,3,192]{2,1,0:T(4,128)(2,1)S(1)}, u32[]{:S(2)}, u32[]{:S(2)}) collective-permute-start(bf16[32,3,192]{2,1,0:T(4,128)(2,1)S(1)} %get-tuple-element.38), channel_id=1, source_target_pairs={{0,1},{1,2},{2,3},{3,4},{4,5},{5,6},{6,7},{7,8},{8,9},{9,10},{10,1... | collective-permute-start | bytes 110600 | tf_op jit(solution)/shard_map/ppermute | solution.py:446
  107.8 6.7 %shard_map.115 = (bf16[32,32,192]{2,1,0:T(8,128)(2,1)}, f32[32,8,192]{2,1,0:T(8,128)S(1)}, f32[32,8,192]{2,1,0:T(8,128)S(1)}) custom-call(bf16[32,32,192]{2,1,0:T(8,128)(2,1)S(1)} %get-tuple-element.32.hidden_ref, bf16[32,32,192]{2,1,0:T(8,128)(2,1)S(1)} %get-tuple-element.33.adjoint_ref, bf16[16,32,384]{2,1,0:T(8,128)(2,1)S(1)} %all-to-all-done.2.rows_ref, ...), custom_call_target="tpu_custom_call" | custom-call | flops 19267584 | bytes 3000000 | tf_op jit(solution)/shard_map/pallas_call | solution.py:382
  114.6 0.0 collective-permute-done.4.right_ref
  114.6 0.0 collective-permute-done.5.left_ref
  114.6 1.8 %shard_map.116 = bf16[32,32,192]{2,1,0:T(8,128)(2,1)} custom-call(bf16[32,32,192]{2,1,0:T(8,128)(2,1)} %get-tuple-element.34.inner_ref, f32[32,8,192]{2,1,0:T(8,128)S(1)} %get-tuple-element.35.west_ref, f32[32,8,192]{2,1,0:T(8,128)S(1)} %get-tuple-element.36.east_ref, ...), custom_call_target="tpu_custom_call", output_to_operand_aliasing={{}: (0, {})} | custom-call | flops 5000000 | bytes 700000 | tf_op jit(solution)/shard_map/pallas_call | solution.py:428
  (1 shorter events, 0.0 us)
Async XLA Ops:
  0.0 30.7 %copy-start = (bf16[2,1,32,32,192]{4,3,2,1,0:T(8,128)(2,1)S(1)}, bf16[2,1,32,32,192]{4,3,2,1,0:T(8,128)(2,1)}, u32[]{:S(2)}) copy-start(bf16[2,1,32,32,192]{4,3,2,1,0:T(8,128)(2,1)} %state_ref.3) | copy-start | bytes 2359300
  1.2 31.9 %collective-permute-start.1 = (bf16[2,32,3,192]{3,2,1,0:T(4,128)(2,1)S(1)}, bf16[2,32,3,192]{3,2,1,0:T(4,128)(2,1)S(1)}, u32[]{:S(2)}, u32[]{:S(2)}) collective-permute-start(bf16[2,32,3,192]{3,2,1,0:T(4,128)(2,1)S(1)} %get-tuple-element.39), channel_id=1, source_target_pairs={{0,1},{1,2},{2,3},{3,4},{4,5},{5,6},{6,7},{7,8},{8,9},{9,10},{10,1... | collective-permute-start | bytes 221192 | tf_op jit(solution)/shard_map/ppermute | solution.py:446
  5.8 27.3 %collective-permute-start = (bf16[2,32,3,192]{3,2,1,0:T(4,128)(2,1)S(1)}, bf16[2,32,3,192]{3,2,1,0:T(4,128)(2,1)S(1)}, u32[]{:S(2)}, u32[]{:S(2)}) collective-permute-start(bf16[2,32,3,192]{3,2,1,0:T(4,128)(2,1)S(1)} %get-tuple-element.40), channel_id=1, source_target_pairs={{1,0},{2,1},{3,2},{4,3},{5,4},{6,5},{7,6},{8,7},{9,8},{10,9},{11,1... | collective-permute-start | bytes 221192 | tf_op jit(solution)/shard_map/ppermute | solution.py:445
  12.0 1.0 copy-start.1
  13.0 0.7 copy-start.7
  13.7 0.7 copy-start.8
  14.4 0.7 copy-start.9
  15.1 28.4 %copy-start.11 = (f32[768]{0:T(1024)S(1)}, f32[768]{0:T(1024)}, u32[]{:S(2)}) copy-start(f32[768]{0:T(1024)} %param.16) | copy-start | bytes 9220
  15.1 28.4 %copy-start.2 = (bf16[1,32,32,192]{3,2,1,0:T(8,128)(2,1)S(1)}, bf16[1,32,32,192]{3,2,1,0:T(8,128)(2,1)}, u32[]{:S(2)}) copy-start(bf16[1,32,32,192]{3,2,1,0:T(8,128)(2,1)} %base_ref.1) | copy-start | bytes 1179652
  15.1 28.4 %copy-start.4 = (f32[7,7,192]{2,1,0:T(8,128)S(1)}, f32[7,7,192]{2,1,0:T(8,128)}, u32[]{:S(2)}) copy-start(f32[7,7,192]{2,1,0:T(8,128)} %kernel_ref.7) | copy-start | bytes 112900
  15.1 28.4 %copy-start.5 = (bf16[192,768]{1,0:T(8,128)(2,1)S(1)}, bf16[192,768]{1,0:T(8,128)(2,1)}, u32[]{:S(2)}) copy-start(bf16[192,768]{1,0:T(8,128)(2,1)} %up_ref.3) | copy-start | bytes 884740
  15.1 28.5 %copy-start.6 = (bf16[768,192]{0,1:T(8,128)(2,1)S(1)}, bf16[768,192]{0,1:T(8,128)(2,1)}, u32[]{:S(2)}) copy-start(bf16[768,192]{0,1:T(8,128)(2,1)} %param.17) | copy-start | bytes 884740
  15.1 28.4 %copy-start.10 = (f32[192]{0:T(256)S(1)}, f32[192]{0:T(256)}, u32[]{:S(2)}) copy-start(f32[192]{0:T(256)} %param.14) | copy-start | bytes 2308
  33.1 27.8 %all-to-all-start.1 = ((bf16[16,32,384]{2,1,0:T(8,128)(2,1)}), bf16[16,32,384]{2,1,0:T(8,128)(2,1)S(1)}, u32[]{:S(2)}, u32[]{:S(2)}) async-start(bf16[16,32,384]{2,1,0:T(8,128)(2,1)} %shard_map.110), calls=%async_computation.1 | async-start | bytes 786432 | tf_op jit(solution)/shard_map/all_to_all | solution.py:455
  60.9 13.7 %copy-start.13 = (bf16[32,3,192]{2,1,0:T(4,128)(2,1)S(1)}, bf16[32,3,192]{2,1,0:T(4,128)(2,1)}, u32[]{:S(2)}) copy-start(bf16[32,3,192]{2,1,0:T(4,128)(2,1)} %get-tuple-element.24) | copy-start | bytes 110596
  60.9 16.4 %copy-start.12 = (bf16[32,3,192]{2,1,0:T(4,128)(2,1)S(1)}, bf16[32,3,192]{2,1,0:T(4,128)(2,1)}, u32[]{:S(2)}) copy-start(bf16[32,3,192]{2,1,0:T(4,128)(2,1)} %get-tuple-element.29) | copy-start | bytes 110596
  60.9 20.6 %copy-start.3 = (bf16[32,32,192]{2,1,0:T(8,128)(2,1)S(1)}, bf16[32,32,192]{2,1,0:T(8,128)(2,1)}, u32[]{:S(2)}) copy-start(bf16[32,32,192]{2,1,0:T(8,128)(2,1)} %get-tuple-element.23.hidden_ref) | copy-start | bytes 1179652
  62.1 30.2 %all-to-all-start.2 = ((bf16[16,32,384]{2,1,0:T(8,128)(2,1)}), bf16[16,32,384]{2,1,0:T(8,128)(2,1)S(1)}, u32[]{:S(2)}, u32[]{:S(2)}) async-start(bf16[16,32,384]{2,1,0:T(8,128)(2,1)} %shard_map.112), calls=%async_computation.2 | async-start | bytes 786432 | tf_op jit(solution)/shard_map/all_to_all | solution.py:455
  74.6 5.6 %collective-permute-start.2 = (bf16[32,3,192]{2,1,0:T(4,128)(2,1)S(1)}, bf16[32,3,192]{2,1,0:T(4,128)(2,1)S(1)}, u32[]{:S(2)}, u32[]{:S(2)}) collective-permute-start(bf16[32,3,192]{2,1,0:T(4,128)(2,1)S(1)} %copy-done.13), channel_id=1, source_target_pairs={{1,0},{2,1},{3,2},{4,3},{5,4},{6,5},{7,6},{8,7},{9,8},{10,9},{11,1... | collective-permute-start | bytes 110600 | tf_op jit(solution)/shard_map/ppermute | solution.py:445
  77.4 4.2 %collective-permute-start.3 = (bf16[32,3,192]{2,1,0:T(4,128)(2,1)S(1)}, bf16[32,3,192]{2,1,0:T(4,128)(2,1)S(1)}, u32[]{:S(2)}, u32[]{:S(2)}) collective-permute-start(bf16[32,3,192]{2,1,0:T(4,128)(2,1)S(1)} %copy-done.12), channel_id=1, source_target_pairs={{0,1},{1,2},{2,3},{3,4},{4,5},{5,6},{6,7},{7,8},{8,9},{9,10},{10,1... | collective-permute-start | bytes 110600 | tf_op jit(solution)/shard_map/ppermute | solution.py:446
  96.4 18.2 %collective-permute-start.4 = (bf16[32,3,192]{2,1,0:T(4,128)(2,1)S(1)}, bf16[32,3,192]{2,1,0:T(4,128)(2,1)S(1)}, u32[]{:S(2)}, u32[]{:S(2)}) collective-permute-start(bf16[32,3,192]{2,1,0:T(4,128)(2,1)S(1)} %get-tuple-element.37), channel_id=1, source_target_pairs={{1,0},{2,1},{3,2},{4,3},{5,4},{6,5},{7,6},{8,7},{9,8},{10,9},{11,1... | collective-permute-start | bytes 110600 | tf_op jit(solution)/shard_map/ppermute | solution.py:445
  105.6 9.0 %collective-permute-start.5 = (bf16[32,3,192]{2,1,0:T(4,128)(2,1)S(1)}, bf16[32,3,192]{2,1,0:T(4,128)(2,1)S(1)}, u32[]{:S(2)}, u32[]{:S(2)}) collective-permute-start(bf16[32,3,192]{2,1,0:T(4,128)(2,1)S(1)} %get-tuple-element.38), channel_id=1, source_target_pairs={{0,1},{1,2},{2,3},{3,4},{4,5},{5,6},{6,7},{7,8},{8,9},{9,10},{10,1... | collective-permute-start | bytes 110600 | tf_op jit(solution)/shard_map/ppermute | solution.py:446

commit v5 on v4

--- a/solution.py
+++ b/solution.py
@@ -52,6 +52,10 @@
     for copy in copies:
         copy.start()
     return copies
+
+
+def far(array):
+    return pltpu.with_memory_space_constraint(array, pltpu.HBM)
 
 
 def clear_rims(shifts, count, width):
@@ -102,7 +106,10 @@
             emit(target, low, high, sums[target])
 
 
-def pack_kernel(cell_ref, count_ref, value_ref, error_ref, out_ref):
+def pack_kernel(cell_far, count_far, value_far, error_far, out_ref, cell_ref, count_ref, value_ref, error_ref, sems):
+    pairs = [(cell_far, cell_ref), (count_far, count_ref), (value_far, value_ref), (error_far, error_ref)]
+    for copy in fetch(pairs, sems):
+        copy.wait()
     member = lax.axis_index("member")
     tiles = cell_ref.shape[2]
     slot = lax.broadcasted_iota(jnp.int32, (CAP, tiles), 0)
@@ -124,9 +131,13 @@
 def pack_observations(cells, counts, values, errors):
     return pl.pallas_call(
         pack_kernel,
-        out_shape=jax.ShapeDtypeStruct((cells.shape[2], 4, 128), f32),
+        out_shape=pltpu.HBM((cells.shape[2], 4, 128), f32),
+        in_specs=[HBM] * 4,
+        out_specs=VM,
+        scratch_shapes=[pltpu.VMEM(array.shape, array.dtype) for array in (cells, counts, values, errors)]
+        + [pltpu.SemaphoreType.DMA((4,))],
         compiler_params=limit(6),
-    )(cells, counts, values, errors)
+    )(far(cells), far(counts), far(values), far(errors))
 
 
 def one_hot(step, got_ref, group):
@@ -138,13 +149,21 @@
     return jnp.concatenate(rows, axis=0).astype(bf16)
 
 
-def gather_kernel(got_ref, state_ref, out_ref):
+def gather_kernel(got_ref, state_far, out_ref, state_ref, sems):
+    pairs = []
     for step in range(2):
+        for half in range(2):
+            rows = slice(half * LAT // 2, (half + 1) * LAT // 2)
+            pairs.append((state_far.at[step, 0, rows], state_ref.at[step, rows]))
+    copies = fetch(pairs, sems)
+    for step in range(2):
+        hots = [one_hot(step, got_ref, group) for group in range(LAT // BLK)]
         for pair in range(2):
+            copies[2 * step + pair].wait()
             found = []
             for group in (2 * pair, 2 * pair + 1):
-                field = state_ref[step, 0, group * BLK : (group + 1) * BLK].reshape(ROWS, CH)
-                rows = jnp.dot(one_hot(step, got_ref, group), field, preferred_element_type=f32)
+                field = state_ref[step, group * BLK : (group + 1) * BLK].reshape(ROWS, CH)
+                rows = jnp.dot(hots[group], field, preferred_element_type=f32)
                 found.append(rows.reshape(CAP, BLK, CH))
             both = jnp.concatenate(found, axis=1).astype(bf16)
             out_ref[:, 2 * BLK * pair : 2 * BLK * (pair + 1), step * CH : (step + 1) * CH] = both
@@ -154,9 +173,11 @@
     return pl.pallas_call(
         gather_kernel,
         out_shape=jax.ShapeDtypeStruct((CAP, LAT, 2 * CH), bf16),
+        in_specs=[VM, HBM],
+        scratch_shapes=[pltpu.VMEM((2, LAT, WID, CH), bf16), pltpu.SemaphoreType.DMA((4,))],
         compiler_params=limit(6),
         cost_estimate=pl.CostEstimate(flops=1000000, bytes_accessed=2000000, transcendentals=0),
-    )(got, states)
+    )(got, far(states))
 
 
 def departure_kernel(rows_ref, got_ref, out_ref):
@@ -213,47 +234,50 @@
     tail_ref[pl.ds(first, BLK)] = block[:, WID - 3 : WID]
 
 
-def forward_kernel(
-    state_ref, right_ref, left_ref, kernel_ref, gain_ref, up_ref, bias_ref, down_ref, adjoint_ref,
-    hidden_out, tail_out, head_out, slope_out, unit_out,
-    shifts, padded, hidden,
-):
+def forward_kernel(step, state_ref, left_ref, right_ref, kernel_ref, gain_ref, up_ref, bias_ref, *rest):
+    shifts, padded, hidden = rest[-3:]
+    if step == 0:
+        later_right, later_left = rest[5:7]
+        later_right[...] = right_ref[1]
+        later_left[...] = left_ref[1]
+        right_ref, left_ref = right_ref.at[0], left_ref.at[0]
     gain = gain_ref[...]
-    for step in range(2):
-        build_shifts(
-            shifts, padded,
-            lambda row: state_ref[step, 0, row],
-            lambda row: left_ref[step, row],
-            lambda row: right_ref[step, row],
-        )
-
-        def block(index, carry):
-            first = index * BLK
-
-            def emit(target, low, high, value):
-                hidden[target, :, low:high] = value
-
-            convolve(shifts, kernel_ref, first, False, emit)
-            unit, inv_std = normalise(hidden[...].reshape(ROWS, CH))
-            normed = (unit * gain).astype(bf16)
-
-            def slope_at(cols):
-                preact = jnp.dot(normed, up_ref[:, cols], preferred_element_type=f32)
-                return gelu_slope(preact + bias_ref[:, cols]) * inv_std
-
-            if step == 0:
-                adjoint = adjoint_ref[0, pl.ds(first, BLK)].reshape(ROWS, CH)
-                result = backward(adjoint, slope_at, down_ref, up_ref, gain, unit)
-                put_hidden(result, first, hidden_out, tail_out, head_out)
-            else:
-                rows = pl.ds(pl.multiple_of(index * ROWS, ROWS), ROWS)
-                for part in range(3):
-                    cols = slice(part * 256, (part + 1) * 256)
-                    slope_out[rows, cols] = slope_at(cols).astype(bf16)
-                unit_out[rows, :] = unit.astype(bf16)
-            return carry
-
-        lax.fori_loop(0, LAT // BLK, block, 0)
+    build_shifts(
+        shifts, padded,
+        lambda row: state_ref[step, 0, row],
+        lambda row: left_ref[row],
+        lambda row: right_ref[row],
+    )
+
+    def block(index, carry):
+        first = index * BLK
+
+        def emit(target, low, high, value):
+            hidden[target, :, low:high] = value
+
+        convolve(shifts, kernel_ref, first, False, emit)
+        unit, inv_std = normalise(hidden[...].reshape(ROWS, CH))
+        normed = (unit * gain).astype(bf16)
+
+        def slope_at(cols):
+            preact = jnp.dot(normed, up_ref[:, cols], preferred_element_type=f32)
+            return gelu_slope(preact + bias_ref[:, cols]) * inv_std
+
+        if step == 0:
+            down_ref, adjoint_ref, hidden_out, tail_out, head_out = rest[:5]
+            adjoint = adjoint_ref[0, pl.ds(first, BLK)].reshape(ROWS, CH)
+            result = backward(adjoint, slope_at, down_ref, up_ref, gain, unit)
+            put_hidden(result, first, hidden_out, tail_out, head_out)
+        else:
+            slope_out, unit_out = rest[:2]
+            rows = pl.ds(pl.multiple_of(index * ROWS, ROWS), ROWS)
+            for part in range(3):
+                cols = slice(part * 256, (part + 1) * 256)
+                slope_out[rows, cols] = slope_at(cols).astype(bf16)
+            unit_out[rows, :] = unit.astype(bf16)
+        return carry
+
+    lax.fori_loop(0, LAT // BLK, block, 0)
 
 
 FAR_EDGE = pltpu.HBM((LAT, 3, CH), bf16)
@@ -262,19 +286,18 @@
 SHIFT_SCRATCH = [pltpu.VMEM((7, LAT + 6, WID, CH), f32), pltpu.VMEM((UNROLL, WID + 8, CH), f32)]
 
 
-def forward(*operands):
-    return pl.pallas_call(
-        forward_kernel,
-        out_shape=(
-            pltpu.HBM((LAT, WID, CH), bf16), FAR_EDGE, FAR_EDGE,
-            pltpu.HBM((CELLS, HID), bf16),
-            pltpu.HBM((CELLS, CH), bf16),
-        ),
-        out_specs=(VM,) * 5,
+def forward(step, states, left, right, *others):
+    shapes = (pltpu.HBM((LAT, WID, CH), bf16),) + (FAR_EDGE,) * 4 if step == 0 else (
+        pltpu.HBM((CELLS, HID), bf16), pltpu.HBM((CELLS, CH), bf16)
+    )
+    return pl.pallas_call(
+        functools.partial(forward_kernel, step),
+        out_shape=shapes,
+        out_specs=(VM,) * len(shapes),
         scratch_shapes=SHIFT_SCRATCH + [pltpu.VMEM((BLK, WID, CH), f32)],
-        compiler_params=limit(18),
-        cost_estimate=pl.CostEstimate(flops=12 * CELLS * CH * HID, bytes_accessed=16000000, transcendentals=2 * CELLS * HID),
-    )(*operands)
+        compiler_params=limit(16),
+        cost_estimate=pl.CostEstimate(flops=6 * CELLS * CH * HID, bytes_accessed=8000000, transcendentals=CELLS * HID),
+    )(states, left, right, *others)
 
 
 def spread_kernel(hidden_ref, right_ref, left_ref, base_ref, kernel_ref, out_ref, shifts, padded):
@@ -335,10 +358,6 @@
         put_hidden(result, first, hidden_out, tail_out, head_out)
 
 
-def far(array):
-    return pltpu.with_memory_space_constraint(array, pltpu.HBM)
-
-
 def second_step(partial, rows, got, slope, unit, gain, up, down):
     return pl.pallas_call(
         second_kernel,
@@ -467,19 +486,20 @@
         obs_cell[:, 0].transpose(0, 2, 1), obs_count, obs_value, obs_error[:, 0].transpose(0, 2, 1)
     )
     got = exchange(packed, "tile")
-    left, right = swap_edges(states[:, 0, :, 0:3], states[:, 0, :, WID - 3 : WID])
-
     rows = gather_rows(got, states)
-    owned = exchange(after(rows, (right, left)), "member")
-
-    hidden, tail, head, slope, unit = forward(
-        states, after(right, rows), left, kernel, gain, up_weight, bias, down, adjoint_final
-    )
-    before, behind = swap_edges(head, tail)
-
-    deps = departures(after(owned, slope), got)
+    owned = exchange(rows, "member")
+
+    source = after(states, rows)[:, 0]
+    left, right = swap_edges(source[:, :, 0:3], source[:, :, WID - 3 : WID])
+    hidden, tail, head, later_right, later_left = forward(
+        0, states, left, right, kernel, gain, up_weight, bias, down, adjoint_final
+    )
+    deps = departures(after(owned, hidden), got)
     back = exchange(deps, "member")
-    partial = spread_back(hidden, after(behind, deps), before, adjoint_final, kernel)
+
+    before, behind = swap_edges(*after((head, tail), deps))
+    slope, unit = forward(1, after(states, deps), later_left, later_right, kernel, gain, up_weight, bias)
+    partial = spread_back(hidden, after(behind, slope), before, adjoint_final, kernel)
 
     hidden, tail, head, adjoint = second_step(
         partial, after(back, partial), got, slope, unit, gain, up_weight, down

time: 117 us -> 111 us (0.949)
  the two profiles are of different devices: /device:TPU:1 before, /device:TPU:63 now
where the time goes in v5:
time: 111 us
  starting transfers between devices  53 us (48%)
  Pallas kernels  42.2 us (38%)
  blocking collectives  11.8 us (11%)
  waiting for transfers between devices  3.21 us (3%)
    all_to_all x2, starting transfers between devices, exchange(): return lax.all_to_all(array, axis, split_axis=0, concat_axis=0, tiled=True)  24.9 us
    ppermute x3, starting transfers between devices, swap_edges(): left = lax.ppermute(tail, 'tile', up)  21.4 us
    pallas_call x2, Pallas kernels, forward(): pl.pallas_call(functools.partial(forward_kernel, step), out_shape=shapes,...  18.2 us
    all_to_all x1, blocking collectives, exchange(): return lax.all_to_all(array, axis, split_axis=0, concat_axis=0, tiled=True)  11.8 us
    pallas_call x1, Pallas kernels, interior(): pl.pallas_call(interior_kernel, out_shape=(FIELD, STRIP, STRIP), scratch_...  6.73 us
    ppermute x3, starting transfers between devices, swap_edges(): right = lax.ppermute(head, 'tile', down)  6.7 us
    pallas_call x1, Pallas kernels, spread_back(): pl.pallas_call(spread_kernel, out_shape=jax.ShapeDtypeStruct((LAT, WID, C...  4.67 us
    pallas_call x1, Pallas kernels, second_step(): pl.pallas_call(second_kernel, out_shape=(FIELD, EDGE, EDGE, FIELD), in_sp...  4.11 us
  transfers between devices with their start and end apart: 8, of which 3 were waited for; matrix products, arithmetic and copies ran while one was open for 0% of the time, Pallas kernels for 27%

profile of v5, /device:TPU:63, one launch (start us, length us, event | category | flops | bytes accessed | tf_op | source)
XLA Modules:
  0.0 110.6 jit_solution(9689555037299690405)
XLA Ops:
  0.0 0.0 copy-start
  0.0 2.2 %shard_map.109 = f32[32,4,128]{2,1,0:T(4,128)} custom-call(s32[2,16,32]{2,1,0:T(8,128)} %bitcast.16, s32[2,1,32]{2,1,0:T(1,128)} %count_far.1, bf16[2,1,32,16,192]{4,3,2,1,0:T(8,128)(2,1)} %value_far.1, bf16[2,16,32]{2,1,0:T(8,128)(2,1)} %bitcast.17), custom_call_target="tpu_custom_call" | custom-call | tf_op jit(solution)/shard_map/pallas_call | solution.py:132
  2.2 0.0 copy-start.9
  2.2 0.0 copy-start.1
  2.3 0.0 copy-start.3
  2.3 0.0 copy-start.4
  2.3 0.0 copy-start.5
  2.3 0.0 copy-start.6
  2.3 11.8 %all_to_all.15.got_ref = f32[32,4,128]{2,1,0:T(4,128)S(1)} all-to-all(f32[32,4,128]{2,1,0:T(4,128)} %shard_map.109), channel_id=1, replica_groups=mesh['member'=16,'tile'=32] {'tile'}, dimensions={0} | all-to-all | bytes 131072 | tf_op jit(solution)/shard_map/all_to_all | solution.py:474
  14.2 3.2 %shard_map.110 = bf16[16,32,384]{2,1,0:T(8,128)(2,1)} custom-call(f32[32,4,128]{2,1,0:T(4,128)S(1)} %all_to_all.15.got_ref, bf16[2,1,32,32,192]{4,3,2,1,0:T(8,128)(2,1)} %state_ref.2), custom_call_target="tpu_custom_call" | custom-call | flops 1000000 | bytes 2000000 | tf_op jit(solution)/shard_map/pallas_call | solution.py:173
  17.4 14.7 %all-to-all-start.1 = ((bf16[16,32,384]{2,1,0:T(8,128)(2,1)}), bf16[16,32,384]{2,1,0:T(8,128)(2,1)S(1)}, u32[]{:S(2)}, u32[]{:S(2)}) async-start(bf16[16,32,384]{2,1,0:T(8,128)(2,1)} %shard_map.110), calls=%async_computation.1 | async-start | bytes 786432 | tf_op jit(solution)/shard_map/all_to_all | solution.py:474
  32.0 0.0 copy-done
  32.0 0.1 fusion
  32.1 2.9 %collective-permute-start.1 = (bf16[2,32,3,192]{3,2,1,0:T(4,128)(2,1)S(1)}, bf16[2,32,3,192]{3,2,1,0:T(4,128)(2,1)S(1)}, u32[]{:S(2)}, u32[]{:S(2)}) collective-permute-start(bf16[2,32,3,192]{3,2,1,0:T(4,128)(2,1)S(1)} %get-tuple-element.47), channel_id=1, source_target_pairs={{1,0},{2,1},{3,2},{4,3},{5,4},{6,5},{7,6},{8,7},{9,8},{10,9},{11,1... | collective-permute-start | bytes 221192 | tf_op jit(solution)/shard_map/ppermute | solution.py:464
  35.0 6.0 %collective-permute-start = (bf16[2,32,3,192]{3,2,1,0:T(4,128)(2,1)S(1)}, bf16[2,32,3,192]{3,2,1,0:T(4,128)(2,1)S(1)}, u32[]{:S(2)}, u32[]{:S(2)}) collective-permute-start(bf16[2,32,3,192]{3,2,1,0:T(4,128)(2,1)S(1)} %get-tuple-element.48), channel_id=1, source_target_pairs={{0,1},{1,2},{2,3},{3,4},{4,5},{5,6},{6,7},{7,8},{8,9},{9,10},{10,1... | collective-permute-start | bytes 221192 | tf_op jit(solution)/shard_map/ppermute | solution.py:465
  41.0 0.0 copy-done.9
  41.1 1.0 collective-permute-done.1.right_ref
  42.0 0.9 collective-permute-done.left_ref
  43.0 0.0 copy-done.1
  43.0 0.0 copy-done.3
  43.0 0.0 copy-done.4
  43.0 0.0 copy-done.5
  43.0 0.0 copy-done.6
  43.0 9.3 %shard_map.111 = (bf16[32,32,192]{2,1,0:T(8,128)(2,1)}, bf16[32,3,192]{2,1,0:T(4,128)(2,1)}, bf16[32,3,192]{2,1,0:T(4,128)(2,1)}, bf16[32,3,192]{2,1,0:T(4,128)(2,1)}, bf16[32,3,192]{2,1,0:T(4,128)(2,1)}) custom-call(bf16[2,1,32,32,192]{4,3,2,1,0:T(8,128)(2,1)S(1)} %copy-done, bf16[2,32,3,192]{3,2,1,0:T(4,128)(2,1)S(1)} %collective-permute-done.left_ref, ...), custom_call_target="tpu_custom_call" | custom-call | flops 905969664 | bytes 8000000 | tf_op jit(solution)/shard_map/pallas_call | solution.py:293
  52.3 0.0 copy-start.11
  52.3 0.0 copy-start.10
  52.3 0.0 copy-start.7
  52.3 0.0 copy-start.8
  52.3 1.3 %all-to-all-done.1.rows_ref = bf16[16,32,384]{2,1,0:T(8,128)(2,1)S(1)} async-done(((bf16[16,32,384]{2,1,0:T(8,128)(2,1)}), bf16[16,32,384]{2,1,0:T(8,128)(2,1)S(1)}, u32[]{:S(2)}, u32[]{:S(2)}) %all-to-all-start.1) | async-done | bytes 393248 | tf_op jit(solution)/shard_map/all_to_all | solution.py:474
  53.6 1.2 %shard_map.112 = bf16[16,32,384]{2,1,0:T(8,128)(2,1)} custom-call(bf16[16,32,384]{2,1,0:T(8,128)(2,1)S(1)} %all-to-all-done.1.rows_ref, f32[32,4,128]{2,1,0:T(4,128)S(1)} %all_to_all.15.got_ref), custom_call_target="tpu_custom_call" | custom-call | flops 1200000 | bytes 1200000 | tf_op jit(solution)/shard_map/pallas_call | solution.py:199
  54.8 10.2 %all-to-all-start.2 = ((bf16[16,32,384]{2,1,0:T(8,128)(2,1)}), bf16[16,32,384]{2,1,0:T(8,128)(2,1)S(1)}, u32[]{:S(2)}, u32[]{:S(2)}) async-start(bf16[16,32,384]{2,1,0:T(8,128)(2,1)} %shard_map.112), calls=%async_computation.2 | async-start | bytes 786432 | tf_op jit(solution)/shard_map/all_to_all | solution.py:474
  65.0 0.0 copy-done.11
  65.0 1.9 %collective-permute-start.2 = (bf16[32,3,192]{2,1,0:T(4,128)(2,1)S(1)}, bf16[32,3,192]{2,1,0:T(4,128)(2,1)S(1)}, u32[]{:S(2)}, u32[]{:S(2)}) collective-permute-start(bf16[32,3,192]{2,1,0:T(4,128)(2,1)S(1)} %copy-done.11), channel_id=1, source_target_pairs={{1,0},{2,1},{3,2},{4,3},{5,4},{6,5},{7,6},{8,7},{9,8},{10,9},{11,1... | collective-permute-start | bytes 110600 | tf_op jit(solution)/shard_map/ppermute | solution.py:464
  66.9 0.0 copy-done.10
  66.9 8.2 %collective-permute-start.3 = (bf16[32,3,192]{2,1,0:T(4,128)(2,1)S(1)}, bf16[32,3,192]{2,1,0:T(4,128)(2,1)S(1)}, u32[]{:S(2)}, u32[]{:S(2)}) collective-permute-start(bf16[32,3,192]{2,1,0:T(4,128)(2,1)S(1)} %copy-done.10), channel_id=1, source_target_pairs={{0,1},{1,2},{2,3},{3,4},{4,5},{5,6},{6,7},{7,8},{8,9},{9,10},{10,1... | collective-permute-start | bytes 110600 | tf_op jit(solution)/shard_map/ppermute | solution.py:465
  75.2 0.0 copy-done.7
  75.2 0.0 copy-done.8
  75.2 0.0 copy-start.2
  75.2 8.9 %shard_map.113 = (bf16[1024,768]{1,0:T(8,128)(2,1)}, bf16[1024,192]{1,0:T(8,128)(2,1)}) custom-call(bf16[2,1,32,32,192]{4,3,2,1,0:T(8,128)(2,1)S(1)} %copy-done, bf16[32,3,192]{2,1,0:T(4,128)(2,1)S(1)} %copy-done.8, bf16[32,3,192]{2,1,0:T(4,128)(2,1)S(1)} %copy-done.7, f32[7,7,192]{2,1,0:T(8,128)S(1)} %copy-done.3, f32[1,192]{1,0:T(1,128)S(1)} %bitcast.14, ...), custom_call_target="tpu_custom_call" | custom-call | flops 905969664 | bytes 8000000 | tf_op jit(solution)/shard_map/pallas_call | solution.py:293
  84.1 0.0 collective-permute-done.2.right_ref
  84.1 0.0 collective-permute-done.3.left_ref
  84.1 0.0 copy-done.2
  84.1 4.7 %shard_map.114.partial_ref = f32[32,32,192]{2,1,0:T(8,128)S(1)} custom-call(bf16[32,32,192]{2,1,0:T(8,128)(2,1)S(1)} %copy-done.2, bf16[32,3,192]{2,1,0:T(4,128)(2,1)S(1)} %collective-permute-done.2.right_ref, bf16[32,3,192]{2,1,0:T(4,128)(2,1)S(1)} %collective-permute-done.3.left_ref, bf16[1,32,32,192]{3,2,1,0:T(8,128)(2,1)S(1)} %copy-done.1, ...), custom_call_target="tpu_custom_call" | custom-call | flops 19267584 | bytes 3000000 | tf_op jit(solution)/shard_map/pallas_call | solution.py:325
  88.8 0.0 all-to-all-done.2.rows_ref
  88.8 4.1 %shard_map.115 = (bf16[32,32,192]{2,1,0:T(8,128)(2,1)S(1)}, bf16[32,3,192]{2,1,0:T(4,128)(2,1)S(1)}, bf16[32,3,192]{2,1,0:T(4,128)(2,1)S(1)}, bf16[32,32,192]{2,1,0:T(8,128)(2,1)S(1)}) custom-call(f32[32,32,192]{2,1,0:T(8,128)S(1)} %shard_map.114.partial_ref, bf16[16,32,384]{2,1,0:T(8,128)(2,1)S(1)} %all-to-all-done.2.rows_ref, ...), custom_call_target="tpu_custom_call" | custom-call | flops 603979776 | bytes 5000000 | tf_op jit(solution)/shard_map/pallas_call | solution.py:362
  92.9 1.9 %collective-permute-start.4 = (bf16[32,3,192]{2,1,0:T(4,128)(2,1)S(1)}, bf16[32,3,192]{2,1,0:T(4,128)(2,1)S(1)}, u32[]{:S(2)}, u32[]{:S(2)}) collective-permute-start(bf16[32,3,192]{2,1,0:T(4,128)(2,1)S(1)} %get-tuple-element.45), channel_id=1, source_target_pairs={{1,0},{2,1},{3,2},{4,3},{5,4},{6,5},{7,6},{8,7},{9,8},{10,9},{11,1... | collective-permute-start | bytes 110600 | tf_op jit(solution)/shard_map/ppermute | solution.py:464
  94.8 7.1 %collective-permute-start.5 = (bf16[32,3,192]{2,1,0:T(4,128)(2,1)S(1)}, bf16[32,3,192]{2,1,0:T(4,128)(2,1)S(1)}, u32[]{:S(2)}, u32[]{:S(2)}) collective-permute-start(bf16[32,3,192]{2,1,0:T(4,128)(2,1)S(1)} %get-tuple-element.46), channel_id=1, source_target_pairs={{0,1},{1,2},{2,3},{3,4},{4,5},{5,6},{6,7},{7,8},{8,9},{9,10},{10,1... | collective-permute-start | bytes 110600 | tf_op jit(solution)/shard_map/ppermute | solution.py:465
  102.0 6.7 %shard_map.116 = (bf16[32,32,192]{2,1,0:T(8,128)(2,1)}, f32[32,8,192]{2,1,0:T(8,128)S(1)}, f32[32,8,192]{2,1,0:T(8,128)S(1)}) custom-call(bf16[32,32,192]{2,1,0:T(8,128)(2,1)S(1)} %get-tuple-element.40.hidden_ref, bf16[32,32,192]{2,1,0:T(8,128)(2,1)S(1)} %get-tuple-element.41.adjoint_ref, bf16[16,32,384]{2,1,0:T(8,128)(2,1)S(1)} %all-to-all-done.2.rows_ref, ...), custom_call_target="tpu_custom_call" | custom-call | flops 19267584 | bytes 3000000 | tf_op jit(solution)/shard_map/pallas_call | solution.py:401
  108.7 0.0 collective-permute-done.4.right_ref
  108.7 0.0 collective-permute-done.5.left_ref
  108.7 1.8 %shard_map.117 = bf16[32,32,192]{2,1,0:T(8,128)(2,1)} custom-call(bf16[32,32,192]{2,1,0:T(8,128)(2,1)} %get-tuple-element.42.inner_ref, f32[32,8,192]{2,1,0:T(8,128)S(1)} %get-tuple-element.43.west_ref, f32[32,8,192]{2,1,0:T(8,128)S(1)} %get-tuple-element.44.east_ref, ...), custom_call_target="tpu_custom_call", output_to_operand_aliasing={{}: (0, {})} | custom-call | flops 5000000 | bytes 700000 | tf_op jit(solution)/shard_map/pallas_call | solution.py:447
  (1 shorter events, 0.0 us)
Async XLA Ops:
  0.0 32.0 %copy-start = (bf16[2,1,32,32,192]{4,3,2,1,0:T(8,128)(2,1)S(1)}, bf16[2,1,32,32,192]{4,3,2,1,0:T(8,128)(2,1)}, u32[]{:S(2)}) copy-start(bf16[2,1,32,32,192]{4,3,2,1,0:T(8,128)(2,1)} %state_ref.2) | copy-start | bytes 2359300
  2.2 38.8 %copy-start.9 = (f32[768]{0:T(1024)S(1)}, f32[768]{0:T(1024)}, u32[]{:S(2)}) copy-start(f32[768]{0:T(1024)} %param.16) | copy-start | bytes 9220
  2.2 40.7 %copy-start.1 = (bf16[1,32,32,192]{3,2,1,0:T(8,128)(2,1)S(1)}, bf16[1,32,32,192]{3,2,1,0:T(8,128)(2,1)}, u32[]{:S(2)}) copy-start(bf16[1,32,32,192]{3,2,1,0:T(8,128)(2,1)} %base_ref.1) | copy-start | bytes 1179652
  2.3 40.7 %copy-start.3 = (f32[7,7,192]{2,1,0:T(8,128)S(1)}, f32[7,7,192]{2,1,0:T(8,128)}, u32[]{:S(2)}) copy-start(f32[7,7,192]{2,1,0:T(8,128)} %kernel_ref.9) | copy-start | bytes 112900
  2.3 40.7 %copy-start.4 = (bf16[192,768]{1,0:T(8,128)(2,1)S(1)}, bf16[192,768]{1,0:T(8,128)(2,1)}, u32[]{:S(2)}) copy-start(bf16[192,768]{1,0:T(8,128)(2,1)} %up_ref.5) | copy-start | bytes 884740
  2.3 40.7 %copy-start.5 = (bf16[768,192]{0,1:T(8,128)(2,1)S(1)}, bf16[768,192]{0,1:T(8,128)(2,1)}, u32[]{:S(2)}) copy-start(bf16[768,192]{0,1:T(8,128)(2,1)} %param.17) | copy-start | bytes 884740
  2.3 40.7 %copy-start.6 = (f32[192]{0:T(256)S(1)}, f32[192]{0:T(256)}, u32[]{:S(2)}) copy-start(f32[192]{0:T(256)} %param.14) | copy-start | bytes 2308
  17.4 36.2 %all-to-all-start.1 = ((bf16[16,32,384]{2,1,0:T(8,128)(2,1)}), bf16[16,32,384]{2,1,0:T(8,128)(2,1)S(1)}, u32[]{:S(2)}, u32[]{:S(2)}) async-start(bf16[16,32,384]{2,1,0:T(8,128)(2,1)} %shard_map.110), calls=%async_computation.1 | async-start | bytes 786432 | tf_op jit(solution)/shard_map/all_to_all | solution.py:474
  32.1 9.9 %collective-permute-start.1 = (bf16[2,32,3,192]{3,2,1,0:T(4,128)(2,1)S(1)}, bf16[2,32,3,192]{3,2,1,0:T(4,128)(2,1)S(1)}, u32[]{:S(2)}, u32[]{:S(2)}) collective-permute-start(bf16[2,32,3,192]{3,2,1,0:T(4,128)(2,1)S(1)} %get-tuple-element.47), channel_id=1, source_target_pairs={{1,0},{2,1},{3,2},{4,3},{5,4},{6,5},{7,6},{8,7},{9,8},{10,9},{11,1... | collective-permute-start | bytes 221192 | tf_op jit(solution)/shard_map/ppermute | solution.py:464
  35.0 8.0 %collective-permute-start = (bf16[2,32,3,192]{3,2,1,0:T(4,128)(2,1)S(1)}, bf16[2,32,3,192]{3,2,1,0:T(4,128)(2,1)S(1)}, u32[]{:S(2)}, u32[]{:S(2)}) collective-permute-start(bf16[2,32,3,192]{3,2,1,0:T(4,128)(2,1)S(1)} %get-tuple-element.48), channel_id=1, source_target_pairs={{0,1},{1,2},{2,3},{3,4},{4,5},{5,6},{6,7},{7,8},{8,9},{9,10},{10,1... | collective-permute-start | bytes 221192 | tf_op jit(solution)/shard_map/ppermute | solution.py:465
  52.3 12.7 %copy-start.11 = (bf16[32,3,192]{2,1,0:T(4,128)(2,1)S(1)}, bf16[32,3,192]{2,1,0:T(4,128)(2,1)}, u32[]{:S(2)}) copy-start(bf16[32,3,192]{2,1,0:T(4,128)(2,1)} %get-tuple-element.31) | copy-start | bytes 110596
  52.3 14.6 %copy-start.10 = (bf16[32,3,192]{2,1,0:T(4,128)(2,1)S(1)}, bf16[32,3,192]{2,1,0:T(4,128)(2,1)}, u32[]{:S(2)}) copy-start(bf16[32,3,192]{2,1,0:T(4,128)(2,1)} %get-tuple-element.37) | copy-start | bytes 110596
  52.3 22.9 %copy-start.7 = (bf16[32,3,192]{2,1,0:T(4,128)(2,1)S(1)}, bf16[32,3,192]{2,1,0:T(4,128)(2,1)}, u32[]{:S(2)}) copy-start(bf16[32,3,192]{2,1,0:T(4,128)(2,1)} %get-tuple-element.34.right_ref) | copy-start | bytes 110596
  52.3 22.9 %copy-start.8 = (bf16[32,3,192]{2,1,0:T(4,128)(2,1)S(1)}, bf16[32,3,192]{2,1,0:T(4,128)(2,1)}, u32[]{:S(2)}) copy-start(bf16[32,3,192]{2,1,0:T(4,128)(2,1)} %get-tuple-element.33.left_ref) | copy-start | bytes 110596
  54.8 34.0 %all-to-all-start.2 = ((bf16[16,32,384]{2,1,0:T(8,128)(2,1)}), bf16[16,32,384]{2,1,0:T(8,128)(2,1)S(1)}, u32[]{:S(2)}, u32[]{:S(2)}) async-start(bf16[16,32,384]{2,1,0:T(8,128)(2,1)} %shard_map.112), calls=%async_computation.2 | async-start | bytes 786432 | tf_op jit(solution)/shard_map/all_to_all | solution.py:474
  65.0 19.1 %collective-permute-start.2 = (bf16[32,3,192]{2,1,0:T(4,128)(2,1)S(1)}, bf16[32,3,192]{2,1,0:T(4,128)(2,1)S(1)}, u32[]{:S(2)}, u32[]{:S(2)}) collective-permute-start(bf16[32,3,192]{2,1,0:T(4,128)(2,1)S(1)} %copy-done.11), channel_id=1, source_target_pairs={{1,0},{2,1},{3,2},{4,3},{5,4},{6,5},{7,6},{8,7},{9,8},{10,9},{11,1... | collective-permute-start | bytes 110600 | tf_op jit(solution)/shard_map/ppermute | solution.py:464
  66.9 17.2 %collective-permute-start.3 = (bf16[32,3,192]{2,1,0:T(4,128)(2,1)S(1)}, bf16[32,3,192]{2,1,0:T(4,128)(2,1)S(1)}, u32[]{:S(2)}, u32[]{:S(2)}) collective-permute-start(bf16[32,3,192]{2,1,0:T(4,128)(2,1)S(1)} %copy-done.10), channel_id=1, source_target_pairs={{0,1},{1,2},{2,3},{3,4},{4,5},{5,6},{6,7},{7,8},{8,9},{9,10},{10,1... | collective-permute-start | bytes 110600 | tf_op jit(solution)/shard_map/ppermute | solution.py:465
  75.2 8.9 %copy-start.2 = (bf16[32,32,192]{2,1,0:T(8,128)(2,1)S(1)}, bf16[32,32,192]{2,1,0:T(8,128)(2,1)}, u32[]{:S(2)}) copy-start(bf16[32,32,192]{2,1,0:T(8,128)(2,1)} %get-tuple-element.27.hidden_ref) | copy-start | bytes 1179652
  92.9 15.8 %collective-permute-start.4 = (bf16[32,3,192]{2,1,0:T(4,128)(2,1)S(1)}, bf16[32,3,192]{2,1,0:T(4,128)(2,1)S(1)}, u32[]{:S(2)}, u32[]{:S(2)}) collective-permute-start(bf16[32,3,192]{2,1,0:T(4,128)(2,1)S(1)} %get-tuple-element.45), channel_id=1, source_target_pairs={{1,0},{2,1},{3,2},{4,3},{5,4},{6,5},{7,6},{8,7},{9,8},{10,9},{11,1... | collective-permute-start | bytes 110600 | tf_op jit(solution)/shard_map/ppermute | solution.py:464
  94.8 13.9 %collective-permute-start.5 = (bf16[32,3,192]{2,1,0:T(4,128)(2,1)S(1)}, bf16[32,3,192]{2,1,0:T(4,128)(2,1)S(1)}, u32[]{:S(2)}, u32[]{:S(2)}) collective-permute-start(bf16[32,3,192]{2,1,0:T(4,128)(2,1)S(1)} %get-tuple-element.46), channel_id=1, source_target_pairs={{0,1},{1,2},{2,3},{3,4},{4,5},{5,6},{6,7},{7,8},{8,9},{9,10},{10,1... | collective-permute-start | bytes 110600 | tf_op jit(solution)/shard_map/ppermute | solution.py:465

commit v6 on v5

--- a/solution.py
+++ b/solution.py
@@ -22,6 +22,7 @@
 BLK = 8
 ROWS = BLK * WID
 UNROLL = 4
+HALF = LAT // 2
 f32 = jnp.float32
 bf16 = jnp.bfloat16
 NT = (((1,), (1,)), ((), ()))
@@ -66,44 +67,94 @@
             shifts[col, LAT + 3 + edge] = zeros
 
 
-def build_shifts(shifts, padded, centre, left=None, right=None):
-    clear_rims(shifts, 7, WID)
+def build_shifts(low, high, padded, centre, left=None, right=None):
+    zeros = jnp.zeros((WID, 128), f32)
+    for edge in range(3):
+        for col in range(7):
+            low[col, edge] = zeros
+            low[col, LAT + 3 + edge] = zeros
     if left is None:
         padded[...] = jnp.zeros(padded.shape, f32)
 
-    def some_rows(index, carry):
-        for lane in range(UNROLL):
-            row = index * UNROLL + lane
+    def spread_rows(rows, part, target, offset):
+        for lane, row in enumerate(rows):
             if left is not None:
-                padded[lane, 0:3] = left(row).astype(f32)
-                padded[lane, WID + 3 : WID + 6] = right(row).astype(f32)
-            padded[lane, 3 : WID + 3] = centre(row).astype(f32)
-        for lane in range(UNROLL):
-            row = index * UNROLL + lane
+                padded[lane, 0:3] = part(left, row)
+                padded[lane, WID + 3 : WID + 6] = part(right, row)
+            padded[lane, 3 : WID + 3] = part(centre, row)
+        for lane, row in enumerate(rows):
             for col in range(7):
-                shifts[col, row + 3] = padded[lane, col : col + WID]
+                target[col, row + offset] = padded[lane, col : col + WID]
+
+    def low_part(source, row):
+        return source(row)[:, 0:128].astype(f32)
+
+    def high_part(source, row):
+        first = source(row - 3)[:, 128:CH].astype(f32) if not isinstance(row, int) or row >= 3 else None
+        second = source(row + HALF - 3)[:, 128:CH].astype(f32) if not isinstance(row, int) or row < 19 else None
+        first = jnp.zeros_like(second) if first is None else first
+        second = jnp.zeros_like(first) if second is None else second
+        return jnp.concatenate([first, second], axis=1)
+
+    def some_low(index, carry):
+        spread_rows([index * UNROLL + lane for lane in range(UNROLL)], low_part, low, 3)
         return carry
 
-    lax.fori_loop(0, LAT // UNROLL, some_rows, 0)
-
-
-def convolve(shifts, kernel_ref, first, flip, emit, cols=range(7), width=WID):
-    for low, high in ((0, 128), (128, CH)):
-        sums = [None] * BLK
-        for place, col in enumerate(cols):
-            taps = []
+    def some_high(index, carry):
+        spread_rows([index * UNROLL + lane + 3 for lane in range(UNROLL)], high_part, high, 0)
+        return carry
+
+    lax.fori_loop(0, LAT // UNROLL, some_low, 0)
+    lax.fori_loop(0, HALF // UNROLL, some_high, 0)
+    spread_rows([0, 1, 2], high_part, high, 0)
+    spread_rows([19, 20, 21], high_part, high, 0)
+
+
+def block_sums(shifts, first, tap, cols=range(7), lanes=slice(0, 128)):
+    sums = [None] * BLK
+    for place, col in enumerate(cols):
+        taps = [tap(row, col) for row in range(7)]
+        for source in range(BLK + 6):
+            field = shifts[place, first + source, :, lanes]
             for row in range(7):
-                down, across = (6 - row, 6 - col) if flip else (row, col)
-                taps.append(jnp.broadcast_to(kernel_ref[down, across : across + 1, low:high], (width, high - low)))
-            for source in range(BLK + 6):
-                field = shifts[place, first + source, :, low:high]
-                for row in range(7):
-                    target = source - row
-                    if 0 <= target < BLK:
-                        term = taps[row] * field
-                        sums[target] = term if sums[target] is None else sums[target] + term
+                target = source - row
+                if 0 <= target < BLK:
+                    term = taps[row] * field
+                    sums[target] = term if sums[target] is None else sums[target] + term
+    return sums
+
+
+def tap_of(kernel_ref, flip, lanes, width):
+    def tap(row, col):
+        down, across = (6 - row, 6 - col) if flip else (row, col)
+        value = kernel_ref[down, across : across + 1, lanes]
+        return jnp.broadcast_to(value, (width, value.shape[1]))
+
+    return tap
+
+
+def convolve(low, high, twice, kernel_ref, flip, emit):
+    for row in range(7):
+        upper = kernel_ref[row, :, 128:CH]
+        twice[row, 0:7] = jnp.concatenate([upper, upper], axis=1)
+
+    def low_block(index, carry):
+        first = index * BLK
+        sums = block_sums(low, first, tap_of(kernel_ref, flip, slice(0, 128), WID))
         for target in range(BLK):
-            emit(target, low, high, sums[target])
+            emit(first + target, 0, 128, sums[target])
+        return carry
+
+    def high_block(index, carry):
+        first = index * BLK
+        sums = block_sums(high, first, tap_of(twice, flip, slice(0, 128), WID))
+        for target in range(BLK):
+            emit(first + target, 128, CH, sums[target][:, 0:64])
+            emit(first + target + HALF, 128, CH, sums[target][:, 64:128])
+        return carry
+
+    lax.fori_loop(0, LAT // BLK, low_block, 0)
+    lax.fori_loop(0, HALF // BLK, high_block, 0)
 
 
 def pack_kernel(cell_far, count_far, value_far, error_far, out_ref, cell_ref, count_ref, value_ref, error_ref, sems):
@@ -146,7 +197,7 @@
     band = lax.broadcasted_iota(jnp.int32, (BLK, ROWS), 0)
     offset = (lane - band * WID).astype(f32)
     rows = [jnp.where(offset == cells[:, slot : slot + 1], 1.0, 0.0) for slot in range(CAP)]
-    return jnp.concatenate(rows, axis=0).astype(bf16)
+    return jnp.concatenate(rows, axis=0)
 
 
 def gather_kernel(got_ref, state_far, out_ref, state_ref, sems):
@@ -157,7 +208,7 @@
             pairs.append((state_far.at[step, 0, rows], state_ref.at[step, rows]))
     copies = fetch(pairs, sems)
     for step in range(2):
-        hots = [one_hot(step, got_ref, group) for group in range(LAT // BLK)]
+        hots = [one_hot(step, got_ref, group).astype(bf16) for group in range(LAT // BLK)]
         for pair in range(2):
             copies[2 * step + pair].wait()
             found = []
@@ -204,10 +255,22 @@
     )(rows, got)
 
 
-def forcing_of(step, rows_ref, got_ref, group):
+def cell_row(step, got_ref, group):
+    cells = got_ref[group * BLK : (group + 1) * BLK, 2 * step + 1, 64 : 64 + CAP]
+    band = lax.broadcasted_iota(jnp.int32, (BLK, CAP), 0).astype(f32)
+    cells = jnp.where(cells < 0.0, -1.0, cells + band * WID)
+    column = jnp.concatenate([cells[:, slot : slot + 1] for slot in range(CAP)], axis=0)
+    return jnp.broadcast_to(column, (CAP * BLK, CAP * BLK)).T[0:1]
+
+
+def forcing_of(step, rows_ref, cell_ref, group):
+    place = step * (LAT // BLK) + group
+    cells = jnp.broadcast_to(cell_ref[place : place + 1, :], (ROWS, CAP * BLK))
+    cell = lax.broadcasted_iota(jnp.int32, (ROWS, CAP * BLK), 0).astype(f32)
+    hot = jnp.where(cell == cells, 1.0, 0.0).astype(bf16)
     rows = rows_ref[:, :, step * CH : (step + 1) * CH].astype(f32)[:, group * BLK : (group + 1) * BLK]
     rows = rows.reshape(CAP * BLK, CH).astype(bf16)
-    return lax.dot_general(one_hot(step, got_ref, group), rows, TN, preferred_element_type=f32)
+    return jnp.dot(hot, rows, preferred_element_type=f32)
 
 
 def normalise(hidden):
@@ -235,7 +298,7 @@
 
 
 def forward_kernel(step, state_ref, left_ref, right_ref, kernel_ref, gain_ref, up_ref, bias_ref, *rest):
-    shifts, padded, hidden = rest[-3:]
+    low, high, twice, padded, hidden = rest[-5:]
     if step == 0:
         later_right, later_left = rest[5:7]
         later_right[...] = right_ref[1]
@@ -243,20 +306,20 @@
         right_ref, left_ref = right_ref.at[0], left_ref.at[0]
     gain = gain_ref[...]
     build_shifts(
-        shifts, padded,
+        low, high, padded,
         lambda row: state_ref[step, 0, row],
         lambda row: left_ref[row],
         lambda row: right_ref[row],
     )
 
+    def emit(row, start, stop, value):
+        hidden[row, :, start:stop] = value
+
+    convolve(low, high, twice, kernel_ref, False, emit)
+
     def block(index, carry):
         first = index * BLK
-
-        def emit(target, low, high, value):
-            hidden[target, :, low:high] = value
-
-        convolve(shifts, kernel_ref, first, False, emit)
-        unit, inv_std = normalise(hidden[...].reshape(ROWS, CH))
+        unit, inv_std = normalise(hidden[pl.ds(first, BLK)].reshape(ROWS, CH))
         normed = (unit * gain).astype(bf16)
 
         def slope_at(cols):
@@ -283,7 +346,12 @@
 FAR_EDGE = pltpu.HBM((LAT, 3, CH), bf16)
 EDGE = jax.ShapeDtypeStruct((LAT, 3, CH), bf16)
 FIELD = jax.ShapeDtypeStruct((LAT, WID, CH), bf16)
-SHIFT_SCRATCH = [pltpu.VMEM((7, LAT + 6, WID, CH), f32), pltpu.VMEM((UNROLL, WID + 8, CH), f32)]
+SHIFT_SCRATCH = [
+    pltpu.VMEM((7, LAT + 6, WID, 128), f32),
+    pltpu.VMEM((7, HALF + 6, WID, 128), f32),
+    pltpu.VMEM((7, 8, 128), f32),
+    pltpu.VMEM((UNROLL, WID + 8, 128), f32),
+]
 
 
 def forward(step, states, left, right, *others):
@@ -294,117 +362,117 @@
         functools.partial(forward_kernel, step),
         out_shape=shapes,
         out_specs=(VM,) * len(shapes),
-        scratch_shapes=SHIFT_SCRATCH + [pltpu.VMEM((BLK, WID, CH), f32)],
+        scratch_shapes=SHIFT_SCRATCH + [pltpu.VMEM((LAT, WID, CH), f32)],
         compiler_params=limit(16),
         cost_estimate=pl.CostEstimate(flops=6 * CELLS * CH * HID, bytes_accessed=8000000, transcendentals=CELLS * HID),
     )(states, left, right, *others)
 
 
-def spread_kernel(hidden_ref, right_ref, left_ref, base_ref, kernel_ref, out_ref, shifts, padded):
+def spread_kernel(
+    hidden_ref, right_ref, left_ref, base_ref, kernel_ref, got_ref, slope_far,
+    out_ref, slope_out, cell_out,
+    low, high, twice, padded, sems,
+):
+    copies = fetch([(slope_far, slope_out)], sems)
+    for step in range(2):
+        for group in range(LAT // BLK):
+            place = step * (LAT // BLK) + group
+            cell_out[place : place + 1, :] = cell_row(step, got_ref, group)
     build_shifts(
-        shifts, padded,
+        low, high, padded,
         lambda row: hidden_ref[row],
         lambda row: left_ref[row],
         lambda row: right_ref[row],
     )
 
-    def block(index, carry):
-        first = index * BLK
-
-        def emit(target, low, high, value):
-            base = base_ref[0, first + target, :, low:high].astype(f32)
-            out_ref[first + target, :, low:high] = base + value
-
-        convolve(shifts, kernel_ref, first, True, emit)
-        return carry
-
-    lax.fori_loop(0, LAT // BLK, block, 0)
-
-
-def spread_back(hidden, right, left, base, kernel):
+    def emit(row, start, stop, value):
+        out_ref[row, :, start:stop] = base_ref[0, row, :, start:stop].astype(f32) + value
+
+    convolve(low, high, twice, kernel_ref, True, emit)
+    for copy in copies:
+        copy.wait()
+
+
+def spread_back(hidden, right, left, base, kernel, got, slope):
     return pl.pallas_call(
         spread_kernel,
-        out_shape=jax.ShapeDtypeStruct((LAT, WID, CH), f32),
-        scratch_shapes=SHIFT_SCRATCH,
-        compiler_params=limit(16),
+        out_shape=(
+            jax.ShapeDtypeStruct((LAT, WID, CH), f32),
+            jax.ShapeDtypeStruct(slope.shape, bf16),
+            jax.ShapeDtypeStruct((2 * LAT // BLK, CAP * BLK), f32),
+        ),
+        in_specs=[VM] * 6 + [HBM],
+        scratch_shapes=SHIFT_SCRATCH + [pltpu.SemaphoreType.DMA((1,))],
+        compiler_params=limit(18),
         cost_estimate=pl.CostEstimate(flops=98 * CELLS * CH, bytes_accessed=3000000, transcendentals=0),
-    )(hidden, right, left, base, kernel)
+    )(hidden, right, left, base, kernel, got, far(slope))
 
 
 def second_kernel(
-    partial_ref, rows_ref, got_ref, slope_ref, unit_ref, gain_ref, up_ref, down_ref,
-    hidden_out, tail_out, head_out, adjoint_out, slope_buf, unit_buf, down_buf, sems,
+    partial_ref, rows_ref, hot_ref, slope_ref, unit_far, gain_ref, up_ref, down_far,
+    hidden_out, tail_out, head_out, adjoint_out, unit_ref, down_ref, sems,
 ):
-    parts = [slice(group * ROWS, (group + 1) * ROWS) for group in range(LAT // BLK)]
-    pairs = [(down_ref, down_buf), (unit_ref, unit_buf)]
-    copies = fetch(pairs + [(slope_ref.at[rows], slope_buf.at[rows]) for rows in parts], sems)
+    copies = fetch([(down_far, down_ref), (unit_far, unit_ref)], sems)
     gain = gain_ref[...]
     for group in range(LAT // BLK):
         first = group * BLK
         rows = slice(group * ROWS, (group + 1) * ROWS)
-        forcing = forcing_of(0, rows_ref, got_ref, group)
+        forcing = forcing_of(0, rows_ref, hot_ref, group)
         adjoint = (partial_ref[first : first + BLK].reshape(ROWS, CH) + forcing).astype(bf16)
         adjoint_out[first : first + BLK] = adjoint.reshape(BLK, WID, CH)
         if group == 0:
-            copies[0].wait()
-            copies[1].wait()
-        copies[2 + group].wait()
+            for copy in copies:
+                copy.wait()
         result = backward(
             adjoint,
-            lambda cols: slope_buf[rows, cols].astype(f32),
-            down_buf, up_ref, gain,
-            unit_buf[rows, :].astype(f32),
+            lambda cols: slope_ref[rows, cols].astype(f32),
+            down_ref, up_ref, gain,
+            unit_ref[rows, :].astype(f32),
         )
         put_hidden(result, first, hidden_out, tail_out, head_out)
 
 
-def second_step(partial, rows, got, slope, unit, gain, up, down):
+def second_step(partial, rows, hot, slope, unit, gain, up, down):
     return pl.pallas_call(
         second_kernel,
         out_shape=(FIELD, EDGE, EDGE, FIELD),
-        in_specs=[VM, VM, VM, HBM, HBM, VM, VM, HBM],
-        scratch_shapes=[
-            pltpu.VMEM((CELLS, HID), bf16), pltpu.VMEM((CELLS, CH), bf16), pltpu.VMEM((CH, HID), bf16),
-            pltpu.SemaphoreType.DMA((6,)),
-        ],
-        compiler_params=limit(12),
+        in_specs=[VM] * 4 + [HBM, VM, VM, HBM],
+        scratch_shapes=[pltpu.VMEM((CELLS, CH), bf16), pltpu.VMEM((CH, HID), bf16), pltpu.SemaphoreType.DMA((2,))],
+        compiler_params=limit(8),
         cost_estimate=pl.CostEstimate(flops=4 * CELLS * CH * HID, bytes_accessed=5000000, transcendentals=0),
-    )(partial, rows, got, far(slope), far(unit), gain, up, far(down))
-
-
-def interior_kernel(hidden_ref, adjoint_ref, rows_ref, got_ref, kernel_ref, out_ref, west_ref, east_ref, shifts, padded, total):
-    build_shifts(shifts, padded, lambda row: hidden_ref[row])
+    )(partial, rows, hot, slope, far(unit), gain, up, far(down))
+
+
+def interior_kernel(
+    hidden_ref, adjoint_ref, rows_ref, hot_ref, kernel_ref, out_ref, west_ref, east_ref,
+    low, high, twice, padded, total,
+):
+    build_shifts(low, high, padded, lambda row: hidden_ref[row])
     for group in range(LAT // BLK):
         first = group * BLK
-        forcing = forcing_of(1, rows_ref, got_ref, group).reshape(BLK, WID, CH)
+        forcing = forcing_of(1, rows_ref, hot_ref, group).reshape(BLK, WID, CH)
         total[first : first + BLK] = adjoint_ref[first : first + BLK].astype(f32) + forcing
 
-    def block(index, carry):
-        first = index * BLK
-
-        def emit(target, low, high, value):
-            value = total[first + target, :, low:high] + value
-            out_ref[first + target, :, low:high] = value.astype(bf16)
-            west_ref[first + target, :, low:high] = value[0:8]
-            east_ref[first + target, :, low:high] = value[WID - 8 : WID]
-
-        convolve(shifts, kernel_ref, first, True, emit)
-        return carry
-
-    lax.fori_loop(0, LAT // BLK, block, 0)
+    def emit(row, start, stop, value):
+        value = total[row, :, start:stop] + value
+        out_ref[row, :, start:stop] = value.astype(bf16)
+        west_ref[row, :, start:stop] = value[0:8]
+        east_ref[row, :, start:stop] = value[WID - 8 : WID]
+
+    convolve(low, high, twice, kernel_ref, True, emit)
 
 
 STRIP = jax.ShapeDtypeStruct((LAT, 8, CH), f32)
 
 
-def interior(hidden, adjoint, rows, got, kernel):
+def interior(hidden, adjoint, rows, hot, kernel):
     return pl.pallas_call(
         interior_kernel,
         out_shape=(FIELD, STRIP, STRIP),
         scratch_shapes=SHIFT_SCRATCH + [pltpu.VMEM((LAT, WID, CH), f32)],
         compiler_params=limit(16),
         cost_estimate=pl.CostEstimate(flops=98 * CELLS * CH, bytes_accessed=3000000, transcendentals=0),
-    )(hidden, adjoint, rows, got, kernel)
+    )(hidden, adjoint, rows, hot, kernel)
 
 
 def edge_kernel(inner_ref, west_ref, east_ref, right_ref, left_ref, kernel_ref, out_ref, shifts, padded):
@@ -425,10 +493,11 @@
         def block(index, carry):
             first = index * BLK
 
-            def emit(target, low, high, value):
-                out_ref[first + target, :, low:high] = (strip_ref[first + target, :, low:high] + value).astype(bf16)
-
-            convolve(shifts, kernel_ref, first, True, emit, cols, 8)
+            for low, high in ((0, 128), (128, CH)):
+                sums = block_sums(shifts, first, tap_of(kernel_ref, True, slice(low, high), 8), cols, slice(low, high))
+                for target in range(BLK):
+                    value = strip_ref[first + target, :, low:high] + sums[target]
+                    out_ref[first + target, :, low:high] = value.astype(bf16)
             return carry
 
         lax.fori_loop(0, LAT // BLK, block, 0)
@@ -499,13 +568,15 @@
 
     before, behind = swap_edges(*after((head, tail), deps))
     slope, unit = forward(1, after(states, deps), later_left, later_right, kernel, gain, up_weight, bias)
-    partial = spread_back(hidden, after(behind, slope), before, adjoint_final, kernel)
+    partial, slope, cells = spread_back(
+        hidden, after(behind, slope), before, adjoint_final, kernel, got, slope
+    )
 
     hidden, tail, head, adjoint = second_step(
-        partial, after(back, partial), got, slope, unit, gain, up_weight, down
+        partial, after(back, partial), cells, slope, unit, gain, up_weight, down
     )
     left, right = swap_edges(head, tail)
-    inner, west, east = interior(hidden, adjoint, back, got, kernel)
+    inner, west, east = interior(hidden, adjoint, back, cells, kernel)
     return finish_edges(inner, west, east, left, right, kernel)[None]
 
 

time: 111 us -> 109 us (0.982)
  the two profiles are of different devices: /device:TPU:63 before, /device:TPU:32 now
where the time goes in v6:
time: 109 us; the launch traced here: 108 us
  starting transfers between devices  41.3 us (38%)
  Pallas kernels  38.7 us (36%)
  blocking collectives  15 us (14%)
  waiting for transfers between devices  12.7 us (12%)
    all_to_all x2, starting transfers between devices, exchange(): return lax.all_to_all(array, axis, split_axis=0, concat_axis=0, tiled=True)  26.2 us
    pallas_call x2, Pallas kernels, forward(): pl.pallas_call(functools.partial(forward_kernel, step), out_shape=shapes,...  16.8 us
    all_to_all x1, blocking collectives, exchange(): return lax.all_to_all(array, axis, split_axis=0, concat_axis=0, tiled=True)  15 us
    ppermute x3, starting transfers between devices, swap_edges(): right = lax.ppermute(head, 'tile', down)  8.84 us
    ppermute x3, waiting for transfers between devices, swap_edges(): left = lax.ppermute(tail, 'tile', up)  8.66 us
    ppermute x3, starting transfers between devices, swap_edges(): left = lax.ppermute(tail, 'tile', up)  6.25 us
    pallas_call x1, Pallas kernels, interior(): pl.pallas_call(interior_kernel, out_shape=(FIELD, STRIP, STRIP), scratch_...  5.43 us
    pallas_call x1, Pallas kernels, spread_back(): pl.pallas_call(spread_kernel, out_shape=(jax.ShapeDtypeStruct((LAT, WID,...  5.33 us
  transfers between devices with their start and end apart: 8, of which 5 were waited for; matrix products, arithmetic and copies ran while one was open for 0% of the time, Pallas kernels for 26%

profile of v6, /device:TPU:32, one launch (start us, length us, event | category | flops | bytes accessed | tf_op | source)
XLA Modules:
  0.0 108.1 jit_solution(5909305655495737463)
XLA Ops:
  0.0 0.0 copy-start
  0.0 2.2 %shard_map.109 = f32[32,4,128]{2,1,0:T(4,128)} custom-call(s32[2,16,32]{2,1,0:T(8,128)} %bitcast.16, s32[2,1,32]{2,1,0:T(1,128)} %count_far.1, bf16[2,1,32,16,192]{4,3,2,1,0:T(8,128)(2,1)} %value_far.1, bf16[2,16,32]{2,1,0:T(8,128)(2,1)} %bitcast.17), custom_call_target="tpu_custom_call" | custom-call | tf_op jit(solution)/shard_map/pallas_call | solution.py:183
  2.2 0.0 copy-start.10
  2.2 0.0 copy-start.1
  2.3 0.0 copy-start.4
  2.3 0.0 copy-start.5
  2.3 0.0 copy-start.6
  2.3 0.0 copy-start.7
  2.3 15.0 %all_to_all.15.got_ref = f32[32,4,128]{2,1,0:T(4,128)S(1)} all-to-all(f32[32,4,128]{2,1,0:T(4,128)} %shard_map.109), channel_id=1, replica_groups=mesh['member'=16,'tile'=32] {'tile'}, dimensions={0} | all-to-all | bytes 131072 | tf_op jit(solution)/shard_map/all_to_all | solution.py:543
  17.3 3.2 %shard_map.110 = bf16[16,32,384]{2,1,0:T(8,128)(2,1)} custom-call(f32[32,4,128]{2,1,0:T(4,128)S(1)} %all_to_all.15.got_ref, bf16[2,1,32,32,192]{4,3,2,1,0:T(8,128)(2,1)} %state_ref.2), custom_call_target="tpu_custom_call" | custom-call | flops 1000000 | bytes 2000000 | tf_op jit(solution)/shard_map/pallas_call | solution.py:224
  20.5 15.2 %all-to-all-start.1 = ((bf16[16,32,384]{2,1,0:T(8,128)(2,1)}), bf16[16,32,384]{2,1,0:T(8,128)(2,1)S(1)}, u32[]{:S(2)}, u32[]{:S(2)}) async-start(bf16[16,32,384]{2,1,0:T(8,128)(2,1)} %shard_map.110), calls=%async_computation.1 | async-start | bytes 786432 | tf_op jit(solution)/shard_map/all_to_all | solution.py:543
  35.7 0.0 copy-done
  35.7 0.1 fusion
  35.9 2.9 %collective-permute-start.1 = (bf16[2,32,3,192]{3,2,1,0:T(4,128)(2,1)S(1)}, bf16[2,32,3,192]{3,2,1,0:T(4,128)(2,1)S(1)}, u32[]{:S(2)}, u32[]{:S(2)}) collective-permute-start(bf16[2,32,3,192]{3,2,1,0:T(4,128)(2,1)S(1)} %get-tuple-element.53), channel_id=1, source_target_pairs={{1,0},{2,1},{3,2},{4,3},{5,4},{6,5},{7,6},{8,7},{9,8},{10,9},{11,1... | collective-permute-start | bytes 221192 | tf_op jit(solution)/shard_map/ppermute | solution.py:533
  38.7 1.9 %collective-permute-start = (bf16[2,32,3,192]{3,2,1,0:T(4,128)(2,1)S(1)}, bf16[2,32,3,192]{3,2,1,0:T(4,128)(2,1)S(1)}, u32[]{:S(2)}, u32[]{:S(2)}) collective-permute-start(bf16[2,32,3,192]{3,2,1,0:T(4,128)(2,1)S(1)} %get-tuple-element.54), channel_id=1, source_target_pairs={{0,1},{1,2},{2,3},{3,4},{4,5},{5,6},{6,7},{7,8},{8,9},{9,10},{10,1... | collective-permute-start | bytes 221192 | tf_op jit(solution)/shard_map/ppermute | solution.py:534
  40.6 0.0 copy-done.10
  40.7 0.5 collective-permute-done.1.right_ref
  41.2 7.1 %collective-permute-done.left_ref = bf16[2,32,3,192]{3,2,1,0:T(4,128)(2,1)S(1)} collective-permute-done((bf16[2,32,3,192]{3,2,1,0:T(4,128)(2,1)S(1)}, bf16[2,32,3,192]{3,2,1,0:T(4,128)(2,1)S(1)}, u32[]{:S(2)}, u32[]{:S(2)}) %collective-permute-start) | collective-permute-done | bytes 73760 | tf_op jit(solution)/shard_map/ppermute | solution.py:534
  48.3 0.0 copy-done.1
  48.3 0.0 copy-done.4
  48.3 0.0 copy-done.5
  48.3 0.0 copy-done.6
  48.3 0.0 copy-done.7
  48.4 8.7 %shard_map.111 = (bf16[32,32,192]{2,1,0:T(8,128)(2,1)}, bf16[32,3,192]{2,1,0:T(4,128)(2,1)}, bf16[32,3,192]{2,1,0:T(4,128)(2,1)}, bf16[32,3,192]{2,1,0:T(4,128)(2,1)}, bf16[32,3,192]{2,1,0:T(4,128)(2,1)}) custom-call(bf16[2,1,32,32,192]{4,3,2,1,0:T(8,128)(2,1)S(1)} %copy-done, bf16[2,32,3,192]{3,2,1,0:T(4,128)(2,1)S(1)} %collective-permute-done.left_ref, ...), custom_call_target="tpu_custom_call" | custom-call | flops 905969664 | bytes 8000000 | tf_op jit(solution)/shard_map/pallas_call | solution.py:361
  57.0 0.0 copy-start.12
  57.0 0.0 copy-start.11
  57.0 0.0 copy-start.8
  57.0 0.0 copy-start.9
  57.0 1.0 all-to-all-done.1.rows_ref
  58.1 1.2 %shard_map.112 = bf16[16,32,384]{2,1,0:T(8,128)(2,1)} custom-call(bf16[16,32,384]{2,1,0:T(8,128)(2,1)S(1)} %all-to-all-done.1.rows_ref, f32[32,4,128]{2,1,0:T(4,128)S(1)} %all_to_all.15.got_ref), custom_call_target="tpu_custom_call" | custom-call | flops 1200000 | bytes 1200000 | tf_op jit(solution)/shard_map/pallas_call | solution.py:250
  59.3 11.0 %all-to-all-start.2 = ((bf16[16,32,384]{2,1,0:T(8,128)(2,1)}), bf16[16,32,384]{2,1,0:T(8,128)(2,1)S(1)}, u32[]{:S(2)}, u32[]{:S(2)}) async-start(bf16[16,32,384]{2,1,0:T(8,128)(2,1)} %shard_map.112), calls=%async_computation.2 | async-start | bytes 786432 | tf_op jit(solution)/shard_map/all_to_all | solution.py:543
  70.3 0.0 copy-done.12
  70.3 1.9 %collective-permute-start.2 = (bf16[32,3,192]{2,1,0:T(4,128)(2,1)S(1)}, bf16[32,3,192]{2,1,0:T(4,128)(2,1)S(1)}, u32[]{:S(2)}, u32[]{:S(2)}) collective-permute-start(bf16[32,3,192]{2,1,0:T(4,128)(2,1)S(1)} %copy-done.12), channel_id=1, source_target_pairs={{1,0},{2,1},{3,2},{4,3},{5,4},{6,5},{7,6},{8,7},{9,8},{10,9},{11,1... | collective-permute-start | bytes 110600 | tf_op jit(solution)/shard_map/ppermute | solution.py:533
  72.2 0.0 copy-done.11
  72.2 2.4 %collective-permute-start.3 = (bf16[32,3,192]{2,1,0:T(4,128)(2,1)S(1)}, bf16[32,3,192]{2,1,0:T(4,128)(2,1)S(1)}, u32[]{:S(2)}, u32[]{:S(2)}) collective-permute-start(bf16[32,3,192]{2,1,0:T(4,128)(2,1)S(1)} %copy-done.11), channel_id=1, source_target_pairs={{0,1},{1,2},{2,3},{3,4},{4,5},{5,6},{6,7},{7,8},{8,9},{9,10},{10,1... | collective-permute-start | bytes 110600 | tf_op jit(solution)/shard_map/ppermute | solution.py:534
  74.6 0.0 copy-done.8
  74.6 0.0 copy-done.9
  74.6 0.0 copy-start.2
  74.7 0.0 copy-start.3
  74.7 8.1 %shard_map.113 = (bf16[1024,768]{1,0:T(8,128)(2,1)}, bf16[1024,192]{1,0:T(8,128)(2,1)}) custom-call(bf16[2,1,32,32,192]{4,3,2,1,0:T(8,128)(2,1)S(1)} %copy-done, bf16[32,3,192]{2,1,0:T(4,128)(2,1)S(1)} %copy-done.9, bf16[32,3,192]{2,1,0:T(4,128)(2,1)S(1)} %copy-done.8, f32[7,7,192]{2,1,0:T(8,128)S(1)} %copy-done.4, f32[1,192]{1,0:T(1,128)S(1)} %bitcast.14, ...), custom_call_target="tpu_custom_call" | custom-call | flops 905969664 | bytes 8000000 | tf_op jit(solution)/shard_map/pallas_call | solution.py:361
  82.8 0.0 collective-permute-done.2.right_ref
  82.8 0.0 collective-permute-done.3.left_ref
  82.8 0.0 copy-done.2
  82.8 0.0 copy-done.3
  82.8 5.3 %shard_map.114 = (f32[32,32,192]{2,1,0:T(8,128)S(1)}, bf16[1024,768]{1,0:T(8,128)(2,1)S(1)}, f32[8,128]{1,0:T(8,128)S(1)}) custom-call(bf16[32,32,192]{2,1,0:T(8,128)(2,1)S(1)} %copy-done.3, bf16[32,3,192]{2,1,0:T(4,128)(2,1)S(1)} %collective-permute-done.2.right_ref, bf16[32,3,192]{2,1,0:T(4,128)(2,1)S(1)} %collective-permute-done.3.left_ref, ...), custom_call_target="tpu_custom_call" | custom-call | flops 19267584 | bytes 3000000 | tf_op jit(solution)/shard_map/pallas_call | solution.py:397
  88.2 2.4 %all-to-all-done.2.rows_ref = bf16[16,32,384]{2,1,0:T(8,128)(2,1)S(1)} async-done(((bf16[16,32,384]{2,1,0:T(8,128)(2,1)}), bf16[16,32,384]{2,1,0:T(8,128)(2,1)S(1)}, u32[]{:S(2)}, u32[]{:S(2)}) %all-to-all-start.2) | async-done | bytes 393248 | tf_op jit(solution)/shard_map/all_to_all | solution.py:543
  90.6 2.7 %shard_map.115 = (bf16[32,32,192]{2,1,0:T(8,128)(2,1)S(1)}, bf16[32,3,192]{2,1,0:T(4,128)(2,1)S(1)}, bf16[32,3,192]{2,1,0:T(4,128)(2,1)S(1)}, bf16[32,32,192]{2,1,0:T(8,128)(2,1)S(1)}) custom-call(f32[32,32,192]{2,1,0:T(8,128)S(1)} %get-tuple-element.41.partial_ref, bf16[16,32,384]{2,1,0:T(8,128)(2,1)S(1)} %all-to-all-done.2.rows_ref, ...), custom_call_target="tpu_custom_call" | custom-call | flops 603979776 | bytes 5000000 | tf_op jit(solution)/shard_map/pallas_call | solution.py:436
  93.3 4.1 %collective-permute-start.4 = (bf16[32,3,192]{2,1,0:T(4,128)(2,1)S(1)}, bf16[32,3,192]{2,1,0:T(4,128)(2,1)S(1)}, u32[]{:S(2)}, u32[]{:S(2)}) collective-permute-start(bf16[32,3,192]{2,1,0:T(4,128)(2,1)S(1)} %get-tuple-element.51), channel_id=1, source_target_pairs={{1,0},{2,1},{3,2},{4,3},{5,4},{6,5},{7,6},{8,7},{9,8},{10,9},{11,1... | collective-permute-start | bytes 110600 | tf_op jit(solution)/shard_map/ppermute | solution.py:533
  97.4 1.9 %collective-permute-start.5 = (bf16[32,3,192]{2,1,0:T(4,128)(2,1)S(1)}, bf16[32,3,192]{2,1,0:T(4,128)(2,1)S(1)}, u32[]{:S(2)}, u32[]{:S(2)}) collective-permute-start(bf16[32,3,192]{2,1,0:T(4,128)(2,1)S(1)} %get-tuple-element.52), channel_id=1, source_target_pairs={{0,1},{1,2},{2,3},{3,4},{4,5},{5,6},{6,7},{7,8},{8,9},{9,10},{10,1... | collective-permute-start | bytes 110600 | tf_op jit(solution)/shard_map/ppermute | solution.py:534
  99.3 5.4 %shard_map.116 = (bf16[32,32,192]{2,1,0:T(8,128)(2,1)}, f32[32,8,192]{2,1,0:T(8,128)S(1)}, f32[32,8,192]{2,1,0:T(8,128)S(1)}) custom-call(bf16[32,32,192]{2,1,0:T(8,128)(2,1)S(1)} %get-tuple-element.46.hidden_ref, bf16[32,32,192]{2,1,0:T(8,128)(2,1)S(1)} %get-tuple-element.47.adjoint_ref, bf16[16,32,384]{2,1,0:T(8,128)(2,1)S(1)} %all-to-all-done.2.rows_ref, ...), custom_call_target="tpu_custom_call" | custom-call | flops 19267584 | bytes 3000000 | tf_op jit(solution)/shard_map/pallas_call | solution.py:469
  104.7 0.0 collective-permute-done.4.right_ref
  104.7 1.5 %collective-permute-done.5.left_ref = bf16[32,3,192]{2,1,0:T(4,128)(2,1)S(1)} collective-permute-done((bf16[32,3,192]{2,1,0:T(4,128)(2,1)S(1)}, bf16[32,3,192]{2,1,0:T(4,128)(2,1)S(1)}, u32[]{:S(2)}, u32[]{:S(2)}) %collective-permute-start.5) | collective-permute-done | bytes 36896 | tf_op jit(solution)/shard_map/ppermute | solution.py:534
  106.3 1.8 %shard_map.117 = bf16[32,32,192]{2,1,0:T(8,128)(2,1)} custom-call(bf16[32,32,192]{2,1,0:T(8,128)(2,1)} %get-tuple-element.48.inner_ref, f32[32,8,192]{2,1,0:T(8,128)S(1)} %get-tuple-element.49.west_ref, f32[32,8,192]{2,1,0:T(8,128)S(1)} %get-tuple-element.50.east_ref, ...), custom_call_target="tpu_custom_call", output_to_operand_aliasing={{}: (0, {})} | custom-call | flops 5000000 | bytes 700000 | tf_op jit(solution)/shard_map/pallas_call | solution.py:516
  (1 shorter events, 0.0 us)
Async XLA Ops:
  0.0 35.7 %copy-start = (bf16[2,1,32,32,192]{4,3,2,1,0:T(8,128)(2,1)S(1)}, bf16[2,1,32,32,192]{4,3,2,1,0:T(8,128)(2,1)}, u32[]{:S(2)}) copy-start(bf16[2,1,32,32,192]{4,3,2,1,0:T(8,128)(2,1)} %state_ref.2) | copy-start | bytes 2359300
  2.2 38.4 %copy-start.10 = (f32[768]{0:T(1024)S(1)}, f32[768]{0:T(1024)}, u32[]{:S(2)}) copy-start(f32[768]{0:T(1024)} %param.16) | copy-start | bytes 9220
  2.2 46.1 %copy-start.1 = (bf16[1,32,32,192]{3,2,1,0:T(8,128)(2,1)S(1)}, bf16[1,32,32,192]{3,2,1,0:T(8,128)(2,1)}, u32[]{:S(2)}) copy-start(bf16[1,32,32,192]{3,2,1,0:T(8,128)(2,1)} %base_ref.1) | copy-start | bytes 1179652
  2.3 46.1 %copy-start.4 = (f32[7,7,192]{2,1,0:T(8,128)S(1)}, f32[7,7,192]{2,1,0:T(8,128)}, u32[]{:S(2)}) copy-start(f32[7,7,192]{2,1,0:T(8,128)} %kernel_ref.9) | copy-start | bytes 112900
  2.3 46.1 %copy-start.5 = (bf16[192,768]{1,0:T(8,128)(2,1)S(1)}, bf16[192,768]{1,0:T(8,128)(2,1)}, u32[]{:S(2)}) copy-start(bf16[192,768]{1,0:T(8,128)(2,1)} %up_ref.5) | copy-start | bytes 884740
  2.3 46.0 %copy-start.6 = (bf16[768,192]{0,1:T(8,128)(2,1)S(1)}, bf16[768,192]{0,1:T(8,128)(2,1)}, u32[]{:S(2)}) copy-start(bf16[768,192]{0,1:T(8,128)(2,1)} %param.17) | copy-start | bytes 884740
  2.3 46.0 %copy-start.7 = (f32[192]{0:T(256)S(1)}, f32[192]{0:T(256)}, u32[]{:S(2)}) copy-start(f32[192]{0:T(256)} %param.14) | copy-start | bytes 2308
  20.5 37.6 %all-to-all-start.1 = ((bf16[16,32,384]{2,1,0:T(8,128)(2,1)}), bf16[16,32,384]{2,1,0:T(8,128)(2,1)S(1)}, u32[]{:S(2)}, u32[]{:S(2)}) async-start(bf16[16,32,384]{2,1,0:T(8,128)(2,1)} %shard_map.110), calls=%async_computation.1 | async-start | bytes 786432 | tf_op jit(solution)/shard_map/all_to_all | solution.py:543
  35.9 5.4 %collective-permute-start.1 = (bf16[2,32,3,192]{3,2,1,0:T(4,128)(2,1)S(1)}, bf16[2,32,3,192]{3,2,1,0:T(4,128)(2,1)S(1)}, u32[]{:S(2)}, u32[]{:S(2)}) collective-permute-start(bf16[2,32,3,192]{3,2,1,0:T(4,128)(2,1)S(1)} %get-tuple-element.53), channel_id=1, source_target_pairs={{1,0},{2,1},{3,2},{4,3},{5,4},{6,5},{7,6},{8,7},{9,8},{10,9},{11,1... | collective-permute-start | bytes 221192 | tf_op jit(solution)/shard_map/ppermute | solution.py:533
  38.7 9.6 %collective-permute-start = (bf16[2,32,3,192]{3,2,1,0:T(4,128)(2,1)S(1)}, bf16[2,32,3,192]{3,2,1,0:T(4,128)(2,1)S(1)}, u32[]{:S(2)}, u32[]{:S(2)}) collective-permute-start(bf16[2,32,3,192]{3,2,1,0:T(4,128)(2,1)S(1)} %get-tuple-element.54), channel_id=1, source_target_pairs={{0,1},{1,2},{2,3},{3,4},{4,5},{5,6},{6,7},{7,8},{8,9},{9,10},{10,1... | collective-permute-start | bytes 221192 | tf_op jit(solution)/shard_map/ppermute | solution.py:534
  57.0 13.2 %copy-start.12 = (bf16[32,3,192]{2,1,0:T(4,128)(2,1)S(1)}, bf16[32,3,192]{2,1,0:T(4,128)(2,1)}, u32[]{:S(2)}) copy-start(bf16[32,3,192]{2,1,0:T(4,128)(2,1)} %get-tuple-element.34) | copy-start | bytes 110596
  57.0 15.2 %copy-start.11 = (bf16[32,3,192]{2,1,0:T(4,128)(2,1)S(1)}, bf16[32,3,192]{2,1,0:T(4,128)(2,1)}, u32[]{:S(2)}) copy-start(bf16[32,3,192]{2,1,0:T(4,128)(2,1)} %get-tuple-element.40) | copy-start | bytes 110596
  57.0 17.6 %copy-start.8 = (bf16[32,3,192]{2,1,0:T(4,128)(2,1)S(1)}, bf16[32,3,192]{2,1,0:T(4,128)(2,1)}, u32[]{:S(2)}) copy-start(bf16[32,3,192]{2,1,0:T(4,128)(2,1)} %get-tuple-element.37.right_ref) | copy-start | bytes 110596
  57.0 17.6 %copy-start.9 = (bf16[32,3,192]{2,1,0:T(4,128)(2,1)S(1)}, bf16[32,3,192]{2,1,0:T(4,128)(2,1)}, u32[]{:S(2)}) copy-start(bf16[32,3,192]{2,1,0:T(4,128)(2,1)} %get-tuple-element.36.left_ref) | copy-start | bytes 110596
  59.3 31.3 %all-to-all-start.2 = ((bf16[16,32,384]{2,1,0:T(8,128)(2,1)}), bf16[16,32,384]{2,1,0:T(8,128)(2,1)S(1)}, u32[]{:S(2)}, u32[]{:S(2)}) async-start(bf16[16,32,384]{2,1,0:T(8,128)(2,1)} %shard_map.112), calls=%async_computation.2 | async-start | bytes 786432 | tf_op jit(solution)/shard_map/all_to_all | solution.py:543
  70.3 12.5 %collective-permute-start.2 = (bf16[32,3,192]{2,1,0:T(4,128)(2,1)S(1)}, bf16[32,3,192]{2,1,0:T(4,128)(2,1)S(1)}, u32[]{:S(2)}, u32[]{:S(2)}) collective-permute-start(bf16[32,3,192]{2,1,0:T(4,128)(2,1)S(1)} %copy-done.12), channel_id=1, source_target_pairs={{1,0},{2,1},{3,2},{4,3},{5,4},{6,5},{7,6},{8,7},{9,8},{10,9},{11,1... | collective-permute-start | bytes 110600 | tf_op jit(solution)/shard_map/ppermute | solution.py:533
  72.2 10.6 %collective-permute-start.3 = (bf16[32,3,192]{2,1,0:T(4,128)(2,1)S(1)}, bf16[32,3,192]{2,1,0:T(4,128)(2,1)S(1)}, u32[]{:S(2)}, u32[]{:S(2)}) collective-permute-start(bf16[32,3,192]{2,1,0:T(4,128)(2,1)S(1)} %copy-done.11), channel_id=1, source_target_pairs={{0,1},{1,2},{2,3},{3,4},{4,5},{5,6},{6,7},{7,8},{8,9},{9,10},{10,1... | collective-permute-start | bytes 110600 | tf_op jit(solution)/shard_map/ppermute | solution.py:534
  74.6 8.2 %copy-start.2 = (bf16[1,32,32,192]{3,2,1,0:T(8,128)(2,1)S(1)}, bf16[1,32,32,192]{3,2,1,0:T(8,128)(2,1)}, u32[]{:S(2)}) copy-start(bf16[1,32,32,192]{3,2,1,0:T(8,128)(2,1)} %base_ref.1) | copy-start | bytes 1179652
  74.7 8.2 %copy-start.3 = (bf16[32,32,192]{2,1,0:T(8,128)(2,1)S(1)}, bf16[32,32,192]{2,1,0:T(8,128)(2,1)}, u32[]{:S(2)}) copy-start(bf16[32,32,192]{2,1,0:T(8,128)(2,1)} %get-tuple-element.30.hidden_ref) | copy-start | bytes 1179652
  93.3 11.4 %collective-permute-start.4 = (bf16[32,3,192]{2,1,0:T(4,128)(2,1)S(1)}, bf16[32,3,192]{2,1,0:T(4,128)(2,1)S(1)}, u32[]{:S(2)}, u32[]{:S(2)}) collective-permute-start(bf16[32,3,192]{2,1,0:T(4,128)(2,1)S(1)} %get-tuple-element.51), channel_id=1, source_target_pairs={{1,0},{2,1},{3,2},{4,3},{5,4},{6,5},{7,6},{8,7},{9,8},{10,9},{11,1... | collective-permute-start | bytes 110600 | tf_op jit(solution)/shard_map/ppermute | solution.py:533
  97.4 8.9 %collective-permute-start.5 = (bf16[32,3,192]{2,1,0:T(4,128)(2,1)S(1)}, bf16[32,3,192]{2,1,0:T(4,128)(2,1)S(1)}, u32[]{:S(2)}, u32[]{:S(2)}) collective-permute-start(bf16[32,3,192]{2,1,0:T(4,128)(2,1)S(1)} %get-tuple-element.52), channel_id=1, source_target_pairs={{0,1},{1,2},{2,3},{3,4},{4,5},{5,6},{6,7},{7,8},{8,9},{9,10},{10,1... | collective-permute-start | bytes 110600 | tf_op jit(solution)/shard_map/ppermute | solution.py:534

commit v7 on v6

--- a/solution.py
+++ b/solution.py
@@ -157,9 +157,13 @@
     lax.fori_loop(0, HALF // BLK, high_block, 0)
 
 
-def pack_kernel(cell_far, count_far, value_far, error_far, out_ref, cell_ref, count_ref, value_ref, error_ref, sems):
+def pack_kernel(
+    cell_far, count_far, value_far, error_far, state_far,
+    out_ref, near_ref, cell_ref, count_ref, value_ref, error_ref, sems,
+):
     pairs = [(cell_far, cell_ref), (count_far, count_ref), (value_far, value_ref), (error_far, error_ref)]
-    for copy in fetch(pairs, sems):
+    copies = fetch(pairs + [(state_far, near_ref)], sems)
+    for copy in copies[:4]:
         copy.wait()
     member = lax.axis_index("member")
     tiles = cell_ref.shape[2]
@@ -177,18 +181,19 @@
         out_ref[:, 2 * step + 1, :] = jnp.concatenate(
             [values[:, 128:CH], turn(cells, same), turn(error_ref[step], own), turn(cells, own), jnp.zeros((tiles, CAP), f32)],
             axis=1)
-
-
-def pack_observations(cells, counts, values, errors):
+    copies[4].wait()
+
+
+def pack_observations(cells, counts, values, errors, states):
     return pl.pallas_call(
         pack_kernel,
-        out_shape=pltpu.HBM((cells.shape[2], 4, 128), f32),
-        in_specs=[HBM] * 4,
-        out_specs=VM,
+        out_shape=(pltpu.HBM((cells.shape[2], 4, 128), f32), pltpu.VMEM(states.shape, bf16)),
+        in_specs=[HBM] * 5,
+        out_specs=(VM, VM),
         scratch_shapes=[pltpu.VMEM(array.shape, array.dtype) for array in (cells, counts, values, errors)]
-        + [pltpu.SemaphoreType.DMA((4,))],
+        + [pltpu.SemaphoreType.DMA((5,))],
         compiler_params=limit(6),
-    )(far(cells), far(counts), far(values), far(errors))
+    )(far(cells), far(counts), far(values), far(errors), far(states))
 
 
 def one_hot(step, got_ref, group):
@@ -200,35 +205,35 @@
     return jnp.concatenate(rows, axis=0)
 
 
-def gather_kernel(got_ref, state_far, out_ref, state_ref, sems):
-    pairs = []
+def gather_kernel(got_ref, state_ref, out_far, out_ref, sems):
+    copies = []
     for step in range(2):
-        for half in range(2):
-            rows = slice(half * LAT // 2, (half + 1) * LAT // 2)
-            pairs.append((state_far.at[step, 0, rows], state_ref.at[step, rows]))
-    copies = fetch(pairs, sems)
-    for step in range(2):
-        hots = [one_hot(step, got_ref, group).astype(bf16) for group in range(LAT // BLK)]
         for pair in range(2):
-            copies[2 * step + pair].wait()
             found = []
             for group in (2 * pair, 2 * pair + 1):
-                field = state_ref[step, group * BLK : (group + 1) * BLK].reshape(ROWS, CH)
-                rows = jnp.dot(hots[group], field, preferred_element_type=f32)
+                field = state_ref[step, 0, group * BLK : (group + 1) * BLK].reshape(ROWS, CH)
+                hot = one_hot(step, got_ref, group).astype(bf16)
+                rows = jnp.dot(hot, field, preferred_element_type=f32)
                 found.append(rows.reshape(CAP, BLK, CH))
             both = jnp.concatenate(found, axis=1).astype(bf16)
             out_ref[:, 2 * BLK * pair : 2 * BLK * (pair + 1), step * CH : (step + 1) * CH] = both
+    for half in range(2):
+        part = slice(half * CAP // 2, (half + 1) * CAP // 2)
+        copies.append(pltpu.make_async_copy(out_ref.at[part], out_far.at[part], sems.at[half]))
+        copies[-1].start()
+    for copy in copies:
+        copy.wait()
 
 
 def gather_rows(got, states):
     return pl.pallas_call(
         gather_kernel,
-        out_shape=jax.ShapeDtypeStruct((CAP, LAT, 2 * CH), bf16),
-        in_specs=[VM, HBM],
-        scratch_shapes=[pltpu.VMEM((2, LAT, WID, CH), bf16), pltpu.SemaphoreType.DMA((4,))],
+        out_shape=pltpu.HBM((CAP, LAT, 2 * CH), bf16),
+        out_specs=HBM,
+        scratch_shapes=[pltpu.VMEM((CAP, LAT, 2 * CH), bf16), pltpu.SemaphoreType.DMA((2,))],
         compiler_params=limit(6),
         cost_estimate=pl.CostEstimate(flops=1000000, bytes_accessed=2000000, transcendentals=0),
-    )(got, far(states))
+    )(got, states)
 
 
 def departure_kernel(rows_ref, got_ref, out_ref):
@@ -409,22 +414,23 @@
 
 
 def second_kernel(
-    partial_ref, rows_ref, hot_ref, slope_ref, unit_far, gain_ref, up_ref, down_far,
+    partial_ref, rows_ref, cell_ref, slope_ref, unit_far, gain_ref, up_ref, down_far,
     hidden_out, tail_out, head_out, adjoint_out, unit_ref, down_ref, sems,
 ):
     copies = fetch([(down_far, down_ref), (unit_far, unit_ref)], sems)
     gain = gain_ref[...]
     for group in range(LAT // BLK):
         first = group * BLK
-        rows = slice(group * ROWS, (group + 1) * ROWS)
-        forcing = forcing_of(0, rows_ref, hot_ref, group)
+        forcing = forcing_of(0, rows_ref, cell_ref, group)
         adjoint = (partial_ref[first : first + BLK].reshape(ROWS, CH) + forcing).astype(bf16)
         adjoint_out[first : first + BLK] = adjoint.reshape(BLK, WID, CH)
-        if group == 0:
-            for copy in copies:
-                copy.wait()
+    for copy in copies:
+        copy.wait()
+    for group in range(LAT // BLK):
+        first = group * BLK
+        rows = slice(group * ROWS, (group + 1) * ROWS)
         result = backward(
-            adjoint,
+            adjoint_out[first : first + BLK].reshape(ROWS, CH),
             lambda cols: slope_ref[rows, cols].astype(f32),
             down_ref, up_ref, gain,
             unit_ref[rows, :].astype(f32),
@@ -475,53 +481,61 @@
     )(hidden, adjoint, rows, hot, kernel)
 
 
-def edge_kernel(inner_ref, west_ref, east_ref, right_ref, left_ref, kernel_ref, out_ref, shifts, padded):
-    def side(halo_ref, strip_ref, place, offset, cols):
-        clear_rims(shifts, 3, 8)
-        padded[...] = jnp.zeros(padded.shape, f32)
-
-        def some_rows(index, carry):
-            for lane in range(BLK):
-                padded[lane, place : place + 3] = halo_ref[index * BLK + lane].astype(f32)
-            for lane in range(BLK):
-                for col in range(3):
-                    shifts[col, index * BLK + lane + 3] = padded[lane, col + offset : col + offset + 8]
-            return carry
-
-        lax.fori_loop(0, LAT // BLK, some_rows, 0)
-
-        def block(index, carry):
-            first = index * BLK
-
-            for low, high in ((0, 128), (128, CH)):
-                sums = block_sums(shifts, first, tap_of(kernel_ref, True, slice(low, high), 8), cols, slice(low, high))
-                for target in range(BLK):
-                    value = strip_ref[first + target, :, low:high] + sums[target]
-                    out_ref[first + target, :, low:high] = value.astype(bf16)
-            return carry
-
-        lax.fori_loop(0, LAT // BLK, block, 0)
-
-    @pl.when(pl.program_id(0) == 0)
-    def _():
-        side(left_ref, west_ref, 0, 0, range(0, 3))
-
-    @pl.when(pl.program_id(0) == 1)
-    def _():
-        side(right_ref, east_ref, 8, 1, range(4, 7))
+def edge_kernel(
+    inner_ref, west_ref, east_ref, right_ref, left_ref, kernel_ref, out_ref,
+    shifts, padded, taps, strips, sems,
+):
+    clear_rims(shifts, 3, 8)
+    padded[...] = jnp.zeros(padded.shape, f32)
+    west_side = lax.broadcasted_iota(jnp.int32, (8, CH), 0) < 4
+    for row in range(7):
+        for turn in range(3):
+            first = jnp.broadcast_to(kernel_ref[6 - row, 6 - turn : 7 - turn, :], (8, CH))
+            last = jnp.broadcast_to(kernel_ref[6 - row, 2 - turn : 3 - turn, :], (8, CH))
+            taps[turn, row] = jnp.where(west_side, first, last)
+
+    def some_rows(index, carry):
+        for lane in range(BLK):
+            padded[lane, 0:3] = left_ref[index * BLK + lane].astype(f32)
+            padded[lane, 7:10] = right_ref[index * BLK + lane].astype(f32)
+        for lane in range(BLK):
+            for turn in range(3):
+                shifts[turn, index * BLK + lane + 3] = padded[lane, turn : turn + 8]
+        return carry
+
+    lax.fori_loop(0, LAT // BLK, some_rows, 0)
+
+    def block(index, carry):
+        first = index * BLK
+        for low, high in ((0, 128), (128, CH)):
+            lanes = slice(low, high)
+            sums = block_sums(shifts, first, lambda row, turn: taps[turn, row, :, lanes], range(3), lanes)
+            side = west_side[:, lanes]
+            for target in range(BLK):
+                west = west_ref[first + target, :, lanes] + jnp.where(side, sums[target], 0.0)
+                east = east_ref[first + target, :, lanes] + jnp.where(side, 0.0, sums[target])
+                strips[0, first + target, :, lanes] = west.astype(bf16)
+                strips[1, first + target, :, lanes] = east.astype(bf16)
+        return carry
+
+    lax.fori_loop(0, LAT // BLK, block, 0)
+    places = [(strips.at[0], out_ref.at[:, 0:8]), (strips.at[1], out_ref.at[:, WID - 8 : WID])]
+    for copy in fetch(places, sems):
+        copy.wait()
 
 
 def finish_edges(inner, west, east, left, right, kernel):
-    whole = lambda array: pl.BlockSpec(array.shape, lambda i: (0,) * array.ndim)
     return pl.pallas_call(
         edge_kernel,
-        grid=(2,),
-        in_specs=[pl.BlockSpec(memory_space=pl.ANY)] + [whole(x) for x in (west, east, right, left, kernel)],
-        out_specs=pl.BlockSpec((LAT, 8, CH), lambda i: (0, 3 * i, 0)),
+        in_specs=[pl.BlockSpec(memory_space=pl.ANY)] + [VM] * 5,
+        out_specs=pl.BlockSpec(memory_space=pl.ANY),
         out_shape=FIELD,
         input_output_aliases={0: 0},
         compiler_params=limit(4),
-        scratch_shapes=[pltpu.VMEM((3, LAT + 6, 8, CH), f32), pltpu.VMEM((BLK, 16, CH), f32)],
+        scratch_shapes=[
+            pltpu.VMEM((3, LAT + 6, 8, CH), f32), pltpu.VMEM((BLK, 16, CH), f32), pltpu.VMEM((3, 7, 8, CH), f32),
+            pltpu.VMEM((2, LAT, 8, CH), bf16), pltpu.SemaphoreType.DMA((2,)),
+        ],
         cost_estimate=pl.CostEstimate(flops=5000000, bytes_accessed=700000, transcendentals=0),
     )(inner, west, east, right, left, kernel)
 
@@ -551,11 +565,11 @@
     bias = up_bias[None]
     down = down_weight.T
 
-    packed = pack_observations(
-        obs_cell[:, 0].transpose(0, 2, 1), obs_count, obs_value, obs_error[:, 0].transpose(0, 2, 1)
+    packed, near = pack_observations(
+        obs_cell[:, 0].transpose(0, 2, 1), obs_count, obs_value, obs_error[:, 0].transpose(0, 2, 1), states
     )
     got = exchange(packed, "tile")
-    rows = gather_rows(got, states)
+    rows = gather_rows(got, near)
     owned = exchange(rows, "member")
 
     source = after(states, rows)[:, 0]

time: 109 us -> 107 us (0.982)
  Pallas kernels: 38.7 us -> 37.2 us
    pallas_call x3, Pallas kernels: 7.27 us -> 5.97 us  [the longest x1 2.46 us: gather_rows(): pl.pallas_call(gather_kernel, out_shape=pltpu.HBM((CAP, LAT, 2 * CH), bf1...]
where the time goes in v7:
time: 107 us
  starting transfers between devices  41.3 us (39%)
  Pallas kernels  37.2 us (35%)
  blocking collectives  15 us (14%)
  waiting for transfers between devices  12.7 us (12%)
    all_to_all x2, starting transfers between devices, exchange(): return lax.all_to_all(array, axis, split_axis=0, concat_axis=0, tiled=True)  26.2 us
    pallas_call x2, Pallas kernels, forward(): pl.pallas_call(functools.partial(forward_kernel, step), out_shape=shapes,...  16.8 us
    all_to_all x1, blocking collectives, exchange(): return lax.all_to_all(array, axis, split_axis=0, concat_axis=0, tiled=True)  15 us
    ppermute x3, starting transfers between devices, swap_edges(): right = lax.ppermute(head, 'tile', down)  8.83 us
    ppermute x3, waiting for transfers between devices, swap_edges(): left = lax.ppermute(tail, 'tile', up)  8.65 us
    ppermute x3, starting transfers between devices, swap_edges(): left = lax.ppermute(tail, 'tile', up)  6.25 us
    pallas_call x1, Pallas kernels, interior(): pl.pallas_call(interior_kernel, out_shape=(FIELD, STRIP, STRIP), scratch_...  5.43 us
    pallas_call x1, Pallas kernels, spread_back(): pl.pallas_call(spread_kernel, out_shape=(jax.ShapeDtypeStruct((LAT, WID,...  5.33 us
  transfers between devices with their start and end apart: 8, of which 5 were waited for; matrix products, arithmetic and copies ran while one was open for 0% of the time, Pallas kernels for 26%

profile of v7, /device:TPU:32, one launch (start us, length us, event | category | flops | bytes accessed | tf_op | source)
XLA Modules:
  0.0 106.6 jit_solution(5636190316287489519)
XLA Ops:
  0.0 2.1 %shard_map.109 = (f32[32,4,128]{2,1,0:T(4,128)}, bf16[2,1,32,32,192]{4,3,2,1,0:T(8,128)(2,1)S(1)}) custom-call(s32[2,16,32]{2,1,0:T(8,128)} %bitcast.16, s32[2,1,32]{2,1,0:T(1,128)} %count_far.1, bf16[2,1,32,16,192]{4,3,2,1,0:T(8,128)(2,1)} %value_far.1, bf16[2,16,32]{2,1,0:T(8,128)(2,1)} %bitcast.17, bf16[2,1,32,32,192]{4,3,2,1,0:T(8,128)(2,1)} %state_ref.2), custom_call_target="tpu_custom_call" | custom-call | tf_op jit(solution)/shard_map/pallas_call | solution.py:188
  2.2 0.0 copy-start
  2.2 0.0 copy-start.10
  2.2 0.0 copy-start.1
  2.2 0.0 copy-start.4
  2.2 0.0 copy-start.5
  2.2 0.0 copy-start.6
  2.2 0.0 copy-start.7
  2.2 15.0 %all_to_all.15.got_ref = f32[32,4,128]{2,1,0:T(4,128)S(1)} all-to-all(f32[32,4,128]{2,1,0:T(4,128)} %get-tuple-element.31), channel_id=1, replica_groups=mesh['member'=16,'tile'=32] {'tile'}, dimensions={0} | all-to-all | bytes 131072 | tf_op jit(solution)/shard_map/all_to_all | solution.py:557
  17.2 2.5 %shard_map.110 = bf16[16,32,384]{2,1,0:T(8,128)(2,1)} custom-call(f32[32,4,128]{2,1,0:T(4,128)S(1)} %all_to_all.15.got_ref, bf16[2,1,32,32,192]{4,3,2,1,0:T(8,128)(2,1)S(1)} %get-tuple-element.32.state_ref), custom_call_target="tpu_custom_call" | custom-call | flops 1000000 | bytes 2000000 | tf_op jit(solution)/shard_map/pallas_call | solution.py:229
  19.7 15.2 %all-to-all-start.1 = ((bf16[16,32,384]{2,1,0:T(8,128)(2,1)}), bf16[16,32,384]{2,1,0:T(8,128)(2,1)S(1)}, u32[]{:S(2)}, u32[]{:S(2)}) async-start(bf16[16,32,384]{2,1,0:T(8,128)(2,1)} %shard_map.110), calls=%async_computation.1 | async-start | bytes 786432 | tf_op jit(solution)/shard_map/all_to_all | solution.py:557
  34.9 0.0 copy-done
  34.9 0.1 fusion
  35.0 2.9 %collective-permute-start.1 = (bf16[2,32,3,192]{3,2,1,0:T(4,128)(2,1)S(1)}, bf16[2,32,3,192]{3,2,1,0:T(4,128)(2,1)S(1)}, u32[]{:S(2)}, u32[]{:S(2)}) collective-permute-start(bf16[2,32,3,192]{3,2,1,0:T(4,128)(2,1)S(1)} %get-tuple-element.57), channel_id=1, source_target_pairs={{1,0},{2,1},{3,2},{4,3},{5,4},{6,5},{7,6},{8,7},{9,8},{10,9},{11,1... | collective-permute-start | bytes 221192 | tf_op jit(solution)/shard_map/ppermute | solution.py:547
  37.9 1.9 %collective-permute-start = (bf16[2,32,3,192]{3,2,1,0:T(4,128)(2,1)S(1)}, bf16[2,32,3,192]{3,2,1,0:T(4,128)(2,1)S(1)}, u32[]{:S(2)}, u32[]{:S(2)}) collective-permute-start(bf16[2,32,3,192]{3,2,1,0:T(4,128)(2,1)S(1)} %get-tuple-element.58), channel_id=1, source_target_pairs={{0,1},{1,2},{2,3},{3,4},{4,5},{5,6},{6,7},{7,8},{8,9},{9,10},{10,1... | collective-permute-start | bytes 221192 | tf_op jit(solution)/shard_map/ppermute | solution.py:548
  39.8 0.0 copy-done.10
  39.8 0.5 collective-permute-done.1.right_ref
  40.4 7.1 %collective-permute-done.left_ref = bf16[2,32,3,192]{3,2,1,0:T(4,128)(2,1)S(1)} collective-permute-done((bf16[2,32,3,192]{3,2,1,0:T(4,128)(2,1)S(1)}, bf16[2,32,3,192]{3,2,1,0:T(4,128)(2,1)S(1)}, u32[]{:S(2)}, u32[]{:S(2)}) %collective-permute-start) | collective-permute-done | bytes 73760 | tf_op jit(solution)/shard_map/ppermute | solution.py:548
  47.5 0.0 copy-done.1
  47.5 0.0 copy-done.4
  47.5 0.0 copy-done.5
  47.5 0.0 copy-done.6
  47.5 0.0 copy-done.7
  47.5 8.7 %shard_map.111 = (bf16[32,32,192]{2,1,0:T(8,128)(2,1)}, bf16[32,3,192]{2,1,0:T(4,128)(2,1)}, bf16[32,3,192]{2,1,0:T(4,128)(2,1)}, bf16[32,3,192]{2,1,0:T(4,128)(2,1)}, bf16[32,3,192]{2,1,0:T(4,128)(2,1)}) custom-call(bf16[2,1,32,32,192]{4,3,2,1,0:T(8,128)(2,1)S(1)} %copy-done, bf16[2,32,3,192]{3,2,1,0:T(4,128)(2,1)S(1)} %collective-permute-done.left_ref, ...), custom_call_target="tpu_custom_call" | custom-call | flops 905969664 | bytes 8000000 | tf_op jit(solution)/shard_map/pallas_call | solution.py:366
  56.2 0.0 copy-start.12
  56.2 0.0 copy-start.11
  56.2 0.0 copy-start.8
  56.2 0.0 copy-start.9
  56.2 1.0 all-to-all-done.1.rows_ref
  57.3 1.2 %shard_map.112 = bf16[16,32,384]{2,1,0:T(8,128)(2,1)} custom-call(bf16[16,32,384]{2,1,0:T(8,128)(2,1)S(1)} %all-to-all-done.1.rows_ref, f32[32,4,128]{2,1,0:T(4,128)S(1)} %all_to_all.15.got_ref), custom_call_target="tpu_custom_call" | custom-call | flops 1200000 | bytes 1200000 | tf_op jit(solution)/shard_map/pallas_call | solution.py:255
  58.4 11.0 %all-to-all-start.2 = ((bf16[16,32,384]{2,1,0:T(8,128)(2,1)}), bf16[16,32,384]{2,1,0:T(8,128)(2,1)S(1)}, u32[]{:S(2)}, u32[]{:S(2)}) async-start(bf16[16,32,384]{2,1,0:T(8,128)(2,1)} %shard_map.112), calls=%async_computation.2 | async-start | bytes 786432 | tf_op jit(solution)/shard_map/all_to_all | solution.py:557
  69.4 0.0 copy-done.12
  69.5 1.9 %collective-permute-start.2 = (bf16[32,3,192]{2,1,0:T(4,128)(2,1)S(1)}, bf16[32,3,192]{2,1,0:T(4,128)(2,1)S(1)}, u32[]{:S(2)}, u32[]{:S(2)}) collective-permute-start(bf16[32,3,192]{2,1,0:T(4,128)(2,1)S(1)} %copy-done.12), channel_id=1, source_target_pairs={{1,0},{2,1},{3,2},{4,3},{5,4},{6,5},{7,6},{8,7},{9,8},{10,9},{11,1... | collective-permute-start | bytes 110600 | tf_op jit(solution)/shard_map/ppermute | solution.py:547
  71.4 0.0 copy-done.11
  71.4 2.4 %collective-permute-start.3 = (bf16[32,3,192]{2,1,0:T(4,128)(2,1)S(1)}, bf16[32,3,192]{2,1,0:T(4,128)(2,1)S(1)}, u32[]{:S(2)}, u32[]{:S(2)}) collective-permute-start(bf16[32,3,192]{2,1,0:T(4,128)(2,1)S(1)} %copy-done.11), channel_id=1, source_target_pairs={{0,1},{1,2},{2,3},{3,4},{4,5},{5,6},{6,7},{7,8},{8,9},{9,10},{10,1... | collective-permute-start | bytes 110600 | tf_op jit(solution)/shard_map/ppermute | solution.py:548
  73.8 0.0 copy-done.8
  73.8 0.0 copy-done.9
  73.8 0.0 copy-start.2
  73.8 0.0 copy-start.3
  73.9 8.1 %shard_map.113 = (bf16[1024,768]{1,0:T(8,128)(2,1)}, bf16[1024,192]{1,0:T(8,128)(2,1)}) custom-call(bf16[2,1,32,32,192]{4,3,2,1,0:T(8,128)(2,1)S(1)} %copy-done, bf16[32,3,192]{2,1,0:T(4,128)(2,1)S(1)} %copy-done.9, bf16[32,3,192]{2,1,0:T(4,128)(2,1)S(1)} %copy-done.8, f32[7,7,192]{2,1,0:T(8,128)S(1)} %copy-done.4, f32[1,192]{1,0:T(1,128)S(1)} %bitcast.14, ...), custom_call_target="tpu_custom_call" | custom-call | flops 905969664 | bytes 8000000 | tf_op jit(solution)/shard_map/pallas_call | solution.py:366
  82.0 0.0 collective-permute-done.2.right_ref
  82.0 0.0 collective-permute-done.3.left_ref
  82.0 0.0 copy-done.2
  82.0 0.0 copy-done.3
  82.0 5.3 %shard_map.114 = (f32[32,32,192]{2,1,0:T(8,128)S(1)}, bf16[1024,768]{1,0:T(8,128)(2,1)S(1)}, f32[8,128]{1,0:T(8,128)S(1)}) custom-call(bf16[32,32,192]{2,1,0:T(8,128)(2,1)S(1)} %copy-done.3, bf16[32,3,192]{2,1,0:T(4,128)(2,1)S(1)} %collective-permute-done.2.right_ref, bf16[32,3,192]{2,1,0:T(4,128)(2,1)S(1)} %collective-permute-done.3.left_ref, ...), custom_call_target="tpu_custom_call" | custom-call | flops 19267584 | bytes 3000000 | tf_op jit(solution)/shard_map/pallas_call | solution.py:402
  87.3 2.4 %all-to-all-done.2.rows_ref = bf16[16,32,384]{2,1,0:T(8,128)(2,1)S(1)} async-done(((bf16[16,32,384]{2,1,0:T(8,128)(2,1)}), bf16[16,32,384]{2,1,0:T(8,128)(2,1)S(1)}, u32[]{:S(2)}, u32[]{:S(2)}) %all-to-all-start.2) | async-done | bytes 393248 | tf_op jit(solution)/shard_map/all_to_all | solution.py:557
  89.8 2.4 %shard_map.115 = (bf16[32,32,192]{2,1,0:T(8,128)(2,1)S(1)}, bf16[32,3,192]{2,1,0:T(4,128)(2,1)S(1)}, bf16[32,3,192]{2,1,0:T(4,128)(2,1)S(1)}, bf16[32,32,192]{2,1,0:T(8,128)(2,1)S(1)}) custom-call(f32[32,32,192]{2,1,0:T(8,128)S(1)} %get-tuple-element.45.partial_ref, bf16[16,32,384]{2,1,0:T(8,128)(2,1)S(1)} %all-to-all-done.2.rows_ref, ...), custom_call_target="tpu_custom_call" | custom-call | flops 603979776 | bytes 5000000 | tf_op jit(solution)/shard_map/pallas_call | solution.py:442
  92.2 4.1 %collective-permute-start.4 = (bf16[32,3,192]{2,1,0:T(4,128)(2,1)S(1)}, bf16[32,3,192]{2,1,0:T(4,128)(2,1)S(1)}, u32[]{:S(2)}, u32[]{:S(2)}) collective-permute-start(bf16[32,3,192]{2,1,0:T(4,128)(2,1)S(1)} %get-tuple-element.55), channel_id=1, source_target_pairs={{1,0},{2,1},{3,2},{4,3},{5,4},{6,5},{7,6},{8,7},{9,8},{10,9},{11,1... | collective-permute-start | bytes 110600 | tf_op jit(solution)/shard_map/ppermute | solution.py:547
  96.3 1.9 %collective-permute-start.5 = (bf16[32,3,192]{2,1,0:T(4,128)(2,1)S(1)}, bf16[32,3,192]{2,1,0:T(4,128)(2,1)S(1)}, u32[]{:S(2)}, u32[]{:S(2)}) collective-permute-start(bf16[32,3,192]{2,1,0:T(4,128)(2,1)S(1)} %get-tuple-element.56), channel_id=1, source_target_pairs={{0,1},{1,2},{2,3},{3,4},{4,5},{5,6},{6,7},{7,8},{8,9},{9,10},{10,1... | collective-permute-start | bytes 110600 | tf_op jit(solution)/shard_map/ppermute | solution.py:548
  98.2 5.4 %shard_map.116 = (bf16[32,32,192]{2,1,0:T(8,128)(2,1)}, f32[32,8,192]{2,1,0:T(8,128)S(1)}, f32[32,8,192]{2,1,0:T(8,128)S(1)}) custom-call(bf16[32,32,192]{2,1,0:T(8,128)(2,1)S(1)} %get-tuple-element.50.hidden_ref, bf16[32,32,192]{2,1,0:T(8,128)(2,1)S(1)} %get-tuple-element.51.adjoint_ref, bf16[16,32,384]{2,1,0:T(8,128)(2,1)S(1)} %all-to-all-done.2.rows_ref, ...), custom_call_target="tpu_custom_call" | custom-call | flops 19267584 | bytes 3000000 | tf_op jit(solution)/shard_map/pallas_call | solution.py:475
  103.6 0.0 collective-permute-done.4.right_ref
  103.6 1.5 %collective-permute-done.5.left_ref = bf16[32,3,192]{2,1,0:T(4,128)(2,1)S(1)} collective-permute-done((bf16[32,3,192]{2,1,0:T(4,128)(2,1)S(1)}, bf16[32,3,192]{2,1,0:T(4,128)(2,1)S(1)}, u32[]{:S(2)}, u32[]{:S(2)}) %collective-permute-start.5) | collective-permute-done | bytes 36896 | tf_op jit(solution)/shard_map/ppermute | solution.py:548
  105.2 1.4 %shard_map.117 = bf16[32,32,192]{2,1,0:T(8,128)(2,1)} custom-call(bf16[32,32,192]{2,1,0:T(8,128)(2,1)} %get-tuple-element.52.inner_ref, f32[32,8,192]{2,1,0:T(8,128)S(1)} %get-tuple-element.53.west_ref, f32[32,8,192]{2,1,0:T(8,128)S(1)} %get-tuple-element.54.east_ref, ...), custom_call_target="tpu_custom_call", output_to_operand_aliasing={{}: (0, {})} | custom-call | flops 5000000 | bytes 700000 | tf_op jit(solution)/shard_map/pallas_call | solution.py:528
  (1 shorter events, 0.0 us)
Async XLA Ops:
  2.2 32.8 %copy-start = (bf16[2,1,32,32,192]{4,3,2,1,0:T(8,128)(2,1)S(1)}, bf16[2,1,32,32,192]{4,3,2,1,0:T(8,128)(2,1)}, u32[]{:S(2)}) copy-start(bf16[2,1,32,32,192]{4,3,2,1,0:T(8,128)(2,1)} %state_ref.2) | copy-start | bytes 2359300
  2.2 37.7 %copy-start.10 = (f32[768]{0:T(1024)S(1)}, f32[768]{0:T(1024)}, u32[]{:S(2)}) copy-start(f32[768]{0:T(1024)} %param.16) | copy-start | bytes 9220
  2.2 45.3 %copy-start.1 = (bf16[1,32,32,192]{3,2,1,0:T(8,128)(2,1)S(1)}, bf16[1,32,32,192]{3,2,1,0:T(8,128)(2,1)}, u32[]{:S(2)}) copy-start(bf16[1,32,32,192]{3,2,1,0:T(8,128)(2,1)} %base_ref.1) | copy-start | bytes 1179652
  2.2 45.3 %copy-start.4 = (f32[7,7,192]{2,1,0:T(8,128)S(1)}, f32[7,7,192]{2,1,0:T(8,128)}, u32[]{:S(2)}) copy-start(f32[7,7,192]{2,1,0:T(8,128)} %kernel_ref.9) | copy-start | bytes 112900
  2.2 45.3 %copy-start.5 = (bf16[192,768]{1,0:T(8,128)(2,1)S(1)}, bf16[192,768]{1,0:T(8,128)(2,1)}, u32[]{:S(2)}) copy-start(bf16[192,768]{1,0:T(8,128)(2,1)} %up_ref.5) | copy-start | bytes 884740
  2.2 45.3 %copy-start.6 = (bf16[768,192]{0,1:T(8,128)(2,1)S(1)}, bf16[768,192]{0,1:T(8,128)(2,1)}, u32[]{:S(2)}) copy-start(bf16[768,192]{0,1:T(8,128)(2,1)} %param.17) | copy-start | bytes 884740
  2.2 45.3 %copy-start.7 = (f32[192]{0:T(256)S(1)}, f32[192]{0:T(256)}, u32[]{:S(2)}) copy-start(f32[192]{0:T(256)} %param.14) | copy-start | bytes 2308
  19.7 37.6 %all-to-all-start.1 = ((bf16[16,32,384]{2,1,0:T(8,128)(2,1)}), bf16[16,32,384]{2,1,0:T(8,128)(2,1)S(1)}, u32[]{:S(2)}, u32[]{:S(2)}) async-start(bf16[16,32,384]{2,1,0:T(8,128)(2,1)} %shard_map.110), calls=%async_computation.1 | async-start | bytes 786432 | tf_op jit(solution)/shard_map/all_to_all | solution.py:557
  35.0 5.4 %collective-permute-start.1 = (bf16[2,32,3,192]{3,2,1,0:T(4,128)(2,1)S(1)}, bf16[2,32,3,192]{3,2,1,0:T(4,128)(2,1)S(1)}, u32[]{:S(2)}, u32[]{:S(2)}) collective-permute-start(bf16[2,32,3,192]{3,2,1,0:T(4,128)(2,1)S(1)} %get-tuple-element.57), channel_id=1, source_target_pairs={{1,0},{2,1},{3,2},{4,3},{5,4},{6,5},{7,6},{8,7},{9,8},{10,9},{11,1... | collective-permute-start | bytes 221192 | tf_op jit(solution)/shard_map/ppermute | solution.py:547
  37.9 9.6 %collective-permute-start = (bf16[2,32,3,192]{3,2,1,0:T(4,128)(2,1)S(1)}, bf16[2,32,3,192]{3,2,1,0:T(4,128)(2,1)S(1)}, u32[]{:S(2)}, u32[]{:S(2)}) collective-permute-start(bf16[2,32,3,192]{3,2,1,0:T(4,128)(2,1)S(1)} %get-tuple-element.58), channel_id=1, source_target_pairs={{0,1},{1,2},{2,3},{3,4},{4,5},{5,6},{6,7},{7,8},{8,9},{9,10},{10,1... | collective-permute-start | bytes 221192 | tf_op jit(solution)/shard_map/ppermute | solution.py:548
  56.2 13.2 %copy-start.12 = (bf16[32,3,192]{2,1,0:T(4,128)(2,1)S(1)}, bf16[32,3,192]{2,1,0:T(4,128)(2,1)}, u32[]{:S(2)}) copy-start(bf16[32,3,192]{2,1,0:T(4,128)(2,1)} %get-tuple-element.38) | copy-start | bytes 110596
  56.2 15.2 %copy-start.11 = (bf16[32,3,192]{2,1,0:T(4,128)(2,1)S(1)}, bf16[32,3,192]{2,1,0:T(4,128)(2,1)}, u32[]{:S(2)}) copy-start(bf16[32,3,192]{2,1,0:T(4,128)(2,1)} %get-tuple-element.44) | copy-start | bytes 110596
  56.2 17.6 %copy-start.8 = (bf16[32,3,192]{2,1,0:T(4,128)(2,1)S(1)}, bf16[32,3,192]{2,1,0:T(4,128)(2,1)}, u32[]{:S(2)}) copy-start(bf16[32,3,192]{2,1,0:T(4,128)(2,1)} %get-tuple-element.41.right_ref) | copy-start | bytes 110596
  56.2 17.6 %copy-start.9 = (bf16[32,3,192]{2,1,0:T(4,128)(2,1)S(1)}, bf16[32,3,192]{2,1,0:T(4,128)(2,1)}, u32[]{:S(2)}) copy-start(bf16[32,3,192]{2,1,0:T(4,128)(2,1)} %get-tuple-element.40.left_ref) | copy-start | bytes 110596
  58.4 31.3 %all-to-all-start.2 = ((bf16[16,32,384]{2,1,0:T(8,128)(2,1)}), bf16[16,32,384]{2,1,0:T(8,128)(2,1)S(1)}, u32[]{:S(2)}, u32[]{:S(2)}) async-start(bf16[16,32,384]{2,1,0:T(8,128)(2,1)} %shard_map.112), calls=%async_computation.2 | async-start | bytes 786432 | tf_op jit(solution)/shard_map/all_to_all | solution.py:557
  69.5 12.5 %collective-permute-start.2 = (bf16[32,3,192]{2,1,0:T(4,128)(2,1)S(1)}, bf16[32,3,192]{2,1,0:T(4,128)(2,1)S(1)}, u32[]{:S(2)}, u32[]{:S(2)}) collective-permute-start(bf16[32,3,192]{2,1,0:T(4,128)(2,1)S(1)} %copy-done.12), channel_id=1, source_target_pairs={{1,0},{2,1},{3,2},{4,3},{5,4},{6,5},{7,6},{8,7},{9,8},{10,9},{11,1... | collective-permute-start | bytes 110600 | tf_op jit(solution)/shard_map/ppermute | solution.py:547
  71.4 10.6 %collective-permute-start.3 = (bf16[32,3,192]{2,1,0:T(4,128)(2,1)S(1)}, bf16[32,3,192]{2,1,0:T(4,128)(2,1)S(1)}, u32[]{:S(2)}, u32[]{:S(2)}) collective-permute-start(bf16[32,3,192]{2,1,0:T(4,128)(2,1)S(1)} %copy-done.11), channel_id=1, source_target_pairs={{0,1},{1,2},{2,3},{3,4},{4,5},{5,6},{6,7},{7,8},{8,9},{9,10},{10,1... | collective-permute-start | bytes 110600 | tf_op jit(solution)/shard_map/ppermute | solution.py:548
  73.8 8.2 %copy-start.2 = (bf16[1,32,32,192]{3,2,1,0:T(8,128)(2,1)S(1)}, bf16[1,32,32,192]{3,2,1,0:T(8,128)(2,1)}, u32[]{:S(2)}) copy-start(bf16[1,32,32,192]{3,2,1,0:T(8,128)(2,1)} %base_ref.1) | copy-start | bytes 1179652
  73.8 8.2 %copy-start.3 = (bf16[32,32,192]{2,1,0:T(8,128)(2,1)S(1)}, bf16[32,32,192]{2,1,0:T(8,128)(2,1)}, u32[]{:S(2)}) copy-start(bf16[32,32,192]{2,1,0:T(8,128)(2,1)} %get-tuple-element.34.hidden_ref) | copy-start | bytes 1179652
  92.2 11.4 %collective-permute-start.4 = (bf16[32,3,192]{2,1,0:T(4,128)(2,1)S(1)}, bf16[32,3,192]{2,1,0:T(4,128)(2,1)S(1)}, u32[]{:S(2)}, u32[]{:S(2)}) collective-permute-start(bf16[32,3,192]{2,1,0:T(4,128)(2,1)S(1)} %get-tuple-element.55), channel_id=1, source_target_pairs={{1,0},{2,1},{3,2},{4,3},{5,4},{6,5},{7,6},{8,7},{9,8},{10,9},{11,1... | collective-permute-start | bytes 110600 | tf_op jit(solution)/shard_map/ppermute | solution.py:547
  96.3 8.9 %collective-permute-start.5 = (bf16[32,3,192]{2,1,0:T(4,128)(2,1)S(1)}, bf16[32,3,192]{2,1,0:T(4,128)(2,1)S(1)}, u32[]{:S(2)}, u32[]{:S(2)}) collective-permute-start(bf16[32,3,192]{2,1,0:T(4,128)(2,1)S(1)} %get-tuple-element.56), channel_id=1, source_target_pairs={{0,1},{1,2},{2,3},{3,4},{4,5},{5,6},{6,7},{7,8},{8,9},{9,10},{10,1... | collective-permute-start | bytes 110600 | tf_op jit(solution)/shard_map/ppermute | solution.py:548

commit v8 on v7

--- a/solution.py
+++ b/solution.py
@@ -133,7 +133,7 @@
     return tap
 
 
-def convolve(low, high, twice, kernel_ref, flip, emit):
+def convolve(low, high, twice, kernel_ref, flip, emit, done=None):
     for row in range(7):
         upper = kernel_ref[row, :, 128:CH]
         twice[row, 0:7] = jnp.concatenate([upper, upper], axis=1)
@@ -151,6 +151,8 @@
         for target in range(BLK):
             emit(first + target, 128, CH, sums[target][:, 0:64])
             emit(first + target + HALF, 128, CH, sums[target][:, 64:128])
+        if done is not None:
+            done(index)
         return carry
 
     lax.fori_loop(0, LAT // BLK, low_block, 0)
@@ -187,7 +189,7 @@
 def pack_observations(cells, counts, values, errors, states):
     return pl.pallas_call(
         pack_kernel,
-        out_shape=(pltpu.HBM((cells.shape[2], 4, 128), f32), pltpu.VMEM(states.shape, bf16)),
+        out_shape=(jax.ShapeDtypeStruct((cells.shape[2], 4, 128), f32), pltpu.VMEM(states.shape, bf16)),
         in_specs=[HBM] * 5,
         out_specs=(VM, VM),
         scratch_shapes=[pltpu.VMEM(array.shape, array.dtype) for array in (cells, counts, values, errors)]
@@ -217,10 +219,10 @@
                 found.append(rows.reshape(CAP, BLK, CH))
             both = jnp.concatenate(found, axis=1).astype(bf16)
             out_ref[:, 2 * BLK * pair : 2 * BLK * (pair + 1), step * CH : (step + 1) * CH] = both
-    for half in range(2):
-        part = slice(half * CAP // 2, (half + 1) * CAP // 2)
-        copies.append(pltpu.make_async_copy(out_ref.at[part], out_far.at[part], sems.at[half]))
-        copies[-1].start()
+            if step == 1:
+                part = slice(2 * BLK * pair, 2 * BLK * (pair + 1))
+                copies.append(pltpu.make_async_copy(out_ref.at[:, part], out_far.at[:, part], sems.at[pair]))
+                copies[-1].start()
     for copy in copies:
         copy.wait()
 
@@ -236,25 +238,36 @@
     )(got, states)
 
 
-def departure_kernel(rows_ref, got_ref, out_ref):
+def departure_kernel(rows_ref, got_ref, out_far, out_ref, sems):
+    stats = []
     for step in range(2):
-        lanes = slice(step * CH, (step + 1) * CH)
-        sampled = rows_ref[:, :, lanes].astype(f32)
+        sampled = rows_ref[:, :, step * CH : (step + 1) * CH].astype(f32)
         members = sampled.shape[0]
         other = got_ref[:, 2 * step + 1, :]
         values = jnp.concatenate([got_ref[:, 2 * step, :], other[:, 0:64]], axis=1)
         ens_mean = jnp.sum(sampled, axis=0) * (1.0 / members)
         ens_var = jnp.sum(sampled * sampled, axis=0) * (1.0 / members) - ens_mean * ens_mean
         weight = 1.0 / (other[:, 64 + CAP : 65 + CAP] + ens_var)
-        ratio = (sampled - values[None]) * weight[None]
-        live = other[:, 64 + 2 * CAP : 65 + 2 * CAP] >= 0.0
-        out_ref[:, :, lanes] = jnp.where(live[None], ratio, 0.0).astype(bf16)
+        stats.append((values, weight, other[:, 64 + 2 * CAP : 65 + 2 * CAP] >= 0.0))
+    copies = []
+    for half in range(2):
+        part = slice(half * CAP // 2, (half + 1) * CAP // 2)
+        for step, (values, weight, live) in enumerate(stats):
+            lanes = slice(step * CH, (step + 1) * CH)
+            ratio = (rows_ref[part, :, lanes].astype(f32) - values[None]) * weight[None]
+            out_ref[part, :, lanes] = jnp.where(live[None], ratio, 0.0).astype(bf16)
+        copies.append(pltpu.make_async_copy(out_ref.at[part], out_far.at[part], sems.at[half]))
+        copies[-1].start()
+    for copy in copies:
+        copy.wait()
 
 
 def departures(rows, got):
     return pl.pallas_call(
         departure_kernel,
-        out_shape=jax.ShapeDtypeStruct((CAP, LAT, 2 * CH), bf16),
+        out_shape=pltpu.HBM((CAP, LAT, 2 * CH), bf16),
+        out_specs=HBM,
+        scratch_shapes=[pltpu.VMEM((CAP, LAT, 2 * CH), bf16), pltpu.SemaphoreType.DMA((2,))],
         compiler_params=limit(6),
         cost_estimate=pl.CostEstimate(flops=1200000, bytes_accessed=1200000, transcendentals=0),
     )(rows, got)
@@ -450,8 +463,8 @@
 
 
 def interior_kernel(
-    hidden_ref, adjoint_ref, rows_ref, hot_ref, kernel_ref, out_ref, west_ref, east_ref,
-    low, high, twice, padded, total,
+    hidden_ref, adjoint_ref, rows_ref, hot_ref, kernel_ref, out_far, west_ref, east_ref,
+    low, high, twice, padded, total, out_ref, sems,
 ):
     build_shifts(low, high, padded, lambda row: hidden_ref[row])
     for group in range(LAT // BLK):
@@ -461,11 +474,21 @@
 
     def emit(row, start, stop, value):
         value = total[row, :, start:stop] + value
-        out_ref[row, :, start:stop] = value.astype(bf16)
+        out_ref[row, :, start:stop] = value[8 : WID - 8].astype(bf16)
         west_ref[row, :, start:stop] = value[0:8]
         east_ref[row, :, start:stop] = value[WID - 8 : WID]
 
-    convolve(low, high, twice, kernel_ref, True, emit)
+    def copy_of(first, place):
+        rows = pl.ds(first, BLK)
+        return pltpu.make_async_copy(out_ref.at[rows], out_far.at[rows, 8 : WID - 8], sems.at[place])
+
+    def done(index):
+        copy_of(index * BLK, index).start()
+        copy_of(index * BLK + HALF, index + 2).start()
+
+    convolve(low, high, twice, kernel_ref, True, emit, done)
+    for place, first in enumerate((0, BLK, HALF, HALF + BLK)):
+        copy_of(first, place).wait()
 
 
 STRIP = jax.ShapeDtypeStruct((LAT, 8, CH), f32)
@@ -474,8 +497,11 @@
 def interior(hidden, adjoint, rows, hot, kernel):
     return pl.pallas_call(
         interior_kernel,
-        out_shape=(FIELD, STRIP, STRIP),
-        scratch_shapes=SHIFT_SCRATCH + [pltpu.VMEM((LAT, WID, CH), f32)],
+        out_shape=(pltpu.HBM((LAT, WID, CH), bf16), STRIP, STRIP),
+        out_specs=(HBM, VM, VM),
+        scratch_shapes=SHIFT_SCRATCH + [
+            pltpu.VMEM((LAT, WID, CH), f32), pltpu.VMEM((LAT, WID - 16, CH), bf16), pltpu.SemaphoreType.DMA((4,)),
+        ],
         compiler_params=limit(16),
         cost_estimate=pl.CostEstimate(flops=98 * CELLS * CH, bytes_accessed=3000000, transcendentals=0),
     )(hidden, adjoint, rows, hot, kernel)

time: 107 us -> 106 us (level)
  no operation moved by 1% of the time
where the time goes in v8:
time: 106 us
  starting transfers between devices  41.3 us (39%)
  Pallas kernels  36.2 us (34%)
  blocking collectives  14.8 us (14%)
  waiting for transfers between devices  13 us (12%)
    all_to_all x2, starting transfers between devices, exchange(): return lax.all_to_all(array, axis, split_axis=0, concat_axis=0, tiled=True)  26.2 us
    pallas_call x2, Pallas kernels, forward(): pl.pallas_call(functools.partial(forward_kernel, step), out_shape=shapes,...  16.8 us
    all_to_all x1, blocking collectives, exchange(): return lax.all_to_all(array, axis, split_axis=0, concat_axis=0, tiled=True)  14.8 us
    ppermute x3, waiting for transfers between devices, swap_edges(): left = lax.ppermute(tail, 'tile', up)  8.96 us
    ppermute x3, starting transfers between devices, swap_edges(): right = lax.ppermute(head, 'tile', down)  8.82 us
    ppermute x3, starting transfers between devices, swap_edges(): left = lax.ppermute(tail, 'tile', up)  6.25 us
    pallas_call x1, Pallas kernels, spread_back(): pl.pallas_call(spread_kernel, out_shape=(jax.ShapeDtypeStruct((LAT, WID,...  5.33 us
    pallas_call x1, Pallas kernels, interior(): pl.pallas_call(interior_kernel, out_shape=(pltpu.HBM((LAT, WID, CH), bf16...  5.11 us
  transfers between devices with their start and end apart: 8, of which 5 were waited for; matrix products, arithmetic and copies ran while one was open for 0% of the time, Pallas kernels for 26%

profile of v8, /device:TPU:32, one launch (start us, length us, event | category | flops | bytes accessed | tf_op | source)
XLA Modules:
  0.0 105.7 jit_solution(17637391717036842163)
XLA Ops:
  0.0 1.5 %shard_map.109 = (f32[32,4,128]{2,1,0:T(4,128)S(1)}, bf16[2,1,32,32,192]{4,3,2,1,0:T(8,128)(2,1)S(1)}) custom-call(s32[2,16,32]{2,1,0:T(8,128)} %bitcast.16, s32[2,1,32]{2,1,0:T(1,128)} %count_far.1, bf16[2,1,32,16,192]{4,3,2,1,0:T(8,128)(2,1)} %value_far.1, bf16[2,16,32]{2,1,0:T(8,128)(2,1)} %bitcast.17, bf16[2,1,32,32,192]{4,3,2,1,0:T(8,128)(2,1)} %state_ref.2), custom_call_target="tpu_custom_call" | custom-call | tf_op jit(solution)/shard_map/pallas_call | solution.py:190
  1.5 0.0 copy-start
  1.5 0.0 copy-start.10
  1.6 0.0 copy-start.1
  1.6 0.0 copy-start.4
  1.6 0.0 copy-start.5
  1.6 0.0 copy-start.6
  1.6 0.0 copy-start.7
  1.6 14.8 %all_to_all.15.got_ref = f32[32,4,128]{2,1,0:T(4,128)S(1)} all-to-all(f32[32,4,128]{2,1,0:T(4,128)S(1)} %get-tuple-element.31), channel_id=1, replica_groups=mesh['member'=16,'tile'=32] {'tile'}, dimensions={0} | all-to-all | bytes 131072 | tf_op jit(solution)/shard_map/all_to_all | solution.py:583
  16.4 2.4 %shard_map.110 = bf16[16,32,384]{2,1,0:T(8,128)(2,1)} custom-call(f32[32,4,128]{2,1,0:T(4,128)S(1)} %all_to_all.15.got_ref, bf16[2,1,32,32,192]{4,3,2,1,0:T(8,128)(2,1)S(1)} %get-tuple-element.32.state_ref), custom_call_target="tpu_custom_call" | custom-call | flops 1000000 | bytes 2000000 | tf_op jit(solution)/shard_map/pallas_call | solution.py:231
  18.8 15.2 %all-to-all-start.1 = ((bf16[16,32,384]{2,1,0:T(8,128)(2,1)}), bf16[16,32,384]{2,1,0:T(8,128)(2,1)S(1)}, u32[]{:S(2)}, u32[]{:S(2)}) async-start(bf16[16,32,384]{2,1,0:T(8,128)(2,1)} %shard_map.110), calls=%async_computation.1 | async-start | bytes 786432 | tf_op jit(solution)/shard_map/all_to_all | solution.py:583
  34.0 0.0 copy-done
  34.0 0.1 fusion
  34.1 2.9 %collective-permute-start.1 = (bf16[2,32,3,192]{3,2,1,0:T(4,128)(2,1)S(1)}, bf16[2,32,3,192]{3,2,1,0:T(4,128)(2,1)S(1)}, u32[]{:S(2)}, u32[]{:S(2)}) collective-permute-start(bf16[2,32,3,192]{3,2,1,0:T(4,128)(2,1)S(1)} %get-tuple-element.57), channel_id=1, source_target_pairs={{1,0},{2,1},{3,2},{4,3},{5,4},{6,5},{7,6},{8,7},{9,8},{10,9},{11,1... | collective-permute-start | bytes 221192 | tf_op jit(solution)/shard_map/ppermute | solution.py:573
  37.0 1.9 %collective-permute-start = (bf16[2,32,3,192]{3,2,1,0:T(4,128)(2,1)S(1)}, bf16[2,32,3,192]{3,2,1,0:T(4,128)(2,1)S(1)}, u32[]{:S(2)}, u32[]{:S(2)}) collective-permute-start(bf16[2,32,3,192]{3,2,1,0:T(4,128)(2,1)S(1)} %get-tuple-element.58), channel_id=1, source_target_pairs={{0,1},{1,2},{2,3},{3,4},{4,5},{5,6},{6,7},{7,8},{8,9},{9,10},{10,1... | collective-permute-start | bytes 221192 | tf_op jit(solution)/shard_map/ppermute | solution.py:574
  38.9 0.0 copy-done.10
  38.9 0.5 collective-permute-done.1.right_ref
  39.5 7.1 %collective-permute-done.left_ref = bf16[2,32,3,192]{3,2,1,0:T(4,128)(2,1)S(1)} collective-permute-done((bf16[2,32,3,192]{3,2,1,0:T(4,128)(2,1)S(1)}, bf16[2,32,3,192]{3,2,1,0:T(4,128)(2,1)S(1)}, u32[]{:S(2)}, u32[]{:S(2)}) %collective-permute-start) | collective-permute-done | bytes 73760 | tf_op jit(solution)/shard_map/ppermute | solution.py:574
  46.6 0.0 copy-done.1
  46.6 0.0 copy-done.4
  46.6 0.0 copy-done.5
  46.6 0.0 copy-done.6
  46.6 0.0 copy-done.7
  46.6 8.7 %shard_map.111 = (bf16[32,32,192]{2,1,0:T(8,128)(2,1)}, bf16[32,3,192]{2,1,0:T(4,128)(2,1)}, bf16[32,3,192]{2,1,0:T(4,128)(2,1)}, bf16[32,3,192]{2,1,0:T(4,128)(2,1)}, bf16[32,3,192]{2,1,0:T(4,128)(2,1)}) custom-call(bf16[2,1,32,32,192]{4,3,2,1,0:T(8,128)(2,1)S(1)} %copy-done, bf16[2,32,3,192]{3,2,1,0:T(4,128)(2,1)S(1)} %collective-permute-done.left_ref, ...), custom_call_target="tpu_custom_call" | custom-call | flops 905969664 | bytes 8000000 | tf_op jit(solution)/shard_map/pallas_call | solution.py:379
  55.3 0.0 copy-start.12
  55.3 0.0 copy-start.11
  55.3 0.0 copy-start.8
  55.3 0.0 copy-start.9
  55.3 1.0 all-to-all-done.1.rows_ref
  56.4 1.2 %shard_map.112 = bf16[16,32,384]{2,1,0:T(8,128)(2,1)} custom-call(bf16[16,32,384]{2,1,0:T(8,128)(2,1)S(1)} %all-to-all-done.1.rows_ref, f32[32,4,128]{2,1,0:T(4,128)S(1)} %all_to_all.15.got_ref), custom_call_target="tpu_custom_call" | custom-call | flops 1200000 | bytes 1200000 | tf_op jit(solution)/shard_map/pallas_call | solution.py:266
  57.6 11.0 %all-to-all-start.2 = ((bf16[16,32,384]{2,1,0:T(8,128)(2,1)}), bf16[16,32,384]{2,1,0:T(8,128)(2,1)S(1)}, u32[]{:S(2)}, u32[]{:S(2)}) async-start(bf16[16,32,384]{2,1,0:T(8,128)(2,1)} %shard_map.112), calls=%async_computation.2 | async-start | bytes 786432 | tf_op jit(solution)/shard_map/all_to_all | solution.py:583
  68.6 0.0 copy-done.12
  68.6 1.9 %collective-permute-start.2 = (bf16[32,3,192]{2,1,0:T(4,128)(2,1)S(1)}, bf16[32,3,192]{2,1,0:T(4,128)(2,1)S(1)}, u32[]{:S(2)}, u32[]{:S(2)}) collective-permute-start(bf16[32,3,192]{2,1,0:T(4,128)(2,1)S(1)} %copy-done.12), channel_id=1, source_target_pairs={{1,0},{2,1},{3,2},{4,3},{5,4},{6,5},{7,6},{8,7},{9,8},{10,9},{11,1... | collective-permute-start | bytes 110600 | tf_op jit(solution)/shard_map/ppermute | solution.py:573
  70.5 0.0 copy-done.11
  70.5 2.4 %collective-permute-start.3 = (bf16[32,3,192]{2,1,0:T(4,128)(2,1)S(1)}, bf16[32,3,192]{2,1,0:T(4,128)(2,1)S(1)}, u32[]{:S(2)}, u32[]{:S(2)}) collective-permute-start(bf16[32,3,192]{2,1,0:T(4,128)(2,1)S(1)} %copy-done.11), channel_id=1, source_target_pairs={{0,1},{1,2},{2,3},{3,4},{4,5},{5,6},{6,7},{7,8},{8,9},{9,10},{10,1... | collective-permute-start | bytes 110600 | tf_op jit(solution)/shard_map/ppermute | solution.py:574
  72.9 0.0 copy-done.8
  72.9 0.0 copy-done.9
  73.0 0.0 copy-start.2
  73.0 0.0 copy-start.3
  73.0 8.1 %shard_map.113 = (bf16[1024,768]{1,0:T(8,128)(2,1)}, bf16[1024,192]{1,0:T(8,128)(2,1)}) custom-call(bf16[2,1,32,32,192]{4,3,2,1,0:T(8,128)(2,1)S(1)} %copy-done, bf16[32,3,192]{2,1,0:T(4,128)(2,1)S(1)} %copy-done.9, bf16[32,3,192]{2,1,0:T(4,128)(2,1)S(1)} %copy-done.8, f32[7,7,192]{2,1,0:T(8,128)S(1)} %copy-done.4, f32[1,192]{1,0:T(1,128)S(1)} %bitcast.14, ...), custom_call_target="tpu_custom_call" | custom-call | flops 905969664 | bytes 8000000 | tf_op jit(solution)/shard_map/pallas_call | solution.py:379
  81.1 0.0 collective-permute-done.2.right_ref
  81.1 0.0 collective-permute-done.3.left_ref
  81.1 0.0 copy-done.2
  81.1 0.0 copy-done.3
  81.1 5.3 %shard_map.114 = (f32[32,32,192]{2,1,0:T(8,128)S(1)}, bf16[1024,768]{1,0:T(8,128)(2,1)S(1)}, f32[8,128]{1,0:T(8,128)S(1)}) custom-call(bf16[32,32,192]{2,1,0:T(8,128)(2,1)S(1)} %copy-done.3, bf16[32,3,192]{2,1,0:T(4,128)(2,1)S(1)} %collective-permute-done.2.right_ref, bf16[32,3,192]{2,1,0:T(4,128)(2,1)S(1)} %collective-permute-done.3.left_ref, ...), custom_call_target="tpu_custom_call" | custom-call | flops 19267584 | bytes 3000000 | tf_op jit(solution)/shard_map/pallas_call | solution.py:415
  86.5 2.4 %all-to-all-done.2.rows_ref = bf16[16,32,384]{2,1,0:T(8,128)(2,1)S(1)} async-done(((bf16[16,32,384]{2,1,0:T(8,128)(2,1)}), bf16[16,32,384]{2,1,0:T(8,128)(2,1)S(1)}, u32[]{:S(2)}, u32[]{:S(2)}) %all-to-all-start.2) | async-done | bytes 393248 | tf_op jit(solution)/shard_map/all_to_all | solution.py:583
  88.9 2.4 %shard_map.115 = (bf16[32,32,192]{2,1,0:T(8,128)(2,1)S(1)}, bf16[32,3,192]{2,1,0:T(4,128)(2,1)S(1)}, bf16[32,3,192]{2,1,0:T(4,128)(2,1)S(1)}, bf16[32,32,192]{2,1,0:T(8,128)(2,1)S(1)}) custom-call(f32[32,32,192]{2,1,0:T(8,128)S(1)} %get-tuple-element.45.partial_ref, bf16[16,32,384]{2,1,0:T(8,128)(2,1)S(1)} %all-to-all-done.2.rows_ref, ...), custom_call_target="tpu_custom_call" | custom-call | flops 603979776 | bytes 5000000 | tf_op jit(solution)/shard_map/pallas_call | solution.py:455
  91.4 4.1 %collective-permute-start.4 = (bf16[32,3,192]{2,1,0:T(4,128)(2,1)S(1)}, bf16[32,3,192]{2,1,0:T(4,128)(2,1)S(1)}, u32[]{:S(2)}, u32[]{:S(2)}) collective-permute-start(bf16[32,3,192]{2,1,0:T(4,128)(2,1)S(1)} %get-tuple-element.55), channel_id=1, source_target_pairs={{1,0},{2,1},{3,2},{4,3},{5,4},{6,5},{7,6},{8,7},{9,8},{10,9},{11,1... | collective-permute-start | bytes 110600 | tf_op jit(solution)/shard_map/ppermute | solution.py:573
  95.4 1.9 %collective-permute-start.5 = (bf16[32,3,192]{2,1,0:T(4,128)(2,1)S(1)}, bf16[32,3,192]{2,1,0:T(4,128)(2,1)S(1)}, u32[]{:S(2)}, u32[]{:S(2)}) collective-permute-start(bf16[32,3,192]{2,1,0:T(4,128)(2,1)S(1)} %get-tuple-element.56), channel_id=1, source_target_pairs={{0,1},{1,2},{2,3},{3,4},{4,5},{5,6},{6,7},{7,8},{8,9},{9,10},{10,1... | collective-permute-start | bytes 110600 | tf_op jit(solution)/shard_map/ppermute | solution.py:574
  97.3 5.1 %shard_map.116 = (bf16[32,32,192]{2,1,0:T(8,128)(2,1)}, f32[32,8,192]{2,1,0:T(8,128)S(1)}, f32[32,8,192]{2,1,0:T(8,128)S(1)}) custom-call(bf16[32,32,192]{2,1,0:T(8,128)(2,1)S(1)} %get-tuple-element.50.hidden_ref, bf16[32,32,192]{2,1,0:T(8,128)(2,1)S(1)} %get-tuple-element.51.adjoint_ref, bf16[16,32,384]{2,1,0:T(8,128)(2,1)S(1)} %all-to-all-done.2.rows_ref, ...), custom_call_target="tpu_custom_call" | custom-call | flops 19267584 | bytes 3000000 | tf_op jit(solution)/shard_map/pallas_call | solution.py:498
  102.5 0.0 collective-permute-done.4.right_ref
  102.5 1.9 %collective-permute-done.5.left_ref = bf16[32,3,192]{2,1,0:T(4,128)(2,1)S(1)} collective-permute-done((bf16[32,3,192]{2,1,0:T(4,128)(2,1)S(1)}, bf16[32,3,192]{2,1,0:T(4,128)(2,1)S(1)}, u32[]{:S(2)}, u32[]{:S(2)}) %collective-permute-start.5) | collective-permute-done | bytes 36896 | tf_op jit(solution)/shard_map/ppermute | solution.py:574
  104.3 1.4 %shard_map.117 = bf16[32,32,192]{2,1,0:T(8,128)(2,1)} custom-call(bf16[32,32,192]{2,1,0:T(8,128)(2,1)} %get-tuple-element.52.inner_ref, f32[32,8,192]{2,1,0:T(8,128)S(1)} %get-tuple-element.53.west_ref, f32[32,8,192]{2,1,0:T(8,128)S(1)} %get-tuple-element.54.east_ref, ...), custom_call_target="tpu_custom_call", output_to_operand_aliasing={{}: (0, {})} | custom-call | flops 5000000 | bytes 700000 | tf_op jit(solution)/shard_map/pallas_call | solution.py:554
  (1 shorter events, 0.0 us)
Async XLA Ops:
  1.5 32.5 %copy-start = (bf16[2,1,32,32,192]{4,3,2,1,0:T(8,128)(2,1)S(1)}, bf16[2,1,32,32,192]{4,3,2,1,0:T(8,128)(2,1)}, u32[]{:S(2)}) copy-start(bf16[2,1,32,32,192]{4,3,2,1,0:T(8,128)(2,1)} %state_ref.2) | copy-start | bytes 2359300
  1.5 37.4 %copy-start.10 = (f32[768]{0:T(1024)S(1)}, f32[768]{0:T(1024)}, u32[]{:S(2)}) copy-start(f32[768]{0:T(1024)} %param.16) | copy-start | bytes 9220
  1.6 45.0 %copy-start.1 = (bf16[1,32,32,192]{3,2,1,0:T(8,128)(2,1)S(1)}, bf16[1,32,32,192]{3,2,1,0:T(8,128)(2,1)}, u32[]{:S(2)}) copy-start(bf16[1,32,32,192]{3,2,1,0:T(8,128)(2,1)} %base_ref.1) | copy-start | bytes 1179652
  1.6 45.0 %copy-start.4 = (f32[7,7,192]{2,1,0:T(8,128)S(1)}, f32[7,7,192]{2,1,0:T(8,128)}, u32[]{:S(2)}) copy-start(f32[7,7,192]{2,1,0:T(8,128)} %kernel_ref.9) | copy-start | bytes 112900
  1.6 45.0 %copy-start.5 = (bf16[192,768]{1,0:T(8,128)(2,1)S(1)}, bf16[192,768]{1,0:T(8,128)(2,1)}, u32[]{:S(2)}) copy-start(bf16[192,768]{1,0:T(8,128)(2,1)} %up_ref.5) | copy-start | bytes 884740
  1.6 45.0 %copy-start.6 = (bf16[768,192]{0,1:T(8,128)(2,1)S(1)}, bf16[768,192]{0,1:T(8,128)(2,1)}, u32[]{:S(2)}) copy-start(bf16[768,192]{0,1:T(8,128)(2,1)} %param.17) | copy-start | bytes 884740
  1.6 45.0 %copy-start.7 = (f32[192]{0:T(256)S(1)}, f32[192]{0:T(256)}, u32[]{:S(2)}) copy-start(f32[192]{0:T(256)} %param.14) | copy-start | bytes 2308
  18.8 37.6 %all-to-all-start.1 = ((bf16[16,32,384]{2,1,0:T(8,128)(2,1)}), bf16[16,32,384]{2,1,0:T(8,128)(2,1)S(1)}, u32[]{:S(2)}, u32[]{:S(2)}) async-start(bf16[16,32,384]{2,1,0:T(8,128)(2,1)} %shard_map.110), calls=%async_computation.1 | async-start | bytes 786432 | tf_op jit(solution)/shard_map/all_to_all | solution.py:583
  34.1 5.4 %collective-permute-start.1 = (bf16[2,32,3,192]{3,2,1,0:T(4,128)(2,1)S(1)}, bf16[2,32,3,192]{3,2,1,0:T(4,128)(2,1)S(1)}, u32[]{:S(2)}, u32[]{:S(2)}) collective-permute-start(bf16[2,32,3,192]{3,2,1,0:T(4,128)(2,1)S(1)} %get-tuple-element.57), channel_id=1, source_target_pairs={{1,0},{2,1},{3,2},{4,3},{5,4},{6,5},{7,6},{8,7},{9,8},{10,9},{11,1... | collective-permute-start | bytes 221192 | tf_op jit(solution)/shard_map/ppermute | solution.py:573
  37.0 9.6 %collective-permute-start = (bf16[2,32,3,192]{3,2,1,0:T(4,128)(2,1)S(1)}, bf16[2,32,3,192]{3,2,1,0:T(4,128)(2,1)S(1)}, u32[]{:S(2)}, u32[]{:S(2)}) collective-permute-start(bf16[2,32,3,192]{3,2,1,0:T(4,128)(2,1)S(1)} %get-tuple-element.58), channel_id=1, source_target_pairs={{0,1},{1,2},{2,3},{3,4},{4,5},{5,6},{6,7},{7,8},{8,9},{9,10},{10,1... | collective-permute-start | bytes 221192 | tf_op jit(solution)/shard_map/ppermute | solution.py:574
  55.3 13.3 %copy-start.12 = (bf16[32,3,192]{2,1,0:T(4,128)(2,1)S(1)}, bf16[32,3,192]{2,1,0:T(4,128)(2,1)}, u32[]{:S(2)}) copy-start(bf16[32,3,192]{2,1,0:T(4,128)(2,1)} %get-tuple-element.38) | copy-start | bytes 110596
  55.3 15.2 %copy-start.11 = (bf16[32,3,192]{2,1,0:T(4,128)(2,1)S(1)}, bf16[32,3,192]{2,1,0:T(4,128)(2,1)}, u32[]{:S(2)}) copy-start(bf16[32,3,192]{2,1,0:T(4,128)(2,1)} %get-tuple-element.44) | copy-start | bytes 110596
  55.3 17.6 %copy-start.8 = (bf16[32,3,192]{2,1,0:T(4,128)(2,1)S(1)}, bf16[32,3,192]{2,1,0:T(4,128)(2,1)}, u32[]{:S(2)}) copy-start(bf16[32,3,192]{2,1,0:T(4,128)(2,1)} %get-tuple-element.41.right_ref) | copy-start | bytes 110596
  55.3 17.6 %copy-start.9 = (bf16[32,3,192]{2,1,0:T(4,128)(2,1)S(1)}, bf16[32,3,192]{2,1,0:T(4,128)(2,1)}, u32[]{:S(2)}) copy-start(bf16[32,3,192]{2,1,0:T(4,128)(2,1)} %get-tuple-element.40.left_ref) | copy-start | bytes 110596
  57.6 31.3 %all-to-all-start.2 = ((bf16[16,32,384]{2,1,0:T(8,128)(2,1)}), bf16[16,32,384]{2,1,0:T(8,128)(2,1)S(1)}, u32[]{:S(2)}, u32[]{:S(2)}) async-start(bf16[16,32,384]{2,1,0:T(8,128)(2,1)} %shard_map.112), calls=%async_computation.2 | async-start | bytes 786432 | tf_op jit(solution)/shard_map/all_to_all | solution.py:583
  68.6 12.5 %collective-permute-start.2 = (bf16[32,3,192]{2,1,0:T(4,128)(2,1)S(1)}, bf16[32,3,192]{2,1,0:T(4,128)(2,1)S(1)}, u32[]{:S(2)}, u32[]{:S(2)}) collective-permute-start(bf16[32,3,192]{2,1,0:T(4,128)(2,1)S(1)} %copy-done.12), channel_id=1, source_target_pairs={{1,0},{2,1},{3,2},{4,3},{5,4},{6,5},{7,6},{8,7},{9,8},{10,9},{11,1... | collective-permute-start | bytes 110600 | tf_op jit(solution)/shard_map/ppermute | solution.py:573
  70.5 10.6 %collective-permute-start.3 = (bf16[32,3,192]{2,1,0:T(4,128)(2,1)S(1)}, bf16[32,3,192]{2,1,0:T(4,128)(2,1)S(1)}, u32[]{:S(2)}, u32[]{:S(2)}) collective-permute-start(bf16[32,3,192]{2,1,0:T(4,128)(2,1)S(1)} %copy-done.11), channel_id=1, source_target_pairs={{0,1},{1,2},{2,3},{3,4},{4,5},{5,6},{6,7},{7,8},{8,9},{9,10},{10,1... | collective-permute-start | bytes 110600 | tf_op jit(solution)/shard_map/ppermute | solution.py:574
  73.0 8.2 %copy-start.2 = (bf16[1,32,32,192]{3,2,1,0:T(8,128)(2,1)S(1)}, bf16[1,32,32,192]{3,2,1,0:T(8,128)(2,1)}, u32[]{:S(2)}) copy-start(bf16[1,32,32,192]{3,2,1,0:T(8,128)(2,1)} %base_ref.1) | copy-start | bytes 1179652
  73.0 8.2 %copy-start.3 = (bf16[32,32,192]{2,1,0:T(8,128)(2,1)S(1)}, bf16[32,32,192]{2,1,0:T(8,128)(2,1)}, u32[]{:S(2)}) copy-start(bf16[32,32,192]{2,1,0:T(8,128)(2,1)} %get-tuple-element.34.hidden_ref) | copy-start | bytes 1179652
  91.4 11.1 %collective-permute-start.4 = (bf16[32,3,192]{2,1,0:T(4,128)(2,1)S(1)}, bf16[32,3,192]{2,1,0:T(4,128)(2,1)S(1)}, u32[]{:S(2)}, u32[]{:S(2)}) collective-permute-start(bf16[32,3,192]{2,1,0:T(4,128)(2,1)S(1)} %get-tuple-element.55), channel_id=1, source_target_pairs={{1,0},{2,1},{3,2},{4,3},{5,4},{6,5},{7,6},{8,7},{9,8},{10,9},{11,1... | collective-permute-start | bytes 110600 | tf_op jit(solution)/shard_map/ppermute | solution.py:573
  95.4 8.9 %collective-permute-start.5 = (bf16[32,3,192]{2,1,0:T(4,128)(2,1)S(1)}, bf16[32,3,192]{2,1,0:T(4,128)(2,1)S(1)}, u32[]{:S(2)}, u32[]{:S(2)}) collective-permute-start(bf16[32,3,192]{2,1,0:T(4,128)(2,1)S(1)} %get-tuple-element.56), channel_id=1, source_target_pairs={{0,1},{1,2},{2,3},{3,4},{4,5},{5,6},{6,7},{7,8},{8,9},{9,10},{10,1... | collective-permute-start | bytes 110600 | tf_op jit(solution)/shard_map/ppermute | solution.py:574

commit v9 on v8

--- a/solution.py
+++ b/solution.py
@@ -207,6 +207,17 @@
     return jnp.concatenate(rows, axis=0)
 
 
+def take_step(ref, step, members=slice(None)):
+    first = ref[members, :, step * 128 : (step + 1) * 128]
+    last = ref[members, :, 256 + step * 64 : 320 + step * 64]
+    return jnp.concatenate([first.astype(f32), last.astype(f32)], axis=2)
+
+
+def put_step(ref, step, members, bands, value):
+    ref[members, bands, step * 128 : (step + 1) * 128] = value[:, :, 0:128]
+    ref[members, bands, 256 + step * 64 : 320 + step * 64] = value[:, :, 128:CH]
+
+
 def gather_kernel(got_ref, state_ref, out_far, out_ref, sems):
     copies = []
     for step in range(2):
@@ -218,7 +229,7 @@
                 rows = jnp.dot(hot, field, preferred_element_type=f32)
                 found.append(rows.reshape(CAP, BLK, CH))
             both = jnp.concatenate(found, axis=1).astype(bf16)
-            out_ref[:, 2 * BLK * pair : 2 * BLK * (pair + 1), step * CH : (step + 1) * CH] = both
+            put_step(out_ref, step, slice(None), slice(2 * BLK * pair, 2 * BLK * (pair + 1)), both)
             if step == 1:
                 part = slice(2 * BLK * pair, 2 * BLK * (pair + 1))
                 copies.append(pltpu.make_async_copy(out_ref.at[:, part], out_far.at[:, part], sems.at[pair]))
@@ -241,7 +252,7 @@
 def departure_kernel(rows_ref, got_ref, out_far, out_ref, sems):
     stats = []
     for step in range(2):
-        sampled = rows_ref[:, :, step * CH : (step + 1) * CH].astype(f32)
+        sampled = take_step(rows_ref, step)
         members = sampled.shape[0]
         other = got_ref[:, 2 * step + 1, :]
         values = jnp.concatenate([got_ref[:, 2 * step, :], other[:, 0:64]], axis=1)
@@ -253,9 +264,8 @@
     for half in range(2):
         part = slice(half * CAP // 2, (half + 1) * CAP // 2)
         for step, (values, weight, live) in enumerate(stats):
-            lanes = slice(step * CH, (step + 1) * CH)
-            ratio = (rows_ref[part, :, lanes].astype(f32) - values[None]) * weight[None]
-            out_ref[part, :, lanes] = jnp.where(live[None], ratio, 0.0).astype(bf16)
+            ratio = (take_step(rows_ref, step, part) - values[None]) * weight[None]
+            put_step(out_ref, step, part, slice(None), jnp.where(live[None], ratio, 0.0).astype(bf16))
         copies.append(pltpu.make_async_copy(out_ref.at[part], out_far.at[part], sems.at[half]))
         copies[-1].start()
     for copy in copies:
@@ -281,12 +291,13 @@
     return jnp.broadcast_to(column, (CAP * BLK, CAP * BLK)).T[0:1]
 
 
-def forcing_of(step, rows_ref, cell_ref, group):
+def forcing_of(step, rows_ref, cell_ref, group, cell=None):
     place = step * (LAT // BLK) + group
-    cells = jnp.broadcast_to(cell_ref[place : place + 1, :], (ROWS, CAP * BLK))
-    cell = lax.broadcasted_iota(jnp.int32, (ROWS, CAP * BLK), 0).astype(f32)
+    if cell is None:
+        cell = lax.broadcasted_iota(jnp.int32, (ROWS, CAP * BLK), 0).astype(f32)
+    cells = jnp.broadcast_to(cell_ref[place : place + 1, :], cell.shape)
     hot = jnp.where(cell == cells, 1.0, 0.0).astype(bf16)
-    rows = rows_ref[:, :, step * CH : (step + 1) * CH].astype(f32)[:, group * BLK : (group + 1) * BLK]
+    rows = take_step(rows_ref, step)[:, group * BLK : (group + 1) * BLK]
     rows = rows.reshape(CAP * BLK, CH).astype(bf16)
     return jnp.dot(hot, rows, preferred_element_type=f32)
 
@@ -426,51 +437,78 @@
     )(hidden, right, left, base, kernel, got, far(slope))
 
 
+STRIPS = {"edge": ((0, 8), (WID - 8, WID)), "middle": ((8, WID - 8),)}
+DEEP = 2 * BLK
+
+
 def second_kernel(
-    partial_ref, rows_ref, cell_ref, slope_ref, unit_far, gain_ref, up_ref, down_far,
-    hidden_out, tail_out, head_out, adjoint_out, unit_ref, down_ref, sems,
+    part, partial_ref, rows_ref, cell_ref, slope_ref, unit_far, gain_ref, up_ref, down_far,
+    hidden_out, adjoint_out, *rest,
 ):
+    unit_ref, down_ref, sems = rest[-3:]
+    strips = STRIPS[part]
+
+    def pick(ref, first, lanes=slice(None)):
+        found = [ref[first : first + DEEP, low:high, lanes] for low, high in strips]
+        whole = found[0].astype(f32) if len(found) == 1 else jnp.concatenate([x.astype(f32) for x in found], axis=1)
+        return whole.reshape(ROWS, whole.shape[2])
+
     copies = fetch([(down_far, down_ref), (unit_far, unit_ref)], sems)
     gain = gain_ref[...]
-    for group in range(LAT // BLK):
-        first = group * BLK
-        forcing = forcing_of(0, rows_ref, cell_ref, group)
-        adjoint = (partial_ref[first : first + BLK].reshape(ROWS, CH) + forcing).astype(bf16)
-        adjoint_out[first : first + BLK] = adjoint.reshape(BLK, WID, CH)
+    row = lax.broadcasted_iota(jnp.int32, (CAP * BLK, CAP * BLK), 0)
+    place = row % 16
+    lon = jnp.where(place < 8, place, place + 16) if part == "edge" else place + 8
+    cell = ((row // 16) * WID + lon).astype(f32)
+    for index in range(LAT // DEEP):
+        first = index * DEEP
+        forcing = [forcing_of(0, rows_ref, cell_ref, 2 * index + half, cell) for half in range(2)]
+        adjoint = (pick(partial_ref, first) + jnp.concatenate(forcing, axis=0)).astype(bf16)
+        adjoint_out[first : first + DEEP] = adjoint.reshape(DEEP, 16, CH)
     for copy in copies:
         copy.wait()
-    for group in range(LAT // BLK):
-        first = group * BLK
-        rows = slice(group * ROWS, (group + 1) * ROWS)
+    for index in range(LAT // DEEP):
+        first = index * DEEP
         result = backward(
-            adjoint_out[first : first + BLK].reshape(ROWS, CH),
-            lambda cols: slope_ref[rows, cols].astype(f32),
+            adjoint_out[first : first + DEEP].reshape(ROWS, CH),
+            lambda cols: pick(slope_ref, first, cols),
             down_ref, up_ref, gain,
-            unit_ref[rows, :].astype(f32),
+            pick(unit_ref, first),
         )
-        put_hidden(result, first, hidden_out, tail_out, head_out)
-
-
-def second_step(partial, rows, hot, slope, unit, gain, up, down):
-    return pl.pallas_call(
-        second_kernel,
-        out_shape=(FIELD, EDGE, EDGE, FIELD),
+        block = result.astype(bf16).reshape(DEEP, 16, CH)
+        hidden_out[first : first + DEEP] = block
+        if part == "edge":
+            tail_out, head_out = rest[:2]
+            head_out[first : first + DEEP] = block[:, 0:3]
+            tail_out[first : first + DEEP] = block[:, 13:16]
+
+
+def second_step(part, partial, rows, cells, slope, unit, gain, up, down):
+    half = jax.ShapeDtypeStruct((LAT, 16, CH), bf16)
+    return pl.pallas_call(
+        functools.partial(second_kernel, part),
+        out_shape=(half, half) + ((EDGE, EDGE) if part == "edge" else ()),
         in_specs=[VM] * 4 + [HBM, VM, VM, HBM],
-        scratch_shapes=[pltpu.VMEM((CELLS, CH), bf16), pltpu.VMEM((CH, HID), bf16), pltpu.SemaphoreType.DMA((2,))],
+        scratch_shapes=[pltpu.VMEM((LAT, WID, CH), bf16), pltpu.VMEM((CH, HID), bf16), pltpu.SemaphoreType.DMA((2,))],
         compiler_params=limit(8),
-        cost_estimate=pl.CostEstimate(flops=4 * CELLS * CH * HID, bytes_accessed=5000000, transcendentals=0),
-    )(partial, rows, hot, slope, far(unit), gain, up, far(down))
+        cost_estimate=pl.CostEstimate(flops=2 * CELLS * CH * HID, bytes_accessed=2500000, transcendentals=0),
+    )(partial, rows, cells, slope, far(unit), gain, up, far(down))
 
 
 def interior_kernel(
-    hidden_ref, adjoint_ref, rows_ref, hot_ref, kernel_ref, out_far, west_ref, east_ref,
+    rim_ref, inner_ref, rim_adjoint, inner_adjoint, rows_ref, hot_ref, kernel_ref, out_far, west_ref, east_ref,
     low, high, twice, padded, total, out_ref, sems,
 ):
-    build_shifts(low, high, padded, lambda row: hidden_ref[row])
+    def whole(rim, inner):
+        axis = rim.ndim - 2
+        first, last = lax.slice_in_dim(rim, 0, 8, axis=axis), lax.slice_in_dim(rim, 8, 16, axis=axis)
+        return jnp.concatenate([first, inner, last], axis=axis)
+
+    build_shifts(low, high, padded, lambda row: whole(rim_ref[row].astype(f32), inner_ref[row].astype(f32)))
     for group in range(LAT // BLK):
         first = group * BLK
         forcing = forcing_of(1, rows_ref, hot_ref, group).reshape(BLK, WID, CH)
-        total[first : first + BLK] = adjoint_ref[first : first + BLK].astype(f32) + forcing
+        band = slice(first, first + BLK)
+        total[band] = whole(rim_adjoint[band].astype(f32), inner_adjoint[band].astype(f32)) + forcing
 
     def emit(row, start, stop, value):
         value = total[row, :, start:stop] + value
@@ -494,7 +532,7 @@
 STRIP = jax.ShapeDtypeStruct((LAT, 8, CH), f32)
 
 
-def interior(hidden, adjoint, rows, hot, kernel):
+def interior(rim, inner, rim_adjoint, inner_adjoint, rows, hot, kernel):
     return pl.pallas_call(
         interior_kernel,
         out_shape=(pltpu.HBM((LAT, WID, CH), bf16), STRIP, STRIP),
@@ -504,11 +542,11 @@
         ],
         compiler_params=limit(16),
         cost_estimate=pl.CostEstimate(flops=98 * CELLS * CH, bytes_accessed=3000000, transcendentals=0),
-    )(hidden, adjoint, rows, hot, kernel)
+    )(rim, inner, rim_adjoint, inner_adjoint, rows, hot, kernel)
 
 
 def edge_kernel(
-    inner_ref, west_ref, east_ref, right_ref, left_ref, kernel_ref, out_ref,
+    inner_ref, west_ref, east_ref, left_ref, right_ref, kernel_ref, out_ref,
     shifts, padded, taps, strips, sems,
 ):
     clear_rims(shifts, 3, 8)
@@ -563,7 +601,7 @@
             pltpu.VMEM((2, LAT, 8, CH), bf16), pltpu.SemaphoreType.DMA((2,)),
         ],
         cost_estimate=pl.CostEstimate(flops=5000000, bytes_accessed=700000, transcendentals=0),
-    )(inner, west, east, right, left, kernel)
+    )(inner, west, east, left, right, kernel)
 
 
 def swap_edges(head, tail):
@@ -612,12 +650,13 @@
         hidden, after(behind, slope), before, adjoint_final, kernel, got, slope
     )
 
-    hidden, tail, head, adjoint = second_step(
-        partial, after(back, partial), cells, slope, unit, gain, up_weight, down
-    )
+    back = after(back, partial)
+    fields = (slope.reshape(LAT, WID, HID), unit.reshape(LAT, WID, CH), gain, up_weight, down)
+    rim, rim_adjoint, tail, head = second_step("edge", partial, back, cells, *fields)
     left, right = swap_edges(head, tail)
-    inner, west, east = interior(hidden, adjoint, back, cells, kernel)
-    return finish_edges(inner, west, east, left, right, kernel)[None]
+    inner, inner_adjoint = second_step("middle", partial, after(back, tail), cells, *fields)
+    field, west, east = interior(rim, inner, rim_adjoint, inner_adjoint, back, cells, kernel)
+    return finish_edges(field, west, east, left, right, kernel)[None]
 
 
 def solution(mesh):

time: 106 us -> 108 us (1.019)
  the two profiles are of different devices: /device:TPU:32 before, /device:TPU:63 now
where the time goes in v9:
time: 108 us; the launch traced here: 107 us
  starting transfers between devices  53.3 us (49%)
  Pallas kernels  37.9 us (35%)
  blocking collectives  11.6 us (11%)
  waiting for transfers between devices  2.86 us (3%)
  local copies, waits for them, and re-layouts  1.21 us (1%)
    all_to_all x2, starting transfers between devices, exchange(): return lax.all_to_all(array, axis, split_axis=0, concat_axis=0, tiled=True)  25.2 us
    ppermute x3, starting transfers between devices, swap_edges(): left = lax.ppermute(tail, 'tile', up)  21.4 us
    pallas_call x2, Pallas kernels, forward(): pl.pallas_call(functools.partial(forward_kernel, step), out_shape=shapes,...  16.8 us
    all_to_all x1, blocking collectives, exchange(): return lax.all_to_all(array, axis, split_axis=0, concat_axis=0, tiled=True)  11.6 us
    ppermute x3, starting transfers between devices, swap_edges(): right = lax.ppermute(head, 'tile', down)  6.7 us
    pallas_call x1, Pallas kernels, spread_back(): pl.pallas_call(spread_kernel, out_shape=(jax.ShapeDtypeStruct((LAT, WID,...  5.33 us
    pallas_call x1, Pallas kernels, interior(): pl.pallas_call(interior_kernel, out_shape=(pltpu.HBM((LAT, WID, CH), bf16...  5.09 us
    pallas_call x2, Pallas kernels, second_step(): pl.pallas_call(functools.partial(second_kernel, part), out_shape=(half, h...  4.16 us
  transfers between devices with their start and end apart: 8, of which 3 were waited for; matrix products, arithmetic and copies ran while one was open for 0% of the time, Pallas kernels for 27%

profile of v9, /device:TPU:63, one launch (start us, length us, event | category | flops | bytes accessed | tf_op | source)
XLA Modules:
  0.0 107.4 jit_solution(10863584892708387209)
XLA Ops:
  0.0 1.5 %shard_map.109 = (f32[32,4,128]{2,1,0:T(4,128)S(1)}, bf16[2,1,32,32,192]{4,3,2,1,0:T(8,128)(2,1)S(1)}) custom-call(s32[2,16,32]{2,1,0:T(8,128)} %bitcast.24, s32[2,1,32]{2,1,0:T(1,128)} %count_far.1, bf16[2,1,32,16,192]{4,3,2,1,0:T(8,128)(2,1)} %value_far.1, bf16[2,16,32]{2,1,0:T(8,128)(2,1)} %bitcast.25, bf16[2,1,32,32,192]{4,3,2,1,0:T(8,128)(2,1)} %state_ref.2), custom_call_target="tpu_custom_call" | custom-call | tf_op jit(solution)/shard_map/pallas_call | solution.py:190
  1.5 0.0 copy-start
  1.5 0.0 copy-start.10
  1.6 0.0 copy-start.1
  1.6 0.0 copy-start.2
  1.6 0.0 copy-start.6
  1.6 0.0 copy-start.7
  1.6 11.6 %all_to_all.15.got_ref = f32[32,4,128]{2,1,0:T(4,128)S(1)} all-to-all(f32[32,4,128]{2,1,0:T(4,128)S(1)} %get-tuple-element.34), channel_id=1, replica_groups=mesh['member'=16,'tile'=32] {'tile'}, dimensions={0} | all-to-all | bytes 131072 | tf_op jit(solution)/shard_map/all_to_all | solution.py:621
  13.2 2.4 %shard_map.110 = bf16[16,32,384]{2,1,0:T(8,128)(2,1)} custom-call(f32[32,4,128]{2,1,0:T(4,128)S(1)} %all_to_all.15.got_ref, bf16[2,1,32,32,192]{4,3,2,1,0:T(8,128)(2,1)S(1)} %get-tuple-element.35.state_ref), custom_call_target="tpu_custom_call" | custom-call | flops 1000000 | bytes 2000000 | tf_op jit(solution)/shard_map/pallas_call | solution.py:242
  15.6 14.7 %all-to-all-start.1 = ((bf16[16,32,384]{2,1,0:T(8,128)(2,1)}), bf16[16,32,384]{2,1,0:T(8,128)(2,1)S(1)}, u32[]{:S(2)}, u32[]{:S(2)}) async-start(bf16[16,32,384]{2,1,0:T(8,128)(2,1)} %shard_map.110), calls=%async_computation.1 | async-start | bytes 786432 | tf_op jit(solution)/shard_map/all_to_all | solution.py:621
  30.3 0.0 copy-done
  30.3 0.1 fusion
  30.4 2.9 %collective-permute-start.1 = (bf16[2,32,3,192]{3,2,1,0:T(4,128)(2,1)S(1)}, bf16[2,32,3,192]{3,2,1,0:T(4,128)(2,1)S(1)}, u32[]{:S(2)}, u32[]{:S(2)}) collective-permute-start(bf16[2,32,3,192]{3,2,1,0:T(4,128)(2,1)S(1)} %get-tuple-element.63), channel_id=1, source_target_pairs={{1,0},{2,1},{3,2},{4,3},{5,4},{6,5},{7,6},{8,7},{9,8},{10,9},{11,1... | collective-permute-start | bytes 221192 | tf_op jit(solution)/shard_map/ppermute | solution.py:611
  33.3 6.0 %collective-permute-start = (bf16[2,32,3,192]{3,2,1,0:T(4,128)(2,1)S(1)}, bf16[2,32,3,192]{3,2,1,0:T(4,128)(2,1)S(1)}, u32[]{:S(2)}, u32[]{:S(2)}) collective-permute-start(bf16[2,32,3,192]{3,2,1,0:T(4,128)(2,1)S(1)} %get-tuple-element.64), channel_id=1, source_target_pairs={{0,1},{1,2},{2,3},{3,4},{4,5},{5,6},{6,7},{7,8},{8,9},{9,10},{10,1... | collective-permute-start | bytes 221192 | tf_op jit(solution)/shard_map/ppermute | solution.py:612
  39.3 0.0 copy-done.10
  39.3 1.0 collective-permute-done.1.right_ref
  40.3 0.9 collective-permute-done.left_ref
  41.2 0.0 copy-done.1
  41.2 0.0 copy-done.2
  41.2 0.0 copy-done.6
  41.2 0.0 copy-done.7
  41.3 0.0 copy-start.3
  41.3 1.0 copy-done.3
  42.3 8.6 %shard_map.111 = (bf16[32,32,192]{2,1,0:T(8,128)(2,1)}, bf16[32,3,192]{2,1,0:T(4,128)(2,1)}, bf16[32,3,192]{2,1,0:T(4,128)(2,1)}, bf16[32,3,192]{2,1,0:T(4,128)(2,1)}, bf16[32,3,192]{2,1,0:T(4,128)(2,1)}) custom-call(bf16[2,1,32,32,192]{4,3,2,1,0:T(8,128)(2,1)S(1)} %copy-done, bf16[2,32,3,192]{3,2,1,0:T(4,128)(2,1)S(1)} %collective-permute-done.left_ref, ...), custom_call_target="tpu_custom_call" | custom-call | flops 905969664 | bytes 8000000 | tf_op jit(solution)/shard_map/pallas_call | solution.py:390
  50.9 0.0 copy-start.12
  50.9 0.0 copy-start.11
  50.9 0.0 copy-start.8
  50.9 0.0 copy-start.9
  50.9 0.9 all-to-all-done.1.rows_ref
  51.9 1.3 %shard_map.112 = bf16[16,32,384]{2,1,0:T(8,128)(2,1)} custom-call(bf16[16,32,384]{2,1,0:T(8,128)(2,1)S(1)} %all-to-all-done.1.rows_ref, f32[32,4,128]{2,1,0:T(4,128)S(1)} %all_to_all.15.got_ref), custom_call_target="tpu_custom_call" | custom-call | flops 1200000 | bytes 1200000 | tf_op jit(solution)/shard_map/pallas_call | solution.py:276
  53.2 10.5 %all-to-all-start.2 = ((bf16[16,32,384]{2,1,0:T(8,128)(2,1)}), bf16[16,32,384]{2,1,0:T(8,128)(2,1)S(1)}, u32[]{:S(2)}, u32[]{:S(2)}) async-start(bf16[16,32,384]{2,1,0:T(8,128)(2,1)} %shard_map.112), calls=%async_computation.2 | async-start | bytes 786432 | tf_op jit(solution)/shard_map/all_to_all | solution.py:621
  63.7 0.0 copy-done.12
  63.7 1.9 %collective-permute-start.2 = (bf16[32,3,192]{2,1,0:T(4,128)(2,1)S(1)}, bf16[32,3,192]{2,1,0:T(4,128)(2,1)S(1)}, u32[]{:S(2)}, u32[]{:S(2)}) collective-permute-start(bf16[32,3,192]{2,1,0:T(4,128)(2,1)S(1)} %copy-done.12), channel_id=1, source_target_pairs={{1,0},{2,1},{3,2},{4,3},{5,4},{6,5},{7,6},{8,7},{9,8},{10,9},{11,1... | collective-permute-start | bytes 110600 | tf_op jit(solution)/shard_map/ppermute | solution.py:611
  65.7 0.0 copy-done.11
  65.7 8.2 %collective-permute-start.3 = (bf16[32,3,192]{2,1,0:T(4,128)(2,1)S(1)}, bf16[32,3,192]{2,1,0:T(4,128)(2,1)S(1)}, u32[]{:S(2)}, u32[]{:S(2)}) collective-permute-start(bf16[32,3,192]{2,1,0:T(4,128)(2,1)S(1)} %copy-done.11), channel_id=1, source_target_pairs={{0,1},{1,2},{2,3},{3,4},{4,5},{5,6},{6,7},{7,8},{8,9},{9,10},{10,1... | collective-permute-start | bytes 110600 | tf_op jit(solution)/shard_map/ppermute | solution.py:612
  73.9 0.0 copy-done.8
  73.9 0.0 copy-done.9
  73.9 0.0 copy-start.4
  74.0 0.0 copy-start.5
  74.0 8.1 %shard_map.113 = (bf16[1024,768]{1,0:T(8,128)(2,1)}, bf16[1024,192]{1,0:T(8,128)(2,1)}) custom-call(bf16[2,1,32,32,192]{4,3,2,1,0:T(8,128)(2,1)S(1)} %copy-done, bf16[32,3,192]{2,1,0:T(4,128)(2,1)S(1)} %copy-done.9, bf16[32,3,192]{2,1,0:T(4,128)(2,1)S(1)} %copy-done.8, f32[7,7,192]{2,1,0:T(8,128)S(1)} %copy-done.6, f32[1,192]{1,0:T(1,128)S(1)} %bitcast.19, ...), custom_call_target="tpu_custom_call" | custom-call | flops 905969664 | bytes 8000000 | tf_op jit(solution)/shard_map/pallas_call | solution.py:390
  82.1 0.0 collective-permute-done.2.right_ref
  82.1 0.0 collective-permute-done.3.left_ref
  82.1 0.0 copy-done.4
  82.1 0.0 copy-done.5
  82.1 5.3 %shard_map.114 = (f32[32,32,192]{2,1,0:T(8,128)S(1)}, bf16[1024,768]{1,0:T(8,128)(2,1)S(1)}, f32[8,128]{1,0:T(8,128)S(1)}) custom-call(bf16[32,32,192]{2,1,0:T(8,128)(2,1)S(1)} %copy-done.5, bf16[32,3,192]{2,1,0:T(4,128)(2,1)S(1)} %collective-permute-done.2.right_ref, bf16[32,3,192]{2,1,0:T(4,128)(2,1)S(1)} %collective-permute-done.3.left_ref, ...), custom_call_target="tpu_custom_call" | custom-call | flops 19267584 | bytes 3000000 | tf_op jit(solution)/shard_map/pallas_call | solution.py:426
  87.5 0.0 all-to-all-done.2.rows_ref
  87.5 2.1 %shard_map.115 = (bf16[32,16,192]{2,1,0:T(8,128)(2,1)S(1)}, bf16[32,16,192]{2,1,0:T(8,128)(2,1)S(1)}, bf16[32,3,192]{2,1,0:T(4,128)(2,1)S(1)}, bf16[32,3,192]{2,1,0:T(4,128)(2,1)S(1)}) custom-call(f32[32,32,192]{2,1,0:T(8,128)S(1)} %get-tuple-element.48.partial_ref, bf16[16,32,384]{2,1,0:T(8,128)(2,1)S(1)} %all-to-all-done.2.rows_ref, ...), custom_call_target="tpu_custom_call" | custom-call | flops 301989888 | bytes 2500000 | tf_op jit(solution)/shard_map/pallas_call | solution.py:487
  89.6 1.9 %collective-permute-start.5 = (bf16[32,3,192]{2,1,0:T(4,128)(2,1)S(1)}, bf16[32,3,192]{2,1,0:T(4,128)(2,1)S(1)}, u32[]{:S(2)}, u32[]{:S(2)}) collective-permute-start(bf16[32,3,192]{2,1,0:T(4,128)(2,1)S(1)} %get-tuple-element.62), channel_id=1, source_target_pairs={{1,0},{2,1},{3,2},{4,3},{5,4},{6,5},{7,6},{8,7},{9,8},{10,9},{11,1... | collective-permute-start | bytes 110600 | tf_op jit(solution)/shard_map/ppermute | solution.py:611
  91.5 7.1 %collective-permute-start.4 = (bf16[32,3,192]{2,1,0:T(4,128)(2,1)S(1)}, bf16[32,3,192]{2,1,0:T(4,128)(2,1)S(1)}, u32[]{:S(2)}, u32[]{:S(2)}) collective-permute-start(bf16[32,3,192]{2,1,0:T(4,128)(2,1)S(1)} %get-tuple-element.54), channel_id=1, source_target_pairs={{0,1},{1,2},{2,3},{3,4},{4,5},{5,6},{6,7},{7,8},{8,9},{9,10},{10,1... | collective-permute-start | bytes 110600 | tf_op jit(solution)/shard_map/ppermute | solution.py:612
  98.7 2.1 %shard_map.116 = (bf16[32,16,192]{2,1,0:T(8,128)(2,1)S(1)}, bf16[32,16,192]{2,1,0:T(8,128)(2,1)S(1)}) custom-call(f32[32,32,192]{2,1,0:T(8,128)S(1)} %get-tuple-element.48.partial_ref, bf16[16,32,384]{2,1,0:T(8,128)(2,1)S(1)} %all-to-all-done.2.rows_ref, f32[8,128]{1,0:T(8,128)S(1)} %get-tuple-element.50.cell_ref.hot_ref, bf16[32,32,768]{2,1,0:T(8,128)(2,1)S(1)} %bitcast.13, ...), custom_call_target="tpu_custom_call" | custom-call | flops 301989888 | bytes 2500000 | tf_op jit(solution)/shard_map/pallas_call | solution.py:487
  100.7 5.1 %shard_map.117 = (bf16[32,32,192]{2,1,0:T(8,128)(2,1)}, f32[32,8,192]{2,1,0:T(8,128)S(1)}, f32[32,8,192]{2,1,0:T(8,128)S(1)}) custom-call(bf16[32,16,192]{2,1,0:T(8,128)(2,1)S(1)} %get-tuple-element.53.rim_ref, bf16[32,16,192]{2,1,0:T(8,128)(2,1)S(1)} %get-tuple-element.56.inner_ref, bf16[32,16,192]{2,1,0:T(8,128)(2,1)S(1)} %get-tuple-element.57.rim_adjoint, ...), custom_call_target="tpu_custom_call" | custom-call | flops 19267584 | bytes 3000000 | tf_op jit(solution)/shard_map/pallas_call | solution.py:536
  105.8 0.0 collective-permute-done.5.right_ref
  105.8 0.0 collective-permute-done.4.left_ref
  105.9 1.4 %shard_map.118 = bf16[32,32,192]{2,1,0:T(8,128)(2,1)} custom-call(bf16[32,32,192]{2,1,0:T(8,128)(2,1)} %get-tuple-element.59.inner_ref, f32[32,8,192]{2,1,0:T(8,128)S(1)} %get-tuple-element.60.west_ref, f32[32,8,192]{2,1,0:T(8,128)S(1)} %get-tuple-element.61.east_ref, ...), custom_call_target="tpu_custom_call", output_to_operand_aliasing={{}: (0, {})} | custom-call | flops 5000000 | bytes 700000 | tf_op jit(solution)/shard_map/pallas_call | solution.py:592
  (1 shorter events, 0.0 us)
Async XLA Ops:
  1.5 28.8 %copy-start = (bf16[2,1,32,32,192]{4,3,2,1,0:T(8,128)(2,1)S(1)}, bf16[2,1,32,32,192]{4,3,2,1,0:T(8,128)(2,1)}, u32[]{:S(2)}) copy-start(bf16[2,1,32,32,192]{4,3,2,1,0:T(8,128)(2,1)} %state_ref.2) | copy-start | bytes 2359300
  1.5 37.8 %copy-start.10 = (f32[768]{0:T(1024)S(1)}, f32[768]{0:T(1024)}, u32[]{:S(2)}) copy-start(f32[768]{0:T(1024)} %param.16) | copy-start | bytes 9220
  1.6 39.7 %copy-start.1 = (bf16[192,768]{1,0:T(8,128)(2,1)S(1)}, bf16[192,768]{1,0:T(8,128)(2,1)}, u32[]{:S(2)}) copy-start(bf16[192,768]{1,0:T(8,128)(2,1)} %up_ref.7) | copy-start | bytes 884740
  1.6 39.7 %copy-start.2 = (bf16[768,192]{0,1:T(8,128)(2,1)S(1)}, bf16[768,192]{0,1:T(8,128)(2,1)}, u32[]{:S(2)}) copy-start(bf16[768,192]{0,1:T(8,128)(2,1)} %param.17) | copy-start | bytes 884740
  1.6 39.7 %copy-start.6 = (f32[7,7,192]{2,1,0:T(8,128)S(1)}, f32[7,7,192]{2,1,0:T(8,128)}, u32[]{:S(2)}) copy-start(f32[7,7,192]{2,1,0:T(8,128)} %kernel_ref.9) | copy-start | bytes 112900
  1.6 39.7 %copy-start.7 = (f32[192]{0:T(256)S(1)}, f32[192]{0:T(256)}, u32[]{:S(2)}) copy-start(f32[192]{0:T(256)} %param.14) | copy-start | bytes 2308
  15.6 36.3 %all-to-all-start.1 = ((bf16[16,32,384]{2,1,0:T(8,128)(2,1)}), bf16[16,32,384]{2,1,0:T(8,128)(2,1)S(1)}, u32[]{:S(2)}, u32[]{:S(2)}) async-start(bf16[16,32,384]{2,1,0:T(8,128)(2,1)} %shard_map.110), calls=%async_computation.1 | async-start | bytes 786432 | tf_op jit(solution)/shard_map/all_to_all | solution.py:621
  30.4 9.9 %collective-permute-start.1 = (bf16[2,32,3,192]{3,2,1,0:T(4,128)(2,1)S(1)}, bf16[2,32,3,192]{3,2,1,0:T(4,128)(2,1)S(1)}, u32[]{:S(2)}, u32[]{:S(2)}) collective-permute-start(bf16[2,32,3,192]{3,2,1,0:T(4,128)(2,1)S(1)} %get-tuple-element.63), channel_id=1, source_target_pairs={{1,0},{2,1},{3,2},{4,3},{5,4},{6,5},{7,6},{8,7},{9,8},{10,9},{11,1... | collective-permute-start | bytes 221192 | tf_op jit(solution)/shard_map/ppermute | solution.py:611
  33.3 8.0 %collective-permute-start = (bf16[2,32,3,192]{3,2,1,0:T(4,128)(2,1)S(1)}, bf16[2,32,3,192]{3,2,1,0:T(4,128)(2,1)S(1)}, u32[]{:S(2)}, u32[]{:S(2)}) collective-permute-start(bf16[2,32,3,192]{3,2,1,0:T(4,128)(2,1)S(1)} %get-tuple-element.64), channel_id=1, source_target_pairs={{0,1},{1,2},{2,3},{3,4},{4,5},{5,6},{6,7},{7,8},{8,9},{9,10},{10,1... | collective-permute-start | bytes 221192 | tf_op jit(solution)/shard_map/ppermute | solution.py:612
  41.3 1.0 copy-start.3
  50.9 12.8 %copy-start.12 = (bf16[32,3,192]{2,1,0:T(4,128)(2,1)S(1)}, bf16[32,3,192]{2,1,0:T(4,128)(2,1)}, u32[]{:S(2)}) copy-start(bf16[32,3,192]{2,1,0:T(4,128)(2,1)} %get-tuple-element.41) | copy-start | bytes 110596
  50.9 14.7 %copy-start.11 = (bf16[32,3,192]{2,1,0:T(4,128)(2,1)S(1)}, bf16[32,3,192]{2,1,0:T(4,128)(2,1)}, u32[]{:S(2)}) copy-start(bf16[32,3,192]{2,1,0:T(4,128)(2,1)} %get-tuple-element.47) | copy-start | bytes 110596
  50.9 23.0 %copy-start.8 = (bf16[32,3,192]{2,1,0:T(4,128)(2,1)S(1)}, bf16[32,3,192]{2,1,0:T(4,128)(2,1)}, u32[]{:S(2)}) copy-start(bf16[32,3,192]{2,1,0:T(4,128)(2,1)} %get-tuple-element.44.right_ref) | copy-start | bytes 110596
  50.9 23.0 %copy-start.9 = (bf16[32,3,192]{2,1,0:T(4,128)(2,1)S(1)}, bf16[32,3,192]{2,1,0:T(4,128)(2,1)}, u32[]{:S(2)}) copy-start(bf16[32,3,192]{2,1,0:T(4,128)(2,1)} %get-tuple-element.43.left_ref) | copy-start | bytes 110596
  53.2 34.3 %all-to-all-start.2 = ((bf16[16,32,384]{2,1,0:T(8,128)(2,1)}), bf16[16,32,384]{2,1,0:T(8,128)(2,1)S(1)}, u32[]{:S(2)}, u32[]{:S(2)}) async-start(bf16[16,32,384]{2,1,0:T(8,128)(2,1)} %shard_map.112), calls=%async_computation.2 | async-start | bytes 786432 | tf_op jit(solution)/shard_map/all_to_all | solution.py:621
  63.7 18.4 %collective-permute-start.2 = (bf16[32,3,192]{2,1,0:T(4,128)(2,1)S(1)}, bf16[32,3,192]{2,1,0:T(4,128)(2,1)S(1)}, u32[]{:S(2)}, u32[]{:S(2)}) collective-permute-start(bf16[32,3,192]{2,1,0:T(4,128)(2,1)S(1)} %copy-done.12), channel_id=1, source_target_pairs={{1,0},{2,1},{3,2},{4,3},{5,4},{6,5},{7,6},{8,7},{9,8},{10,9},{11,1... | collective-permute-start | bytes 110600 | tf_op jit(solution)/shard_map/ppermute | solution.py:611
  65.7 16.4 %collective-permute-start.3 = (bf16[32,3,192]{2,1,0:T(4,128)(2,1)S(1)}, bf16[32,3,192]{2,1,0:T(4,128)(2,1)S(1)}, u32[]{:S(2)}, u32[]{:S(2)}) collective-permute-start(bf16[32,3,192]{2,1,0:T(4,128)(2,1)S(1)} %copy-done.11), channel_id=1, source_target_pairs={{0,1},{1,2},{2,3},{3,4},{4,5},{5,6},{6,7},{7,8},{8,9},{9,10},{10,1... | collective-permute-start | bytes 110600 | tf_op jit(solution)/shard_map/ppermute | solution.py:612
  73.9 8.2 %copy-start.4 = (bf16[1,32,32,192]{3,2,1,0:T(8,128)(2,1)S(1)}, bf16[1,32,32,192]{3,2,1,0:T(8,128)(2,1)}, u32[]{:S(2)}) copy-start(bf16[1,32,32,192]{3,2,1,0:T(8,128)(2,1)} %base_ref.1) | copy-start | bytes 1179652
  74.0 8.2 %copy-start.5 = (bf16[32,32,192]{2,1,0:T(8,128)(2,1)S(1)}, bf16[32,32,192]{2,1,0:T(8,128)(2,1)}, u32[]{:S(2)}) copy-start(bf16[32,32,192]{2,1,0:T(8,128)(2,1)} %get-tuple-element.37.hidden_ref) | copy-start | bytes 1179652
  89.6 16.3 %collective-permute-start.5 = (bf16[32,3,192]{2,1,0:T(4,128)(2,1)S(1)}, bf16[32,3,192]{2,1,0:T(4,128)(2,1)S(1)}, u32[]{:S(2)}, u32[]{:S(2)}) collective-permute-start(bf16[32,3,192]{2,1,0:T(4,128)(2,1)S(1)} %get-tuple-element.62), channel_id=1, source_target_pairs={{1,0},{2,1},{3,2},{4,3},{5,4},{6,5},{7,6},{8,7},{9,8},{10,9},{11,1... | collective-permute-start | bytes 110600 | tf_op jit(solution)/shard_map/ppermute | solution.py:611
  91.5 14.3 %collective-permute-start.4 = (bf16[32,3,192]{2,1,0:T(4,128)(2,1)S(1)}, bf16[32,3,192]{2,1,0:T(4,128)(2,1)S(1)}, u32[]{:S(2)}, u32[]{:S(2)}) collective-permute-start(bf16[32,3,192]{2,1,0:T(4,128)(2,1)S(1)} %get-tuple-element.54), channel_id=1, source_target_pairs={{0,1},{1,2},{2,3},{3,4},{4,5},{5,6},{6,7},{7,8},{8,9},{9,10},{10,1... | collective-permute-start | bytes 110600 | tf_op jit(solution)/shard_map/ppermute | solution.py:612

commit v10 on v8

--- a/solution.py
+++ b/solution.py
@@ -21,7 +21,7 @@
 SLOTS = LAT * CAP
 BLK = 8
 ROWS = BLK * WID
-UNROLL = 4
+UNROLL = 8
 HALF = LAT // 2
 f32 = jnp.float32
 bf16 = jnp.bfloat16
@@ -163,17 +163,19 @@
     cell_far, count_far, value_far, error_far, state_far,
     out_ref, near_ref, cell_ref, count_ref, value_ref, error_ref, sems,
 ):
-    pairs = [(cell_far, cell_ref), (count_far, count_ref), (value_far, value_ref), (error_far, error_ref)]
+    member = lax.axis_index("member")
+    base = pl.multiple_of(member // 8 * 8, 8)
+    near_slots = value_far.at[:, :, :, pl.ds(base, 8), :]
+    pairs = [(cell_far, cell_ref), (count_far, count_ref), (near_slots, value_ref), (error_far, error_ref)]
     copies = fetch(pairs + [(state_far, near_ref)], sems)
     for copy in copies[:4]:
         copy.wait()
-    member = lax.axis_index("member")
     tiles = cell_ref.shape[2]
     slot = lax.broadcasted_iota(jnp.int32, (CAP, tiles), 0)
     across = lax.broadcasted_iota(jnp.int32, (CAP, CAP), 1)
     same = jnp.where(lax.broadcasted_iota(jnp.int32, (CAP, CAP), 0) == across, 1.0, 0.0).astype(bf16)
     own = jnp.where(lax.broadcasted_iota(jnp.int32, (CAP, CAP), 0) == member, 1.0, 0.0).astype(bf16)
-    deep = lax.broadcasted_iota(jnp.int32, (tiles, CAP, CH), 1)
+    deep = lax.broadcasted_iota(jnp.int32, (tiles, 8, CH), 1) + base
     for step in range(2):
         live = slot < count_ref[step]
         cells = jnp.where(live, cell_ref[step], -1).astype(f32).astype(bf16)
@@ -192,7 +194,7 @@
         out_shape=(jax.ShapeDtypeStruct((cells.shape[2], 4, 128), f32), pltpu.VMEM(states.shape, bf16)),
         in_specs=[HBM] * 5,
         out_specs=(VM, VM),
-        scratch_shapes=[pltpu.VMEM(array.shape, array.dtype) for array in (cells, counts, values, errors)]
+        scratch_shapes=[pltpu.VMEM(array.shape, array.dtype) for array in (cells, counts, values[:, :, :, :8], errors)]
         + [pltpu.SemaphoreType.DMA((5,))],
         compiler_params=limit(6),
     )(far(cells), far(counts), far(values), far(errors), far(states))

time: 106 us -> 106 us (level)
  transfers between devices with their start and end apart: 8 -> 8, of which waited for: 5 -> 5; matrix products, arithmetic and copies ran while one was open for 0% -> 0% of each run, Pallas kernels for 26% -> 25%
where the time goes in v10:
time: 106 us; the launch traced here: 105 us
  starting transfers between devices  40.7 us (38%)
  Pallas kernels  35.3 us (33%)
  blocking collectives  14.8 us (14%)
  waiting for transfers between devices  13.8 us (13%)
    all_to_all x2, starting transfers between devices, exchange(): return lax.all_to_all(array, axis, split_axis=0, concat_axis=0, tiled=True)  26.1 us
    pallas_call x2, Pallas kernels, forward(): pl.pallas_call(functools.partial(forward_kernel, step), out_shape=shapes,...  16.5 us
    all_to_all x1, blocking collectives, exchange(): return lax.all_to_all(array, axis, split_axis=0, concat_axis=0, tiled=True)  14.8 us
    ppermute x3, waiting for transfers between devices, swap_edges(): left = lax.ppermute(tail, 'tile', up)  9.12 us
    ppermute x3, starting transfers between devices, swap_edges(): right = lax.ppermute(head, 'tile', down)  8.37 us
    ppermute x3, starting transfers between devices, swap_edges(): left = lax.ppermute(tail, 'tile', up)  6.25 us
    pallas_call x1, Pallas kernels, spread_back(): pl.pallas_call(spread_kernel, out_shape=(jax.ShapeDtypeStruct((LAT, WID,...  5.16 us
    pallas_call x1, Pallas kernels, interior(): pl.pallas_call(interior_kernel, out_shape=(pltpu.HBM((LAT, WID, CH), bf16...  4.94 us
  transfers between devices with their start and end apart: 8, of which 5 were waited for; matrix products, arithmetic and copies ran while one was open for 0% of the time, Pallas kernels for 25%

profile of v10, /device:TPU:32, one launch (start us, length us, event | category | flops | bytes accessed | tf_op | source)
XLA Modules:
  0.0 105.0 jit_solution(14788030772978306600)
XLA Ops:
  0.0 1.4 %shard_map.109 = (f32[32,4,128]{2,1,0:T(4,128)S(1)}, bf16[2,1,32,32,192]{4,3,2,1,0:T(8,128)(2,1)S(1)}) custom-call(s32[2,16,32]{2,1,0:T(8,128)} %bitcast.16, s32[2,1,32]{2,1,0:T(1,128)} %count_far.1, bf16[2,1,32,16,192]{4,3,2,1,0:T(8,128)(2,1)} %value_far.1, bf16[2,16,32]{2,1,0:T(8,128)(2,1)} %bitcast.17, bf16[2,1,32,32,192]{4,3,2,1,0:T(8,128)(2,1)} %state_ref.2), custom_call_target="tpu_custom_call" | custom-call | tf_op jit(solution)/shard_map/pallas_call | solution.py:192
  1.4 0.0 copy-start
  1.4 0.0 copy-start.10
  1.4 0.0 copy-start.1
  1.4 0.0 copy-start.4
  1.5 0.0 copy-start.5
  1.5 0.0 copy-start.6
  1.5 0.0 copy-start.7
  1.5 14.8 %all_to_all.15.got_ref = f32[32,4,128]{2,1,0:T(4,128)S(1)} all-to-all(f32[32,4,128]{2,1,0:T(4,128)S(1)} %get-tuple-element.31), channel_id=1, replica_groups=mesh['member'=16,'tile'=32] {'tile'}, dimensions={0} | all-to-all | bytes 131072 | tf_op jit(solution)/shard_map/all_to_all | solution.py:585
  16.3 2.4 %shard_map.110 = bf16[16,32,384]{2,1,0:T(8,128)(2,1)} custom-call(f32[32,4,128]{2,1,0:T(4,128)S(1)} %all_to_all.15.got_ref, bf16[2,1,32,32,192]{4,3,2,1,0:T(8,128)(2,1)S(1)} %get-tuple-element.32.state_ref), custom_call_target="tpu_custom_call" | custom-call | flops 1000000 | bytes 2000000 | tf_op jit(solution)/shard_map/pallas_call | solution.py:233
  18.7 15.2 %all-to-all-start.1 = ((bf16[16,32,384]{2,1,0:T(8,128)(2,1)}), bf16[16,32,384]{2,1,0:T(8,128)(2,1)S(1)}, u32[]{:S(2)}, u32[]{:S(2)}) async-start(bf16[16,32,384]{2,1,0:T(8,128)(2,1)} %shard_map.110), calls=%async_computation.1 | async-start | bytes 786432 | tf_op jit(solution)/shard_map/all_to_all | solution.py:585
  33.9 0.0 copy-done
  33.9 0.1 fusion
  34.0 2.9 %collective-permute-start.1 = (bf16[2,32,3,192]{3,2,1,0:T(4,128)(2,1)S(1)}, bf16[2,32,3,192]{3,2,1,0:T(4,128)(2,1)S(1)}, u32[]{:S(2)}, u32[]{:S(2)}) collective-permute-start(bf16[2,32,3,192]{3,2,1,0:T(4,128)(2,1)S(1)} %get-tuple-element.57), channel_id=1, source_target_pairs={{1,0},{2,1},{3,2},{4,3},{5,4},{6,5},{7,6},{8,7},{9,8},{10,9},{11,1... | collective-permute-start | bytes 221192 | tf_op jit(solution)/shard_map/ppermute | solution.py:575
  36.9 1.9 %collective-permute-start = (bf16[2,32,3,192]{3,2,1,0:T(4,128)(2,1)S(1)}, bf16[2,32,3,192]{3,2,1,0:T(4,128)(2,1)S(1)}, u32[]{:S(2)}, u32[]{:S(2)}) collective-permute-start(bf16[2,32,3,192]{3,2,1,0:T(4,128)(2,1)S(1)} %get-tuple-element.58), channel_id=1, source_target_pairs={{0,1},{1,2},{2,3},{3,4},{4,5},{5,6},{6,7},{7,8},{8,9},{9,10},{10,1... | collective-permute-start | bytes 221192 | tf_op jit(solution)/shard_map/ppermute | solution.py:576
  38.8 0.0 copy-done.10
  38.8 0.5 collective-permute-done.1.right_ref
  39.4 7.1 %collective-permute-done.left_ref = bf16[2,32,3,192]{3,2,1,0:T(4,128)(2,1)S(1)} collective-permute-done((bf16[2,32,3,192]{3,2,1,0:T(4,128)(2,1)S(1)}, bf16[2,32,3,192]{3,2,1,0:T(4,128)(2,1)S(1)}, u32[]{:S(2)}, u32[]{:S(2)}) %collective-permute-start) | collective-permute-done | bytes 73760 | tf_op jit(solution)/shard_map/ppermute | solution.py:576
  46.5 0.0 copy-done.1
  46.5 0.0 copy-done.4
  46.5 0.0 copy-done.5
  46.5 0.0 copy-done.6
  46.5 0.0 copy-done.7
  46.5 8.5 %shard_map.111 = (bf16[32,32,192]{2,1,0:T(8,128)(2,1)}, bf16[32,3,192]{2,1,0:T(4,128)(2,1)}, bf16[32,3,192]{2,1,0:T(4,128)(2,1)}, bf16[32,3,192]{2,1,0:T(4,128)(2,1)}, bf16[32,3,192]{2,1,0:T(4,128)(2,1)}) custom-call(bf16[2,1,32,32,192]{4,3,2,1,0:T(8,128)(2,1)S(1)} %copy-done, bf16[2,32,3,192]{3,2,1,0:T(4,128)(2,1)S(1)} %collective-permute-done.left_ref, ...), custom_call_target="tpu_custom_call" | custom-call | flops 905969664 | bytes 8000000 | tf_op jit(solution)/shard_map/pallas_call | solution.py:381
  55.0 0.0 copy-start.12
  55.0 0.0 copy-start.11
  55.0 0.0 copy-start.8
  55.0 0.0 copy-start.9
  55.0 1.2 %all-to-all-done.1.rows_ref = bf16[16,32,384]{2,1,0:T(8,128)(2,1)S(1)} async-done(((bf16[16,32,384]{2,1,0:T(8,128)(2,1)}), bf16[16,32,384]{2,1,0:T(8,128)(2,1)S(1)}, u32[]{:S(2)}, u32[]{:S(2)}) %all-to-all-start.1) | async-done | bytes 393248 | tf_op jit(solution)/shard_map/all_to_all | solution.py:585
  56.2 1.2 %shard_map.112 = bf16[16,32,384]{2,1,0:T(8,128)(2,1)} custom-call(bf16[16,32,384]{2,1,0:T(8,128)(2,1)S(1)} %all-to-all-done.1.rows_ref, f32[32,4,128]{2,1,0:T(4,128)S(1)} %all_to_all.15.got_ref), custom_call_target="tpu_custom_call" | custom-call | flops 1200000 | bytes 1200000 | tf_op jit(solution)/shard_map/pallas_call | solution.py:268
  57.4 10.8 %all-to-all-start.2 = ((bf16[16,32,384]{2,1,0:T(8,128)(2,1)}), bf16[16,32,384]{2,1,0:T(8,128)(2,1)S(1)}, u32[]{:S(2)}, u32[]{:S(2)}) async-start(bf16[16,32,384]{2,1,0:T(8,128)(2,1)} %shard_map.112), calls=%async_computation.2 | async-start | bytes 786432 | tf_op jit(solution)/shard_map/all_to_all | solution.py:585
  68.3 0.0 copy-done.12
  68.3 1.9 %collective-permute-start.2 = (bf16[32,3,192]{2,1,0:T(4,128)(2,1)S(1)}, bf16[32,3,192]{2,1,0:T(4,128)(2,1)S(1)}, u32[]{:S(2)}, u32[]{:S(2)}) collective-permute-start(bf16[32,3,192]{2,1,0:T(4,128)(2,1)S(1)} %copy-done.12), channel_id=1, source_target_pairs={{1,0},{2,1},{3,2},{4,3},{5,4},{6,5},{7,6},{8,7},{9,8},{10,9},{11,1... | collective-permute-start | bytes 110600 | tf_op jit(solution)/shard_map/ppermute | solution.py:575
  70.2 0.0 copy-done.11
  70.2 2.4 %collective-permute-start.3 = (bf16[32,3,192]{2,1,0:T(4,128)(2,1)S(1)}, bf16[32,3,192]{2,1,0:T(4,128)(2,1)S(1)}, u32[]{:S(2)}, u32[]{:S(2)}) collective-permute-start(bf16[32,3,192]{2,1,0:T(4,128)(2,1)S(1)} %copy-done.11), channel_id=1, source_target_pairs={{0,1},{1,2},{2,3},{3,4},{4,5},{5,6},{6,7},{7,8},{8,9},{9,10},{10,1... | collective-permute-start | bytes 110600 | tf_op jit(solution)/shard_map/ppermute | solution.py:576
  72.6 0.0 copy-done.8
  72.6 0.0 copy-done.9
  72.7 0.0 copy-start.2
  72.7 0.0 copy-start.3
  72.7 8.0 %shard_map.113 = (bf16[1024,768]{1,0:T(8,128)(2,1)}, bf16[1024,192]{1,0:T(8,128)(2,1)}) custom-call(bf16[2,1,32,32,192]{4,3,2,1,0:T(8,128)(2,1)S(1)} %copy-done, bf16[32,3,192]{2,1,0:T(4,128)(2,1)S(1)} %copy-done.9, bf16[32,3,192]{2,1,0:T(4,128)(2,1)S(1)} %copy-done.8, f32[7,7,192]{2,1,0:T(8,128)S(1)} %copy-done.4, f32[1,192]{1,0:T(1,128)S(1)} %bitcast.14, ...), custom_call_target="tpu_custom_call" | custom-call | flops 905969664 | bytes 8000000 | tf_op jit(solution)/shard_map/pallas_call | solution.py:381
  80.6 0.0 collective-permute-done.2.right_ref
  80.6 0.0 collective-permute-done.3.left_ref
  80.6 0.0 copy-done.2
  80.7 0.0 copy-done.3
  80.7 5.2 %shard_map.114 = (f32[32,32,192]{2,1,0:T(8,128)S(1)}, bf16[1024,768]{1,0:T(8,128)(2,1)S(1)}, f32[8,128]{1,0:T(8,128)S(1)}) custom-call(bf16[32,32,192]{2,1,0:T(8,128)(2,1)S(1)} %copy-done.3, bf16[32,3,192]{2,1,0:T(4,128)(2,1)S(1)} %collective-permute-done.2.right_ref, bf16[32,3,192]{2,1,0:T(4,128)(2,1)S(1)} %collective-permute-done.3.left_ref, ...), custom_call_target="tpu_custom_call" | custom-call | flops 19267584 | bytes 3000000 | tf_op jit(solution)/shard_map/pallas_call | solution.py:417
  85.8 2.9 %all-to-all-done.2.rows_ref = bf16[16,32,384]{2,1,0:T(8,128)(2,1)S(1)} async-done(((bf16[16,32,384]{2,1,0:T(8,128)(2,1)}), bf16[16,32,384]{2,1,0:T(8,128)(2,1)S(1)}, u32[]{:S(2)}, u32[]{:S(2)}) %all-to-all-start.2) | async-done | bytes 393248 | tf_op jit(solution)/shard_map/all_to_all | solution.py:585
  88.7 2.4 %shard_map.115 = (bf16[32,32,192]{2,1,0:T(8,128)(2,1)S(1)}, bf16[32,3,192]{2,1,0:T(4,128)(2,1)S(1)}, bf16[32,3,192]{2,1,0:T(4,128)(2,1)S(1)}, bf16[32,32,192]{2,1,0:T(8,128)(2,1)S(1)}) custom-call(f32[32,32,192]{2,1,0:T(8,128)S(1)} %get-tuple-element.45.partial_ref, bf16[16,32,384]{2,1,0:T(8,128)(2,1)S(1)} %all-to-all-done.2.rows_ref, ...), custom_call_target="tpu_custom_call" | custom-call | flops 603979776 | bytes 5000000 | tf_op jit(solution)/shard_map/pallas_call | solution.py:457
  91.2 3.6 %collective-permute-start.4 = (bf16[32,3,192]{2,1,0:T(4,128)(2,1)S(1)}, bf16[32,3,192]{2,1,0:T(4,128)(2,1)S(1)}, u32[]{:S(2)}, u32[]{:S(2)}) collective-permute-start(bf16[32,3,192]{2,1,0:T(4,128)(2,1)S(1)} %get-tuple-element.55), channel_id=1, source_target_pairs={{1,0},{2,1},{3,2},{4,3},{5,4},{6,5},{7,6},{8,7},{9,8},{10,9},{11,1... | collective-permute-start | bytes 110600 | tf_op jit(solution)/shard_map/ppermute | solution.py:575
  94.8 1.9 %collective-permute-start.5 = (bf16[32,3,192]{2,1,0:T(4,128)(2,1)S(1)}, bf16[32,3,192]{2,1,0:T(4,128)(2,1)S(1)}, u32[]{:S(2)}, u32[]{:S(2)}) collective-permute-start(bf16[32,3,192]{2,1,0:T(4,128)(2,1)S(1)} %get-tuple-element.56), channel_id=1, source_target_pairs={{0,1},{1,2},{2,3},{3,4},{4,5},{5,6},{6,7},{7,8},{8,9},{9,10},{10,1... | collective-permute-start | bytes 110600 | tf_op jit(solution)/shard_map/ppermute | solution.py:576
  96.7 4.9 %shard_map.116 = (bf16[32,32,192]{2,1,0:T(8,128)(2,1)}, f32[32,8,192]{2,1,0:T(8,128)S(1)}, f32[32,8,192]{2,1,0:T(8,128)S(1)}) custom-call(bf16[32,32,192]{2,1,0:T(8,128)(2,1)S(1)} %get-tuple-element.50.hidden_ref, bf16[32,32,192]{2,1,0:T(8,128)(2,1)S(1)} %get-tuple-element.51.adjoint_ref, bf16[16,32,384]{2,1,0:T(8,128)(2,1)S(1)} %all-to-all-done.2.rows_ref, ...), custom_call_target="tpu_custom_call" | custom-call | flops 19267584 | bytes 3000000 | tf_op jit(solution)/shard_map/pallas_call | solution.py:500
  101.6 0.0 collective-permute-done.4.right_ref
  101.7 2.0 %collective-permute-done.5.left_ref = bf16[32,3,192]{2,1,0:T(4,128)(2,1)S(1)} collective-permute-done((bf16[32,3,192]{2,1,0:T(4,128)(2,1)S(1)}, bf16[32,3,192]{2,1,0:T(4,128)(2,1)S(1)}, u32[]{:S(2)}, u32[]{:S(2)}) %collective-permute-start.5) | collective-permute-done | bytes 36896 | tf_op jit(solution)/shard_map/ppermute | solution.py:576
  103.7 1.4 %shard_map.117 = bf16[32,32,192]{2,1,0:T(8,128)(2,1)} custom-call(bf16[32,32,192]{2,1,0:T(8,128)(2,1)} %get-tuple-element.52.inner_ref, f32[32,8,192]{2,1,0:T(8,128)S(1)} %get-tuple-element.53.west_ref, f32[32,8,192]{2,1,0:T(8,128)S(1)} %get-tuple-element.54.east_ref, ...), custom_call_target="tpu_custom_call", output_to_operand_aliasing={{}: (0, {})} | custom-call | flops 5000000 | bytes 700000 | tf_op jit(solution)/shard_map/pallas_call | solution.py:556
  (1 shorter events, 0.0 us)
Async XLA Ops:
  1.4 32.5 %copy-start = (bf16[2,1,32,32,192]{4,3,2,1,0:T(8,128)(2,1)S(1)}, bf16[2,1,32,32,192]{4,3,2,1,0:T(8,128)(2,1)}, u32[]{:S(2)}) copy-start(bf16[2,1,32,32,192]{4,3,2,1,0:T(8,128)(2,1)} %state_ref.2) | copy-start | bytes 2359300
  1.4 37.4 %copy-start.10 = (f32[768]{0:T(1024)S(1)}, f32[768]{0:T(1024)}, u32[]{:S(2)}) copy-start(f32[768]{0:T(1024)} %param.16) | copy-start | bytes 9220
  1.4 45.0 %copy-start.1 = (bf16[1,32,32,192]{3,2,1,0:T(8,128)(2,1)S(1)}, bf16[1,32,32,192]{3,2,1,0:T(8,128)(2,1)}, u32[]{:S(2)}) copy-start(bf16[1,32,32,192]{3,2,1,0:T(8,128)(2,1)} %base_ref.1) | copy-start | bytes 1179652
  1.4 45.0 %copy-start.4 = (f32[7,7,192]{2,1,0:T(8,128)S(1)}, f32[7,7,192]{2,1,0:T(8,128)}, u32[]{:S(2)}) copy-start(f32[7,7,192]{2,1,0:T(8,128)} %kernel_ref.9) | copy-start | bytes 112900
  1.5 45.0 %copy-start.5 = (bf16[192,768]{1,0:T(8,128)(2,1)S(1)}, bf16[192,768]{1,0:T(8,128)(2,1)}, u32[]{:S(2)}) copy-start(bf16[192,768]{1,0:T(8,128)(2,1)} %up_ref.5) | copy-start | bytes 884740
  1.5 45.0 %copy-start.6 = (bf16[768,192]{0,1:T(8,128)(2,1)S(1)}, bf16[768,192]{0,1:T(8,128)(2,1)}, u32[]{:S(2)}) copy-start(bf16[768,192]{0,1:T(8,128)(2,1)} %param.17) | copy-start | bytes 884740
  1.5 45.0 %copy-start.7 = (f32[192]{0:T(256)S(1)}, f32[192]{0:T(256)}, u32[]{:S(2)}) copy-start(f32[192]{0:T(256)} %param.14) | copy-start | bytes 2308
  18.7 37.6 %all-to-all-start.1 = ((bf16[16,32,384]{2,1,0:T(8,128)(2,1)}), bf16[16,32,384]{2,1,0:T(8,128)(2,1)S(1)}, u32[]{:S(2)}, u32[]{:S(2)}) async-start(bf16[16,32,384]{2,1,0:T(8,128)(2,1)} %shard_map.110), calls=%async_computation.1 | async-start | bytes 786432 | tf_op jit(solution)/shard_map/all_to_all | solution.py:585
  34.0 5.4 %collective-permute-start.1 = (bf16[2,32,3,192]{3,2,1,0:T(4,128)(2,1)S(1)}, bf16[2,32,3,192]{3,2,1,0:T(4,128)(2,1)S(1)}, u32[]{:S(2)}, u32[]{:S(2)}) collective-permute-start(bf16[2,32,3,192]{3,2,1,0:T(4,128)(2,1)S(1)} %get-tuple-element.57), channel_id=1, source_target_pairs={{1,0},{2,1},{3,2},{4,3},{5,4},{6,5},{7,6},{8,7},{9,8},{10,9},{11,1... | collective-permute-start | bytes 221192 | tf_op jit(solution)/shard_map/ppermute | solution.py:575
  36.9 9.6 %collective-permute-start = (bf16[2,32,3,192]{3,2,1,0:T(4,128)(2,1)S(1)}, bf16[2,32,3,192]{3,2,1,0:T(4,128)(2,1)S(1)}, u32[]{:S(2)}, u32[]{:S(2)}) collective-permute-start(bf16[2,32,3,192]{3,2,1,0:T(4,128)(2,1)S(1)} %get-tuple-element.58), channel_id=1, source_target_pairs={{0,1},{1,2},{2,3},{3,4},{4,5},{5,6},{6,7},{7,8},{8,9},{9,10},{10,1... | collective-permute-start | bytes 221192 | tf_op jit(solution)/shard_map/ppermute | solution.py:576
  55.0 13.3 %copy-start.12 = (bf16[32,3,192]{2,1,0:T(4,128)(2,1)S(1)}, bf16[32,3,192]{2,1,0:T(4,128)(2,1)}, u32[]{:S(2)}) copy-start(bf16[32,3,192]{2,1,0:T(4,128)(2,1)} %get-tuple-element.38) | copy-start | bytes 110596
  55.0 15.2 %copy-start.11 = (bf16[32,3,192]{2,1,0:T(4,128)(2,1)S(1)}, bf16[32,3,192]{2,1,0:T(4,128)(2,1)}, u32[]{:S(2)}) copy-start(bf16[32,3,192]{2,1,0:T(4,128)(2,1)} %get-tuple-element.44) | copy-start | bytes 110596
  55.0 17.6 %copy-start.8 = (bf16[32,3,192]{2,1,0:T(4,128)(2,1)S(1)}, bf16[32,3,192]{2,1,0:T(4,128)(2,1)}, u32[]{:S(2)}) copy-start(bf16[32,3,192]{2,1,0:T(4,128)(2,1)} %get-tuple-element.41.right_ref) | copy-start | bytes 110596
  55.0 17.6 %copy-start.9 = (bf16[32,3,192]{2,1,0:T(4,128)(2,1)S(1)}, bf16[32,3,192]{2,1,0:T(4,128)(2,1)}, u32[]{:S(2)}) copy-start(bf16[32,3,192]{2,1,0:T(4,128)(2,1)} %get-tuple-element.40.left_ref) | copy-start | bytes 110596
  57.4 31.3 %all-to-all-start.2 = ((bf16[16,32,384]{2,1,0:T(8,128)(2,1)}), bf16[16,32,384]{2,1,0:T(8,128)(2,1)S(1)}, u32[]{:S(2)}, u32[]{:S(2)}) async-start(bf16[16,32,384]{2,1,0:T(8,128)(2,1)} %shard_map.112), calls=%async_computation.2 | async-start | bytes 786432 | tf_op jit(solution)/shard_map/all_to_all | solution.py:585
  68.3 12.4 %collective-permute-start.2 = (bf16[32,3,192]{2,1,0:T(4,128)(2,1)S(1)}, bf16[32,3,192]{2,1,0:T(4,128)(2,1)S(1)}, u32[]{:S(2)}, u32[]{:S(2)}) collective-permute-start(bf16[32,3,192]{2,1,0:T(4,128)(2,1)S(1)} %copy-done.12), channel_id=1, source_target_pairs={{1,0},{2,1},{3,2},{4,3},{5,4},{6,5},{7,6},{8,7},{9,8},{10,9},{11,1... | collective-permute-start | bytes 110600 | tf_op jit(solution)/shard_map/ppermute | solution.py:575
  70.2 10.4 %collective-permute-start.3 = (bf16[32,3,192]{2,1,0:T(4,128)(2,1)S(1)}, bf16[32,3,192]{2,1,0:T(4,128)(2,1)S(1)}, u32[]{:S(2)}, u32[]{:S(2)}) collective-permute-start(bf16[32,3,192]{2,1,0:T(4,128)(2,1)S(1)} %copy-done.11), channel_id=1, source_target_pairs={{0,1},{1,2},{2,3},{3,4},{4,5},{5,6},{6,7},{7,8},{8,9},{9,10},{10,1... | collective-permute-start | bytes 110600 | tf_op jit(solution)/shard_map/ppermute | solution.py:576
  72.7 8.0 %copy-start.2 = (bf16[1,32,32,192]{3,2,1,0:T(8,128)(2,1)S(1)}, bf16[1,32,32,192]{3,2,1,0:T(8,128)(2,1)}, u32[]{:S(2)}) copy-start(bf16[1,32,32,192]{3,2,1,0:T(8,128)(2,1)} %base_ref.1) | copy-start | bytes 1179652
  72.7 8.0 %copy-start.3 = (bf16[32,32,192]{2,1,0:T(8,128)(2,1)S(1)}, bf16[32,32,192]{2,1,0:T(8,128)(2,1)}, u32[]{:S(2)}) copy-start(bf16[32,32,192]{2,1,0:T(8,128)(2,1)} %get-tuple-element.34.hidden_ref) | copy-start | bytes 1179652
  91.2 10.5 %collective-permute-start.4 = (bf16[32,3,192]{2,1,0:T(4,128)(2,1)S(1)}, bf16[32,3,192]{2,1,0:T(4,128)(2,1)S(1)}, u32[]{:S(2)}, u32[]{:S(2)}) collective-permute-start(bf16[32,3,192]{2,1,0:T(4,128)(2,1)S(1)} %get-tuple-element.55), channel_id=1, source_target_pairs={{1,0},{2,1},{3,2},{4,3},{5,4},{6,5},{7,6},{8,7},{9,8},{10,9},{11,1... | collective-permute-start | bytes 110600 | tf_op jit(solution)/shard_map/ppermute | solution.py:575
  94.8 8.9 %collective-permute-start.5 = (bf16[32,3,192]{2,1,0:T(4,128)(2,1)S(1)}, bf16[32,3,192]{2,1,0:T(4,128)(2,1)S(1)}, u32[]{:S(2)}, u32[]{:S(2)}) collective-permute-start(bf16[32,3,192]{2,1,0:T(4,128)(2,1)S(1)} %get-tuple-element.56), channel_id=1, source_target_pairs={{0,1},{1,2},{2,3},{3,4},{4,5},{5,6},{6,7},{7,8},{8,9},{9,10},{10,1... | collective-permute-start | bytes 110600 | tf_op jit(solution)/shard_map/ppermute | solution.py:576

commit v11 on v10

--- a/solution.py
+++ b/solution.py
@@ -21,7 +21,7 @@
 SLOTS = LAT * CAP
 BLK = 8
 ROWS = BLK * WID
-UNROLL = 8
+UNROLL = 16
 HALF = LAT // 2
 f32 = jnp.float32
 bf16 = jnp.bfloat16

time: 106 us -> 105 us (level)
  no operation moved by 1% of the time
where the time goes in v11:
time: 105 us
  starting transfers between devices  40.6 us (39%)
  Pallas kernels  34.8 us (33%)
  blocking collectives  14.8 us (14%)
  waiting for transfers between devices  14 us (13%)
    all_to_all x2, starting transfers between devices, exchange(): return lax.all_to_all(array, axis, split_axis=0, concat_axis=0, tiled=True)  25.9 us
    pallas_call x2, Pallas kernels, forward(): pl.pallas_call(functools.partial(forward_kernel, step), out_shape=shapes,...  16.2 us
    all_to_all x1, blocking collectives, exchange(): return lax.all_to_all(array, axis, split_axis=0, concat_axis=0, tiled=True)  14.8 us
    ppermute x3, waiting for transfers between devices, swap_edges(): left = lax.ppermute(tail, 'tile', up)  9.27 us
    ppermute x3, starting transfers between devices, swap_edges(): right = lax.ppermute(head, 'tile', down)  8.42 us
    ppermute x3, starting transfers between devices, swap_edges(): left = lax.ppermute(tail, 'tile', up)  6.25 us
    pallas_call x1, Pallas kernels, spread_back(): pl.pallas_call(spread_kernel, out_shape=(jax.ShapeDtypeStruct((LAT, WID,...  5.02 us
    pallas_call x1, Pallas kernels, interior(): pl.pallas_call(interior_kernel, out_shape=(pltpu.HBM((LAT, WID, CH), bf16...  4.8 us
  transfers between devices with their start and end apart: 8, of which 5 were waited for; matrix products, arithmetic and copies ran while one was open for 0% of the time, Pallas kernels for 25%

profile of v11, /device:TPU:32, one launch (start us, length us, event | category | flops | bytes accessed | tf_op | source)
XLA Modules:
  0.0 104.6 jit_solution(1381572960818839621)
XLA Ops:
  0.0 1.4 %shard_map.109 = (f32[32,4,128]{2,1,0:T(4,128)S(1)}, bf16[2,1,32,32,192]{4,3,2,1,0:T(8,128)(2,1)S(1)}) custom-call(s32[2,16,32]{2,1,0:T(8,128)} %bitcast.16, s32[2,1,32]{2,1,0:T(1,128)} %count_far.1, bf16[2,1,32,16,192]{4,3,2,1,0:T(8,128)(2,1)} %value_far.1, bf16[2,16,32]{2,1,0:T(8,128)(2,1)} %bitcast.17, bf16[2,1,32,32,192]{4,3,2,1,0:T(8,128)(2,1)} %state_ref.2), custom_call_target="tpu_custom_call" | custom-call | tf_op jit(solution)/shard_map/pallas_call | solution.py:192
  1.4 0.0 copy-start
  1.4 0.0 copy-start.10
  1.4 0.0 copy-start.1
  1.4 0.0 copy-start.4
  1.5 0.0 copy-start.5
  1.5 0.0 copy-start.6
  1.5 0.0 copy-start.7
  1.5 14.8 %all_to_all.15.got_ref = f32[32,4,128]{2,1,0:T(4,128)S(1)} all-to-all(f32[32,4,128]{2,1,0:T(4,128)S(1)} %get-tuple-element.31), channel_id=1, replica_groups=mesh['member'=16,'tile'=32] {'tile'}, dimensions={0} | all-to-all | bytes 131072 | tf_op jit(solution)/shard_map/all_to_all | solution.py:585
  16.3 2.4 %shard_map.110 = bf16[16,32,384]{2,1,0:T(8,128)(2,1)} custom-call(f32[32,4,128]{2,1,0:T(4,128)S(1)} %all_to_all.15.got_ref, bf16[2,1,32,32,192]{4,3,2,1,0:T(8,128)(2,1)S(1)} %get-tuple-element.32.state_ref), custom_call_target="tpu_custom_call" | custom-call | flops 1000000 | bytes 2000000 | tf_op jit(solution)/shard_map/pallas_call | solution.py:233
  18.7 15.2 %all-to-all-start.1 = ((bf16[16,32,384]{2,1,0:T(8,128)(2,1)}), bf16[16,32,384]{2,1,0:T(8,128)(2,1)S(1)}, u32[]{:S(2)}, u32[]{:S(2)}) async-start(bf16[16,32,384]{2,1,0:T(8,128)(2,1)} %shard_map.110), calls=%async_computation.1 | async-start | bytes 786432 | tf_op jit(solution)/shard_map/all_to_all | solution.py:585
  33.9 0.0 copy-done
  33.9 0.1 fusion
  34.0 2.9 %collective-permute-start.1 = (bf16[2,32,3,192]{3,2,1,0:T(4,128)(2,1)S(1)}, bf16[2,32,3,192]{3,2,1,0:T(4,128)(2,1)S(1)}, u32[]{:S(2)}, u32[]{:S(2)}) collective-permute-start(bf16[2,32,3,192]{3,2,1,0:T(4,128)(2,1)S(1)} %get-tuple-element.57), channel_id=1, source_target_pairs={{1,0},{2,1},{3,2},{4,3},{5,4},{6,5},{7,6},{8,7},{9,8},{10,9},{11,1... | collective-permute-start | bytes 221192 | tf_op jit(solution)/shard_map/ppermute | solution.py:575
  36.9 1.9 %collective-permute-start = (bf16[2,32,3,192]{3,2,1,0:T(4,128)(2,1)S(1)}, bf16[2,32,3,192]{3,2,1,0:T(4,128)(2,1)S(1)}, u32[]{:S(2)}, u32[]{:S(2)}) collective-permute-start(bf16[2,32,3,192]{3,2,1,0:T(4,128)(2,1)S(1)} %get-tuple-element.58), channel_id=1, source_target_pairs={{0,1},{1,2},{2,3},{3,4},{4,5},{5,6},{6,7},{7,8},{8,9},{9,10},{10,1... | collective-permute-start | bytes 221192 | tf_op jit(solution)/shard_map/ppermute | solution.py:576
  38.8 0.0 copy-done.10
  38.8 0.5 collective-permute-done.1.right_ref
  39.4 7.1 %collective-permute-done.left_ref = bf16[2,32,3,192]{3,2,1,0:T(4,128)(2,1)S(1)} collective-permute-done((bf16[2,32,3,192]{3,2,1,0:T(4,128)(2,1)S(1)}, bf16[2,32,3,192]{3,2,1,0:T(4,128)(2,1)S(1)}, u32[]{:S(2)}, u32[]{:S(2)}) %collective-permute-start) | collective-permute-done | bytes 73760 | tf_op jit(solution)/shard_map/ppermute | solution.py:576
  46.5 0.0 copy-done.1
  46.5 0.0 copy-done.4
  46.5 0.0 copy-done.5
  46.5 0.0 copy-done.6
  46.5 0.0 copy-done.7
  46.5 8.4 %shard_map.111 = (bf16[32,32,192]{2,1,0:T(8,128)(2,1)}, bf16[32,3,192]{2,1,0:T(4,128)(2,1)}, bf16[32,3,192]{2,1,0:T(4,128)(2,1)}, bf16[32,3,192]{2,1,0:T(4,128)(2,1)}, bf16[32,3,192]{2,1,0:T(4,128)(2,1)}) custom-call(bf16[2,1,32,32,192]{4,3,2,1,0:T(8,128)(2,1)S(1)} %copy-done, bf16[2,32,3,192]{3,2,1,0:T(4,128)(2,1)S(1)} %collective-permute-done.left_ref, ...), custom_call_target="tpu_custom_call" | custom-call | flops 905969664 | bytes 8000000 | tf_op jit(solution)/shard_map/pallas_call | solution.py:381
  54.9 0.0 copy-start.12
  54.9 0.0 copy-start.11
  54.9 0.0 copy-start.8
  54.9 0.0 copy-start.9
  54.9 1.3 %all-to-all-done.1.rows_ref = bf16[16,32,384]{2,1,0:T(8,128)(2,1)S(1)} async-done(((bf16[16,32,384]{2,1,0:T(8,128)(2,1)}), bf16[16,32,384]{2,1,0:T(8,128)(2,1)S(1)}, u32[]{:S(2)}, u32[]{:S(2)}) %all-to-all-start.1) | async-done | bytes 393248 | tf_op jit(solution)/shard_map/all_to_all | solution.py:585
  56.2 1.2 %shard_map.112 = bf16[16,32,384]{2,1,0:T(8,128)(2,1)} custom-call(bf16[16,32,384]{2,1,0:T(8,128)(2,1)S(1)} %all-to-all-done.1.rows_ref, f32[32,4,128]{2,1,0:T(4,128)S(1)} %all_to_all.15.got_ref), custom_call_target="tpu_custom_call" | custom-call | flops 1200000 | bytes 1200000 | tf_op jit(solution)/shard_map/pallas_call | solution.py:268
  57.4 10.7 %all-to-all-start.2 = ((bf16[16,32,384]{2,1,0:T(8,128)(2,1)}), bf16[16,32,384]{2,1,0:T(8,128)(2,1)S(1)}, u32[]{:S(2)}, u32[]{:S(2)}) async-start(bf16[16,32,384]{2,1,0:T(8,128)(2,1)} %shard_map.112), calls=%async_computation.2 | async-start | bytes 786432 | tf_op jit(solution)/shard_map/all_to_all | solution.py:585
  68.2 0.0 copy-done.12
  68.2 1.9 %collective-permute-start.2 = (bf16[32,3,192]{2,1,0:T(4,128)(2,1)S(1)}, bf16[32,3,192]{2,1,0:T(4,128)(2,1)S(1)}, u32[]{:S(2)}, u32[]{:S(2)}) collective-permute-start(bf16[32,3,192]{2,1,0:T(4,128)(2,1)S(1)} %copy-done.12), channel_id=1, source_target_pairs={{1,0},{2,1},{3,2},{4,3},{5,4},{6,5},{7,6},{8,7},{9,8},{10,9},{11,1... | collective-permute-start | bytes 110600 | tf_op jit(solution)/shard_map/ppermute | solution.py:575
  70.1 0.0 copy-done.11
  70.1 2.4 %collective-permute-start.3 = (bf16[32,3,192]{2,1,0:T(4,128)(2,1)S(1)}, bf16[32,3,192]{2,1,0:T(4,128)(2,1)S(1)}, u32[]{:S(2)}, u32[]{:S(2)}) collective-permute-start(bf16[32,3,192]{2,1,0:T(4,128)(2,1)S(1)} %copy-done.11), channel_id=1, source_target_pairs={{0,1},{1,2},{2,3},{3,4},{4,5},{5,6},{6,7},{7,8},{8,9},{9,10},{10,1... | collective-permute-start | bytes 110600 | tf_op jit(solution)/shard_map/ppermute | solution.py:576
  72.5 0.0 copy-done.8
  72.5 0.0 copy-done.9
  72.5 0.0 copy-start.2
  72.5 0.0 copy-start.3
  72.6 7.8 %shard_map.113 = (bf16[1024,768]{1,0:T(8,128)(2,1)}, bf16[1024,192]{1,0:T(8,128)(2,1)}) custom-call(bf16[2,1,32,32,192]{4,3,2,1,0:T(8,128)(2,1)S(1)} %copy-done, bf16[32,3,192]{2,1,0:T(4,128)(2,1)S(1)} %copy-done.9, bf16[32,3,192]{2,1,0:T(4,128)(2,1)S(1)} %copy-done.8, f32[7,7,192]{2,1,0:T(8,128)S(1)} %copy-done.4, f32[1,192]{1,0:T(1,128)S(1)} %bitcast.14, ...), custom_call_target="tpu_custom_call" | custom-call | flops 905969664 | bytes 8000000 | tf_op jit(solution)/shard_map/pallas_call | solution.py:381
  80.4 0.0 collective-permute-done.2.right_ref
  80.4 0.0 collective-permute-done.3.left_ref
  80.4 0.0 copy-done.2
  80.4 0.0 copy-done.3
  80.4 5.0 %shard_map.114 = (f32[32,32,192]{2,1,0:T(8,128)S(1)}, bf16[1024,768]{1,0:T(8,128)(2,1)S(1)}, f32[8,128]{1,0:T(8,128)S(1)}) custom-call(bf16[32,32,192]{2,1,0:T(8,128)(2,1)S(1)} %copy-done.3, bf16[32,3,192]{2,1,0:T(4,128)(2,1)S(1)} %collective-permute-done.2.right_ref, bf16[32,3,192]{2,1,0:T(4,128)(2,1)S(1)} %collective-permute-done.3.left_ref, ...), custom_call_target="tpu_custom_call" | custom-call | flops 19267584 | bytes 3000000 | tf_op jit(solution)/shard_map/pallas_call | solution.py:417
  85.4 2.8 %all-to-all-done.2.rows_ref = bf16[16,32,384]{2,1,0:T(8,128)(2,1)S(1)} async-done(((bf16[16,32,384]{2,1,0:T(8,128)(2,1)}), bf16[16,32,384]{2,1,0:T(8,128)(2,1)S(1)}, u32[]{:S(2)}, u32[]{:S(2)}) %all-to-all-start.2) | async-done | bytes 393248 | tf_op jit(solution)/shard_map/all_to_all | solution.py:585
  88.3 2.4 %shard_map.115 = (bf16[32,32,192]{2,1,0:T(8,128)(2,1)S(1)}, bf16[32,3,192]{2,1,0:T(4,128)(2,1)S(1)}, bf16[32,3,192]{2,1,0:T(4,128)(2,1)S(1)}, bf16[32,32,192]{2,1,0:T(8,128)(2,1)S(1)}) custom-call(f32[32,32,192]{2,1,0:T(8,128)S(1)} %get-tuple-element.45.partial_ref, bf16[16,32,384]{2,1,0:T(8,128)(2,1)S(1)} %all-to-all-done.2.rows_ref, ...), custom_call_target="tpu_custom_call" | custom-call | flops 603979776 | bytes 5000000 | tf_op jit(solution)/shard_map/pallas_call | solution.py:457
  90.7 3.6 %collective-permute-start.4 = (bf16[32,3,192]{2,1,0:T(4,128)(2,1)S(1)}, bf16[32,3,192]{2,1,0:T(4,128)(2,1)S(1)}, u32[]{:S(2)}, u32[]{:S(2)}) collective-permute-start(bf16[32,3,192]{2,1,0:T(4,128)(2,1)S(1)} %get-tuple-element.55), channel_id=1, source_target_pairs={{1,0},{2,1},{3,2},{4,3},{5,4},{6,5},{7,6},{8,7},{9,8},{10,9},{11,1... | collective-permute-start | bytes 110600 | tf_op jit(solution)/shard_map/ppermute | solution.py:575
  94.4 1.9 %collective-permute-start.5 = (bf16[32,3,192]{2,1,0:T(4,128)(2,1)S(1)}, bf16[32,3,192]{2,1,0:T(4,128)(2,1)S(1)}, u32[]{:S(2)}, u32[]{:S(2)}) collective-permute-start(bf16[32,3,192]{2,1,0:T(4,128)(2,1)S(1)} %get-tuple-element.56), channel_id=1, source_target_pairs={{0,1},{1,2},{2,3},{3,4},{4,5},{5,6},{6,7},{7,8},{8,9},{9,10},{10,1... | collective-permute-start | bytes 110600 | tf_op jit(solution)/shard_map/ppermute | solution.py:576
  96.3 4.8 %shard_map.116 = (bf16[32,32,192]{2,1,0:T(8,128)(2,1)}, f32[32,8,192]{2,1,0:T(8,128)S(1)}, f32[32,8,192]{2,1,0:T(8,128)S(1)}) custom-call(bf16[32,32,192]{2,1,0:T(8,128)(2,1)S(1)} %get-tuple-element.50.hidden_ref, bf16[32,32,192]{2,1,0:T(8,128)(2,1)S(1)} %get-tuple-element.51.adjoint_ref, bf16[16,32,384]{2,1,0:T(8,128)(2,1)S(1)} %all-to-all-done.2.rows_ref, ...), custom_call_target="tpu_custom_call" | custom-call | flops 19267584 | bytes 3000000 | tf_op jit(solution)/shard_map/pallas_call | solution.py:500
  101.1 0.0 collective-permute-done.4.right_ref
  101.1 2.2 %collective-permute-done.5.left_ref = bf16[32,3,192]{2,1,0:T(4,128)(2,1)S(1)} collective-permute-done((bf16[32,3,192]{2,1,0:T(4,128)(2,1)S(1)}, bf16[32,3,192]{2,1,0:T(4,128)(2,1)S(1)}, u32[]{:S(2)}, u32[]{:S(2)}) %collective-permute-start.5) | collective-permute-done | bytes 36896 | tf_op jit(solution)/shard_map/ppermute | solution.py:576
  103.3 1.4 %shard_map.117 = bf16[32,32,192]{2,1,0:T(8,128)(2,1)} custom-call(bf16[32,32,192]{2,1,0:T(8,128)(2,1)} %get-tuple-element.52.inner_ref, f32[32,8,192]{2,1,0:T(8,128)S(1)} %get-tuple-element.53.west_ref, f32[32,8,192]{2,1,0:T(8,128)S(1)} %get-tuple-element.54.east_ref, ...), custom_call_target="tpu_custom_call", output_to_operand_aliasing={{}: (0, {})} | custom-call | flops 5000000 | bytes 700000 | tf_op jit(solution)/shard_map/pallas_call | solution.py:556
  (1 shorter events, 0.0 us)
Async XLA Ops:
  1.4 32.5 %copy-start = (bf16[2,1,32,32,192]{4,3,2,1,0:T(8,128)(2,1)S(1)}, bf16[2,1,32,32,192]{4,3,2,1,0:T(8,128)(2,1)}, u32[]{:S(2)}) copy-start(bf16[2,1,32,32,192]{4,3,2,1,0:T(8,128)(2,1)} %state_ref.2) | copy-start | bytes 2359300
  1.4 37.4 %copy-start.10 = (f32[768]{0:T(1024)S(1)}, f32[768]{0:T(1024)}, u32[]{:S(2)}) copy-start(f32[768]{0:T(1024)} %param.16) | copy-start | bytes 9220
  1.4 45.0 %copy-start.1 = (bf16[1,32,32,192]{3,2,1,0:T(8,128)(2,1)S(1)}, bf16[1,32,32,192]{3,2,1,0:T(8,128)(2,1)}, u32[]{:S(2)}) copy-start(bf16[1,32,32,192]{3,2,1,0:T(8,128)(2,1)} %base_ref.1) | copy-start | bytes 1179652
  1.4 45.0 %copy-start.4 = (f32[7,7,192]{2,1,0:T(8,128)S(1)}, f32[7,7,192]{2,1,0:T(8,128)}, u32[]{:S(2)}) copy-start(f32[7,7,192]{2,1,0:T(8,128)} %kernel_ref.9) | copy-start | bytes 112900
  1.5 45.0 %copy-start.5 = (bf16[192,768]{1,0:T(8,128)(2,1)S(1)}, bf16[192,768]{1,0:T(8,128)(2,1)}, u32[]{:S(2)}) copy-start(bf16[192,768]{1,0:T(8,128)(2,1)} %up_ref.5) | copy-start | bytes 884740
  1.5 45.0 %copy-start.6 = (bf16[768,192]{0,1:T(8,128)(2,1)S(1)}, bf16[768,192]{0,1:T(8,128)(2,1)}, u32[]{:S(2)}) copy-start(bf16[768,192]{0,1:T(8,128)(2,1)} %param.17) | copy-start | bytes 884740
  1.5 45.0 %copy-start.7 = (f32[192]{0:T(256)S(1)}, f32[192]{0:T(256)}, u32[]{:S(2)}) copy-start(f32[192]{0:T(256)} %param.14) | copy-start | bytes 2308
  18.7 37.6 %all-to-all-start.1 = ((bf16[16,32,384]{2,1,0:T(8,128)(2,1)}), bf16[16,32,384]{2,1,0:T(8,128)(2,1)S(1)}, u32[]{:S(2)}, u32[]{:S(2)}) async-start(bf16[16,32,384]{2,1,0:T(8,128)(2,1)} %shard_map.110), calls=%async_computation.1 | async-start | bytes 786432 | tf_op jit(solution)/shard_map/all_to_all | solution.py:585
  34.0 5.4 %collective-permute-start.1 = (bf16[2,32,3,192]{3,2,1,0:T(4,128)(2,1)S(1)}, bf16[2,32,3,192]{3,2,1,0:T(4,128)(2,1)S(1)}, u32[]{:S(2)}, u32[]{:S(2)}) collective-permute-start(bf16[2,32,3,192]{3,2,1,0:T(4,128)(2,1)S(1)} %get-tuple-element.57), channel_id=1, source_target_pairs={{1,0},{2,1},{3,2},{4,3},{5,4},{6,5},{7,6},{8,7},{9,8},{10,9},{11,1... | collective-permute-start | bytes 221192 | tf_op jit(solution)/shard_map/ppermute | solution.py:575
  36.9 9.6 %collective-permute-start = (bf16[2,32,3,192]{3,2,1,0:T(4,128)(2,1)S(1)}, bf16[2,32,3,192]{3,2,1,0:T(4,128)(2,1)S(1)}, u32[]{:S(2)}, u32[]{:S(2)}) collective-permute-start(bf16[2,32,3,192]{3,2,1,0:T(4,128)(2,1)S(1)} %get-tuple-element.58), channel_id=1, source_target_pairs={{0,1},{1,2},{2,3},{3,4},{4,5},{5,6},{6,7},{7,8},{8,9},{9,10},{10,1... | collective-permute-start | bytes 221192 | tf_op jit(solution)/shard_map/ppermute | solution.py:576
  54.9 13.3 %copy-start.12 = (bf16[32,3,192]{2,1,0:T(4,128)(2,1)S(1)}, bf16[32,3,192]{2,1,0:T(4,128)(2,1)}, u32[]{:S(2)}) copy-start(bf16[32,3,192]{2,1,0:T(4,128)(2,1)} %get-tuple-element.38) | copy-start | bytes 110596
  54.9 15.2 %copy-start.11 = (bf16[32,3,192]{2,1,0:T(4,128)(2,1)S(1)}, bf16[32,3,192]{2,1,0:T(4,128)(2,1)}, u32[]{:S(2)}) copy-start(bf16[32,3,192]{2,1,0:T(4,128)(2,1)} %get-tuple-element.44) | copy-start | bytes 110596
  54.9 17.6 %copy-start.8 = (bf16[32,3,192]{2,1,0:T(4,128)(2,1)S(1)}, bf16[32,3,192]{2,1,0:T(4,128)(2,1)}, u32[]{:S(2)}) copy-start(bf16[32,3,192]{2,1,0:T(4,128)(2,1)} %get-tuple-element.41.right_ref) | copy-start | bytes 110596
  54.9 17.6 %copy-start.9 = (bf16[32,3,192]{2,1,0:T(4,128)(2,1)S(1)}, bf16[32,3,192]{2,1,0:T(4,128)(2,1)}, u32[]{:S(2)}) copy-start(bf16[32,3,192]{2,1,0:T(4,128)(2,1)} %get-tuple-element.40.left_ref) | copy-start | bytes 110596
  57.4 30.8 %all-to-all-start.2 = ((bf16[16,32,384]{2,1,0:T(8,128)(2,1)}), bf16[16,32,384]{2,1,0:T(8,128)(2,1)S(1)}, u32[]{:S(2)}, u32[]{:S(2)}) async-start(bf16[16,32,384]{2,1,0:T(8,128)(2,1)} %shard_map.112), calls=%async_computation.2 | async-start | bytes 786432 | tf_op jit(solution)/shard_map/all_to_all | solution.py:585
  68.2 12.2 %collective-permute-start.2 = (bf16[32,3,192]{2,1,0:T(4,128)(2,1)S(1)}, bf16[32,3,192]{2,1,0:T(4,128)(2,1)S(1)}, u32[]{:S(2)}, u32[]{:S(2)}) collective-permute-start(bf16[32,3,192]{2,1,0:T(4,128)(2,1)S(1)} %copy-done.12), channel_id=1, source_target_pairs={{1,0},{2,1},{3,2},{4,3},{5,4},{6,5},{7,6},{8,7},{9,8},{10,9},{11,1... | collective-permute-start | bytes 110600 | tf_op jit(solution)/shard_map/ppermute | solution.py:575
  70.1 10.3 %collective-permute-start.3 = (bf16[32,3,192]{2,1,0:T(4,128)(2,1)S(1)}, bf16[32,3,192]{2,1,0:T(4,128)(2,1)S(1)}, u32[]{:S(2)}, u32[]{:S(2)}) collective-permute-start(bf16[32,3,192]{2,1,0:T(4,128)(2,1)S(1)} %copy-done.11), channel_id=1, source_target_pairs={{0,1},{1,2},{2,3},{3,4},{4,5},{5,6},{6,7},{7,8},{8,9},{9,10},{10,1... | collective-permute-start | bytes 110600 | tf_op jit(solution)/shard_map/ppermute | solution.py:576
  72.5 7.9 %copy-start.2 = (bf16[1,32,32,192]{3,2,1,0:T(8,128)(2,1)S(1)}, bf16[1,32,32,192]{3,2,1,0:T(8,128)(2,1)}, u32[]{:S(2)}) copy-start(bf16[1,32,32,192]{3,2,1,0:T(8,128)(2,1)} %base_ref.1) | copy-start | bytes 1179652
  72.5 7.9 %copy-start.3 = (bf16[32,32,192]{2,1,0:T(8,128)(2,1)S(1)}, bf16[32,32,192]{2,1,0:T(8,128)(2,1)}, u32[]{:S(2)}) copy-start(bf16[32,32,192]{2,1,0:T(8,128)(2,1)} %get-tuple-element.34.hidden_ref) | copy-start | bytes 1179652
  90.7 10.4 %collective-permute-start.4 = (bf16[32,3,192]{2,1,0:T(4,128)(2,1)S(1)}, bf16[32,3,192]{2,1,0:T(4,128)(2,1)S(1)}, u32[]{:S(2)}, u32[]{:S(2)}) collective-permute-start(bf16[32,3,192]{2,1,0:T(4,128)(2,1)S(1)} %get-tuple-element.55), channel_id=1, source_target_pairs={{1,0},{2,1},{3,2},{4,3},{5,4},{6,5},{7,6},{8,7},{9,8},{10,9},{11,1... | collective-permute-start | bytes 110600 | tf_op jit(solution)/shard_map/ppermute | solution.py:575
  94.4 8.9 %collective-permute-start.5 = (bf16[32,3,192]{2,1,0:T(4,128)(2,1)S(1)}, bf16[32,3,192]{2,1,0:T(4,128)(2,1)S(1)}, u32[]{:S(2)}, u32[]{:S(2)}) collective-permute-start(bf16[32,3,192]{2,1,0:T(4,128)(2,1)S(1)} %get-tuple-element.56), channel_id=1, source_target_pairs={{0,1},{1,2},{2,3},{3,4},{4,5},{5,6},{6,7},{7,8},{8,9},{9,10},{10,1... | collective-permute-start | bytes 110600 | tf_op jit(solution)/shard_map/ppermute | solution.py:576
